TPU v7x, 128 devices: a whole 4x4x4 slice. The times are simulated.
128 devices in a mesh: row: 8 (over y, core), col: 16 (over x, z).
Axes of the slice: x: 4, y: 4, z: 4, core: 2. Of those that a mesh axis runs over, the one named last changes fastest.
Arguments:
- coords: float32 [3, 32, 256, 128], P(None, 'row', 'col'), may hold values from 0 to 256
- sources: float32 [8, 32, 256, 128], P(None, 'row', 'col'), may hold values from -6 to 6
- neighbour_mask: int32 [9, 32, 256], P(None, 'row', 'col'), may hold values 0 or 1
- compress: float32 [32, 256, 32, 128], P('row', 'col'), may hold values from -0.5 to 0.5
- expand: float32 [32, 256, 32, 128], P('row', 'col'), may hold values from -1 to 1
- row_transfer: float32 [2, 8, 16, 32, 32], P(None, 'row', 'col'), may hold values from -0.75 to 0.75
- col_transfer: float32 [2, 8, 16, 32, 32], P(None, 'row', 'col'), may hold values from -0.75 to 0.75
Outputs:
- potential: float32 [8, 32, 256, 128], P(None, 'row', 'col')
All inputs are finite; a program needn't handle non-finite values. No bound on the sum of `neighbour_mask` on one device may be relied on, other than what follows from the above.
Results may differ from a plain program's by a relative error of at most 0.0003.
Values sent between devices are 32-bit elements; how exact they have to be, the bound alone decides.
No kernel may reach another device: no remote copies, remote signals or barrier semaphores. Data moves between devices by JAX's collectives and lax.ppermute only.
A program may use at most 64 MiB of HBM per device.

v0:
```python
import jax
import jax.numpy as jnp
from jax import lax
from jax.sharding import PartitionSpec as P

wave_number = 6.0
softening = 0.05
near_scale = 1.0 / 32.0
highest = lax.Precision.HIGHEST


def extended(value, sides, width):
    for axis, dim in sides:
        size, length = (lax.axis_size(axis), value.shape[dim])
        up = [(i, (i + 1) % size) for i in range(size - 1)]
        down = [(j, i) for i, j in up]
        last = lax.slice_in_dim(value, length - width, length, axis=dim)
        initial = lax.slice_in_dim(value, 0, width, axis=dim)
        before = lax.ppermute(last, axis, up)
        after = lax.ppermute(initial, axis, down)
        value = jnp.concatenate([before, value, after], axis=dim)
    return value


def partner_2(block, axis, distance):
    count = lax.axis_size(axis)
    route = []
    for low in range(count):
        high = low | 1 << distance
        if high != low and high < count:
            route += [(low, high), (high, low)]
    return lax.ppermute(block, axis, route)


def near_row(window, mask_row):
    leaf_cols = window.shape[2] - 2
    points = window.shape[3]
    target = window[0:3, 1, 1 : leaf_cols + 1]
    accumulated = jnp.zeros((window.shape[0] - 3, leaf_cols, points), jnp.float32)
    for row_shift in range(3):
        for col_shift in range(3):
            source_leaf = window[:, row_shift, col_shift : col_shift + leaf_cols]
            distance_sq = jnp.zeros((leaf_cols, points, points), jnp.float32)
            for component in range(3):
                spacing = target[component][:, :, None] - source_leaf[component][:, None, :]
                distance_sq = distance_sq + spacing * spacing
            kernel = jnp.cos(wave_number * jnp.sqrt(distance_sq)) / jnp.sqrt(
                distance_sq + softening * softening
            )
            part_sum = jnp.einsum("cts,xcs->xct", kernel, source_leaf[3:], precision=highest)
            weight = mask_row[row_shift * 3 + col_shift].astype(jnp.float32)
            accumulated = accumulated + part_sum * weight[None, :, None]
    return near_scale * accumulated


def near_field(padded, neighbour_mask):

    def one_row(leaf_row):
        window = lax.dynamic_slice_in_dim(padded, leaf_row, 3, 1)
        mask_row = lax.dynamic_index_in_dim(neighbour_mask, leaf_row, 1, keepdims=False)
        return near_row(window, mask_row)

    rows_out = lax.map(one_row, jnp.arange(neighbour_mask.shape[1], dtype=jnp.int32))
    return jnp.transpose(rows_out, (1, 0, 2, 3))


def pair_level(blocks, coeffs, partner):
    own_term = jnp.dot(blocks[0], coeffs, precision=highest, preferred_element_type=jnp.float32)
    other_term = jnp.dot(blocks[1], partner, precision=highest, preferred_element_type=jnp.float32)
    return own_term + other_term


def shards(coords, sources, neighbour_mask, compress, expand, row_transfer, col_transfer):
    stacked = jnp.concatenate([coords, sources], axis=0)
    padded = extended(stacked, (("row", 1), ("col", 2)), 1)
    near = near_field(padded, neighbour_mask)
    rhs_count, leaf_rows, leaf_cols = (sources.shape[0], sources.shape[1], sources.shape[2])
    rank_size = compress.shape[2]
    coeffs = jnp.einsum("lmqs,xlms->qxlm", compress, sources, precision=highest)
    coeffs = coeffs.reshape(rank_size, rhs_count * leaf_rows * leaf_cols)
    row_blocks = row_transfer[:, 0, 0]
    for bit in range(lax.axis_size("row").bit_length() - 1):
        partner = partner_2(coeffs, "row", bit)
        coeffs = pair_level(row_blocks, coeffs, partner)
    col_blocks = col_transfer[:, 0, 0]
    for bit in range(lax.axis_size("col").bit_length() - 1):
        partner = partner_2(coeffs, "col", bit)
        coeffs = pair_level(col_blocks, coeffs, partner)
    coeffs = coeffs.reshape(rank_size, rhs_count, leaf_rows, leaf_cols)
    far = jnp.einsum("lmqt,qxlm->xlmt", expand, coeffs, precision=highest)
    return near + far


def solution(mesh):
    in_specs = (
        P(None, "row", "col", None),
        P(None, "row", "col", None),
        P(None, "row", "col"),
        P("row", "col", None, None),
        P("row", "col", None, None),
        P(None, "row", "col", None, None),
        P(None, "row", "col", None, None),
    )
    out_specs = P(None, "row", "col", None)
    return jax.shard_map(shards, mesh=mesh, in_specs=in_specs, out_specs=out_specs, check_vma=False)
```

profile of v0, /device:TPU:0, one launch (start us, length us, event | category | flops | bytes accessed | tf_op | source)
XLA Modules:
  0.0 334.1 jit_solution(4701159569245625070)
XLA Ops:
  0.0 3.2 convolution_bitcast_fusion.1
  3.3 0.8 copy-done.1
  4.4 1.6 collective-permute-start
  6.0 1.3 collective-permute-start.1
  8.2 2.7 collective-permute-done.1
  10.9 3.8 %collective-permute-start.2 = (f32[11,6,1,128]{3,0,2,1:T(8,128)S(1)}, f32[11,6,1,128]{3,0,2,1:T(8,128)S(1)}, u32[]{:S(2)}, u32[]{:S(2)}) collective-permute-start(f32[11,6,1,128]{3,0,2,1:T(8,128)S(1)} %get-tuple-element.79), channel_id=1, source_target_pairs={{0,1},{1,2},{2,3},{3,4},{4,5},{5,6},{6,7},{7,8},{8,9},{9,10},{10,1... | collective-permute-start | bytes 101384 | tf_op jit(solution)/shard_map/ppermute | solution.py:19
  14.7 1.3 collective-permute-start.3
  16.2 3.4 %collective-permute-start.5 = (f32[32,512]{1,0:T(8,128)S(1)}, f32[32,512]{1,0:T(8,128)S(1)}, u32[]{:S(2)}, u32[]{:S(2)}) collective-permute-start(f32[32,512]{1,0:T(8,128)S(1)} %bitcast.226), channel_id=1, source_target_pairs={{0,32},{32,0},{16,48},{48,16},{64,96},{96,64},{80,112},{112,80},{1... | collective-permute-start | bytes 196616 | tf_op jit(solution)/shard_map/ppermute | solution.py:32
  19.6 1.1 collective-permute-done.3
  20.8 281.6 %while.10 = (s32[]{:T(128)}, f32[4,8,16,128]{3,1,2,0:T(8,128)S(1)}, s32[4]{0:T(128)S(1)}, f32[11,6,18,128]{3,0,2,1:T(8,128)S(1)}, s32[9,4,16]{2,1,0:T(4,128)}, /...) while((s32[]{:T(128)}, f32[4,8,16,128]{3,1,2,0:T(8,128)S(1)}, ...), condition=%wide.region_1.2_spmd, body=%wide.region_0.1_spmd.sunk | while | flops 252739744 | bytes 2594936 | solution.py:63
  24.5 0.8 fusion.336
  25.3 7.3 %convolution_multiply_fusion.10 = f32[16,8,128]{2,1,0:T(8,128)S(1)} fusion(f32[16,128]{1,0:T(8,128)S(1)} %bitcast.280, f32[16,128]{1,0:T(8,128)S(1)} %bitcast.234, f32[16,128]{1,0:T(8,128)S(1)} %bitcast.281, f32[16,128]{1,0:T(8,128)S(1)} %bitcast.243, f32[16,128]{1,0:T(8,128)S(1)} %bitcast.282, f32[16,128]{1,0:T(8,128)S(1)} %bitcast.252, ...), kind=kOutput, calls=%fused_computation.19.clone.1 | convolution fusion | flops 28065792 | bytes 180744 | tf_op jit(solution)/shard_map/while/body/eval_jaxpr/cts,xcs->xct/dot_general | solution.py:50
  32.6 7.3 %fusion.337 = f32[16,8,128]{2,1,0:T(8,128)S(1)} fusion(f32[16,8,128]{2,1,0:T(8,128)S(1)} %convolution_multiply_fusion.10, f32[16,128]{1,0:T(8,128)S(1)} %bitcast.277, f32[16,128]{1,0:T(8,128)S(1)} %bitcast.278, f32[16,128]{1,0:T(8,128)S(1)} %bitcast.279, f32[16,128]{1,0:T(8,128)S(1)} %bitcast.235, f32[16,128]{1,0:T(8,128)S(1)} %bitcast.244, ...), kind=kOutput, calls=%fused_computation.18.clone.1 | convolution fusion | flops 28082176 | bytes 246284 | tf_op jit(solution)/shard_map/while/body/eval_jaxpr/cts,xcs->xct/dot_general | solution.py:50
  39.9 7.3 %fusion.338 = f32[16,8,128]{2,1,0:T(8,128)S(1)} fusion(f32[16,8,128]{2,1,0:T(8,128)S(1)} %fusion.337, f32[16,128]{1,0:T(8,128)S(1)} %bitcast.274, f32[16,128]{1,0:T(8,128)S(1)} %bitcast.275, f32[16,128]{1,0:T(8,128)S(1)} %bitcast.276, f32[16,128]{1,0:T(8,128)S(1)} %bitcast.236, f32[16,128]{1,0:T(8,128)S(1)} %bitcast.245, ...), kind=kOutput, calls=%fused_computation.16.clone.1 | convolution fusion | flops 28082176 | bytes 246284 | tf_op jit(solution)/shard_map/while/body/eval_jaxpr/cts,xcs->xct/dot_general | solution.py:50
  47.3 7.3 %fusion.339 = f32[16,8,128]{2,1,0:T(8,128)S(1)} fusion(f32[16,8,128]{2,1,0:T(8,128)S(1)} %fusion.338, f32[16,128]{1,0:T(8,128)S(1)} %bitcast.271, f32[16,128]{1,0:T(8,128)S(1)} %bitcast.272, f32[16,128]{1,0:T(8,128)S(1)} %bitcast.273, f32[16,128]{1,0:T(8,128)S(1)} %bitcast.237, f32[16,128]{1,0:T(8,128)S(1)} %bitcast.246, ...), kind=kOutput, calls=%fused_computation.14.clone.1 | convolution fusion | flops 28082176 | bytes 246280 | tf_op jit(solution)/shard_map/while/body/eval_jaxpr/cts,xcs->xct/dot_general | solution.py:50
  54.6 7.3 %fusion.340 = f32[16,8,128]{2,1,0:T(8,128)S(1)} fusion(f32[16,8,128]{2,1,0:T(8,128)S(1)} %fusion.339, f32[16,128]{1,0:T(8,128)S(1)} %bitcast.238, f32[16,128]{1,0:T(8,128)S(1)} %bitcast.247, f32[16,128]{1,0:T(8,128)S(1)} %bitcast.256, f32[11,6,18,128]{3,0,2,1:T(8,128)S(1)} %get-tuple-element.223, s32[]{:T(128)S(6)} %add.489, s32[]{:T(128)S(6)} %add.488, ...), kind=kOutput, calls=%fused_computation.12.clone.1 | convolution fusion | flops 28082176 | bytes 246284 | tf_op jit(solution)/shard_map/while/body/eval_jaxpr/cts,xcs->xct/dot_general | solution.py:50
  61.9 7.3 %fusion.341 = f32[16,8,128]{2,1,0:T(8,128)S(1)} fusion(f32[16,8,128]{2,1,0:T(8,128)S(1)} %fusion.340, f32[16,128]{1,0:T(8,128)S(1)} %bitcast.268, f32[16,128]{1,0:T(8,128)S(1)} %bitcast.269, f32[16,128]{1,0:T(8,128)S(1)} %bitcast.270, f32[16,128]{1,0:T(8,128)S(1)} %bitcast.239, f32[16,128]{1,0:T(8,128)S(1)} %bitcast.248, ...), kind=kOutput, calls=%fused_computation.10.clone.1 | convolution fusion | flops 28082176 | bytes 246284 | tf_op jit(solution)/shard_map/while/body/eval_jaxpr/cts,xcs->xct/dot_general | solution.py:50
  69.2 7.3 %fusion.342 = f32[16,8,128]{2,1,0:T(8,128)S(1)} fusion(f32[16,8,128]{2,1,0:T(8,128)S(1)} %fusion.341, f32[16,128]{1,0:T(8,128)S(1)} %bitcast.265, f32[16,128]{1,0:T(8,128)S(1)} %bitcast.266, f32[16,128]{1,0:T(8,128)S(1)} %bitcast.267, f32[16,128]{1,0:T(8,128)S(1)} %bitcast.240, f32[16,128]{1,0:T(8,128)S(1)} %bitcast.249, ...), kind=kOutput, calls=%fused_computation.8.clone.1 | convolution fusion | flops 28082176 | bytes 246280 | tf_op jit(solution)/shard_map/while/body/eval_jaxpr/cts,xcs->xct/dot_general | solution.py:50
  76.5 7.3 %fusion.343 = f32[16,8,128]{2,1,0:T(8,128)S(1)} fusion(f32[16,8,128]{2,1,0:T(8,128)S(1)} %fusion.342, f32[16,128]{1,0:T(8,128)S(1)} %bitcast.262, f32[16,128]{1,0:T(8,128)S(1)} %bitcast.263, f32[16,128]{1,0:T(8,128)S(1)} %bitcast.264, f32[16,128]{1,0:T(8,128)S(1)} %bitcast.241, f32[16,128]{1,0:T(8,128)S(1)} %bitcast.250, ...), kind=kOutput, calls=%fused_computation.6.clone.1 | convolution fusion | flops 28082176 | bytes 246284 | tf_op jit(solution)/shard_map/while/body/eval_jaxpr/cts,xcs->xct/dot_general | solution.py:50
  83.8 7.3 %fusion.344 = f32[4,8,16,128]{3,1,2,0:T(8,128)S(1)} fusion(f32[4,8,16,128]{3,1,2,0:T(8,128)S(1)} %get-tuple-element.204, s32[]{:T(128)} %get-tuple-element.203, f32[16,8,128]{2,1,0:T(8,128)S(1)} %fusion.343, f32[16,128]{1,0:T(8,128)S(1)} %bitcast.261, f32[16,128]{1,0:T(8,128)S(1)} %bitcast.233, f32[16,128]{1,0:T(8,128)S(1)} %bitcast.232, ...), kind=kOutput, calls=%fused_computation.4.clone.1 | convolution fusion | flops 28098560 | bytes 246288 | tf_op jit(solution)/shard_map/while/body/eval_jaxpr/cts,xcs->xct/dot_general | solution.py:50
  91.2 0.6 dynamic_slice.12
  94.9 0.8 fusion.336
  95.7 7.3 %convolution_multiply_fusion.10 = f32[16,8,128]{2,1,0:T(8,128)S(1)} fusion(f32[16,128]{1,0:T(8,128)S(1)} %bitcast.280, f32[16,128]{1,0:T(8,128)S(1)} %bitcast.234, f32[16,128]{1,0:T(8,128)S(1)} %bitcast.281, f32[16,128]{1,0:T(8,128)S(1)} %bitcast.243, f32[16,128]{1,0:T(8,128)S(1)} %bitcast.282, f32[16,128]{1,0:T(8,128)S(1)} %bitcast.252, ...), kind=kOutput, calls=%fused_computation.19.clone.1 | convolution fusion | flops 28065792 | bytes 180744 | tf_op jit(solution)/shard_map/while/body/eval_jaxpr/cts,xcs->xct/dot_general | solution.py:50
  103.0 7.3 %fusion.337 = f32[16,8,128]{2,1,0:T(8,128)S(1)} fusion(f32[16,8,128]{2,1,0:T(8,128)S(1)} %convolution_multiply_fusion.10, f32[16,128]{1,0:T(8,128)S(1)} %bitcast.277, f32[16,128]{1,0:T(8,128)S(1)} %bitcast.278, f32[16,128]{1,0:T(8,128)S(1)} %bitcast.279, f32[16,128]{1,0:T(8,128)S(1)} %bitcast.235, f32[16,128]{1,0:T(8,128)S(1)} %bitcast.244, ...), kind=kOutput, calls=%fused_computation.18.clone.1 | convolution fusion | flops 28082176 | bytes 246284 | tf_op jit(solution)/shard_map/while/body/eval_jaxpr/cts,xcs->xct/dot_general | solution.py:50
  110.3 7.3 %fusion.338 = f32[16,8,128]{2,1,0:T(8,128)S(1)} fusion(f32[16,8,128]{2,1,0:T(8,128)S(1)} %fusion.337, f32[16,128]{1,0:T(8,128)S(1)} %bitcast.274, f32[16,128]{1,0:T(8,128)S(1)} %bitcast.275, f32[16,128]{1,0:T(8,128)S(1)} %bitcast.276, f32[16,128]{1,0:T(8,128)S(1)} %bitcast.236, f32[16,128]{1,0:T(8,128)S(1)} %bitcast.245, ...), kind=kOutput, calls=%fused_computation.16.clone.1 | convolution fusion | flops 28082176 | bytes 246284 | tf_op jit(solution)/shard_map/while/body/eval_jaxpr/cts,xcs->xct/dot_general | solution.py:50
  117.6 7.3 %fusion.339 = f32[16,8,128]{2,1,0:T(8,128)S(1)} fusion(f32[16,8,128]{2,1,0:T(8,128)S(1)} %fusion.338, f32[16,128]{1,0:T(8,128)S(1)} %bitcast.271, f32[16,128]{1,0:T(8,128)S(1)} %bitcast.272, f32[16,128]{1,0:T(8,128)S(1)} %bitcast.273, f32[16,128]{1,0:T(8,128)S(1)} %bitcast.237, f32[16,128]{1,0:T(8,128)S(1)} %bitcast.246, ...), kind=kOutput, calls=%fused_computation.14.clone.1 | convolution fusion | flops 28082176 | bytes 246280 | tf_op jit(solution)/shard_map/while/body/eval_jaxpr/cts,xcs->xct/dot_general | solution.py:50
  125.0 7.3 %fusion.340 = f32[16,8,128]{2,1,0:T(8,128)S(1)} fusion(f32[16,8,128]{2,1,0:T(8,128)S(1)} %fusion.339, f32[16,128]{1,0:T(8,128)S(1)} %bitcast.238, f32[16,128]{1,0:T(8,128)S(1)} %bitcast.247, f32[16,128]{1,0:T(8,128)S(1)} %bitcast.256, f32[11,6,18,128]{3,0,2,1:T(8,128)S(1)} %get-tuple-element.223, s32[]{:T(128)S(6)} %add.489, s32[]{:T(128)S(6)} %add.488, ...), kind=kOutput, calls=%fused_computation.12.clone.1 | convolution fusion | flops 28082176 | bytes 246284 | tf_op jit(solution)/shard_map/while/body/eval_jaxpr/cts,xcs->xct/dot_general | solution.py:50
  132.3 7.3 %fusion.341 = f32[16,8,128]{2,1,0:T(8,128)S(1)} fusion(f32[16,8,128]{2,1,0:T(8,128)S(1)} %fusion.340, f32[16,128]{1,0:T(8,128)S(1)} %bitcast.268, f32[16,128]{1,0:T(8,128)S(1)} %bitcast.269, f32[16,128]{1,0:T(8,128)S(1)} %bitcast.270, f32[16,128]{1,0:T(8,128)S(1)} %bitcast.239, f32[16,128]{1,0:T(8,128)S(1)} %bitcast.248, ...), kind=kOutput, calls=%fused_computation.10.clone.1 | convolution fusion | flops 28082176 | bytes 246284 | tf_op jit(solution)/shard_map/while/body/eval_jaxpr/cts,xcs->xct/dot_general | solution.py:50
  139.6 7.3 %fusion.342 = f32[16,8,128]{2,1,0:T(8,128)S(1)} fusion(f32[16,8,128]{2,1,0:T(8,128)S(1)} %fusion.341, f32[16,128]{1,0:T(8,128)S(1)} %bitcast.265, f32[16,128]{1,0:T(8,128)S(1)} %bitcast.266, f32[16,128]{1,0:T(8,128)S(1)} %bitcast.267, f32[16,128]{1,0:T(8,128)S(1)} %bitcast.240, f32[16,128]{1,0:T(8,128)S(1)} %bitcast.249, ...), kind=kOutput, calls=%fused_computation.8.clone.1 | convolution fusion | flops 28082176 | bytes 246280 | tf_op jit(solution)/shard_map/while/body/eval_jaxpr/cts,xcs->xct/dot_general | solution.py:50
  146.9 7.3 %fusion.343 = f32[16,8,128]{2,1,0:T(8,128)S(1)} fusion(f32[16,8,128]{2,1,0:T(8,128)S(1)} %fusion.342, f32[16,128]{1,0:T(8,128)S(1)} %bitcast.262, f32[16,128]{1,0:T(8,128)S(1)} %bitcast.263, f32[16,128]{1,0:T(8,128)S(1)} %bitcast.264, f32[16,128]{1,0:T(8,128)S(1)} %bitcast.241, f32[16,128]{1,0:T(8,128)S(1)} %bitcast.250, ...), kind=kOutput, calls=%fused_computation.6.clone.1 | convolution fusion | flops 28082176 | bytes 246284 | tf_op jit(solution)/shard_map/while/body/eval_jaxpr/cts,xcs->xct/dot_general | solution.py:50
  154.2 7.3 %fusion.344 = f32[4,8,16,128]{3,1,2,0:T(8,128)S(1)} fusion(f32[4,8,16,128]{3,1,2,0:T(8,128)S(1)} %get-tuple-element.204, s32[]{:T(128)} %get-tuple-element.203, f32[16,8,128]{2,1,0:T(8,128)S(1)} %fusion.343, f32[16,128]{1,0:T(8,128)S(1)} %bitcast.261, f32[16,128]{1,0:T(8,128)S(1)} %bitcast.233, f32[16,128]{1,0:T(8,128)S(1)} %bitcast.232, ...), kind=kOutput, calls=%fused_computation.4.clone.1 | convolution fusion | flops 28098560 | bytes 246288 | tf_op jit(solution)/shard_map/while/body/eval_jaxpr/cts,xcs->xct/dot_general | solution.py:50
  161.6 0.6 dynamic_slice.12
  165.3 0.8 fusion.336
  166.1 7.3 %convolution_multiply_fusion.10 = f32[16,8,128]{2,1,0:T(8,128)S(1)} fusion(f32[16,128]{1,0:T(8,128)S(1)} %bitcast.280, f32[16,128]{1,0:T(8,128)S(1)} %bitcast.234, f32[16,128]{1,0:T(8,128)S(1)} %bitcast.281, f32[16,128]{1,0:T(8,128)S(1)} %bitcast.243, f32[16,128]{1,0:T(8,128)S(1)} %bitcast.282, f32[16,128]{1,0:T(8,128)S(1)} %bitcast.252, ...), kind=kOutput, calls=%fused_computation.19.clone.1 | convolution fusion | flops 28065792 | bytes 180744 | tf_op jit(solution)/shard_map/while/body/eval_jaxpr/cts,xcs->xct/dot_general | solution.py:50
  173.4 7.3 %fusion.337 = f32[16,8,128]{2,1,0:T(8,128)S(1)} fusion(f32[16,8,128]{2,1,0:T(8,128)S(1)} %convolution_multiply_fusion.10, f32[16,128]{1,0:T(8,128)S(1)} %bitcast.277, f32[16,128]{1,0:T(8,128)S(1)} %bitcast.278, f32[16,128]{1,0:T(8,128)S(1)} %bitcast.279, f32[16,128]{1,0:T(8,128)S(1)} %bitcast.235, f32[16,128]{1,0:T(8,128)S(1)} %bitcast.244, ...), kind=kOutput, calls=%fused_computation.18.clone.1 | convolution fusion | flops 28082176 | bytes 246284 | tf_op jit(solution)/shard_map/while/body/eval_jaxpr/cts,xcs->xct/dot_general | solution.py:50
  180.7 7.3 %fusion.338 = f32[16,8,128]{2,1,0:T(8,128)S(1)} fusion(f32[16,8,128]{2,1,0:T(8,128)S(1)} %fusion.337, f32[16,128]{1,0:T(8,128)S(1)} %bitcast.274, f32[16,128]{1,0:T(8,128)S(1)} %bitcast.275, f32[16,128]{1,0:T(8,128)S(1)} %bitcast.276, f32[16,128]{1,0:T(8,128)S(1)} %bitcast.236, f32[16,128]{1,0:T(8,128)S(1)} %bitcast.245, ...), kind=kOutput, calls=%fused_computation.16.clone.1 | convolution fusion | flops 28082176 | bytes 246284 | tf_op jit(solution)/shard_map/while/body/eval_jaxpr/cts,xcs->xct/dot_general | solution.py:50
  188.0 7.3 %fusion.339 = f32[16,8,128]{2,1,0:T(8,128)S(1)} fusion(f32[16,8,128]{2,1,0:T(8,128)S(1)} %fusion.338, f32[16,128]{1,0:T(8,128)S(1)} %bitcast.271, f32[16,128]{1,0:T(8,128)S(1)} %bitcast.272, f32[16,128]{1,0:T(8,128)S(1)} %bitcast.273, f32[16,128]{1,0:T(8,128)S(1)} %bitcast.237, f32[16,128]{1,0:T(8,128)S(1)} %bitcast.246, ...), kind=kOutput, calls=%fused_computation.14.clone.1 | convolution fusion | flops 28082176 | bytes 246280 | tf_op jit(solution)/shard_map/while/body/eval_jaxpr/cts,xcs->xct/dot_general | solution.py:50
  195.4 7.3 %fusion.340 = f32[16,8,128]{2,1,0:T(8,128)S(1)} fusion(f32[16,8,128]{2,1,0:T(8,128)S(1)} %fusion.339, f32[16,128]{1,0:T(8,128)S(1)} %bitcast.238, f32[16,128]{1,0:T(8,128)S(1)} %bitcast.247, f32[16,128]{1,0:T(8,128)S(1)} %bitcast.256, f32[11,6,18,128]{3,0,2,1:T(8,128)S(1)} %get-tuple-element.223, s32[]{:T(128)S(6)} %add.489, s32[]{:T(128)S(6)} %add.488, ...), kind=kOutput, calls=%fused_computation.12.clone.1 | convolution fusion | flops 28082176 | bytes 246284 | tf_op jit(solution)/shard_map/while/body/eval_jaxpr/cts,xcs->xct/dot_general | solution.py:50
  202.7 7.3 %fusion.341 = f32[16,8,128]{2,1,0:T(8,128)S(1)} fusion(f32[16,8,128]{2,1,0:T(8,128)S(1)} %fusion.340, f32[16,128]{1,0:T(8,128)S(1)} %bitcast.268, f32[16,128]{1,0:T(8,128)S(1)} %bitcast.269, f32[16,128]{1,0:T(8,128)S(1)} %bitcast.270, f32[16,128]{1,0:T(8,128)S(1)} %bitcast.239, f32[16,128]{1,0:T(8,128)S(1)} %bitcast.248, ...), kind=kOutput, calls=%fused_computation.10.clone.1 | convolution fusion | flops 28082176 | bytes 246284 | tf_op jit(solution)/shard_map/while/body/eval_jaxpr/cts,xcs->xct/dot_general | solution.py:50
  210.0 7.3 %fusion.342 = f32[16,8,128]{2,1,0:T(8,128)S(1)} fusion(f32[16,8,128]{2,1,0:T(8,128)S(1)} %fusion.341, f32[16,128]{1,0:T(8,128)S(1)} %bitcast.265, f32[16,128]{1,0:T(8,128)S(1)} %bitcast.266, f32[16,128]{1,0:T(8,128)S(1)} %bitcast.267, f32[16,128]{1,0:T(8,128)S(1)} %bitcast.240, f32[16,128]{1,0:T(8,128)S(1)} %bitcast.249, ...), kind=kOutput, calls=%fused_computation.8.clone.1 | convolution fusion | flops 28082176 | bytes 246280 | tf_op jit(solution)/shard_map/while/body/eval_jaxpr/cts,xcs->xct/dot_general | solution.py:50
  217.3 7.3 %fusion.343 = f32[16,8,128]{2,1,0:T(8,128)S(1)} fusion(f32[16,8,128]{2,1,0:T(8,128)S(1)} %fusion.342, f32[16,128]{1,0:T(8,128)S(1)} %bitcast.262, f32[16,128]{1,0:T(8,128)S(1)} %bitcast.263, f32[16,128]{1,0:T(8,128)S(1)} %bitcast.264, f32[16,128]{1,0:T(8,128)S(1)} %bitcast.241, f32[16,128]{1,0:T(8,128)S(1)} %bitcast.250, ...), kind=kOutput, calls=%fused_computation.6.clone.1 | convolution fusion | flops 28082176 | bytes 246284 | tf_op jit(solution)/shard_map/while/body/eval_jaxpr/cts,xcs->xct/dot_general | solution.py:50
  224.6 7.3 %fusion.344 = f32[4,8,16,128]{3,1,2,0:T(8,128)S(1)} fusion(f32[4,8,16,128]{3,1,2,0:T(8,128)S(1)} %get-tuple-element.204, s32[]{:T(128)} %get-tuple-element.203, f32[16,8,128]{2,1,0:T(8,128)S(1)} %fusion.343, f32[16,128]{1,0:T(8,128)S(1)} %bitcast.261, f32[16,128]{1,0:T(8,128)S(1)} %bitcast.233, f32[16,128]{1,0:T(8,128)S(1)} %bitcast.232, ...), kind=kOutput, calls=%fused_computation.4.clone.1 | convolution fusion | flops 28098560 | bytes 246288 | tf_op jit(solution)/shard_map/while/body/eval_jaxpr/cts,xcs->xct/dot_general | solution.py:50
  235.6 0.8 fusion.336
  236.5 7.3 %convolution_multiply_fusion.10 = f32[16,8,128]{2,1,0:T(8,128)S(1)} fusion(f32[16,128]{1,0:T(8,128)S(1)} %bitcast.280, f32[16,128]{1,0:T(8,128)S(1)} %bitcast.234, f32[16,128]{1,0:T(8,128)S(1)} %bitcast.281, f32[16,128]{1,0:T(8,128)S(1)} %bitcast.243, f32[16,128]{1,0:T(8,128)S(1)} %bitcast.282, f32[16,128]{1,0:T(8,128)S(1)} %bitcast.252, ...), kind=kOutput, calls=%fused_computation.19.clone.1 | convolution fusion | flops 28065792 | bytes 180744 | tf_op jit(solution)/shard_map/while/body/eval_jaxpr/cts,xcs->xct/dot_general | solution.py:50
  243.8 7.3 %fusion.337 = f32[16,8,128]{2,1,0:T(8,128)S(1)} fusion(f32[16,8,128]{2,1,0:T(8,128)S(1)} %convolution_multiply_fusion.10, f32[16,128]{1,0:T(8,128)S(1)} %bitcast.277, f32[16,128]{1,0:T(8,128)S(1)} %bitcast.278, f32[16,128]{1,0:T(8,128)S(1)} %bitcast.279, f32[16,128]{1,0:T(8,128)S(1)} %bitcast.235, f32[16,128]{1,0:T(8,128)S(1)} %bitcast.244, ...), kind=kOutput, calls=%fused_computation.18.clone.1 | convolution fusion | flops 28082176 | bytes 246284 | tf_op jit(solution)/shard_map/while/body/eval_jaxpr/cts,xcs->xct/dot_general | solution.py:50
  251.1 7.3 %fusion.338 = f32[16,8,128]{2,1,0:T(8,128)S(1)} fusion(f32[16,8,128]{2,1,0:T(8,128)S(1)} %fusion.337, f32[16,128]{1,0:T(8,128)S(1)} %bitcast.274, f32[16,128]{1,0:T(8,128)S(1)} %bitcast.275, f32[16,128]{1,0:T(8,128)S(1)} %bitcast.276, f32[16,128]{1,0:T(8,128)S(1)} %bitcast.236, f32[16,128]{1,0:T(8,128)S(1)} %bitcast.245, ...), kind=kOutput, calls=%fused_computation.16.clone.1 | convolution fusion | flops 28082176 | bytes 246284 | tf_op jit(solution)/shard_map/while/body/eval_jaxpr/cts,xcs->xct/dot_general | solution.py:50
  258.4 7.3 %fusion.339 = f32[16,8,128]{2,1,0:T(8,128)S(1)} fusion(f32[16,8,128]{2,1,0:T(8,128)S(1)} %fusion.338, f32[16,128]{1,0:T(8,128)S(1)} %bitcast.271, f32[16,128]{1,0:T(8,128)S(1)} %bitcast.272, f32[16,128]{1,0:T(8,128)S(1)} %bitcast.273, f32[16,128]{1,0:T(8,128)S(1)} %bitcast.237, f32[16,128]{1,0:T(8,128)S(1)} %bitcast.246, ...), kind=kOutput, calls=%fused_computation.14.clone.1 | convolution fusion | flops 28082176 | bytes 246280 | tf_op jit(solution)/shard_map/while/body/eval_jaxpr/cts,xcs->xct/dot_general | solution.py:50
  265.7 7.3 %fusion.340 = f32[16,8,128]{2,1,0:T(8,128)S(1)} fusion(f32[16,8,128]{2,1,0:T(8,128)S(1)} %fusion.339, f32[16,128]{1,0:T(8,128)S(1)} %bitcast.238, f32[16,128]{1,0:T(8,128)S(1)} %bitcast.247, f32[16,128]{1,0:T(8,128)S(1)} %bitcast.256, f32[11,6,18,128]{3,0,2,1:T(8,128)S(1)} %get-tuple-element.223, s32[]{:T(128)S(6)} %add.489, s32[]{:T(128)S(6)} %add.488, ...), kind=kOutput, calls=%fused_computation.12.clone.1 | convolution fusion | flops 28082176 | bytes 246284 | tf_op jit(solution)/shard_map/while/body/eval_jaxpr/cts,xcs->xct/dot_general | solution.py:50
  273.1 7.3 %fusion.341 = f32[16,8,128]{2,1,0:T(8,128)S(1)} fusion(f32[16,8,128]{2,1,0:T(8,128)S(1)} %fusion.340, f32[16,128]{1,0:T(8,128)S(1)} %bitcast.268, f32[16,128]{1,0:T(8,128)S(1)} %bitcast.269, f32[16,128]{1,0:T(8,128)S(1)} %bitcast.270, f32[16,128]{1,0:T(8,128)S(1)} %bitcast.239, f32[16,128]{1,0:T(8,128)S(1)} %bitcast.248, ...), kind=kOutput, calls=%fused_computation.10.clone.1 | convolution fusion | flops 28082176 | bytes 246284 | tf_op jit(solution)/shard_map/while/body/eval_jaxpr/cts,xcs->xct/dot_general | solution.py:50
  280.4 7.3 %fusion.342 = f32[16,8,128]{2,1,0:T(8,128)S(1)} fusion(f32[16,8,128]{2,1,0:T(8,128)S(1)} %fusion.341, f32[16,128]{1,0:T(8,128)S(1)} %bitcast.265, f32[16,128]{1,0:T(8,128)S(1)} %bitcast.266, f32[16,128]{1,0:T(8,128)S(1)} %bitcast.267, f32[16,128]{1,0:T(8,128)S(1)} %bitcast.240, f32[16,128]{1,0:T(8,128)S(1)} %bitcast.249, ...), kind=kOutput, calls=%fused_computation.8.clone.1 | convolution fusion | flops 28082176 | bytes 246280 | tf_op jit(solution)/shard_map/while/body/eval_jaxpr/cts,xcs->xct/dot_general | solution.py:50
  287.7 7.3 %fusion.343 = f32[16,8,128]{2,1,0:T(8,128)S(1)} fusion(f32[16,8,128]{2,1,0:T(8,128)S(1)} %fusion.342, f32[16,128]{1,0:T(8,128)S(1)} %bitcast.262, f32[16,128]{1,0:T(8,128)S(1)} %bitcast.263, f32[16,128]{1,0:T(8,128)S(1)} %bitcast.264, f32[16,128]{1,0:T(8,128)S(1)} %bitcast.241, f32[16,128]{1,0:T(8,128)S(1)} %bitcast.250, ...), kind=kOutput, calls=%fused_computation.6.clone.1 | convolution fusion | flops 28082176 | bytes 246284 | tf_op jit(solution)/shard_map/while/body/eval_jaxpr/cts,xcs->xct/dot_general | solution.py:50
  295.0 7.3 %fusion.344 = f32[4,8,16,128]{3,1,2,0:T(8,128)S(1)} fusion(f32[4,8,16,128]{3,1,2,0:T(8,128)S(1)} %get-tuple-element.204, s32[]{:T(128)} %get-tuple-element.203, f32[16,8,128]{2,1,0:T(8,128)S(1)} %fusion.343, f32[16,128]{1,0:T(8,128)S(1)} %bitcast.261, f32[16,128]{1,0:T(8,128)S(1)} %bitcast.233, f32[16,128]{1,0:T(8,128)S(1)} %bitcast.232, ...), kind=kOutput, calls=%fused_computation.4.clone.1 | convolution fusion | flops 28098560 | bytes 246288 | tf_op jit(solution)/shard_map/while/body/eval_jaxpr/cts,xcs->xct/dot_general | solution.py:50
  302.6 5.1 %collective-permute-start.6 = (f32[32,512]{1,0:T(8,128)S(1)}, f32[32,512]{1,0:T(8,128)S(1)}, u32[]{:S(2)}, u32[]{:S(2)}) collective-permute-start(f32[32,512]{1,0:T(8,128)S(1)} %bitcast.227), channel_id=1, source_target_pairs={{0,64},{64,0},{16,80},{80,16},{32,96},{96,32},{48,112},{112,48},{1... | collective-permute-start | bytes 196616 | tf_op jit(solution)/shard_map/ppermute | solution.py:32
  307.9 2.5 collective-permute-done.6
  310.7 2.0 collective-permute-start.7
  312.9 2.1 collective-permute-done.7
  315.2 3.9 %collective-permute-start.8 = (f32[32,512]{1,0:T(8,128)S(1)}, f32[32,512]{1,0:T(8,128)S(1)}, u32[]{:S(2)}, u32[]{:S(2)}) collective-permute-start(f32[32,512]{1,0:T(8,128)S(1)} %bitcast.229), channel_id=1, source_target_pairs={{0,2},{2,0},{1,3},{3,1},{4,6},{6,4},{5,7},{7,5},{8,10},{10,8},{9,1... | collective-permute-start | bytes 196616 | tf_op jit(solution)/shard_map/ppermute | solution.py:32
  319.3 2.0 collective-permute-done.8
  321.5 1.6 collective-permute-start.9
  323.3 2.6 collective-permute-done.9
  326.1 3.2 collective-permute-start.10
  329.5 2.5 collective-permute-done.10
  332.3 1.1 fusion.254
  333.4 0.8 copy.19
  (43 shorter events, 6.1 us)
Async XLA Ops:
  0.0 332.3 %copy-start = (f32[4,16,32,128]{3,2,1,0:T(8,128)S(1)}, f32[4,16,32,128]{3,2,1,0:T(8,128)}, u32[]{:S(2)}) copy-start(f32[4,16,32,128]{3,2,1,0:T(8,128)} %param.13) | copy-start | bytes 3145732
  3.2 1.0 copy-start.1
  3.2 1.1 copy-start.4
  3.2 4.5 %collective-permute-start.4 = (f32[32,512]{0,1:T(8,128)S(1)}, f32[32,512]{0,1:T(8,128)S(1)}, u32[]{:S(2)}, u32[]{:S(2)}) collective-permute-start(f32[32,512]{0,1:T(8,128)S(1)} %bitcast.224), channel_id=1, source_target_pairs={{0,16},{16,0},{32,48},{48,32},{64,80},{80,64},{96,112},{112,96},{1... | collective-permute-start | bytes 196616 | tf_op jit(solution)/shard_map/ppermute | solution.py:32
  4.4 3.0 copy-start.3
  4.4 3.8 %collective-permute-start = (f32[11,1,16,128]{3,0,2,1:T(8,128)S(1)}, f32[11,1,16,128]{3,0,2,1:T(8,128)S(1)}, u32[]{:S(2)}, u32[]{:S(2)}) collective-permute-start(f32[11,1,16,128]{3,0,2,1:T(8,128)S(1)} %get-tuple-element.81), channel_id=1, source_target_pairs={{0,16},{16,32},{32,48},{48,64},{64,80},{80,96},{96,112},{1,17},{17... | collective-permute-start | bytes 270344 | tf_op jit(solution)/shard_map/ppermute | solution.py:19
  6.0 4.8 %collective-permute-start.1 = (f32[11,1,16,128]{3,0,2,1:T(8,128)S(1)}, f32[11,1,16,128]{3,0,2,1:T(8,128)S(1)}, u32[]{:S(2)}, u32[]{:S(2)}) collective-permute-start(f32[11,1,16,128]{3,0,2,1:T(8,128)S(1)} %get-tuple-element.82), channel_id=1, source_target_pairs={{16,0},{32,16},{48,32},{64,48},{80,64},{96,80},{112,96},{17,1},{33... | collective-permute-start | bytes 270344 | tf_op jit(solution)/shard_map/ppermute | solution.py:20
  10.9 8.7 %collective-permute-start.2 = (f32[11,6,1,128]{3,0,2,1:T(8,128)S(1)}, f32[11,6,1,128]{3,0,2,1:T(8,128)S(1)}, u32[]{:S(2)}, u32[]{:S(2)}) collective-permute-start(f32[11,6,1,128]{3,0,2,1:T(8,128)S(1)} %get-tuple-element.79), channel_id=1, source_target_pairs={{0,1},{1,2},{2,3},{3,4},{4,5},{5,6},{6,7},{7,8},{8,9},{9,10},{10,1... | collective-permute-start | bytes 101384 | tf_op jit(solution)/shard_map/ppermute | solution.py:19
  14.7 6.0 %collective-permute-start.3 = (f32[11,6,1,128]{3,0,2,1:T(8,128)S(1)}, f32[11,6,1,128]{3,0,2,1:T(8,128)S(1)}, u32[]{:S(2)}, u32[]{:S(2)}) collective-permute-start(f32[11,6,1,128]{3,0,2,1:T(8,128)S(1)} %get-tuple-element.80), channel_id=1, source_target_pairs={{1,0},{2,1},{3,2},{4,3},{5,4},{6,5},{7,6},{8,7},{9,8},{10,9},{11,1... | collective-permute-start | bytes 101384 | tf_op jit(solution)/shard_map/ppermute | solution.py:20
  16.2 286.1 %collective-permute-start.5 = (f32[32,512]{1,0:T(8,128)S(1)}, f32[32,512]{1,0:T(8,128)S(1)}, u32[]{:S(2)}, u32[]{:S(2)}) collective-permute-start(f32[32,512]{1,0:T(8,128)S(1)} %bitcast.226), channel_id=1, source_target_pairs={{0,32},{32,0},{16,48},{48,16},{64,96},{96,64},{80,112},{112,80},{1... | collective-permute-start | bytes 196616 | tf_op jit(solution)/shard_map/ppermute | solution.py:32
  302.6 7.9 %collective-permute-start.6 = (f32[32,512]{1,0:T(8,128)S(1)}, f32[32,512]{1,0:T(8,128)S(1)}, u32[]{:S(2)}, u32[]{:S(2)}) collective-permute-start(f32[32,512]{1,0:T(8,128)S(1)} %bitcast.227), channel_id=1, source_target_pairs={{0,64},{64,0},{16,80},{80,16},{32,96},{96,32},{48,112},{112,48},{1... | collective-permute-start | bytes 196616 | tf_op jit(solution)/shard_map/ppermute | solution.py:32
  307.9 4.8 %copy-start.2 = (f32[2,1,1,32,32]{4,3,2,1,0:T(8,128)S(1)}, f32[2,1,1,32,32]{4,3,2,1,0:T(8,128)}, u32[]{:S(2)}) copy-start(f32[2,1,1,32,32]{4,3,2,1,0:T(8,128)} %param.15) | copy-start | bytes 24580
  310.7 4.3 %collective-permute-start.7 = (f32[32,512]{1,0:T(8,128)S(1)}, f32[32,512]{1,0:T(8,128)S(1)}, u32[]{:S(2)}, u32[]{:S(2)}) collective-permute-start(f32[32,512]{1,0:T(8,128)S(1)} %bitcast.228), channel_id=1, source_target_pairs={{0,1},{1,0},{2,3},{3,2},{4,5},{5,4},{6,7},{7,6},{8,9},{9,8},{10,11... | collective-permute-start | bytes 196616 | tf_op jit(solution)/shard_map/ppermute | solution.py:32
  315.2 6.1 %collective-permute-start.8 = (f32[32,512]{1,0:T(8,128)S(1)}, f32[32,512]{1,0:T(8,128)S(1)}, u32[]{:S(2)}, u32[]{:S(2)}) collective-permute-start(f32[32,512]{1,0:T(8,128)S(1)} %bitcast.229), channel_id=1, source_target_pairs={{0,2},{2,0},{1,3},{3,1},{4,6},{6,4},{5,7},{7,5},{8,10},{10,8},{9,1... | collective-permute-start | bytes 196616 | tf_op jit(solution)/shard_map/ppermute | solution.py:32
  321.5 4.3 %collective-permute-start.9 = (f32[32,512]{1,0:T(8,128)S(1)}, f32[32,512]{1,0:T(8,128)S(1)}, u32[]{:S(2)}, u32[]{:S(2)}) collective-permute-start(f32[32,512]{1,0:T(8,128)S(1)} %bitcast.230), channel_id=1, source_target_pairs={{0,4},{4,0},{1,5},{5,1},{2,6},{6,2},{3,7},{7,3},{8,12},{12,8},{9,1... | collective-permute-start | bytes 196616 | tf_op jit(solution)/shard_map/ppermute | solution.py:32
  326.1 5.8 %collective-permute-start.10 = (f32[32,512]{1,0:T(8,128)S(1)}, f32[32,512]{1,0:T(8,128)S(1)}, u32[]{:S(2)}, u32[]{:S(2)}) collective-permute-start(f32[32,512]{1,0:T(8,128)S(1)} %bitcast.231), channel_id=1, source_target_pairs={{0,8},{8,0},{1,9},{9,1},{2,10},{10,2},{3,11},{11,3},{4,12},{12,4},... | collective-permute-start | bytes 196616 | tf_op jit(solution)/shard_map/ppermute | solution.py:32
where the time goes:
time: 335 us; the launch traced here: 334 us
  matrix products  271 us (81%)
  starting transfers between devices  27.3 us (8%)
  waiting for transfers between devices  15.5 us (5%)
  loops' own time  11.3 us (3%)
  local copies, waits for them, and re-layouts  5.46 us (2%)
  other arithmetic  3.48 us (1%)
    dot_general x36, matrix products, near_row(): jnp.einsum('cts,xcs->xct', kernel, source_leaf[3:], precision=highest)  263 us
    ppermute x7, starting transfers between devices, partner_2(): return lax.ppermute(block, axis, route)  19.2 us
    ppermute x7, waiting for transfers between devices, partner_2(): return lax.ppermute(block, axis, route)  11.7 us
    another operation x1, loops' own time, near_field(): lax.map(one_row, jnp.arange(neighbour_mask.shape[1], dtype=jnp.int32))  11.3 us
  transfers between devices with their start and end apart: 11, of which 7 were waited for; matrix products, arithmetic and copies ran while one was open for 82% of the time, Pallas kernels for 0%

commit v1 on v0

v1 whole, which is shorter than its diff:
```python
import functools

import jax
import jax.numpy as jnp
import numpy as np
from jax import lax
from jax.experimental import pallas as pl
from jax.experimental.pallas import tpu as pltpu
from jax.sharding import PartitionSpec as P

wave_number = 6.0
softening = 0.05
near_scale = 1.0 / 32.0
highest = lax.Precision.HIGHEST
f32, bf16 = jnp.float32, jnp.bfloat16

turns = wave_number / (2.0 * np.pi)
eps_sq = (softening * turns) ** 2
sine = (3.14157435, -5.16695951, 2.54064763, -0.55204997)
b0, b1, b2 = (sine[0] / sine[3], sine[1] / sine[3], sine[2] / sine[3])
half_gain = 1.0 / (2.0 * sine[3] ** 2)
near_gain = -2.0 * sine[3] ** 2 * turns * near_scale

leaf_rows, leaf_cols, points, rank, rhs = 4, 16, 128, 32, 8
leaves = leaf_rows * leaf_cols
side_cols = leaf_cols + 2
padded_leaves = (leaf_rows + 2) * side_cols
stage_items = 2
vmem = pl.BlockSpec(memory_space=pltpu.VMEM)
smem = pl.BlockSpec(memory_space=pltpu.SMEM)


def inside(i, j):
    return 0 <= i < leaf_rows and 0 <= j < leaf_cols


def slot(i, j):
    return (i + 1) * side_cols + j + 1


def offset_index(i, j, si, sj):
    return 3 * (si - i + 1) + sj - j + 1


def pack_item(source, target, both):
    (si, sj), (ti, tj) = source, target
    word = slot(si, sj) | slot(ti, tj) << 7 | offset_index(ti, tj, si, sj) << 14
    if both:
        word |= 1 << 18
    return word | 1 << 19


def interior_items():
    items = []
    for i in range(leaf_rows):
        for j in range(leaf_cols):
            items.append(pack_item((i, j), (i, j), False))
            for di, dj in ((0, 1), (1, -1), (1, 0), (1, 1)):
                if inside(i + di, j + dj):
                    items.append(pack_item((i, j), (i + di, j + dj), True))
    return items


def halo_items():
    items = []
    for i in range(-1, leaf_rows + 1):
        for j in range(-1, leaf_cols + 1):
            if inside(i, j):
                continue
            for di in (-1, 0, 1):
                for dj in (-1, 0, 1):
                    if inside(i + di, j + dj):
                        items.append(pack_item((i, j), (i + di, j + dj), False))
    return items


def item_table(items):
    step = 2 * stage_items
    idle = pack_item((0, 0), (0, 0), False) & ~(1 << 19)
    padded = items + [idle] * (-len(items) % step)
    return np.array(padded + [idle] * step, np.int32), len(padded) // step


def split(value):
    high = value.astype(bf16)
    return high, (value - high.astype(f32)).astype(bf16)


def dot(left, right):
    return jnp.dot(left, right, preferred_element_type=f32)


def dot_t(left, right):
    return lax.dot_general(left, right, (((1,), (1,)), ((), ())), preferred_element_type=f32)


def prep_kernel(coords, sources, rows, halves):
    start = [coords[pl.ds(c * padded_leaves + slot(0, 0), 1), 0:1] for c in range(3)]
    unroll = 4

    def body(step, carry):
        for k in range(unroll):
            leaf = step * unroll + k
            for c in range(3):
                row = coords[pl.ds(c * padded_leaves + leaf, 1), :]
                rows[pl.ds(leaf * 8 + c, 1), :] = (row - start[c]) * turns
            high, low = split(sources[pl.ds(leaf, rhs, stride=padded_leaves), :])
            halves[pl.ds(pl.multiple_of(leaf * 16, 16), 16), :] = jnp.concatenate([high, low], axis=0)
        return carry

    lax.fori_loop(0, padded_leaves // unroll, body, 0)


def near_kernel(trips, table, mask, rows, halves, seed, acc, splat_a, splat_b, kern_a, kern_b):
    acc[...] = seed[...]
    kern_b[...] = jnp.zeros_like(kern_b)

    def fields(at):
        word = table[at]
        return word & 127, word >> 7 & 127, word >> 14 & 15, word >> 18 & 1, word >> 19 & 1

    def spread(at, splat):
        for n in range(stage_items):
            source = fields(at + n)[0]
            for c in range(3):
                row = rows[pl.ds(source * 8 + c, 1), :]
                splat[n, c] = jnp.broadcast_to(row, (points, points)).T

    def evaluate(at, splat, kern):
        for n in range(stage_items):
            target = fields(at + n)[1]
            other = [rows[pl.ds(target * 8 + c, 1), :] for c in range(3)]
            for g in range(points // 32):
                at_rows = slice(32 * g, 32 * g + 32)
                distance_sq = None
                for c in range(3):
                    spacing = splat[n, c, at_rows] - other[c]
                    term = spacing * spacing
                    distance_sq = term if distance_sq is None else distance_sq + term
                safe = jnp.maximum(distance_sq, 1e-30)
                turn = safe * lax.rsqrt(safe)
                f = turn - jnp.round(turn)
                u = f * f
                m = f * (((u + b2) * u + b1) * u + b0)
                value = (m * m - half_gain) * lax.rsqrt(distance_sq + eps_sq)
                high, low = split(value)
                kern[n, 0, at_rows] = high
                kern[n, 1, at_rows] = low

    def mask_of(leaf_slot, k):
        i = leaf_slot // side_cols - 1
        return mask[k, jnp.clip(i, 0, leaf_rows - 1), jnp.clip(leaf_slot - (i + 1) * side_cols - 1, 0, leaf_cols - 1)]

    def apply(at, kern):
        for n in range(stage_items):
            source, target, k, both, valid = fields(at + n)
            high, low = kern[n, 0], kern[n, 1]
            left = halves[pl.ds(pl.multiple_of(source * 16, 16), 16), :]
            got = dot(left, high) + dot(left, low)
            weight = (mask_of(target, k) * valid).astype(f32)
            acc[pl.ds(target * 8, 8), :] += (got[:8] + got[8:]) * weight
            left = halves[pl.ds(pl.multiple_of(target * 16, 16), 16), :]
            got = dot_t(left, high) + dot_t(left, low)
            weight = (mask_of(source, 8 - k) * both).astype(f32)
            acc[pl.ds(source * 8, 8), :] += (got[:8] + got[8:]) * weight

    def body(trip, carry):
        a = trip * 2 * stage_items
        b = a + stage_items
        spread(b, splat_b)
        evaluate(a, splat_a, kern_a)
        apply(jnp.maximum(a - stage_items, 0), kern_b)
        spread(b + stage_items, splat_a)
        evaluate(b, splat_b, kern_b)
        apply(a, kern_a)
        return carry

    spread(0, splat_a)
    lax.fori_loop(0, trips, body, 0)
    apply(trips * 2 * stage_items - stage_items, kern_b)


def near_piece(items, mask, rows, halves, seed):
    table, trips = item_table(items)
    return pl.pallas_call(
        functools.partial(near_kernel, trips),
        out_shape=jax.ShapeDtypeStruct(seed.shape, f32),
        in_specs=[smem, smem, vmem, vmem, vmem],
        out_specs=vmem,
        scratch_shapes=[pltpu.VMEM((stage_items, 3, points, points), f32)] * 2
        + [pltpu.VMEM((stage_items, 2, points, points), bf16)] * 2,
        compiler_params=pltpu.CompilerParams(vmem_limit_bytes=24 << 20),
        cost_estimate=pl.CostEstimate(flops=len(items) * 60 * points * points, bytes_accessed=1 << 20, transcendentals=0),
        name="near",
    )(jnp.asarray(table), mask, rows, halves, seed)


def extended(value, sides, width):
    for axis, dim in sides:
        size, length = (lax.axis_size(axis), value.shape[dim])
        up = [(i, (i + 1) % size) for i in range(size - 1)]
        down = [(j, i) for i, j in up]
        last = lax.slice_in_dim(value, length - width, length, axis=dim)
        initial = lax.slice_in_dim(value, 0, width, axis=dim)
        before = lax.ppermute(last, axis, up)
        after = lax.ppermute(initial, axis, down)
        value = jnp.concatenate([before, value, after], axis=dim)
    return value


def partner_2(block, axis, distance):
    count = lax.axis_size(axis)
    route = []
    for low in range(count):
        high = low | 1 << distance
        if high != low and high < count:
            route += [(low, high), (high, low)]
    return lax.ppermute(block, axis, route)


def pair_level(blocks, coeffs, partner):
    own_term = jnp.dot(blocks[0], coeffs, precision=highest, preferred_element_type=f32)
    other_term = jnp.dot(blocks[1], partner, precision=highest, preferred_element_type=f32)
    return own_term + other_term


def shards(coords, sources, neighbour_mask, compress, expand, row_transfer, col_transfer):
    stacked = jnp.concatenate([coords, sources], axis=0)
    padded = extended(stacked, (("row", 1), ("col", 2)), 1)
    rows, halves = pl.pallas_call(
        prep_kernel,
        out_shape=(
            jax.ShapeDtypeStruct((padded_leaves * 8, points), f32),
            jax.ShapeDtypeStruct((padded_leaves * 16, points), bf16),
        ),
        in_specs=[vmem, vmem],
        out_specs=(vmem, vmem),
        compiler_params=pltpu.CompilerParams(vmem_limit_bytes=16 << 20),
        name="prep",
    )(padded[:3].reshape(-1, points), padded[3:].reshape(-1, points))
    seed = jnp.zeros((padded_leaves * 8, points), f32)
    near = near_piece(interior_items() + halo_items(), neighbour_mask, rows, halves, seed)
    near = near.reshape(leaf_rows + 2, side_cols, rhs, points)[1:-1, 1:-1] * near_gain
    near = jnp.transpose(near, (2, 0, 1, 3))
    coeffs = jnp.einsum("lmqs,xlms->qxlm", compress, sources, precision=highest)
    coeffs = coeffs.reshape(rank, rhs * leaves)
    row_blocks = row_transfer[:, 0, 0]
    for bit in range(lax.axis_size("row").bit_length() - 1):
        partner = partner_2(coeffs, "row", bit)
        coeffs = pair_level(row_blocks, coeffs, partner)
    col_blocks = col_transfer[:, 0, 0]
    for bit in range(lax.axis_size("col").bit_length() - 1):
        partner = partner_2(coeffs, "col", bit)
        coeffs = pair_level(col_blocks, coeffs, partner)
    coeffs = coeffs.reshape(rank, rhs, leaf_rows, leaf_cols)
    far = jnp.einsum("lmqt,qxlm->xlmt", expand, coeffs, precision=highest)
    return near + far


def solution(mesh):
    in_specs = (
        P(None, "row", "col", None),
        P(None, "row", "col", None),
        P(None, "row", "col"),
        P("row", "col", None, None),
        P("row", "col", None, None),
        P(None, "row", "col", None, None),
        P(None, "row", "col", None, None),
    )
    out_specs = P(None, "row", "col", None)
    return jax.shard_map(shards, mesh=mesh, in_specs=in_specs, out_specs=out_specs, check_vma=False)
```

time: 335 us -> 98.8 us (0.29)
  matrix products: 271 us -> 7 us
  Pallas kernels: 0 us -> 41.5 us
  loops' own time: 11.3 us -> 0 us
  starting transfers between devices: 27.3 us -> 33 us
    dot_general x50 -> x14, matrix products: 267 us -> 3.15 us  [the longest x7 1.59 us: pair_level(): jnp.dot(blocks[1], partner, precision=highest, preferred_element_type=f32)]
    pallas_call x0 -> x2, Pallas kernels: none -> 41.5 us  [the longest x1 39.5 us: near_piece(): pl.pallas_call(functools.partial(near_kernel, trips), out_shape=jax.Shape...]
    another operation x1 -> x0, loops' own time: 11.3 us -> none  [near_field(): lax.map(one_row, jnp.arange(neighbour_mask.shape[1], dtype=jnp.int32))]
    ppermute x2, waiting for transfers between devices: 3.76 us -> 0.01 us  [extended(): after = lax.ppermute(initial, axis, down)]
    ppermute x7, starting transfers between devices: 19.2 us -> 22.8 us  [partner_2(): return lax.ppermute(block, axis, route)]
    convert_element_type x4 -> x0, other arithmetic: 3.35 us -> none  [near_row(): weight = mask_row[row_shift * 3 + col_shift].astype(jnp.float32)]
  transfers between devices with their start and end apart: 11 -> 11, of which waited for: 7 -> 6; matrix products, arithmetic and copies ran while one was open for 82% -> 5% of each run, Pallas kernels for 0% -> 42%
where the time goes in v1:
time: 98.8 us; the launch traced here: 98.3 us
  Pallas kernels  41.5 us (42%)
  starting transfers between devices  33 us (33%)
  waiting for transfers between devices  12.5 us (13%)
  matrix products  7 us (7%)
  local copies, waits for them, and re-layouts  3.74 us (4%)
    pallas_call x1, Pallas kernels, near_piece(): pl.pallas_call(functools.partial(near_kernel, trips), out_shape=jax.Shape...  39.5 us
    ppermute x7, starting transfers between devices, partner_2(): return lax.ppermute(block, axis, route)  22.8 us
    ppermute x7, waiting for transfers between devices, partner_2(): return lax.ppermute(block, axis, route)  12.5 us
    ppermute x2, starting transfers between devices, extended(): before = lax.ppermute(last, axis, up)  7.6 us
    dot_general x1, matrix products, shards(): coeffs = jnp.einsum('lmqs,xlms->qxlm', compress, sources, precision=highest)  2.75 us
    ppermute x2, starting transfers between devices, extended(): after = lax.ppermute(initial, axis, down)  2.58 us
    pallas_call x1, Pallas kernels, shards(): pl.pallas_call(prep_kernel, out_shape=(jax.ShapeDtypeStruct((padded_leave...  2.01 us
  transfers between devices with their start and end apart: 11, of which 6 were waited for; matrix products, arithmetic and copies ran while one was open for 5% of the time, Pallas kernels for 42%

profile of v1, /device:TPU:0, one launch (start us, length us, event | category | flops | bytes accessed | tf_op | source)
XLA Modules:
  0.0 98.3 jit_solution(16013523653354353525)
XLA Ops:
  0.0 0.0 copy-start
  0.0 0.0 copy-start.3
  0.0 1.0 %constant_dynamic-update-slice_fusion.1 = f32[11,4,16,128]{3,2,1,0:T(8,128)S(1)} fusion(f32[3,4,16,128]{3,2,1,0:T(8,128)} %param.8), kind=kLoop, calls=%fused_computation.58 | loop fusion | bytes 196608
  1.1 1.0 constant_dynamic-update-slice_fusion
  2.0 1.3 %collective-permute-start.1 = (f32[11,1,16,128]{3,2,1,0:T(8,128)S(1)}, f32[11,1,16,128]{3,2,1,0:T(8,128)S(1)}, u32[]{:S(2)}, u32[]{:S(2)}) collective-permute-start(f32[11,1,16,128]{3,2,1,0:T(8,128)S(1)} %get-tuple-element.12), channel_id=1, source_target_pairs={{16,0},{32,16},{48,32},{64,48},{80,64},{96,80},{112,96},{17,1},{33... | collective-permute-start | bytes 270344 | tf_op jit(solution)/shard_map/ppermute | solution.py:206
  3.3 3.0 %collective-permute-start = (f32[11,1,16,128]{3,2,1,0:T(8,128)S(1)}, f32[11,1,16,128]{3,2,1,0:T(8,128)S(1)}, u32[]{:S(2)}, u32[]{:S(2)}) collective-permute-start(f32[11,1,16,128]{3,2,1,0:T(8,128)S(1)} %get-tuple-element.11), channel_id=1, source_target_pairs={{0,16},{16,32},{32,48},{48,64},{64,80},{80,96},{96,112},{1,17},{17... | collective-permute-start | bytes 270344 | tf_op jit(solution)/shard_map/ppermute | solution.py:205
  6.4 0.0 copy-done.3
  6.4 2.8 %convolution_bitcast_fusion = f32[32,8,4,16]{0,1,3,2:T(8,128)S(1)} fusion(f32[4,16,32,128]{3,2,1,0:T(8,128)S(1)} %copy-done.3, f32[8,4,16,128]{3,2,1,0:T(8,128)} %param.9), kind=kOutput, calls=%fused_computation | convolution fusion | flops 25165824 | bytes 1376256 | tf_op jit(solution)/shard_map/lmqs,xlms->qxlm/dot_general | solution.py:245
  9.2 0.0 copy-start.5
  9.2 0.1 copy.13
  9.2 1.4 %collective-permute-start.4 = (f32[32,512]{0,1:T(8,128)S(1)}, f32[32,512]{0,1:T(8,128)S(1)}, u32[]{:S(2)}, u32[]{:S(2)}) collective-permute-start(f32[32,512]{0,1:T(8,128)S(1)} %bitcast.65), channel_id=1, source_target_pairs={{0,16},{16,0},{32,48},{48,32},{64,80},{80,64},{96,112},{112,96},{1... | collective-permute-start | bytes 196616 | tf_op jit(solution)/shard_map/ppermute | solution.py:218
  10.6 0.0 copy-done.5
  10.6 0.4 fusion.23
  11.0 0.8 collective-permute-done.4
  11.7 0.4 convolution_add_fusion.7
  12.1 0.0 collective-permute-done.1
  12.2 0.0 collective-permute-done
  12.2 0.1 pad_maximum_fusion.7
  12.2 1.3 %collective-permute-start.3 = (f32[11,6,1,128]{3,2,1,0:T(1,128)S(1)}, f32[11,6,1,128]{3,2,1,0:T(1,128)S(1)}, u32[]{:S(2)}, u32[]{:S(2)}) collective-permute-start(f32[11,6,1,128]{3,2,1,0:T(1,128)S(1)} %get-tuple-element.10), channel_id=1, source_target_pairs={{1,0},{2,1},{3,2},{4,3},{5,4},{6,5},{7,6},{8,7},{9,8},{10,9},{11,1... | collective-permute-start | bytes 101384 | tf_op jit(solution)/shard_map/ppermute | solution.py:206
  13.5 4.6 %collective-permute-start.2 = (f32[11,6,1,128]{3,2,1,0:T(1,128)S(1)}, f32[11,6,1,128]{3,2,1,0:T(1,128)S(1)}, u32[]{:S(2)}, u32[]{:S(2)}) collective-permute-start(f32[11,6,1,128]{3,2,1,0:T(1,128)S(1)} %get-tuple-element.9), channel_id=1, source_target_pairs={{0,1},{1,2},{2,3},{3,4},{4,5},{5,6},{6,7},{7,8},{8,9},{9,10},{10,1... | collective-permute-start | bytes 101384 | tf_op jit(solution)/shard_map/ppermute | solution.py:205
  18.1 0.2 fusion.21
  18.3 1.7 %collective-permute-start.5 = (f32[32,512]{1,0:T(8,128)S(1)}, f32[32,512]{1,0:T(8,128)S(1)}, u32[]{:S(2)}, u32[]{:S(2)}) collective-permute-start(f32[32,512]{1,0:T(8,128)S(1)} %bitcast.67), channel_id=1, source_target_pairs={{0,32},{32,0},{16,48},{48,16},{64,96},{96,64},{80,112},{112,80},{1... | collective-permute-start | bytes 196616 | tf_op jit(solution)/shard_map/ppermute | solution.py:218
  19.9 0.0 collective-permute-done.3
  20.0 0.0 collective-permute-done.2
  20.0 0.1 pad_maximum_fusion
  20.2 2.0 %prep.1 = (f32[864,128]{1,0:T(8,128)S(1)}, bf16[1728,128]{1,0:T(8,128)(2,1)S(1)}) custom-call(f32[324,128]{1,0:T(8,128)S(1)} %reshape.23.coords, f32[864,128]{1,0:T(8,128)S(1)} %reshape.24.sources), custom_call_target="tpu_custom_call" | custom-call | tf_op jit(solution)/shard_map/prep/pallas_call | solution.py:230
  22.2 0.0 copy-start.1
  22.2 0.0 copy-start.2
  22.2 0.7 copy-done.1
  22.9 0.0 copy-done.2
  22.9 39.5 %near.1 = f32[864,128]{1,0:T(8,128)S(1)} custom-call(s32[384]{0:T(512)S(1)} %copy-done.2, s32[9,4,16]{2,1,0:T(4,128)S(1)} %copy-done.1, f32[864,128]{1,0:T(8,128)S(1)} %get-tuple-element.7.rows, bf16[1728,128]{1,0:T(8,128)(2,1)S(1)} %get-tuple-element.8.halves, f32[864,128]{1,0:T(8,128)S(1)} %broadcast_in_dim.3.seed), custom_call_target="tpu_custom_call" | custom-call | flops 371589120 | bytes 1048576 | tf_op jit(solution)/shard_map/near/pallas_call | solution.py:185
  62.4 0.0 collective-permute-done.5
  62.4 0.2 convolution_add_fusion.6
  62.7 2.9 %collective-permute-start.6 = (f32[32,512]{1,0:T(8,128)S(1)}, f32[32,512]{1,0:T(8,128)S(1)}, u32[]{:S(2)}, u32[]{:S(2)}) collective-permute-start(f32[32,512]{1,0:T(8,128)S(1)} %bitcast.68), channel_id=1, source_target_pairs={{0,64},{64,0},{16,80},{80,16},{32,96},{96,32},{48,112},{112,48},{1... | collective-permute-start | bytes 196616 | tf_op jit(solution)/shard_map/ppermute | solution.py:218
  65.5 0.2 fusion.19
  65.7 0.0 copy-start.4
  65.7 2.8 %collective-permute-done.6 = f32[32,512]{1,0:T(8,128)S(1)} collective-permute-done((f32[32,512]{1,0:T(8,128)S(1)}, f32[32,512]{1,0:T(8,128)S(1)}, u32[]{:S(2)}, u32[]{:S(2)}) %collective-permute-start.6) | collective-permute-done | bytes 65568 | tf_op jit(solution)/shard_map/ppermute | solution.py:218
  68.5 0.2 convolution_add_fusion.5
  68.7 2.1 %collective-permute-start.7 = (f32[32,512]{1,0:T(8,128)S(1)}, f32[32,512]{1,0:T(8,128)S(1)}, u32[]{:S(2)}, u32[]{:S(2)}) collective-permute-start(f32[32,512]{1,0:T(8,128)S(1)} %bitcast.69), channel_id=1, source_target_pairs={{0,1},{1,0},{2,3},{3,2},{4,5},{5,4},{6,7},{7,6},{8,9},{9,8},{10,11... | collective-permute-start | bytes 196616 | tf_op jit(solution)/shard_map/ppermute | solution.py:218
  70.8 0.0 copy-done.4
  70.8 0.2 fusion.14
  71.0 2.0 %collective-permute-done.7 = f32[32,512]{1,0:T(8,128)S(1)} collective-permute-done((f32[32,512]{1,0:T(8,128)S(1)}, f32[32,512]{1,0:T(8,128)S(1)}, u32[]{:S(2)}, u32[]{:S(2)}) %collective-permute-start.7) | collective-permute-done | bytes 65568 | tf_op jit(solution)/shard_map/ppermute | solution.py:218
  73.1 0.2 convolution_add_fusion.4
  73.3 5.7 %collective-permute-start.8 = (f32[32,512]{1,0:T(8,128)S(1)}, f32[32,512]{1,0:T(8,128)S(1)}, u32[]{:S(2)}, u32[]{:S(2)}) collective-permute-start(f32[32,512]{1,0:T(8,128)S(1)} %bitcast.70), channel_id=1, source_target_pairs={{0,2},{2,0},{1,3},{3,1},{4,6},{6,4},{5,7},{7,5},{8,10},{10,8},{9,1... | collective-permute-start | bytes 196616 | tf_op jit(solution)/shard_map/ppermute | solution.py:218
  78.9 0.2 fusion.12
  79.1 2.0 %collective-permute-done.8 = f32[32,512]{1,0:T(8,128)S(1)} collective-permute-done((f32[32,512]{1,0:T(8,128)S(1)}, f32[32,512]{1,0:T(8,128)S(1)}, u32[]{:S(2)}, u32[]{:S(2)}) %collective-permute-start.8) | collective-permute-done | bytes 65568 | tf_op jit(solution)/shard_map/ppermute | solution.py:218
  81.2 0.2 convolution_add_fusion.3
  81.4 6.0 %collective-permute-start.9 = (f32[32,512]{1,0:T(8,128)S(1)}, f32[32,512]{1,0:T(8,128)S(1)}, u32[]{:S(2)}, u32[]{:S(2)}) collective-permute-start(f32[32,512]{1,0:T(8,128)S(1)} %bitcast.71), channel_id=1, source_target_pairs={{0,4},{4,0},{1,5},{5,1},{2,6},{6,2},{3,7},{7,3},{8,12},{12,8},{9,1... | collective-permute-start | bytes 196616 | tf_op jit(solution)/shard_map/ppermute | solution.py:218
  87.4 0.2 fusion.10
  87.6 2.5 %collective-permute-done.9 = f32[32,512]{1,0:T(8,128)S(1)} collective-permute-done((f32[32,512]{1,0:T(8,128)S(1)}, f32[32,512]{1,0:T(8,128)S(1)}, u32[]{:S(2)}, u32[]{:S(2)}) %collective-permute-start.9) | collective-permute-done | bytes 65568 | tf_op jit(solution)/shard_map/ppermute | solution.py:218
  90.1 0.2 convolution_add_fusion.2
  90.3 3.2 %collective-permute-start.10 = (f32[32,512]{1,0:T(8,128)S(1)}, f32[32,512]{1,0:T(8,128)S(1)}, u32[]{:S(2)}, u32[]{:S(2)}) collective-permute-start(f32[32,512]{1,0:T(8,128)S(1)} %bitcast.72), channel_id=1, source_target_pairs={{0,8},{8,0},{1,9},{9,1},{2,10},{10,2},{3,11},{11,3},{4,12},{12,4},... | collective-permute-start | bytes 196616 | tf_op jit(solution)/shard_map/ppermute | solution.py:218
  93.5 0.2 fusion.8
  93.7 2.5 %collective-permute-done.10 = f32[32,512]{1,0:T(8,128)S(1)} collective-permute-done((f32[32,512]{1,0:T(8,128)S(1)}, f32[32,512]{1,0:T(8,128)S(1)}, u32[]{:S(2)}, u32[]{:S(2)}) %collective-permute-start.10) | collective-permute-done | bytes 65568 | tf_op jit(solution)/shard_map/ppermute | solution.py:218
  96.1 0.2 fusion.1
  96.3 0.1 copy.14
  96.4 0.0 copy-done
  96.5 1.1 %fusion = f32[8,4,16,128]{3,0,2,1:T(8,128)S(1)} fusion(f32[4,16,32,128]{3,2,1,0:T(8,128)S(1)} %copy-done, f32[6,18,8,128]{3,2,1,0:T(8,128)S(1)} %bitcast.63, f32[32,8,4,16]{0,3,2,1:T(8,128)S(1)} %bitcast.64), kind=kOutput, calls=%fused_computation.2 | convolution fusion | flops 25296896 | bytes 1638400 | tf_op jit(solution)/shard_map/lmqt,qxlm->xlmt/dot_general | solution.py:256
  97.5 0.8 copy.16
  (5 shorter events, 0.1 us)
Async XLA Ops:
  0.0 96.4 %copy-start = (f32[4,16,32,128]{3,2,1,0:T(8,128)S(1)}, f32[4,16,32,128]{3,2,1,0:T(8,128)}, u32[]{:S(2)}) copy-start(f32[4,16,32,128]{3,2,1,0:T(8,128)} %param.12) | copy-start | bytes 3145732
  0.0 6.4 %copy-start.3 = (f32[4,16,32,128]{3,2,1,0:T(8,128)S(1)}, f32[4,16,32,128]{3,2,1,0:T(8,128)}, u32[]{:S(2)}) copy-start(f32[4,16,32,128]{3,2,1,0:T(8,128)} %param.11) | copy-start | bytes 3145732
  2.0 10.1 %collective-permute-start.1 = (f32[11,1,16,128]{3,2,1,0:T(8,128)S(1)}, f32[11,1,16,128]{3,2,1,0:T(8,128)S(1)}, u32[]{:S(2)}, u32[]{:S(2)}) collective-permute-start(f32[11,1,16,128]{3,2,1,0:T(8,128)S(1)} %get-tuple-element.12), channel_id=1, source_target_pairs={{16,0},{32,16},{48,32},{64,48},{80,64},{96,80},{112,96},{17,1},{33... | collective-permute-start | bytes 270344 | tf_op jit(solution)/shard_map/ppermute | solution.py:206
  3.3 8.8 %collective-permute-start = (f32[11,1,16,128]{3,2,1,0:T(8,128)S(1)}, f32[11,1,16,128]{3,2,1,0:T(8,128)S(1)}, u32[]{:S(2)}, u32[]{:S(2)}) collective-permute-start(f32[11,1,16,128]{3,2,1,0:T(8,128)S(1)} %get-tuple-element.11), channel_id=1, source_target_pairs={{0,16},{16,32},{32,48},{48,64},{64,80},{80,96},{96,112},{1,17},{17... | collective-permute-start | bytes 270344 | tf_op jit(solution)/shard_map/ppermute | solution.py:205
  9.2 1.4 %copy-start.5 = (f32[2,1,1,32,32]{4,3,2,1,0:T(8,128)S(1)}, f32[2,1,1,32,32]{4,3,2,1,0:T(8,128)}, u32[]{:S(2)}) copy-start(f32[2,1,1,32,32]{4,3,2,1,0:T(8,128)} %param.13) | copy-start | bytes 24580
  9.2 2.5 %collective-permute-start.4 = (f32[32,512]{0,1:T(8,128)S(1)}, f32[32,512]{0,1:T(8,128)S(1)}, u32[]{:S(2)}, u32[]{:S(2)}) collective-permute-start(f32[32,512]{0,1:T(8,128)S(1)} %bitcast.65), channel_id=1, source_target_pairs={{0,16},{16,0},{32,48},{48,32},{64,80},{80,64},{96,112},{112,96},{1... | collective-permute-start | bytes 196616 | tf_op jit(solution)/shard_map/ppermute | solution.py:218
  12.2 7.7 %collective-permute-start.3 = (f32[11,6,1,128]{3,2,1,0:T(1,128)S(1)}, f32[11,6,1,128]{3,2,1,0:T(1,128)S(1)}, u32[]{:S(2)}, u32[]{:S(2)}) collective-permute-start(f32[11,6,1,128]{3,2,1,0:T(1,128)S(1)} %get-tuple-element.10), channel_id=1, source_target_pairs={{1,0},{2,1},{3,2},{4,3},{5,4},{6,5},{7,6},{8,7},{9,8},{10,9},{11,1... | collective-permute-start | bytes 101384 | tf_op jit(solution)/shard_map/ppermute | solution.py:206
  13.5 6.4 %collective-permute-start.2 = (f32[11,6,1,128]{3,2,1,0:T(1,128)S(1)}, f32[11,6,1,128]{3,2,1,0:T(1,128)S(1)}, u32[]{:S(2)}, u32[]{:S(2)}) collective-permute-start(f32[11,6,1,128]{3,2,1,0:T(1,128)S(1)} %get-tuple-element.9), channel_id=1, source_target_pairs={{0,1},{1,2},{2,3},{3,4},{4,5},{5,6},{6,7},{7,8},{8,9},{9,10},{10,1... | collective-permute-start | bytes 101384 | tf_op jit(solution)/shard_map/ppermute | solution.py:205
  18.3 44.1 %collective-permute-start.5 = (f32[32,512]{1,0:T(8,128)S(1)}, f32[32,512]{1,0:T(8,128)S(1)}, u32[]{:S(2)}, u32[]{:S(2)}) collective-permute-start(f32[32,512]{1,0:T(8,128)S(1)} %bitcast.67), channel_id=1, source_target_pairs={{0,32},{32,0},{16,48},{48,16},{64,96},{96,64},{80,112},{112,80},{1... | collective-permute-start | bytes 196616 | tf_op jit(solution)/shard_map/ppermute | solution.py:218
  22.2 0.7 copy-start.1
  22.2 0.7 copy-start.2
  62.7 5.8 %collective-permute-start.6 = (f32[32,512]{1,0:T(8,128)S(1)}, f32[32,512]{1,0:T(8,128)S(1)}, u32[]{:S(2)}, u32[]{:S(2)}) collective-permute-start(f32[32,512]{1,0:T(8,128)S(1)} %bitcast.68), channel_id=1, source_target_pairs={{0,64},{64,0},{16,80},{80,16},{32,96},{96,32},{48,112},{112,48},{1... | collective-permute-start | bytes 196616 | tf_op jit(solution)/shard_map/ppermute | solution.py:218
  65.7 5.1 %copy-start.4 = (f32[2,1,1,32,32]{4,3,2,1,0:T(8,128)S(1)}, f32[2,1,1,32,32]{4,3,2,1,0:T(8,128)}, u32[]{:S(2)}) copy-start(f32[2,1,1,32,32]{4,3,2,1,0:T(8,128)} %param.14) | copy-start | bytes 24580
  68.7 4.4 %collective-permute-start.7 = (f32[32,512]{1,0:T(8,128)S(1)}, f32[32,512]{1,0:T(8,128)S(1)}, u32[]{:S(2)}, u32[]{:S(2)}) collective-permute-start(f32[32,512]{1,0:T(8,128)S(1)} %bitcast.69), channel_id=1, source_target_pairs={{0,1},{1,0},{2,3},{3,2},{4,5},{5,4},{6,7},{7,6},{8,9},{9,8},{10,11... | collective-permute-start | bytes 196616 | tf_op jit(solution)/shard_map/ppermute | solution.py:218
  73.3 7.9 %collective-permute-start.8 = (f32[32,512]{1,0:T(8,128)S(1)}, f32[32,512]{1,0:T(8,128)S(1)}, u32[]{:S(2)}, u32[]{:S(2)}) collective-permute-start(f32[32,512]{1,0:T(8,128)S(1)} %bitcast.70), channel_id=1, source_target_pairs={{0,2},{2,0},{1,3},{3,1},{4,6},{6,4},{5,7},{7,5},{8,10},{10,8},{9,1... | collective-permute-start | bytes 196616 | tf_op jit(solution)/shard_map/ppermute | solution.py:218
  81.4 8.7 %collective-permute-start.9 = (f32[32,512]{1,0:T(8,128)S(1)}, f32[32,512]{1,0:T(8,128)S(1)}, u32[]{:S(2)}, u32[]{:S(2)}) collective-permute-start(f32[32,512]{1,0:T(8,128)S(1)} %bitcast.71), channel_id=1, source_target_pairs={{0,4},{4,0},{1,5},{5,1},{2,6},{6,2},{3,7},{7,3},{8,12},{12,8},{9,1... | collective-permute-start | bytes 196616 | tf_op jit(solution)/shard_map/ppermute | solution.py:218
  90.3 5.8 %collective-permute-start.10 = (f32[32,512]{1,0:T(8,128)S(1)}, f32[32,512]{1,0:T(8,128)S(1)}, u32[]{:S(2)}, u32[]{:S(2)}) collective-permute-start(f32[32,512]{1,0:T(8,128)S(1)} %bitcast.72), channel_id=1, source_target_pairs={{0,8},{8,0},{1,9},{9,1},{2,10},{10,2},{3,11},{11,3},{4,12},{12,4},... | collective-permute-start | bytes 196616 | tf_op jit(solution)/shard_map/ppermute | solution.py:218

commit v2 on v0

v2 whole, which is shorter than its diff:
```python
import functools

import jax
import jax.numpy as jnp
import numpy as np
from jax import lax
from jax.experimental import pallas as pl
from jax.experimental.pallas import tpu as pltpu
from jax.sharding import PartitionSpec as P

wave_number = 6.0
softening = 0.05
near_scale = 1.0 / 32.0
highest = lax.Precision.HIGHEST
f32, bf16 = jnp.float32, jnp.bfloat16

turns = wave_number / (2.0 * np.pi)
eps_sq = (softening * turns) ** 2
sine = (3.14157435, -5.16695951, 2.54064763, -0.55204997)
b0, b1, b2 = (sine[0] / sine[3], sine[1] / sine[3], sine[2] / sine[3])
half_gain = 1.0 / (2.0 * sine[3] ** 2)
near_gain = -2.0 * sine[3] ** 2 * turns * near_scale

leaf_rows, leaf_cols, points, rank, rhs = 4, 16, 128, 32, 8
leaves = leaf_rows * leaf_cols
halo_leaves = 48
group = points // rank
groups = leaves // group
batch = 4
vmem = pl.BlockSpec(memory_space=pltpu.VMEM)
smem = pl.BlockSpec(memory_space=pltpu.SMEM)


def params(mib):
    return pltpu.CompilerParams(vmem_limit_bytes=mib << 20)


def cost(cycles):
    return pl.CostEstimate(flops=int(cycles * 400_000), bytes_accessed=1 << 18, transcendentals=0)


def inside(i, j):
    return 0 <= i < leaf_rows and 0 <= j < leaf_cols


def own_slot(i, j):
    return i * leaf_cols + j


def halo_slot(i, j):
    if 0 <= j < leaf_cols:
        return j if i < 0 else leaf_cols + j
    return 2 * leaf_cols + (0 if j < 0 else leaf_rows + 2) + i + 1


def pack_item(source, target, di, dj, both):
    return source | target << 7 | (3 * (di + 1) + dj + 1) << 14 | both << 18 | 1 << 19


def interior_items():
    items = []
    for i in range(leaf_rows):
        for j in range(leaf_cols):
            here = own_slot(i, j)
            items.append(pack_item(here, here, 0, 0, 0))
            for di, dj in ((0, 1), (1, -1), (1, 0), (1, 1)):
                if inside(i + di, j + dj):
                    items.append(pack_item(here, own_slot(i + di, j + dj), -di, -dj, 1))
    return items


def halo_items():
    items = []
    for i in range(-1, leaf_rows + 1):
        for j in range(-1, leaf_cols + 1):
            if inside(i, j):
                continue
            for di in (-1, 0, 1):
                for dj in (-1, 0, 1):
                    if inside(i - di, j - dj):
                        items.append(pack_item(halo_slot(i, j), own_slot(i - di, j - dj), di, dj, 0))
    return items


def item_table(items):
    idle = pack_item(0, 0, 0, 0, 0) & ~(1 << 19)
    padded = items + [idle] * (-len(items) % batch)
    return np.array(padded + [idle] * batch, np.int32), len(padded) // batch


def split(value):
    high = value.astype(bf16)
    return high, (value - high.astype(f32)).astype(bf16)


def thirds(value):
    high = value.astype(bf16).astype(f32)
    rest = value - high
    middle = rest.astype(bf16).astype(f32)
    return high, middle, rest - middle


def dot(left, right):
    return jnp.dot(left, right, preferred_element_type=f32)


def dot_t(left, right):
    return lax.dot_general(left, right, (((1,), (1,)), ((), ())), preferred_element_type=f32)


def dot_tn(left, right):
    return lax.dot_general(left, right, (((0,), (0,)), ((), ())), preferred_element_type=f32)


def sixteen(leaf):
    return pl.ds(leaf * 16 if isinstance(leaf, int) else pl.multiple_of(leaf * 16, 16), 16)


def fill_tables(count, start, coords, sources, tall, right, heights, halves, wide):
    parts = []
    for c in range(3):
        moved = (coords[pl.ds(c * count, count), :] - start[c]) * turns
        if c == 2:
            heights[...] = moved
        else:
            parts.append(thirds(moved))
    k = lax.broadcasted_iota(jnp.int32, (16, points), 0)
    ones_x = jnp.where(k < 3, 1.0, 0.0)
    ones_y = jnp.where((k >= 3) & (k < 6), 1.0, 0.0)
    ones_t = jnp.where((k >= 6) & (k < 9), 1.0, 0.0)
    for role in range(3):
        for leaf in range(count):
            wide[pl.ds(leaf * 16, 16), :] = (ones_t, ones_x, ones_y)[role]
        for first in range(0, count, 8):
            for m in range(3):
                for c in range(2):
                    part = parts[c][m][first : first + 8]
                    if role == 0:
                        wide[pl.ds(first * 16 + 3 * c + m, 8, stride=16), :] = part
                    elif role == c + 1:
                        wide[pl.ds(first * 16 + 6 + m, 8, stride=16), :] = -part
        if role == 0:
            tall[...] = wide[...].astype(bf16)
        else:
            right[:, points * (role - 1) : points * role] = wide[...].astype(bf16)
    for leaf in range(count):
        high, low = split(sources[pl.ds(leaf, rhs, stride=count), :])
        halves[sixteen(leaf), :] = jnp.concatenate([high, low], axis=0)


def lane_block(n):
    return lax.broadcasted_iota(jnp.int32, (rhs, points), 1) // rank == n


def prep_kernel(coords, sources, compress, tall, right, heights, halves, coeffs, wide):
    start = [coords[c * leaves : c * leaves + 1, 0:1] for c in range(3)]
    fill_tables(leaves, start, coords, sources, tall, right, heights, halves, wide)
    for g in range(groups):
        high, low = split(compress[g * points : (g + 1) * points, :])
        got = dot_t(halves[g * 16 * group : (g + 1) * 16 * group, :], jnp.concatenate([high, low], axis=0))
        got = got[:, :points] + got[:, points:]
        total = jnp.zeros((rhs, points), f32)
        for n in range(group):
            total = jnp.where(lane_block(n), got[n * 16 : n * 16 + 8] + got[n * 16 + 8 : n * 16 + 16], total)
        coeffs[g * rhs : (g + 1) * rhs, :] = total


def halo_prep_kernel(start_at, coords, sources, tall, right, heights, halves, wide):
    start = [start_at[c * leaves : c * leaves + 1, 0:1] for c in range(3)]
    fill_tables(halo_leaves, start, coords, sources, tall, right, heights, halves, wide)


def near_kernel(trips, both_ways, table, mask, tall, source_heights, source_halves, right, heights, halves, seed, acc, gap, splat, kern):
    acc[...] = seed[...]
    kern[...] = jnp.zeros_like(kern)

    def fields(at):
        word = table[at]
        return word & 127, word >> 7 & 127, word >> 14 & 15, word >> 18 & 1, word >> 19 & 1

    def subtract(at, n):
        source, target = fields(at + n)[:2]
        gap[n] = dot_tn(tall[sixteen(source), :], right[sixteen(target), :])
        splat[n] = jnp.broadcast_to(source_heights[pl.ds(source, 1), :], (points, points)).T

    def evaluate(at, n):
        target = fields(at + n)[1]
        height = heights[pl.ds(target, 1), :]
        for g in range(points // 32):
            at_rows = slice(32 * g, 32 * g + 32)
            dx, dy, dz = gap[n, at_rows, :points], gap[n, at_rows, points:], splat[n, at_rows] - height
            distance_sq = dx * dx + dy * dy + dz * dz
            safe = jnp.maximum(distance_sq, 1e-30)
            turn = safe * lax.rsqrt(safe)
            f = turn - jnp.round(turn)
            u = f * f
            m = f * (((u + b2) * u + b1) * u + b0)
            value = (m * m - half_gain) * lax.rsqrt(distance_sq + eps_sq)
            high, low = split(value)
            kern[n, at_rows, :points] = high
            kern[n, at_rows, points:] = low

    def weight_of(leaf, k, on):
        return (mask[k, leaf // leaf_cols, leaf % leaf_cols] * on).astype(f32)

    def apply(at, n):
        source, target, k, both, valid = fields(at + n)
        pair = kern[n]
        got = dot(source_halves[sixteen(source), :], pair)
        got = got[:, :points] + got[:, points:]
        acc[pl.ds(target * 8, 8), :] += (got[:8] + got[8:]) * weight_of(target, k, valid)
        if both_ways:
            left = halves[sixteen(target), :]
            got = dot_t(jnp.concatenate([left, left], axis=1), pair)
            acc[pl.ds(source * 8, 8), :] += (got[:8] + got[8:]) * weight_of(source, 8 - k, both)

    def body(trip, carry):
        at = trip * batch
        for n in range(batch):
            apply(jnp.maximum(at - batch, 0), n)
            evaluate(at, n)
            subtract(at + batch, n)
        return carry

    for n in range(batch):
        subtract(0, n)
    lax.fori_loop(0, trips, body, 0)
    for n in range(batch):
        apply((trips - 1) * batch, n)


def near_piece(items, both_ways, mask, source_tables, target_tables, seed):
    table, trips = item_table(items)
    tall, _, source_heights, source_halves = source_tables
    _, right, heights, halves = target_tables
    return pl.pallas_call(
        functools.partial(near_kernel, trips, both_ways),
        out_shape=jax.ShapeDtypeStruct(seed.shape, f32),
        in_specs=[smem, smem] + [vmem] * 7,
        out_specs=vmem,
        scratch_shapes=[
            pltpu.VMEM((batch, points, 2 * points), f32),
            pltpu.VMEM((batch, points, points), f32),
            pltpu.VMEM((batch, points, 2 * points), bf16),
        ],
        compiler_params=params(16),
        cost_estimate=cost(len(items) * 110),
        name="near",
    )(jnp.asarray(table), mask, tall, source_heights, source_halves, right, heights, halves, seed)


def finish_kernel(coeffs, expand, acc, out):
    for g in range(groups):
        mine = coeffs[g * rhs : (g + 1) * rhs, :]
        rows = jnp.concatenate([jnp.where(lane_block(n), mine, 0.0) for n in range(group)], axis=0)
        high, low = split(rows)
        e_high, e_low = split(expand[g * points : (g + 1) * points, :])
        got = dot(jnp.concatenate([high, low], axis=0), jnp.concatenate([e_high, e_low], axis=1))
        got = got[:, :points] + got[:, points:]
        got = got[: group * rhs] + got[group * rhs :]
        for n in range(group):
            leaf = g * group + n
            near = acc[leaf * rhs : (leaf + 1) * rhs, :] * near_gain
            out[pl.ds(leaf, rhs, stride=leaves), :] = near + got[n * rhs : (n + 1) * rhs]


def table_shapes(count):
    return (
        jax.ShapeDtypeStruct((count * 16, points), bf16),
        jax.ShapeDtypeStruct((count * 16, 2 * points), bf16),
        jax.ShapeDtypeStruct((count, points), f32),
        jax.ShapeDtypeStruct((count * 16, points), bf16),
    )


def shifted(value, axis, up):
    size = lax.axis_size(axis)
    route = [(i, i + 1) if up else (i + 1, i) for i in range(size - 1)]
    return lax.ppermute(value, axis, route)


def partner_of(block, axis, distance):
    route = [(i, i ^ (1 << distance)) for i in range(lax.axis_size(axis))]
    return lax.ppermute(block, axis, route)


def level_blocks(transfer):
    spread = jnp.kron(jnp.eye(group, dtype=f32)[None], jnp.swapaxes(transfer[:, 0, 0], 1, 2))
    return spread


def shards(coords, sources, neighbour_mask, compress, expand, row_transfer, col_transfer):
    stacked = jnp.concatenate([coords, sources], axis=0)
    above = shifted(stacked[:, leaf_rows - 1 :], "row", True)
    below = shifted(stacked[:, :1], "row", False)
    flat_coords = coords.reshape(-1, points)
    flat_sources = sources.reshape(-1, points)
    *own, coeffs = pl.pallas_call(
        prep_kernel,
        out_shape=table_shapes(leaves) + (jax.ShapeDtypeStruct((points, points), f32),),
        in_specs=[vmem] * 3,
        out_specs=(vmem,) * 5,
        scratch_shapes=[pltpu.VMEM((leaves * 16, points), f32)],
        compiler_params=params(16),
        cost_estimate=cost(3000),
        name="prep",
    )(flat_coords, flat_sources, compress.reshape(-1, points))
    row_blocks, col_blocks = level_blocks(row_transfer), level_blocks(col_transfer)
    tall_cols = [jnp.concatenate([above[:, :, j : j + 1], stacked[:, :, j : j + 1], below[:, :, j : j + 1]], axis=1) for j in (0, leaf_cols - 1)]
    to_right = shifted(tall_cols[1], "col", True)
    to_left = shifted(tall_cols[0], "col", False)

    levels = [("row", bit, row_blocks) for bit in range(lax.axis_size("row").bit_length() - 1)]
    levels += [("col", bit, col_blocks) for bit in range(lax.axis_size("col").bit_length() - 1)]
    items = interior_items()
    pieces = len(levels) - 1
    cuts = [len(items) * n // pieces // batch * batch for n in range(pieces)] + [len(items)]
    acc = jnp.zeros((leaves * rhs, points), f32)
    for n, (axis, bit, blocks) in enumerate(levels):
        partner = partner_of(coeffs, axis, bit)
        coeffs, acc = lax.optimization_barrier((coeffs, acc))
        if n < pieces:
            acc = near_piece(items[cuts[n] : cuts[n + 1]], True, neighbour_mask, own, own, acc)
        else:
            halo = jnp.concatenate(
                [above[:, 0], below[:, 0], to_right[:, :, 0], to_left[:, :, 0], jnp.zeros((3 + rhs, 4, points), f32)], axis=1
            )
            around = pl.pallas_call(
                halo_prep_kernel,
                out_shape=table_shapes(halo_leaves),
                in_specs=[vmem] * 3,
                out_specs=(vmem,) * 4,
                scratch_shapes=[pltpu.VMEM((halo_leaves * 16, points), f32)],
                compiler_params=params(16),
                cost_estimate=cost(1000),
                name="halo_prep",
            )(flat_coords, halo[:3].reshape(-1, points), halo[3:].reshape(-1, points))
            acc = near_piece(halo_items(), False, neighbour_mask, around, own, acc)
        mine = jnp.dot(coeffs, blocks[0], precision=highest, preferred_element_type=f32)
        partner, acc = lax.optimization_barrier((partner, acc))
        coeffs = mine + jnp.dot(partner, blocks[1], precision=highest, preferred_element_type=f32)
    out = pl.pallas_call(
        finish_kernel,
        out_shape=jax.ShapeDtypeStruct((rhs * leaves, points), f32),
        in_specs=[vmem] * 3,
        out_specs=vmem,
        compiler_params=params(16),
        cost_estimate=cost(2000),
        name="finish",
    )(coeffs, expand.reshape(-1, points), acc)
    return out.reshape(rhs, leaf_rows, leaf_cols, points)


def solution(mesh):
    in_specs = (
        P(None, "row", "col", None),
        P(None, "row", "col", None),
        P(None, "row", "col"),
        P("row", "col", None, None),
        P("row", "col", None, None),
        P(None, "row", "col", None, None),
        P(None, "row", "col", None, None),
    )
    out_specs = P(None, "row", "col", None)
    return jax.shard_map(shards, mesh=mesh, in_specs=in_specs, out_specs=out_specs, check_vma=False)
```

time: 335 us -> 87 us (0.26)
  matrix products: 271 us -> 2.86 us
  Pallas kernels: 0 us -> 50.5 us
  waiting for transfers between devices: 15.5 us -> 0.03 us
  loops' own time: 11.3 us -> 0 us
    dot_general x52 -> x14, matrix products: 271 us -> 2.86 us  [the longest x7 1.45 us: shards(): jnp.dot(partner, blocks[1], precision=highest, preferred_element_type=f32)]
    pallas_call x0 -> x10, Pallas kernels: none -> 50.5 us  [the longest x7 47.6 us: near_piece(): pl.pallas_call(functools.partial(near_kernel, trips, both_ways), out_shap...]
    ppermute x11, waiting for transfers between devices: 15.5 us -> 0.03 us  [the longest x7 0.02 us: partner_of(): return lax.ppermute(block, axis, route)]
    another operation x1 -> x0, loops' own time: 11.3 us -> none  [near_field(): lax.map(one_row, jnp.arange(neighbour_mask.shape[1], dtype=jnp.int32))]
    unnamed x12 -> x29, local copies, waits for them, and re-layouts: 1.04 us -> 4.98 us
  transfers between devices with their start and end apart: 11 -> 11, of which waited for: 7 -> 0; matrix products, arithmetic and copies ran while one was open for 82% -> 3% of each run, Pallas kernels for 0% -> 57%
where the time goes in v2:
time: 87 us; the launch traced here: 86.5 us
  Pallas kernels  50.5 us (58%)
  starting transfers between devices  25 us (29%)
  local copies, waits for them, and re-layouts  7.31 us (8%)
  matrix products  2.86 us (3%)
    pallas_call x7, Pallas kernels, near_piece(): pl.pallas_call(functools.partial(near_kernel, trips, both_ways), out_shap...  47.6 us
    ppermute x7, starting transfers between devices, partner_of(): return lax.ppermute(block, axis, route)  15.6 us
    ppermute x4, starting transfers between devices, shifted(): return lax.ppermute(value, axis, route)  9.44 us
    unnamed x29, local copies, waits for them, and re-layouts  4.98 us
  transfers between devices with their start and end apart: 11, of which 0 were waited for; matrix products, arithmetic and copies ran while one was open for 3% of the time, Pallas kernels for 57%

profile of v2, /device:TPU:0, one launch (start us, length us, event | category | flops | bytes accessed | tf_op | source)
XLA Modules:
  0.0 86.5 jit_solution(9231832597438340553)
XLA Ops:
  0.0 0.9 %copy_dynamic-update-slice_fusion.1 = f32[11,4,16,128]{3,1,0,2:T(4,128)S(1)} fusion(f32[3,4,16,128]{3,2,1,0:T(8,128)} %param.14), kind=kLoop, calls=%fused_computation.10 | loop fusion | bytes 196608
  0.9 1.1 %copy_dynamic-update-slice_fusion = f32[11,4,16,128]{3,1,0,2:T(4,128)S(1)} fusion(f32[11,4,16,128]{3,1,0,2:T(4,128)S(1)} %copy_dynamic-update-slice_fusion.1, f32[8,4,16,128]{3,2,1,0:T(8,128)} %param.15), kind=kLoop, calls=%fused_computation.7 | loop fusion | bytes 524288 | tf_op jit(solution)/shard_map/concatenate | solution.py:293
  2.0 0.0 copy-start
  2.0 0.0 copy-start.1
  2.0 0.1 fusion.4
  2.2 1.3 %collective-permute-start.8 = (f32[11,1,16,128]{3,1,0,2:T(1,128)S(1)}, f32[11,1,16,128]{3,1,0,2:T(1,128)S(1)}, u32[]{:S(2)}, u32[]{:S(2)}) collective-permute-start(f32[11,1,16,128]{3,1,0,2:T(1,128)S(1)} %get-tuple-element.83), channel_id=1, source_target_pairs={{16,0},{32,16},{48,32},{64,48},{80,64},{96,80},{112,96},{17,1},{33... | collective-permute-start | bytes 270344 | tf_op jit(solution)/shard_map/ppermute | solution.py:279
  3.5 3.0 %collective-permute-start.7 = (f32[11,1,16,128]{3,1,0,2:T(1,128)S(1)}, f32[11,1,16,128]{3,1,0,2:T(1,128)S(1)}, u32[]{:S(2)}, u32[]{:S(2)}) collective-permute-start(f32[11,1,16,128]{3,1,0,2:T(1,128)S(1)} %get-tuple-element.84), channel_id=1, source_target_pairs={{0,16},{16,32},{32,48},{48,64},{64,80},{80,96},{96,112},{1,17},{17... | collective-permute-start | bytes 270344 | tf_op jit(solution)/shard_map/ppermute | solution.py:279
  6.5 0.0 copy-start.2
  6.6 1.2 %copy-done.2 = f32[4,16,32,128]{3,2,1,0:T(8,128)S(1)} copy-done((f32[4,16,32,128]{3,2,1,0:T(8,128)S(1)}, f32[4,16,32,128]{3,2,1,0:T(8,128)}, u32[]{:S(2)}) %copy-start.2) | copy-done | bytes 1048600
  7.8 0.8 prep.1
  8.6 1.4 %collective-permute-start = (f32[128,128]{1,0:T(8,128)S(1)}, f32[128,128]{1,0:T(8,128)S(1)}, u32[]{:S(2)}, u32[]{:S(2)}) collective-permute-start(f32[128,128]{1,0:T(8,128)S(1)} %get-tuple-element.42), channel_id=1, source_target_pairs={{0,16},{16,0},{32,48},{48,32},{64,80},{80,64},{96,112},{112,96},{1... | collective-permute-start | bytes 196616 | tf_op jit(solution)/shard_map/ppermute | solution.py:284
  9.9 0.7 copy-done.12
  10.7 0.1 copy.28
  10.8 0.7 copy-done.13
  11.4 0.1 copy.29
  11.5 0.2 broadcast_multiply_fusion
  11.7 0.1 fusion.1
  11.8 0.2 squeeze.41
  12.0 0.2 fusion.7
  12.2 0.0 copy-start.4
  12.2 0.0 copy-start.11
  12.2 0.7 copy-done.4
  12.9 5.4 %near.7.seed = f32[512,128]{1,0:T(8,128)S(1)} custom-call(s32[44]{0:T(128)S(1)} %copy-done.11, s32[9,4,16]{2,1,0:T(4,128)S(1)} %copy-done.4, bf16[1024,128]{1,0:T(8,128)(2,1)S(1)} %get-tuple-element.43.tall, f32[64,128]{1,0:T(8,128)S(1)} %get-tuple-element.44.source_heights.heights, bf16[1024,128]{1,0:T(8,128)(2,1)S(1)} %get-tuple-element.45.source_halves.halves, ...), custom_call_target="tpu_custom_call" | custom-call | flops 1760000000 | bytes 262144 | tf_op jit(solution)/shard_map/near/pallas_call | solution.py:236
  18.3 0.2 squeeze.45
  18.5 0.2 squeeze.44
  18.6 0.2 squeeze.42
  18.8 0.2 convolution_add_fusion.6
  19.0 1.7 %collective-permute-start.1 = (f32[128,128]{1,0:T(8,128)S(1)}, f32[128,128]{1,0:T(8,128)S(1)}, u32[]{:S(2)}, u32[]{:S(2)}) collective-permute-start(f32[128,128]{1,0:T(8,128)S(1)} %convolution_add_fusion.6), channel_id=1, source_target_pairs={{0,32},{16,48},{32,0},{48,16},{64,96},{80,112},{96,64},{112,80},{1... | collective-permute-start | bytes 196616 | tf_op jit(solution)/shard_map/ppermute | solution.py:284
  20.7 0.2 fusion.8
  21.0 3.8 %collective-permute-start.9 = (f32[11,6,1,128]{3,1,0,2:T(8,128)S(1)}, f32[11,6,1,128]{3,1,0,2:T(8,128)S(1)}, u32[]{:S(2)}, u32[]{:S(2)}) collective-permute-start(f32[11,6,1,128]{3,1,0,2:T(8,128)S(1)} %pad_maximum_fusion), channel_id=1, source_target_pairs={{0,1},{1,2},{2,3},{3,4},{4,5},{5,6},{6,7},{7,8},{8,9},{9,10},{10,1... | collective-permute-start | bytes 101384 | tf_op jit(solution)/shard_map/ppermute | solution.py:279
  24.8 0.0 copy-start.10
  24.8 1.3 %collective-permute-start.10 = (f32[11,6,1,128]{3,1,0,2:T(8,128)S(1)}, f32[11,6,1,128]{3,1,0,2:T(8,128)S(1)}, u32[]{:S(2)}, u32[]{:S(2)}) collective-permute-start(f32[11,6,1,128]{3,1,0,2:T(8,128)S(1)} %pad_maximum_fusion.1), channel_id=1, source_target_pairs={{1,0},{2,1},{3,2},{4,3},{5,4},{6,5},{7,6},{8,7},{9,8},{10,9},{11,1... | collective-permute-start | bytes 101384 | tf_op jit(solution)/shard_map/ppermute | solution.py:279
  26.2 5.8 %near.8.seed = f32[512,128]{1,0:T(8,128)S(1)} custom-call(s32[48]{0:T(128)S(1)} %copy-done.10, s32[9,4,16]{2,1,0:T(4,128)S(1)} %copy-done.4, bf16[1024,128]{1,0:T(8,128)(2,1)S(1)} %get-tuple-element.43.tall, f32[64,128]{1,0:T(8,128)S(1)} %get-tuple-element.44.source_heights.heights, bf16[1024,128]{1,0:T(8,128)(2,1)S(1)} %get-tuple-element.45.source_halves.halves, ...), custom_call_target="tpu_custom_call" | custom-call | flops 1936000000 | bytes 262144 | tf_op jit(solution)/shard_map/near/pallas_call | solution.py:236
  32.0 0.2 concatenate.15
  32.2 1.1 %halo_prep.1 = (bf16[768,128]{1,0:T(8,128)(2,1)S(1)}, bf16[768,256]{1,0:T(8,128)(2,1)}, f32[48,128]{1,0:T(8,128)S(1)}, bf16[768,128]{1,0:T(8,128)(2,1)S(1)}) custom-call(f32[192,128]{1,0:T(8,128)S(1)} %bitcast.52, f32[144,128]{1,0:T(8,128)S(1)} %bitcast.53, f32[384,128]{1,0:T(8,128)S(1)} %bitcast.50), custom_call_target="tpu_custom_call" | custom-call | flops 400000000 | bytes 262144 | tf_op jit(solution)/shard_map/halo_prep/pallas_call | solution.py:328
  33.3 0.2 convolution_add_fusion.5
  33.5 0.0 copy-start.9
  33.5 1.8 %collective-permute-start.2 = (f32[128,128]{1,0:T(8,128)S(1)}, f32[128,128]{1,0:T(8,128)S(1)}, u32[]{:S(2)}, u32[]{:S(2)}) collective-permute-start(f32[128,128]{1,0:T(8,128)S(1)} %convolution_add_fusion.5), channel_id=1, source_target_pairs={{0,64},{16,80},{32,96},{48,112},{64,0},{80,16},{96,32},{112,48},{1... | collective-permute-start | bytes 196616 | tf_op jit(solution)/shard_map/ppermute | solution.py:284
  35.3 0.2 fusion.9
  35.5 5.8 %near.9.seed = f32[512,128]{1,0:T(8,128)S(1)} custom-call(s32[48]{0:T(128)S(1)} %copy-done.9, s32[9,4,16]{2,1,0:T(4,128)S(1)} %copy-done.4, bf16[1024,128]{1,0:T(8,128)(2,1)S(1)} %get-tuple-element.43.tall, f32[64,128]{1,0:T(8,128)S(1)} %get-tuple-element.44.source_heights.heights, bf16[1024,128]{1,0:T(8,128)(2,1)S(1)} %get-tuple-element.45.source_halves.halves, ...), custom_call_target="tpu_custom_call" | custom-call | flops 1936000000 | bytes 262144 | tf_op jit(solution)/shard_map/near/pallas_call | solution.py:236
  41.3 0.0 collective-permute-done.2
  41.3 0.2 convolution_add_fusion.4
  41.5 0.0 copy-start.8
  41.6 2.7 %collective-permute-start.3 = (f32[128,128]{1,0:T(8,128)S(1)}, f32[128,128]{1,0:T(8,128)S(1)}, u32[]{:S(2)}, u32[]{:S(2)}) collective-permute-start(f32[128,128]{1,0:T(8,128)S(1)} %convolution_add_fusion.4), channel_id=1, source_target_pairs={{0,1},{1,0},{2,3},{3,2},{4,5},{5,4},{6,7},{7,6},{8,9},{9,8},{10,11... | collective-permute-start | bytes 196616 | tf_op jit(solution)/shard_map/ppermute | solution.py:284
  44.3 0.2 fusion.10
  44.5 5.8 %near.10.seed = f32[512,128]{1,0:T(8,128)S(1)} custom-call(s32[48]{0:T(128)S(1)} %copy-done.8, s32[9,4,16]{2,1,0:T(4,128)S(1)} %copy-done.4, bf16[1024,128]{1,0:T(8,128)(2,1)S(1)} %get-tuple-element.43.tall, f32[64,128]{1,0:T(8,128)S(1)} %get-tuple-element.44.source_heights.heights, bf16[1024,128]{1,0:T(8,128)(2,1)S(1)} %get-tuple-element.45.source_halves.halves, ...), custom_call_target="tpu_custom_call" | custom-call | flops 1936000000 | bytes 262144 | tf_op jit(solution)/shard_map/near/pallas_call | solution.py:236
  50.3 0.0 collective-permute-done.3
  50.3 0.2 convolution_add_fusion.3
  50.5 0.0 copy-start.7
  50.5 3.7 %collective-permute-start.4 = (f32[128,128]{1,0:T(8,128)S(1)}, f32[128,128]{1,0:T(8,128)S(1)}, u32[]{:S(2)}, u32[]{:S(2)}) collective-permute-start(f32[128,128]{1,0:T(8,128)S(1)} %convolution_add_fusion.3), channel_id=1, source_target_pairs={{0,2},{1,3},{2,0},{3,1},{4,6},{5,7},{6,4},{7,5},{8,10},{9,11},{10,... | collective-permute-start | bytes 196616 | tf_op jit(solution)/shard_map/ppermute | solution.py:284
  54.2 0.2 fusion.11
  54.4 5.8 %near.11.seed = f32[512,128]{1,0:T(8,128)S(1)} custom-call(s32[48]{0:T(128)S(1)} %copy-done.7, s32[9,4,16]{2,1,0:T(4,128)S(1)} %copy-done.4, bf16[1024,128]{1,0:T(8,128)(2,1)S(1)} %get-tuple-element.43.tall, f32[64,128]{1,0:T(8,128)S(1)} %get-tuple-element.44.source_heights.heights, bf16[1024,128]{1,0:T(8,128)(2,1)S(1)} %get-tuple-element.45.source_halves.halves, ...), custom_call_target="tpu_custom_call" | custom-call | flops 1936000000 | bytes 262144 | tf_op jit(solution)/shard_map/near/pallas_call | solution.py:236
  60.2 0.2 convolution_add_fusion.2
  60.4 0.0 copy-start.6
  60.5 1.6 %collective-permute-start.5 = (f32[128,128]{1,0:T(8,128)S(1)}, f32[128,128]{1,0:T(8,128)S(1)}, u32[]{:S(2)}, u32[]{:S(2)}) collective-permute-start(f32[128,128]{1,0:T(8,128)S(1)} %convolution_add_fusion.2), channel_id=1, source_target_pairs={{0,4},{1,5},{2,6},{3,7},{4,0},{5,1},{6,2},{7,3},{8,12},{9,13},{10,... | collective-permute-start | bytes 196616 | tf_op jit(solution)/shard_map/ppermute | solution.py:284
  62.0 0.2 fusion.12
  62.2 6.2 %near.12.seed = f32[512,128]{1,0:T(8,128)S(1)} custom-call(s32[52]{0:T(128)S(1)} %copy-done.6, s32[9,4,16]{2,1,0:T(4,128)S(1)} %copy-done.4, bf16[1024,128]{1,0:T(8,128)(2,1)S(1)} %get-tuple-element.43.tall, f32[64,128]{1,0:T(8,128)S(1)} %get-tuple-element.44.source_heights.heights, bf16[1024,128]{1,0:T(8,128)(2,1)S(1)} %get-tuple-element.45.source_halves.halves, ...), custom_call_target="tpu_custom_call" | custom-call | flops 2024000000 | bytes 262144 | tf_op jit(solution)/shard_map/near/pallas_call | solution.py:236
  68.4 0.2 convolution_add_fusion.1
  68.7 2.8 %collective-permute-start.6 = (f32[128,128]{1,0:T(8,128)S(1)}, f32[128,128]{1,0:T(8,128)S(1)}, u32[]{:S(2)}, u32[]{:S(2)}) collective-permute-start(f32[128,128]{1,0:T(8,128)S(1)} %convolution_add_fusion.1), channel_id=1, source_target_pairs={{0,8},{1,9},{2,10},{3,11},{4,12},{5,13},{6,14},{7,15},{8,0},{9,1},... | collective-permute-start | bytes 196616 | tf_op jit(solution)/shard_map/ppermute | solution.py:284
  71.5 0.7 copy-done.5
  72.1 12.9 %near.13.acc = f32[512,128]{1,0:T(8,128)S(1)} custom-call(s32[120]{0:T(128)S(1)} %copy-done.5, s32[9,4,16]{2,1,0:T(4,128)S(1)} %copy-done.4, bf16[768,128]{1,0:T(8,128)(2,1)S(1)} %get-tuple-element.71.tall, f32[48,128]{1,0:T(8,128)S(1)} %get-tuple-element.72.source_heights, bf16[768,128]{1,0:T(8,128)(2,1)S(1)} %get-tuple-element.73.source_halves, ...), custom_call_target="tpu_custom_call" | custom-call | flops 5104000000 | bytes 262144 | tf_op jit(solution)/shard_map/near/pallas_call | solution.py:236
  85.0 0.2 fusion.13
  85.2 0.2 convolution_add_fusion.coeffs
  85.5 1.1 %finish.1 = f32[512,128]{1,0:T(8,128)} custom-call(f32[128,128]{1,0:T(8,128)S(1)} %convolution_add_fusion.coeffs, f32[2048,128]{1,0:T(8,128)S(1)} %bitcast.55, f32[512,128]{1,0:T(8,128)S(1)} %near.13.acc), custom_call_target="tpu_custom_call" | custom-call | flops 800000000 | bytes 262144 | tf_op jit(solution)/shard_map/finish/pallas_call | solution.py:342
  (34 shorter events, 0.2 us)
Async XLA Ops:
  2.0 4.5 %copy-start = (f32[8,4,16,128]{3,2,1,0:T(8,128)S(1)}, f32[8,4,16,128]{3,2,1,0:T(8,128)}, u32[]{:S(2)}) copy-start(f32[8,4,16,128]{3,2,1,0:T(8,128)} %param.15) | copy-start | bytes 786436
  2.0 4.5 %copy-start.1 = (f32[3,4,16,128]{3,2,1,0:T(8,128)S(1)}, f32[3,4,16,128]{3,2,1,0:T(8,128)}, u32[]{:S(2)}) copy-start(f32[3,4,16,128]{3,2,1,0:T(8,128)} %param.14) | copy-start | bytes 294916
  2.2 18.7 %collective-permute-start.8 = (f32[11,1,16,128]{3,1,0,2:T(1,128)S(1)}, f32[11,1,16,128]{3,1,0,2:T(1,128)S(1)}, u32[]{:S(2)}, u32[]{:S(2)}) collective-permute-start(f32[11,1,16,128]{3,1,0,2:T(1,128)S(1)} %get-tuple-element.83), channel_id=1, source_target_pairs={{16,0},{32,16},{48,32},{64,48},{80,64},{96,80},{112,96},{17,1},{33... | collective-permute-start | bytes 270344 | tf_op jit(solution)/shard_map/ppermute | solution.py:279
  3.5 17.4 %collective-permute-start.7 = (f32[11,1,16,128]{3,1,0,2:T(1,128)S(1)}, f32[11,1,16,128]{3,1,0,2:T(1,128)S(1)}, u32[]{:S(2)}, u32[]{:S(2)}) collective-permute-start(f32[11,1,16,128]{3,1,0,2:T(1,128)S(1)} %get-tuple-element.84), channel_id=1, source_target_pairs={{0,16},{16,32},{32,48},{48,64},{64,80},{80,96},{96,112},{1,17},{17... | collective-permute-start | bytes 270344 | tf_op jit(solution)/shard_map/ppermute | solution.py:279
  6.5 1.2 %copy-start.2 = (f32[4,16,32,128]{3,2,1,0:T(8,128)S(1)}, f32[4,16,32,128]{3,2,1,0:T(8,128)}, u32[]{:S(2)}) copy-start(f32[4,16,32,128]{3,2,1,0:T(8,128)} %param.17) | copy-start | bytes 3145732
  8.6 10.2 %collective-permute-start = (f32[128,128]{1,0:T(8,128)S(1)}, f32[128,128]{1,0:T(8,128)S(1)}, u32[]{:S(2)}, u32[]{:S(2)}) collective-permute-start(f32[128,128]{1,0:T(8,128)S(1)} %get-tuple-element.42), channel_id=1, source_target_pairs={{0,16},{16,0},{32,48},{48,32},{64,80},{80,64},{96,112},{112,96},{1... | collective-permute-start | bytes 196616 | tf_op jit(solution)/shard_map/ppermute | solution.py:284
  9.9 0.8 copy-start.12
  10.7 0.8 copy-start.13
  12.2 0.7 copy-start.4
  12.2 0.7 copy-start.11
  19.0 14.2 %collective-permute-start.1 = (f32[128,128]{1,0:T(8,128)S(1)}, f32[128,128]{1,0:T(8,128)S(1)}, u32[]{:S(2)}, u32[]{:S(2)}) collective-permute-start(f32[128,128]{1,0:T(8,128)S(1)} %convolution_add_fusion.6), channel_id=1, source_target_pairs={{0,32},{16,48},{32,0},{48,16},{64,96},{80,112},{96,64},{112,80},{1... | collective-permute-start | bytes 196616 | tf_op jit(solution)/shard_map/ppermute | solution.py:284
  21.0 11.0 %collective-permute-start.9 = (f32[11,6,1,128]{3,1,0,2:T(8,128)S(1)}, f32[11,6,1,128]{3,1,0,2:T(8,128)S(1)}, u32[]{:S(2)}, u32[]{:S(2)}) collective-permute-start(f32[11,6,1,128]{3,1,0,2:T(8,128)S(1)} %pad_maximum_fusion), channel_id=1, source_target_pairs={{0,1},{1,2},{2,3},{3,4},{4,5},{5,6},{6,7},{7,8},{8,9},{9,10},{10,1... | collective-permute-start | bytes 101384 | tf_op jit(solution)/shard_map/ppermute | solution.py:279
  24.8 1.3 %copy-start.10 = (s32[48]{0:T(128)S(1)}, s32[48]{0:T(128)}, u32[]{:S(2)}) copy-start(s32[48]{0:T(128)} %constant.18.clone.table) | copy-start | bytes 580
  24.8 7.2 %collective-permute-start.10 = (f32[11,6,1,128]{3,1,0,2:T(8,128)S(1)}, f32[11,6,1,128]{3,1,0,2:T(8,128)S(1)}, u32[]{:S(2)}, u32[]{:S(2)}) collective-permute-start(f32[11,6,1,128]{3,1,0,2:T(8,128)S(1)} %pad_maximum_fusion.1), channel_id=1, source_target_pairs={{1,0},{2,1},{3,2},{4,3},{5,4},{6,5},{7,6},{8,7},{9,8},{10,9},{11,1... | collective-permute-start | bytes 101384 | tf_op jit(solution)/shard_map/ppermute | solution.py:279
  33.5 2.0 %copy-start.9 = (s32[48]{0:T(128)S(1)}, s32[48]{0:T(128)}, u32[]{:S(2)}) copy-start(s32[48]{0:T(128)} %constant.19.clone.table) | copy-start | bytes 580
  33.5 7.8 %collective-permute-start.2 = (f32[128,128]{1,0:T(8,128)S(1)}, f32[128,128]{1,0:T(8,128)S(1)}, u32[]{:S(2)}, u32[]{:S(2)}) collective-permute-start(f32[128,128]{1,0:T(8,128)S(1)} %convolution_add_fusion.5), channel_id=1, source_target_pairs={{0,64},{16,80},{32,96},{48,112},{64,0},{80,16},{96,32},{112,48},{1... | collective-permute-start | bytes 196616 | tf_op jit(solution)/shard_map/ppermute | solution.py:284
  41.5 3.0 %copy-start.8 = (s32[48]{0:T(128)S(1)}, s32[48]{0:T(128)}, u32[]{:S(2)}) copy-start(s32[48]{0:T(128)} %constant.20.clone.table) | copy-start | bytes 580
  41.6 8.7 %collective-permute-start.3 = (f32[128,128]{1,0:T(8,128)S(1)}, f32[128,128]{1,0:T(8,128)S(1)}, u32[]{:S(2)}, u32[]{:S(2)}) collective-permute-start(f32[128,128]{1,0:T(8,128)S(1)} %convolution_add_fusion.4), channel_id=1, source_target_pairs={{0,1},{1,0},{2,3},{3,2},{4,5},{5,4},{6,7},{7,6},{8,9},{9,8},{10,11... | collective-permute-start | bytes 196616 | tf_op jit(solution)/shard_map/ppermute | solution.py:284
  50.5 3.9 %copy-start.7 = (s32[48]{0:T(128)S(1)}, s32[48]{0:T(128)}, u32[]{:S(2)}) copy-start(s32[48]{0:T(128)} %constant.21.clone.table) | copy-start | bytes 580
  50.5 9.7 %collective-permute-start.4 = (f32[128,128]{1,0:T(8,128)S(1)}, f32[128,128]{1,0:T(8,128)S(1)}, u32[]{:S(2)}, u32[]{:S(2)}) collective-permute-start(f32[128,128]{1,0:T(8,128)S(1)} %convolution_add_fusion.3), channel_id=1, source_target_pairs={{0,2},{1,3},{2,0},{3,1},{4,6},{5,7},{6,4},{7,5},{8,10},{9,11},{10,... | collective-permute-start | bytes 196616 | tf_op jit(solution)/shard_map/ppermute | solution.py:284
  60.4 1.8 %copy-start.6 = (s32[52]{0:T(128)S(1)}, s32[52]{0:T(128)}, u32[]{:S(2)}) copy-start(s32[52]{0:T(128)} %constant.22.clone.table) | copy-start | bytes 628
  60.5 8.0 %collective-permute-start.5 = (f32[128,128]{1,0:T(8,128)S(1)}, f32[128,128]{1,0:T(8,128)S(1)}, u32[]{:S(2)}, u32[]{:S(2)}) collective-permute-start(f32[128,128]{1,0:T(8,128)S(1)} %convolution_add_fusion.2), channel_id=1, source_target_pairs={{0,4},{1,5},{2,6},{3,7},{4,0},{5,1},{6,2},{7,3},{8,12},{9,13},{10,... | collective-permute-start | bytes 196616 | tf_op jit(solution)/shard_map/ppermute | solution.py:284
  68.7 16.6 %collective-permute-start.6 = (f32[128,128]{1,0:T(8,128)S(1)}, f32[128,128]{1,0:T(8,128)S(1)}, u32[]{:S(2)}, u32[]{:S(2)}) collective-permute-start(f32[128,128]{1,0:T(8,128)S(1)} %convolution_add_fusion.1), channel_id=1, source_target_pairs={{0,8},{1,9},{2,10},{3,11},{4,12},{5,13},{6,14},{7,15},{8,0},{9,1},... | collective-permute-start | bytes 196616 | tf_op jit(solution)/shard_map/ppermute | solution.py:284
  71.5 0.7 copy-start.5
  72.1 13.3 %copy-start.3 = (f32[4,16,32,128]{3,2,1,0:T(8,128)S(1)}, f32[4,16,32,128]{3,2,1,0:T(8,128)}, u32[]{:S(2)}) copy-start(f32[4,16,32,128]{3,2,1,0:T(8,128)} %param.18) | copy-start | bytes 3145732

commit v3 on v2

v3 whole, which is shorter than its diff:
```python
import functools

import jax
import jax.numpy as jnp
import numpy as np
from jax import lax
from jax.experimental import pallas as pl
from jax.experimental.pallas import tpu as pltpu
from jax.sharding import PartitionSpec as P

wave_number = 6.0
softening = 0.05
near_scale = 1.0 / 32.0
highest = lax.Precision.HIGHEST
f32, bf16 = jnp.float32, jnp.bfloat16

turns = wave_number / (2.0 * np.pi)
eps_sq = (softening * turns) ** 2
sine = (3.14157435, -5.16695951, 2.54064763, -0.55204997)
b0, b1, b2 = (sine[0] / sine[3], sine[1] / sine[3], sine[2] / sine[3])
half_gain = 1.0 / (2.0 * sine[3] ** 2)
near_gain = -2.0 * sine[3] ** 2 * turns * near_scale

leaf_rows, leaf_cols, points, rank, rhs = 4, 16, 128, 32, 8
leaves = leaf_rows * leaf_cols
edge_leaves = 2 * leaf_cols
side_leaves = 16
edge_rows = (3 + rhs) * leaf_cols
side_rows = 72
group = points // rank
groups = leaves // group
batch = 4
vmem = pl.BlockSpec(memory_space=pltpu.VMEM)
smem = pl.BlockSpec(memory_space=pltpu.SMEM)


def params(mib):
    return pltpu.CompilerParams(vmem_limit_bytes=mib << 20)


def cost(cycles):
    return pl.CostEstimate(flops=int(cycles * 400_000), bytes_accessed=1 << 18, transcendentals=0)


def inside(i, j):
    return 0 <= i < leaf_rows and 0 <= j < leaf_cols


def own_slot(i, j):
    return i * leaf_cols + j


def halo_slot(i, j):
    if 0 <= j < leaf_cols:
        return j if i < 0 else leaf_cols + j
    return i + 1 if j < 0 else 8 + i + 1


def pack_item(source, target, di, dj, both):
    return source | target << 7 | (3 * (di + 1) + dj + 1) << 14 | both << 18 | 1 << 19


def interior_items():
    items = []
    for i in range(leaf_rows):
        for j in range(leaf_cols):
            here = own_slot(i, j)
            items.append(pack_item(here, here, 0, 0, 0))
            for di, dj in ((0, 1), (1, -1), (1, 0), (1, 1)):
                if inside(i + di, j + dj):
                    items.append(pack_item(here, own_slot(i + di, j + dj), -di, -dj, 1))
    return items


def halo_items(sides):
    items = []
    for i in range(-1, leaf_rows + 1):
        for j in range(-1, leaf_cols + 1):
            if inside(i, j) or sides == (0 <= j < leaf_cols):
                continue
            for di in (-1, 0, 1):
                for dj in (-1, 0, 1):
                    if inside(i - di, j - dj):
                        items.append(pack_item(halo_slot(i, j), own_slot(i - di, j - dj), di, dj, 0))
    return items


def item_table(items):
    idle = pack_item(0, 0, 0, 0, 0) & ~(1 << 19)
    padded = items + [idle] * (-len(items) % (2 * batch))
    return np.array(padded + [idle] * batch, np.int32), len(padded) // (2 * batch)


def split(value):
    high = value.astype(bf16)
    return high, (value - high.astype(f32)).astype(bf16)


def thirds(value):
    high = value.astype(bf16).astype(f32)
    rest = value - high
    middle = rest.astype(bf16).astype(f32)
    return high, middle, rest - middle


def dot(left, right):
    return jnp.dot(left, right, preferred_element_type=f32)


def dot_t(left, right):
    return lax.dot_general(left, right, (((1,), (1,)), ((), ())), preferred_element_type=f32)


def sixteen(leaf):
    return pl.ds(leaf * 16 if isinstance(leaf, int) else pl.multiple_of(leaf * 16, 16), 16)


def fill_tables(count, start, coords, sources, left, right, heights, halves, wide):
    parts = []
    for c in range(3):
        moved = (coords[pl.ds(c * count, count), :] - start[c]) * turns
        if c == 2:
            heights[...] = moved
        else:
            parts.append(thirds(moved))
    k = lax.broadcasted_iota(jnp.int32, (16, points), 0)
    ones_x = jnp.where(k < 3, 1.0, 0.0)
    ones_y = jnp.where((k >= 3) & (k < 6), 1.0, 0.0)
    ones_t = jnp.where((k >= 6) & (k < 9), 1.0, 0.0)
    for role in range(3):
        for leaf in range(count):
            wide[pl.ds(leaf * 16, 16), :] = (ones_t, ones_x, ones_y)[role]
        for first in range(0, count, 8):
            for m in range(3):
                for c in range(2):
                    part = parts[c][m][first : first + 8]
                    if role == 0:
                        wide[pl.ds(first * 16 + 3 * c + m, 8, stride=16), :] = part
                    elif role == c + 1:
                        wide[pl.ds(first * 16 + 6 + m, 8, stride=16), :] = -part
        if role == 0:
            for leaf in range(count):
                left[leaf * points : (leaf + 1) * points, :] = wide[leaf * 16 : leaf * 16 + 16, :].T.astype(bf16)
        else:
            right[:, points * (role - 1) : points * role] = wide[...].astype(bf16)
    for leaf in range(count):
        high, low = split(sources[pl.ds(leaf, rhs, stride=count), :])
        halves[sixteen(leaf), :] = jnp.concatenate([high, low], axis=0)


def lane_block(n):
    return lax.broadcasted_iota(jnp.int32, (rhs, points), 1) // rank == n


def spread_blocks(transfer, blocks):
    same = lax.broadcasted_iota(jnp.int32, (points, points), 0) // rank == lax.broadcasted_iota(jnp.int32, (points, points), 1) // rank
    for n in range(2):
        wide = jnp.concatenate([transfer[n]] * group, axis=1)
        wide = jnp.where(same, jnp.concatenate([wide] * group, axis=0), 0.0)
        blocks[2 * n], blocks[2 * n + 1] = split(wide)


def prep_kernel(place, coords, sources, row_transfer, col_transfer, compress_far, left, right, heights, halves, payload, row_blocks, col_blocks, wide, compress, arrived):
    fetch = pltpu.make_async_copy(compress_far, compress, arrived)
    fetch.start()
    start = [coords[c * leaves : c * leaves + 1, 0:1] for c in range(3)]
    fill_tables(leaves, start, coords, sources, left, right, heights, halves, wide)
    spread_blocks(row_transfer, row_blocks)
    spread_blocks(col_transfer, col_blocks)
    odd = place[0] % 2
    for k in range(2):
        row = (leaf_rows - 1) * (1 - odd if k == 0 else odd)
        for c in range(3 + rhs):
            ref, at = (coords, c) if c < 3 else (sources, c - 3)
            to = points + k * edge_rows + c * leaf_cols
            payload[to : to + leaf_cols, :] = ref[pl.ds(pl.multiple_of(at * leaves + row * leaf_cols, 8), leaf_cols), :]
    fetch.wait()
    for g in range(groups):
        high, low = split(compress[g * points : (g + 1) * points, :])
        got = dot_t(halves[g * 16 * group : (g + 1) * 16 * group, :], jnp.concatenate([high, low], axis=0))
        got = got[:, :points] + got[:, points:]
        total = jnp.zeros((rhs, points), f32)
        for n in range(group):
            total = jnp.where(lane_block(n), got[n * 16 : n * 16 + 8] + got[n * 16 + 8 : n * 16 + 16], total)
        payload[g * rhs : (g + 1) * rhs, :] = total


def halo_prep_kernel(count, start_at, values, left, right, heights, halves, wide):
    start = [start_at[c * leaves : c * leaves + 1, 0:1] for c in range(3)]
    fill_tables(count, start, values.at[: 3 * count], values.at[3 * count :], left, right, heights, halves, wide)


def halo_prep(count, coords, values):
    return pl.pallas_call(
        functools.partial(halo_prep_kernel, count),
        out_shape=table_shapes(count),
        in_specs=[vmem] * 2,
        out_specs=(vmem,) * 4,
        scratch_shapes=[pltpu.VMEM((count * 16, points), f32)],
        compiler_params=params(16),
        cost_estimate=cost(1000),
        name="halo_prep",
    )(coords, values)


def level(mine, theirs, blocks):
    total = None
    for value, n in ((mine, 0), (theirs, 2)):
        high, low = split(value)
        got = dot_t(jnp.concatenate([high, low], axis=0), jnp.concatenate([blocks[n], blocks[n + 1]], axis=0))
        got = got[:, :points] + got[:, points:]
        got = got[:points] + got[points:]
        total = got if total is None else total + got
    return total


def level_kernel(forward, mine, theirs, blocks, payload):
    payload[:points, :] = level(mine[:points, :], theirs[:points, :], blocks)
    payload[points:, :] = theirs[forward:, :]


def turn_kernel(place, mine, theirs, blocks, coords, sources, first, second, payload, edges):
    payload[:points, :] = level(mine[:points, :], theirs[:points, :], blocks)
    row, col = place[0], place[1]
    odd = row % 2 == 1
    around = (row % 4 == 1) | (row % 4 == 2)
    inner = (row > 0) & (row < lax.axis_size("row") - 1)
    for c in range(3 + rhs):
        at = slice(points + c * leaf_cols, points + (c + 1) * leaf_cols)
        near = first[at, :]
        far = jnp.where(inner, jnp.where(around, second[at, :], theirs[at, :]), 0.0)
        edges[c * edge_leaves : c * edge_leaves + leaf_cols, :] = jnp.where(odd, near, far)
        edges[c * edge_leaves + leaf_cols : (c + 1) * edge_leaves, :] = jnp.where(odd, far, near)
    for k in range(2):
        j = (leaf_cols - 1) * (1 - col % 2 if k == 0 else col % 2)
        base = points + k * side_rows
        for c in range(3 + rhs):
            ref, at = (coords, c) if c < 3 else (sources, c - 3)
            payload[base + 6 * c : base + 6 * c + 1, :] = edges[pl.ds(c * edge_leaves + j, 1), :]
            for i in range(leaf_rows):
                payload[base + 6 * c + 1 + i : base + 6 * c + 2 + i, :] = ref[pl.ds(at * leaves + i * leaf_cols + j, 1), :]
            payload[base + 6 * c + 5 : base + 6 * c + 6, :] = edges[pl.ds(c * edge_leaves + leaf_cols + j, 1), :]
        payload[base + 66 : base + side_rows, :] = jnp.zeros((side_rows - 66, points), f32)


def sides_kernel(place, mine, theirs, blocks, first, second, third, coeffs, sides):
    coeffs[...] = level(mine[:points, :], theirs[:points, :], blocks)
    col = place[1]
    odd = col % 2 == 1
    inner = (col > 0) & (col < lax.axis_size("col") - 1)
    at = slice(points, points + side_rows)
    near = first[at, :]
    far = jnp.where((col % 8 == 3) | (col % 8 == 4), third[at, :], theirs[at, :])
    far = jnp.where((col % 4 == 1) | (col % 4 == 2), second[at, :], far)
    far = jnp.where(inner, far, 0.0)
    to_left, to_right = jnp.where(odd, near, far), jnp.where(odd, far, near)
    gap = jnp.zeros((2, points), f32)
    for c in range(3 + rhs):
        at = slice(6 * c, 6 * c + 6)
        sides[c * side_leaves : (c + 1) * side_leaves, :] = jnp.concatenate([to_left[at], gap, to_right[at], gap], axis=0)


def near_kernel(trips, both_ways, table, mask, left, source_heights, source_halves, right, heights, halves, seed, acc, gap_a, gap_b, splat_a, splat_b, kern_a, kern_b):
    acc[...] = seed[...]
    kern_b[...] = jnp.zeros_like(kern_b)
    buffers_a, buffers_b = (gap_a, splat_a, kern_a), (gap_b, splat_b, kern_b)

    def fields(at):
        word = table[at]
        return word & 127, word >> 7 & 127, word >> 14 & 15, word >> 18 & 1, word >> 19 & 1

    def subtract(at, n, gap, splat):
        source, target = fields(at + n)[:2]
        gap[n] = dot(left[pl.ds(pl.multiple_of(source * points, points), points), :], right[sixteen(target), :])
        splat[n] = jnp.broadcast_to(source_heights[pl.ds(source, 1), :], (points, points)).T

    def evaluate(at, n, gap, splat, kern):
        target = fields(at + n)[1]
        height = heights[pl.ds(target, 1), :]
        for g in range(points // 32):
            at_rows = slice(32 * g, 32 * g + 32)
            dx, dy, dz = gap[n, at_rows, :points], gap[n, at_rows, points:], splat[n, at_rows] - height
            distance_sq = dx * dx + dy * dy + dz * dz
            safe = jnp.maximum(distance_sq, 1e-30)
            turn = safe * lax.rsqrt(safe)
            f = turn - jnp.round(turn)
            u = f * f
            m = f * (((u + b2) * u + b1) * u + b0)
            value = (m * m - half_gain) * lax.rsqrt(distance_sq + eps_sq)
            high, low = split(value)
            kern[n, 0, at_rows] = high
            kern[n, 1, at_rows] = low

    def weight_of(leaf, k, on):
        return (mask[k, leaf // leaf_cols, leaf % leaf_cols] * on).astype(f32)

    def apply(at, n, kern):
        source, target, k, both, valid = fields(at + n)
        pair = jnp.concatenate([kern[n, 0], kern[n, 1]], axis=1)
        got = dot(source_halves[sixteen(source), :], pair)
        got = got[:, :points] + got[:, points:]
        acc[pl.ds(target * 8, 8), :] += (got[:8] + got[8:]) * weight_of(target, k, valid)
        if both_ways:
            mine = halves[sixteen(target), :]
            got = dot_t(jnp.concatenate([mine, mine], axis=1), pair)
            acc[pl.ds(source * 8, 8), :] += (got[:8] + got[8:]) * weight_of(source, 8 - k, both)

    def stage(at, here, there):
        for n in range(batch):
            apply(jnp.maximum(at - batch, 0), n, there[2])
        for n in range(batch):
            subtract(at + batch, n, *there[:2])
        for n in range(batch):
            evaluate(at, n, *here)

    def body(trip, carry):
        stage(trip * 2 * batch, buffers_a, buffers_b)
        stage(trip * 2 * batch + batch, buffers_b, buffers_a)
        return carry

    for n in range(batch):
        subtract(0, n, *buffers_a[:2])
    lax.fori_loop(0, trips, body, 0)
    for n in range(batch):
        apply(trips * 2 * batch - batch, n, buffers_b[2])


def near_piece(items, both_ways, mask, source_tables, target_tables, seed):
    table, trips = item_table(items)
    left, _, source_heights, source_halves = source_tables
    _, right, heights, halves = target_tables
    return pl.pallas_call(
        functools.partial(near_kernel, trips, both_ways),
        out_shape=jax.ShapeDtypeStruct(seed.shape, f32),
        in_specs=[smem, smem] + [vmem] * 7,
        out_specs=vmem,
        scratch_shapes=[
            shape
            for shape in (
                pltpu.VMEM((batch, points, 2 * points), f32),
                pltpu.VMEM((batch, points, points), f32),
                pltpu.VMEM((batch, 2, points, points), bf16),
            )
            for _ in range(2)
        ],
        compiler_params=params(16),
        cost_estimate=cost(len(items) * 110),
        name="near",
    )(jnp.asarray(table), mask, left, source_heights, source_halves, right, heights, halves, seed)


def finish_kernel(coeffs, expand, acc, out):
    for g in range(groups):
        mine = coeffs[g * rhs : (g + 1) * rhs, :]
        rows = jnp.concatenate([jnp.where(lane_block(n), mine, 0.0) for n in range(group)], axis=0)
        high, low = split(rows)
        e_high, e_low = split(expand[g * points : (g + 1) * points, :])
        got = dot(jnp.concatenate([high, low], axis=0), jnp.concatenate([e_high, e_low], axis=1))
        got = got[:, :points] + got[:, points:]
        got = got[: group * rhs] + got[group * rhs :]
        for n in range(group):
            leaf = g * group + n
            near = acc[leaf * rhs : (leaf + 1) * rhs, :] * near_gain
            out[pl.ds(leaf, rhs, stride=leaves), :] = near + got[n * rhs : (n + 1) * rhs]


def table_shapes(count):
    return (
        jax.ShapeDtypeStruct((count * points, 16), bf16),
        jax.ShapeDtypeStruct((count * 16, 2 * points), bf16),
        jax.ShapeDtypeStruct((count, points), f32),
        jax.ShapeDtypeStruct((count * 16, points), bf16),
    )


def partner_of(block, axis, distance):
    route = [(i, i ^ (1 << distance)) for i in range(lax.axis_size(axis))]
    return lax.ppermute(block, axis, route)


def array(*shape):
    return jax.ShapeDtypeStruct(shape, f32)


def small_call(body, name, out_shape, scalars, *operands):
    single = not isinstance(out_shape, tuple)
    return pl.pallas_call(
        body,
        out_shape=out_shape,
        in_specs=[smem] * scalars + [vmem] * (len(operands) - scalars),
        out_specs=vmem if single else (vmem,) * len(out_shape),
        compiler_params=params(16),
        cost_estimate=cost(600),
        name=name,
    )(*operands)


def shards(coords, sources, neighbour_mask, compress, expand, row_transfer, col_transfer):
    place = jnp.stack([lax.axis_index("row"), lax.axis_index("col")]).astype(jnp.int32)
    coords = coords.reshape(-1, points)
    sources = sources.reshape(-1, points)
    block_shape = jax.ShapeDtypeStruct((4, points, points), bf16)
    *own, payload, row_blocks, col_blocks = pl.pallas_call(
        prep_kernel,
        out_shape=table_shapes(leaves) + (array(points + 2 * edge_rows, points), block_shape, block_shape),
        in_specs=[smem] + [vmem] * 4 + [pl.BlockSpec(memory_space=pl.ANY)],
        out_specs=(vmem,) * 7,
        scratch_shapes=[pltpu.VMEM((leaves * 16, points), f32), pltpu.VMEM((leaves * rank, points), f32), pltpu.SemaphoreType.DMA],
        compiler_params=params(24),
        cost_estimate=cost(3000),
        name="prep",
    )(place, coords, sources, row_transfer[:, 0, 0], col_transfer[:, 0, 0], compress.reshape(-1, points))
    items = interior_items()
    row_items, col_items = halo_items(False), halo_items(True)
    row_bits, col_bits = (lax.axis_size(axis).bit_length() - 1 for axis in ("row", "col"))
    inner_pieces = row_bits + col_bits - 2
    cuts = [len(items) * n // inner_pieces // 8 * 8 for n in range(inner_pieces)] + [len(items)]
    half = len(row_items) // 2 // 8 * 8
    acc = jnp.zeros((leaves * rhs, points), f32)
    above_below = None
    received = []
    for n in range(row_bits + col_bits):
        over_row = n < row_bits
        blocks = row_blocks if over_row else col_blocks
        theirs = partner_of(payload, "row" if over_row else "col", n if over_row else n - row_bits)
        payload, acc = lax.optimization_barrier((payload, acc))
        if n < inner_pieces:
            acc = near_piece(items[cuts[n] : cuts[n + 1]], True, neighbour_mask, own, own, acc)
        else:
            some = row_items[:half] if n == inner_pieces else row_items[half:]
            acc = near_piece(some, False, neighbour_mask, above_below, own, acc)
        theirs, acc = lax.optimization_barrier((theirs, acc))
        received.append(theirs)
        if n == row_bits - 1:
            payload, edges = small_call(
                turn_kernel,
                "turn",
                (array(points + 2 * side_rows, points), array((3 + rhs) * edge_leaves, points)),
                1,
                place, payload, theirs, blocks, coords, sources, received[0], received[1],
            )
        elif n == row_bits + col_bits - 1:
            coeffs, sides = small_call(
                sides_kernel,
                "sides",
                (array(points, points), array((3 + rhs) * side_leaves, points)),
                1,
                place, payload, theirs, blocks, received[row_bits], received[row_bits + 1], received[row_bits + 2],
            )
        else:
            rows = edge_rows if over_row else side_rows
            skip = points + rows if n in (0, row_bits) else points
            payload = small_call(functools.partial(level_kernel, skip), "level", array(points + rows, points), 0, payload, theirs, blocks)
        if n == row_bits:
            above_below = halo_prep(edge_leaves, coords, edges)
    acc = near_piece(col_items, False, neighbour_mask, halo_prep(side_leaves, coords, sides), own, acc)
    out = pl.pallas_call(
        finish_kernel,
        out_shape=array(rhs * leaves, points),
        in_specs=[vmem] * 3,
        out_specs=vmem,
        compiler_params=params(16),
        cost_estimate=cost(2000),
        name="finish",
    )(coeffs, expand.reshape(-1, points), acc)
    return out.reshape(rhs, leaf_rows, leaf_cols, points)


def solution(mesh):
    in_specs = (
        P(None, "row", "col", None),
        P(None, "row", "col", None),
        P(None, "row", "col"),
        P("row", "col", None, None),
        P("row", "col", None, None),
        P(None, "row", "col", None, None),
        P(None, "row", "col", None, None),
    )
    out_specs = P(None, "row", "col", None)
    return jax.shard_map(shards, mesh=mesh, in_specs=in_specs, out_specs=out_specs, check_vma=False)
```

time: 87 us -> 67.2 us (0.77)
  starting transfers between devices: 25 us -> 14.8 us
  Pallas kernels: 50.5 us -> 47 us
  matrix products: 2.86 us -> 0 us
  local copies, waits for them, and re-layouts: 7.31 us -> 4.65 us
    ppermute x4 -> x0, starting transfers between devices: 9.44 us -> none  [shifted(): return lax.ppermute(value, axis, route)]
    pallas_call x7 -> x8, Pallas kernels: 47.6 us -> 39.3 us  [near_piece(): pl.pallas_call(functools.partial(near_kernel, trips, both_ways), out_shap...]
    pallas_call x3 -> x11, Pallas kernels: 2.92 us -> 7.73 us  [the longest x7 2.74 us: small_call(): pl.pallas_call(body, out_shape=out_shape, in_specs=[smem] * scalars + [vm...]
    dot_general x14 -> x0, matrix products: 2.86 us -> none  [the longest x7 1.45 us: shards(): jnp.dot(partner, blocks[1], precision=highest, preferred_element_type=f32)]
    concatenate x2 -> x0, local copies, waits for them, and re-layouts: 1.23 us -> none  [the longest x1 1.07 us: shards(): stacked = jnp.concatenate([coords, sources], axis=0)]
    unnamed x29 -> x30, local copies, waits for them, and re-layouts: 4.98 us -> 4.63 us
  transfers between devices with their start and end apart: 11 -> 7, of which waited for: 0 -> 0; matrix products, arithmetic and copies ran while one was open for 3% -> 0% of each run, Pallas kernels for 57% -> 56%
where the time goes in v3:
time: 67.2 us; the launch traced here: 66.8 us
  Pallas kernels  47 us (70%)
  starting transfers between devices  14.8 us (22%)
  local copies, waits for them, and re-layouts  4.65 us (7%)
    pallas_call x8, Pallas kernels, near_piece(): pl.pallas_call(functools.partial(near_kernel, trips, both_ways), out_shap...  39.3 us
    ppermute x7, starting transfers between devices, partner_of(): return lax.ppermute(block, axis, route)  14.8 us
    unnamed x30, local copies, waits for them, and re-layouts  4.63 us
    pallas_call x7, Pallas kernels, small_call(): pl.pallas_call(body, out_shape=out_shape, in_specs=[smem] * scalars + [vm...  2.74 us
    pallas_call x1, Pallas kernels, shards(): pl.pallas_call(prep_kernel, out_shape=table_shapes(leaves) + (array(point...  2.26 us
    pallas_call x2, Pallas kernels, halo_prep(): pl.pallas_call(functools.partial(halo_prep_kernel, count), out_shape=tabl...  1.65 us
  transfers between devices with their start and end apart: 7, of which 0 were waited for; matrix products, arithmetic and copies ran while one was open for 0% of the time, Pallas kernels for 56%

profile of v3, /device:TPU:0, one launch (start us, length us, event | category | flops | bytes accessed | tf_op | source)
XLA Modules:
  0.0 66.8 jit_solution(15272845215781900186)
XLA Ops:
  0.0 0.1 pad_add_fusion.place
  0.1 0.0 copy-start
  0.1 0.9 %copy-done = f32[8,4,16,128]{3,2,1,0:T(8,128)S(1)} copy-done((f32[8,4,16,128]{3,2,1,0:T(8,128)S(1)}, f32[8,4,16,128]{3,2,1,0:T(8,128)}, u32[]{:S(2)}) %copy-start) | copy-done | bytes 262168
  1.0 0.0 copy-start.1
  1.0 0.9 %copy-done.1 = f32[3,4,16,128]{3,2,1,0:T(8,128)S(1)} copy-done((f32[3,4,16,128]{3,2,1,0:T(8,128)S(1)}, f32[3,4,16,128]{3,2,1,0:T(8,128)}, u32[]{:S(2)}) %copy-start.1) | copy-done | bytes 98328
  1.9 0.0 copy-start.2
  1.9 1.2 %copy-done.2 = f32[4,16,32,128]{3,2,1,0:T(8,128)S(1)} copy-done((f32[4,16,32,128]{3,2,1,0:T(8,128)S(1)}, f32[4,16,32,128]{3,2,1,0:T(8,128)}, u32[]{:S(2)}) %copy-start.2) | copy-done | bytes 1048600
  3.1 0.0 copy-start.4
  3.1 0.8 %copy-done.4 = f32[2,1,1,32,32]{4,3,2,1,0:T(8,128)S(1)} copy-done((f32[2,1,1,32,32]{4,3,2,1,0:T(8,128)S(1)}, f32[2,1,1,32,32]{4,3,2,1,0:T(8,128)}, u32[]{:S(2)}) %copy-start.4) | copy-done | bytes 8216
  3.9 0.0 copy-start.5
  3.9 0.8 %copy-done.5 = f32[2,1,1,32,32]{4,3,2,1,0:T(8,128)S(1)} copy-done((f32[2,1,1,32,32]{4,3,2,1,0:T(8,128)S(1)}, f32[2,1,1,32,32]{4,3,2,1,0:T(8,128)}, u32[]{:S(2)}) %copy-start.5) | copy-done | bytes 8216
  4.7 0.0 copy-start.6
  4.7 0.0 copy-start.14
  4.7 2.3 %prep.1 = (bf16[8192,16]{1,0:T(8,128)(2,1)S(1)}, bf16[1024,256]{1,0:T(8,128)(2,1)S(1)}, f32[64,128]{1,0:T(8,128)S(1)}, bf16[1024,128]{1,0:T(8,128)(2,1)S(1)}, f3...) custom-call(s32[2]{0:T(128)S(1)} %pad_add_fusion.place, ...), custom_call_target="tpu_custom_call" | custom-call | flops 1200000000 | bytes 262144 | tf_op jit(solution)/shard_map/prep/pallas_call | solution.py:403
  6.9 0.1 collective-permute-start
  7.1 0.0 copy-done.6
  7.1 0.0 copy-done.14
  7.1 0.0 copy-start.13
  7.1 4.9 %near.8.seed = f32[512,128]{1,0:T(8,128)S(1)} custom-call(s32[52]{0:T(128)S(1)} %copy-done.14, s32[9,4,16]{2,1,0:T(4,128)S(1)} %copy-done.6, bf16[8192,16]{1,0:T(8,128)(2,1)S(1)} %get-tuple-element.52.left, f32[64,128]{1,0:T(8,128)S(1)} %get-tuple-element.53.source_heights.heights, bf16[1024,128]{1,0:T(8,128)(2,1)S(1)} %get-tuple-element.54.source_halves.halves, ...), custom_call_target="tpu_custom_call" | custom-call | flops 2112000000 | bytes 262144 | tf_op jit(solution)/shard_map/near/pallas_call | solution.py:332
  12.0 0.0 collective-permute-done.theirs.first
  12.0 0.2 level.5.mine
  12.3 0.0 copy-start.12
  12.3 1.7 %collective-permute-start.1 = (f32[304,128]{1,0:T(8,128)S(1)}, f32[304,128]{1,0:T(8,128)S(1)}, u32[]{:S(2)}, u32[]{:S(2)}) collective-permute-start(f32[304,128]{1,0:T(8,128)S(1)} %level.5.mine), channel_id=1, source_target_pairs={{0,32},{16,48},{32,0},{48,16},{64,96},{80,112},{96,64},{112,80},{1... | collective-permute-start | bytes 466952 | tf_op jit(solution)/shard_map/ppermute | solution.py:378
  14.0 0.0 copy-done.13
  14.0 5.5 %near.9.seed = f32[512,128]{1,0:T(8,128)S(1)} custom-call(s32[60]{0:T(128)S(1)} %copy-done.13, s32[9,4,16]{2,1,0:T(4,128)S(1)} %copy-done.6, bf16[8192,16]{1,0:T(8,128)(2,1)S(1)} %get-tuple-element.52.left, f32[64,128]{1,0:T(8,128)S(1)} %get-tuple-element.53.source_heights.heights, bf16[1024,128]{1,0:T(8,128)(2,1)S(1)} %get-tuple-element.54.source_halves.halves, ...), custom_call_target="tpu_custom_call" | custom-call | flops 2464000000 | bytes 262144 | tf_op jit(solution)/shard_map/near/pallas_call | solution.py:332
  19.6 0.0 collective-permute-done.1.theirs.second
  19.6 0.2 level.6.mine
  19.8 3.0 %collective-permute-start.2 = (f32[304,128]{1,0:T(8,128)S(1)}, f32[304,128]{1,0:T(8,128)S(1)}, u32[]{:S(2)}, u32[]{:S(2)}) collective-permute-start(f32[304,128]{1,0:T(8,128)S(1)} %level.6.mine), channel_id=1, source_target_pairs={{0,64},{16,80},{32,96},{48,112},{64,0},{80,16},{96,32},{112,48},{1... | collective-permute-start | bytes 466952 | tf_op jit(solution)/shard_map/ppermute | solution.py:378
  22.8 0.0 copy-done.12
  22.8 4.9 %near.10.seed = f32[512,128]{1,0:T(8,128)S(1)} custom-call(s32[52]{0:T(128)S(1)} %copy-done.12, s32[9,4,16]{2,1,0:T(4,128)S(1)} %copy-done.6, bf16[8192,16]{1,0:T(8,128)(2,1)S(1)} %get-tuple-element.52.left, f32[64,128]{1,0:T(8,128)S(1)} %get-tuple-element.53.source_heights.heights, bf16[1024,128]{1,0:T(8,128)(2,1)S(1)} %get-tuple-element.54.source_halves.halves, ...), custom_call_target="tpu_custom_call" | custom-call | flops 2112000000 | bytes 262144 | tf_op jit(solution)/shard_map/near/pallas_call | solution.py:332
  27.7 0.0 copy-start.11
  27.7 0.0 collective-permute-done.2.theirs
  27.7 0.8 %turn.1 = (f32[272,128]{1,0:T(8,128)S(1)}, f32[352,128]{1,0:T(8,128)S(1)}) custom-call(s32[2]{0:T(128)S(1)} %pad_add_fusion.place, f32[304,128]{1,0:T(8,128)S(1)} %level.6.mine, f32[304,128]{1,0:T(8,128)S(1)} %collective-permute-done.2.theirs, bf16[4,128,128]{2,1,0:T(8,128)(2,1)S(1)} %get-tuple-element.58.blocks, f32[192,128]{1,0:T(8,128)S(1)} %bitcast.12, ...), custom_call_target="tpu_custom_call" | custom-call | flops 240000000 | bytes 262144 | tf_op jit(solution)/shard_map/turn/pallas_call | solution.py:387
  28.5 2.0 %collective-permute-start.3 = (f32[272,128]{1,0:T(8,128)S(1)}, f32[272,128]{1,0:T(8,128)S(1)}, u32[]{:S(2)}, u32[]{:S(2)}) collective-permute-start(f32[272,128]{1,0:T(8,128)S(1)} %get-tuple-element.69.mine), channel_id=1, source_target_pairs={{0,1},{1,0},{2,3},{3,2},{4,5},{5,4},{6,7},{7,6},{8,9},{9,8},{10,11... | collective-permute-start | bytes 417800 | tf_op jit(solution)/shard_map/ppermute | solution.py:378
  30.5 0.9 %halo_prep.2 = (bf16[4096,16]{1,0:T(8,128)(2,1)S(1)}, bf16[512,256]{1,0:T(8,128)(2,1)}, f32[32,128]{1,0:T(8,128)S(1)}, bf16[512,128]{1,0:T(8,128)(2,1)S(1)}) custom-call(f32[192,128]{1,0:T(8,128)S(1)} %bitcast.13, f32[352,128]{1,0:T(8,128)S(1)} %get-tuple-element.79.values), custom_call_target="tpu_custom_call" | custom-call | flops 400000000 | bytes 262144 | tf_op jit(solution)/shard_map/halo_prep/pallas_call | solution.py:194
  31.4 0.0 copy-done.11
  31.4 0.0 copy-start.10
  31.4 5.5 %near.11.seed = f32[512,128]{1,0:T(8,128)S(1)} custom-call(s32[60]{0:T(128)S(1)} %copy-done.11, s32[9,4,16]{2,1,0:T(4,128)S(1)} %copy-done.6, bf16[8192,16]{1,0:T(8,128)(2,1)S(1)} %get-tuple-element.52.left, f32[64,128]{1,0:T(8,128)S(1)} %get-tuple-element.53.source_heights.heights, bf16[1024,128]{1,0:T(8,128)(2,1)S(1)} %get-tuple-element.54.source_halves.halves, ...), custom_call_target="tpu_custom_call" | custom-call | flops 2464000000 | bytes 262144 | tf_op jit(solution)/shard_map/near/pallas_call | solution.py:332
  36.9 0.0 collective-permute-done.3.theirs.first
  37.0 0.2 level.7.mine
  37.2 0.0 copy-start.9
  37.2 3.7 %collective-permute-start.4 = (f32[200,128]{1,0:T(8,128)S(1)}, f32[200,128]{1,0:T(8,128)S(1)}, u32[]{:S(2)}, u32[]{:S(2)}) collective-permute-start(f32[200,128]{1,0:T(8,128)S(1)} %level.7.mine), channel_id=1, source_target_pairs={{0,2},{1,3},{2,0},{3,1},{4,6},{5,7},{6,4},{7,5},{8,10},{9,11},{10,... | collective-permute-start | bytes 307208 | tf_op jit(solution)/shard_map/ppermute | solution.py:378
  40.9 0.0 copy-done.10
  40.9 5.5 %near.12.seed = f32[512,128]{1,0:T(8,128)S(1)} custom-call(s32[60]{0:T(128)S(1)} %copy-done.10, s32[9,4,16]{2,1,0:T(4,128)S(1)} %copy-done.6, bf16[8192,16]{1,0:T(8,128)(2,1)S(1)} %get-tuple-element.52.left, f32[64,128]{1,0:T(8,128)S(1)} %get-tuple-element.53.source_heights.heights, bf16[1024,128]{1,0:T(8,128)(2,1)S(1)} %get-tuple-element.54.source_halves.halves, ...), custom_call_target="tpu_custom_call" | custom-call | flops 2376000000 | bytes 262144 | tf_op jit(solution)/shard_map/near/pallas_call | solution.py:332
  46.4 0.0 collective-permute-done.4.theirs.second
  46.4 0.2 level.8.mine
  46.7 1.6 %collective-permute-start.5 = (f32[200,128]{1,0:T(8,128)S(1)}, f32[200,128]{1,0:T(8,128)S(1)}, u32[]{:S(2)}, u32[]{:S(2)}) collective-permute-start(f32[200,128]{1,0:T(8,128)S(1)} %level.8.mine), channel_id=1, source_target_pairs={{0,4},{1,5},{2,6},{3,7},{4,0},{5,1},{6,2},{7,3},{8,12},{9,13},{10,... | collective-permute-start | bytes 307208 | tf_op jit(solution)/shard_map/ppermute | solution.py:378
  48.2 0.0 copy-done.9
  48.2 0.0 copy-start.8
  48.2 4.3 %near.13.seed = f32[512,128]{1,0:T(8,128)S(1)} custom-call(s32[44]{0:T(128)S(1)} %copy-done.9, s32[9,4,16]{2,1,0:T(4,128)S(1)} %copy-done.6, bf16[4096,16]{1,0:T(8,128)(2,1)S(1)} %get-tuple-element.80.left, f32[32,128]{1,0:T(8,128)S(1)} %get-tuple-element.81.source_heights, bf16[512,128]{1,0:T(8,128)(2,1)S(1)} %get-tuple-element.82.source_halves, ...), custom_call_target="tpu_custom_call" | custom-call | flops 1760000000 | bytes 262144 | tf_op jit(solution)/shard_map/near/pallas_call | solution.py:332
  52.5 0.0 collective-permute-done.5.theirs.third
  52.5 0.2 level.9.mine
  52.8 2.8 %collective-permute-start.6 = (f32[200,128]{1,0:T(8,128)S(1)}, f32[200,128]{1,0:T(8,128)S(1)}, u32[]{:S(2)}, u32[]{:S(2)}) collective-permute-start(f32[200,128]{1,0:T(8,128)S(1)} %level.9.mine), channel_id=1, source_target_pairs={{0,8},{1,9},{2,10},{3,11},{4,12},{5,13},{6,14},{7,15},{8,0},{9,1},... | collective-permute-start | bytes 307208 | tf_op jit(solution)/shard_map/ppermute | solution.py:378
  55.6 0.0 copy-done.8
  55.6 5.5 %near.14.seed = f32[512,128]{1,0:T(8,128)S(1)} custom-call(s32[60]{0:T(128)S(1)} %copy-done.8, s32[9,4,16]{2,1,0:T(4,128)S(1)} %copy-done.6, bf16[4096,16]{1,0:T(8,128)(2,1)S(1)} %get-tuple-element.80.left, f32[32,128]{1,0:T(8,128)S(1)} %get-tuple-element.81.source_heights, bf16[512,128]{1,0:T(8,128)(2,1)S(1)} %get-tuple-element.82.source_halves, ...), custom_call_target="tpu_custom_call" | custom-call | flops 2288000000 | bytes 262144 | tf_op jit(solution)/shard_map/near/pallas_call | solution.py:332
  61.1 0.0 copy-start.7
  61.1 0.0 collective-permute-done.6.theirs
  61.1 0.8 %sides.1 = (f32[128,128]{1,0:T(8,128)S(1)}, f32[176,128]{1,0:T(8,128)S(1)}) custom-call(s32[2]{0:T(128)S(1)} %pad_add_fusion.place, f32[200,128]{1,0:T(8,128)S(1)} %level.9.mine, f32[200,128]{1,0:T(8,128)S(1)} %collective-permute-done.6.theirs, bf16[4,128,128]{2,1,0:T(8,128)(2,1)S(1)} %get-tuple-element.72.blocks, ...), custom_call_target="tpu_custom_call" | custom-call | flops 240000000 | bytes 262144 | tf_op jit(solution)/shard_map/sides/pallas_call | solution.py:387
  61.9 0.8 %halo_prep.3 = (bf16[2048,16]{1,0:T(8,128)(2,1)S(1)}, bf16[256,256]{1,0:T(8,128)(2,1)}, f32[16,128]{1,0:T(8,128)S(1)}, bf16[256,128]{1,0:T(8,128)(2,1)S(1)}) custom-call(f32[192,128]{1,0:T(8,128)S(1)} %bitcast.14, f32[176,128]{1,0:T(8,128)S(1)} %get-tuple-element.90.values), custom_call_target="tpu_custom_call" | custom-call | flops 400000000 | bytes 262144 | tf_op jit(solution)/shard_map/halo_prep/pallas_call | solution.py:194
  62.7 0.0 copy-start.3
  62.7 0.0 copy-done.7
  62.7 3.1 %near.15.acc = f32[512,128]{1,0:T(8,128)S(1)} custom-call(s32[28]{0:T(128)S(1)} %copy-done.7, s32[9,4,16]{2,1,0:T(4,128)S(1)} %copy-done.6, bf16[2048,16]{1,0:T(8,128)(2,1)S(1)} %get-tuple-element.91.left, f32[16,128]{1,0:T(8,128)S(1)} %get-tuple-element.92.source_heights, bf16[256,128]{1,0:T(8,128)(2,1)S(1)} %get-tuple-element.93.source_halves, ...), custom_call_target="tpu_custom_call" | custom-call | flops 1056000000 | bytes 262144 | tf_op jit(solution)/shard_map/near/pallas_call | solution.py:332
  65.8 0.0 copy-done.3
  65.8 1.1 %finish.1 = f32[512,128]{1,0:T(8,128)} custom-call(f32[128,128]{1,0:T(8,128)S(1)} %get-tuple-element.89.coeffs, f32[2048,128]{1,0:T(8,128)S(1)} %bitcast.16, f32[512,128]{1,0:T(8,128)S(1)} %near.15.acc), custom_call_target="tpu_custom_call" | custom-call | flops 800000000 | bytes 262144 | tf_op jit(solution)/shard_map/finish/pallas_call | solution.py:457
  (1 shorter events, 0.0 us)
Async XLA Ops:
  0.1 0.9 %copy-start = (f32[8,4,16,128]{3,2,1,0:T(8,128)S(1)}, f32[8,4,16,128]{3,2,1,0:T(8,128)}, u32[]{:S(2)}) copy-start(f32[8,4,16,128]{3,2,1,0:T(8,128)} %param.16) | copy-start | bytes 786436
  1.0 0.9 %copy-start.1 = (f32[3,4,16,128]{3,2,1,0:T(8,128)S(1)}, f32[3,4,16,128]{3,2,1,0:T(8,128)}, u32[]{:S(2)}) copy-start(f32[3,4,16,128]{3,2,1,0:T(8,128)} %param.15) | copy-start | bytes 294916
  1.9 1.2 %copy-start.2 = (f32[4,16,32,128]{3,2,1,0:T(8,128)S(1)}, f32[4,16,32,128]{3,2,1,0:T(8,128)}, u32[]{:S(2)}) copy-start(f32[4,16,32,128]{3,2,1,0:T(8,128)} %param.18) | copy-start | bytes 3145732
  3.1 0.8 %copy-start.4 = (f32[2,1,1,32,32]{4,3,2,1,0:T(8,128)S(1)}, f32[2,1,1,32,32]{4,3,2,1,0:T(8,128)}, u32[]{:S(2)}) copy-start(f32[2,1,1,32,32]{4,3,2,1,0:T(8,128)} %param.20) | copy-start | bytes 24580
  3.9 0.8 %copy-start.5 = (f32[2,1,1,32,32]{4,3,2,1,0:T(8,128)S(1)}, f32[2,1,1,32,32]{4,3,2,1,0:T(8,128)}, u32[]{:S(2)}) copy-start(f32[2,1,1,32,32]{4,3,2,1,0:T(8,128)} %param.21) | copy-start | bytes 24580
  4.7 2.4 %copy-start.6 = (s32[9,4,16]{2,1,0:T(4,128)S(1)}, s32[9,4,16]{2,1,0:T(4,128)}, u32[]{:S(2)}) copy-start(s32[9,4,16]{2,1,0:T(4,128)} %mask.15) | copy-start | bytes 6916
  4.7 2.4 %copy-start.14 = (s32[52]{0:T(128)S(1)}, s32[52]{0:T(128)}, u32[]{:S(2)}) copy-start(s32[52]{0:T(128)} %constant.27.clone.table) | copy-start | bytes 628
  6.9 5.1 %collective-permute-start = (f32[480,128]{1,0:T(8,128)S(1)}, f32[480,128]{1,0:T(8,128)S(1)}, u32[]{:S(2)}, u32[]{:S(2)}) collective-permute-start(f32[480,128]{1,0:T(8,128)S(1)} %get-tuple-element.51.mine), channel_id=1, source_target_pairs={{0,16},{16,0},{32,48},{48,32},{64,80},{80,64},{96,112},{112,96},{1... | collective-permute-start | bytes 737288 | tf_op jit(solution)/shard_map/ppermute | solution.py:378
  7.1 7.0 %copy-start.13 = (s32[60]{0:T(128)S(1)}, s32[60]{0:T(128)}, u32[]{:S(2)}) copy-start(s32[60]{0:T(128)} %constant.28.clone.table) | copy-start | bytes 724
  12.3 10.5 %copy-start.12 = (s32[52]{0:T(128)S(1)}, s32[52]{0:T(128)}, u32[]{:S(2)}) copy-start(s32[52]{0:T(128)} %constant.29.clone.table) | copy-start | bytes 628
  12.3 7.3 %collective-permute-start.1 = (f32[304,128]{1,0:T(8,128)S(1)}, f32[304,128]{1,0:T(8,128)S(1)}, u32[]{:S(2)}, u32[]{:S(2)}) collective-permute-start(f32[304,128]{1,0:T(8,128)S(1)} %level.5.mine), channel_id=1, source_target_pairs={{0,32},{16,48},{32,0},{48,16},{64,96},{80,112},{96,64},{112,80},{1... | collective-permute-start | bytes 466952 | tf_op jit(solution)/shard_map/ppermute | solution.py:378
  19.8 7.9 %collective-permute-start.2 = (f32[304,128]{1,0:T(8,128)S(1)}, f32[304,128]{1,0:T(8,128)S(1)}, u32[]{:S(2)}, u32[]{:S(2)}) collective-permute-start(f32[304,128]{1,0:T(8,128)S(1)} %level.6.mine), channel_id=1, source_target_pairs={{0,64},{16,80},{32,96},{48,112},{64,0},{80,16},{96,32},{112,48},{1... | collective-permute-start | bytes 466952 | tf_op jit(solution)/shard_map/ppermute | solution.py:378
  27.7 3.7 %copy-start.11 = (s32[60]{0:T(128)S(1)}, s32[60]{0:T(128)}, u32[]{:S(2)}) copy-start(s32[60]{0:T(128)} %constant.30.clone.table) | copy-start | bytes 724
  28.5 8.4 %collective-permute-start.3 = (f32[272,128]{1,0:T(8,128)S(1)}, f32[272,128]{1,0:T(8,128)S(1)}, u32[]{:S(2)}, u32[]{:S(2)}) collective-permute-start(f32[272,128]{1,0:T(8,128)S(1)} %get-tuple-element.69.mine), channel_id=1, source_target_pairs={{0,1},{1,0},{2,3},{3,2},{4,5},{5,4},{6,7},{7,6},{8,9},{9,8},{10,11... | collective-permute-start | bytes 417800 | tf_op jit(solution)/shard_map/ppermute | solution.py:378
  31.4 9.5 %copy-start.10 = (s32[60]{0:T(128)S(1)}, s32[60]{0:T(128)}, u32[]{:S(2)}) copy-start(s32[60]{0:T(128)} %constant.31.clone.table) | copy-start | bytes 724
  37.2 11.0 %copy-start.9 = (s32[44]{0:T(128)S(1)}, s32[44]{0:T(128)}, u32[]{:S(2)}) copy-start(s32[44]{0:T(128)} %constant.32.clone.table) | copy-start | bytes 532
  37.2 9.2 %collective-permute-start.4 = (f32[200,128]{1,0:T(8,128)S(1)}, f32[200,128]{1,0:T(8,128)S(1)}, u32[]{:S(2)}, u32[]{:S(2)}) collective-permute-start(f32[200,128]{1,0:T(8,128)S(1)} %level.7.mine), channel_id=1, source_target_pairs={{0,2},{1,3},{2,0},{3,1},{4,6},{5,7},{6,4},{7,5},{8,10},{9,11},{10,... | collective-permute-start | bytes 307208 | tf_op jit(solution)/shard_map/ppermute | solution.py:378
  46.7 5.9 %collective-permute-start.5 = (f32[200,128]{1,0:T(8,128)S(1)}, f32[200,128]{1,0:T(8,128)S(1)}, u32[]{:S(2)}, u32[]{:S(2)}) collective-permute-start(f32[200,128]{1,0:T(8,128)S(1)} %level.8.mine), channel_id=1, source_target_pairs={{0,4},{1,5},{2,6},{3,7},{4,0},{5,1},{6,2},{7,3},{8,12},{9,13},{10,... | collective-permute-start | bytes 307208 | tf_op jit(solution)/shard_map/ppermute | solution.py:378
  48.2 7.4 %copy-start.8 = (s32[60]{0:T(128)S(1)}, s32[60]{0:T(128)}, u32[]{:S(2)}) copy-start(s32[60]{0:T(128)} %constant.33.clone.table) | copy-start | bytes 724
  52.8 8.3 %collective-permute-start.6 = (f32[200,128]{1,0:T(8,128)S(1)}, f32[200,128]{1,0:T(8,128)S(1)}, u32[]{:S(2)}, u32[]{:S(2)}) collective-permute-start(f32[200,128]{1,0:T(8,128)S(1)} %level.9.mine), channel_id=1, source_target_pairs={{0,8},{1,9},{2,10},{3,11},{4,12},{5,13},{6,14},{7,15},{8,0},{9,1},... | collective-permute-start | bytes 307208 | tf_op jit(solution)/shard_map/ppermute | solution.py:378
  61.1 1.6 %copy-start.7 = (s32[28]{0:T(128)S(1)}, s32[28]{0:T(128)}, u32[]{:S(2)}) copy-start(s32[28]{0:T(128)} %constant.34.clone.table) | copy-start | bytes 340
  62.7 3.1 %copy-start.3 = (f32[4,16,32,128]{3,2,1,0:T(8,128)S(1)}, f32[4,16,32,128]{3,2,1,0:T(8,128)}, u32[]{:S(2)}) copy-start(f32[4,16,32,128]{3,2,1,0:T(8,128)} %param.19) | copy-start | bytes 3145732

commit v4 on v3

--- a/solution.py
+++ b/solution.py
@@ -31,7 +31,6 @@
 groups = leaves // group
 batch = 4
 vmem = pl.BlockSpec(memory_space=pltpu.VMEM)
-smem = pl.BlockSpec(memory_space=pltpu.SMEM)
 
 
 def params(mib):
@@ -42,53 +41,66 @@
     return pl.CostEstimate(flops=int(cycles * 400_000), bytes_accessed=1 << 18, transcendentals=0)
 
 
-def inside(i, j):
-    return 0 <= i < leaf_rows and 0 <= j < leaf_cols
-
-
-def own_slot(i, j):
-    return i * leaf_cols + j
-
-
-def halo_slot(i, j):
-    if 0 <= j < leaf_cols:
-        return j if i < 0 else leaf_cols + j
-    return i + 1 if j < 0 else 8 + i + 1
-
-
-def pack_item(source, target, di, dj, both):
-    return source | target << 7 | (3 * (di + 1) + dj + 1) << 14 | both << 18 | 1 << 19
-
-
-def interior_items():
-    items = []
-    for i in range(leaf_rows):
-        for j in range(leaf_cols):
-            here = own_slot(i, j)
-            items.append(pack_item(here, here, 0, 0, 0))
-            for di, dj in ((0, 1), (1, -1), (1, 0), (1, 1)):
-                if inside(i + di, j + dj):
-                    items.append(pack_item(here, own_slot(i + di, j + dj), -di, -dj, 1))
-    return items
-
-
-def halo_items(sides):
-    items = []
-    for i in range(-1, leaf_rows + 1):
-        for j in range(-1, leaf_cols + 1):
-            if inside(i, j) or sides == (0 <= j < leaf_cols):
-                continue
-            for di in (-1, 0, 1):
-                for dj in (-1, 0, 1):
-                    if inside(i - di, j - dj):
-                        items.append(pack_item(halo_slot(i, j), own_slot(i - di, j - dj), di, dj, 0))
-    return items
-
-
-def item_table(items):
-    idle = pack_item(0, 0, 0, 0, 0) & ~(1 << 19)
-    padded = items + [idle] * (-len(items) % (2 * batch))
-    return np.array(padded + [idle] * batch, np.int32), len(padded) // (2 * batch)
+class Run:
+    def __init__(self, count, skip, source, step, target, offset, both):
+        self.count, self.skip, self.source, self.step, self.target = count, skip, source, step, target
+        self.offset, self.both = offset, both
+
+
+def interior_runs():
+    across, down = leaf_rows * (leaf_cols - 1), (leaf_rows - 1) * (leaf_cols - 1)
+    return [
+        Run(leaves, 0, 0, 1, 0, 4, False),
+        Run(across, 1, 0, 1, 1, 3, True),
+        Run(leaves - leaf_cols, 0, 0, 1, leaf_cols, 1, True),
+        Run(down, 1, 0, 1, leaf_cols + 1, 0, True),
+        Run(down, 1, 1, 1, leaf_cols, 2, True),
+    ]
+
+
+def edge_runs():
+    runs = []
+    for first, row, di in ((0, 0, -1), (leaf_cols, leaf_rows - 1, 1)):
+        for dj in (-1, 0, 1):
+            start = max(0, -dj)
+            at = row * leaf_cols + start
+            runs.append(Run(leaf_cols - abs(dj), 0, first + start + dj, 1, at, 3 * (di + 1) + dj + 1, False))
+    return runs
+
+
+def side_runs():
+    runs = []
+    for first, column, dj in ((0, 0, -1), (8, leaf_cols - 1, 1)):
+        for di in (-1, 0, 1):
+            runs.append(Run(leaf_rows, 0, first + 1 + di, leaf_cols, column, 3 * (di + 1) + dj + 1, False))
+    return runs
+
+
+def cut_runs(runs, first, last):
+    pieces, at = [], 0
+    for run in runs:
+        low, high = max(first - at, 0), min(last - at, run.count)
+        if low < high:
+            pieces.append((run, low, high))
+        at += run.count
+    return pieces
+
+
+zero_row = 9 * leaves
+
+
+def fields(pieces, at):
+    found, begin = None, 0
+    for run, low, high in pieces:
+        q = at - begin + low
+        begin += high - low
+        moved = q + (q * 274 >> 12) if run.skip else q
+        source, target = moved + run.source, run.step * moved + run.target
+        here = [source, target, run.offset * leaves + target, (8 - run.offset) * leaves + source if run.both else zero_row]
+        found = here if found is None else [jnp.where(inside_run, old, new) for old, new in zip(found, here)]
+        inside_run = at < begin
+    idle = [0, 0, zero_row, zero_row]
+    return [jnp.where(inside_run, old, new) for old, new in zip(found, idle)]
 
 
 def split(value):
@@ -160,21 +172,28 @@
         blocks[2 * n], blocks[2 * n + 1] = split(wide)
 
 
-def prep_kernel(place, coords, sources, row_transfer, col_transfer, compress_far, left, right, heights, halves, payload, row_blocks, col_blocks, wide, compress, arrived):
-    fetch = pltpu.make_async_copy(compress_far, compress, arrived)
-    fetch.start()
+def prep_kernel(
+    coords_far, sources_far, mask_far, row_far, col_far, compress_far,
+    left, right, heights, halves, payload, row_blocks, col_blocks, weights,
+    wide, coords, sources, mask, row_transfer, col_transfer, compress, arrived,
+):
+    fars = (coords_far, sources_far, compress_far, row_far, col_far, mask_far)
+    heres = (coords, sources, compress, row_transfer, col_transfer, mask)
+    copies = [pltpu.make_async_copy(far, here, arrived.at[n]) for n, (far, here) in enumerate(zip(fars, heres))]
+    for copy in copies:
+        copy.start()
+    copies[0].wait()
+    copies[1].wait()
     start = [coords[c * leaves : c * leaves + 1, 0:1] for c in range(3)]
     fill_tables(leaves, start, coords, sources, left, right, heights, halves, wide)
-    spread_blocks(row_transfer, row_blocks)
-    spread_blocks(col_transfer, col_blocks)
-    odd = place[0] % 2
+    odd = lax.axis_index("row") % 2
     for k in range(2):
         row = (leaf_rows - 1) * (1 - odd if k == 0 else odd)
         for c in range(3 + rhs):
             ref, at = (coords, c) if c < 3 else (sources, c - 3)
             to = points + k * edge_rows + c * leaf_cols
             payload[to : to + leaf_cols, :] = ref[pl.ds(pl.multiple_of(at * leaves + row * leaf_cols, 8), leaf_cols), :]
-    fetch.wait()
+    copies[2].wait()
     for g in range(groups):
         high, low = split(compress[g * points : (g + 1) * points, :])
         got = dot_t(halves[g * 16 * group : (g + 1) * 16 * group, :], jnp.concatenate([high, low], axis=0))
@@ -183,6 +202,18 @@
         for n in range(group):
             total = jnp.where(lane_block(n), got[n * 16 : n * 16 + 8] + got[n * 16 + 8 : n * 16 + 16], total)
         payload[g * rhs : (g + 1) * rhs, :] = total
+    for copy in copies[3:]:
+        copy.wait()
+    spread_blocks(row_transfer, row_blocks)
+    spread_blocks(col_transfer, col_blocks)
+    diagonal = lax.broadcasted_iota(jnp.int32, (leaf_cols, leaf_cols), 0) == lax.broadcasted_iota(jnp.int32, (leaf_cols, leaf_cols), 1)
+    ones = jnp.ones((leaf_cols, points), bf16)
+    for k in range(9):
+        for i in range(leaf_rows):
+            spread = jnp.where(diagonal, mask[k, i : i + 1, :].astype(f32), 0.0).astype(bf16)
+            at = k * leaves + i * leaf_cols
+            weights[at : at + leaf_cols, :] = dot(spread, ones)
+    weights[zero_row : zero_row + 8, :] = jnp.zeros((8, points), f32)
 
 
 def halo_prep_kernel(count, start_at, values, left, right, heights, halves, wide):
@@ -219,9 +250,9 @@
     payload[points:, :] = theirs[forward:, :]
 
 
-def turn_kernel(place, mine, theirs, blocks, coords, sources, first, second, payload, edges):
+def turn_kernel(mine, theirs, blocks, coords, sources, first, second, payload, edges):
     payload[:points, :] = level(mine[:points, :], theirs[:points, :], blocks)
-    row, col = place[0], place[1]
+    row, col = lax.axis_index("row"), lax.axis_index("col")
     odd = row % 2 == 1
     around = (row % 4 == 1) | (row % 4 == 2)
     inner = (row > 0) & (row < lax.axis_size("row") - 1)
@@ -243,9 +274,9 @@
         payload[base + 66 : base + side_rows, :] = jnp.zeros((side_rows - 66, points), f32)
 
 
-def sides_kernel(place, mine, theirs, blocks, first, second, third, coeffs, sides):
+def sides_kernel(mine, theirs, blocks, first, second, third, coeffs, sides):
     coeffs[...] = level(mine[:points, :], theirs[:points, :], blocks)
-    col = place[1]
+    col = lax.axis_index("col")
     odd = col % 2 == 1
     inner = (col > 0) & (col < lax.axis_size("col") - 1)
     at = slice(points, points + side_rows)
@@ -260,23 +291,18 @@
         sides[c * side_leaves : (c + 1) * side_leaves, :] = jnp.concatenate([to_left[at], gap, to_right[at], gap], axis=0)
 
 
-def near_kernel(trips, both_ways, table, mask, left, source_heights, source_halves, right, heights, halves, seed, acc, gap_a, gap_b, splat_a, splat_b, kern_a, kern_b):
+def near_kernel(pieces, trips, both_ways, weights, left, source_heights, source_halves, right, heights, halves, seed, acc, gap_a, gap_b, splat_a, splat_b, kern_a, kern_b):
     acc[...] = seed[...]
     kern_b[...] = jnp.zeros_like(kern_b)
     buffers_a, buffers_b = (gap_a, splat_a, kern_a), (gap_b, splat_b, kern_b)
 
-    def fields(at):
-        word = table[at]
-        return word & 127, word >> 7 & 127, word >> 14 & 15, word >> 18 & 1, word >> 19 & 1
-
-    def subtract(at, n, gap, splat):
-        source, target = fields(at + n)[:2]
+    def subtract(item, n, gap, splat):
+        source, target = item[:2]
         gap[n] = dot(left[pl.ds(pl.multiple_of(source * points, points), points), :], right[sixteen(target), :])
         splat[n] = jnp.broadcast_to(source_heights[pl.ds(source, 1), :], (points, points)).T
 
-    def evaluate(at, n, gap, splat, kern):
-        target = fields(at + n)[1]
-        height = heights[pl.ds(target, 1), :]
+    def evaluate(item, n, gap, splat, kern):
+        height = heights[pl.ds(item[1], 1), :]
         for g in range(points // 32):
             at_rows = slice(32 * g, 32 * g + 32)
             dx, dy, dz = gap[n, at_rows, :points], gap[n, at_rows, points:], splat[n, at_rows] - height
@@ -291,48 +317,52 @@
             kern[n, 0, at_rows] = high
             kern[n, 1, at_rows] = low
 
-    def weight_of(leaf, k, on):
-        return (mask[k, leaf // leaf_cols, leaf % leaf_cols] * on).astype(f32)
-
-    def apply(at, n, kern):
-        source, target, k, both, valid = fields(at + n)
+    def apply(item, n, kern):
+        source, target, target_weight, source_weight = item
         pair = jnp.concatenate([kern[n, 0], kern[n, 1]], axis=1)
         got = dot(source_halves[sixteen(source), :], pair)
         got = got[:, :points] + got[:, points:]
-        acc[pl.ds(target * 8, 8), :] += (got[:8] + got[8:]) * weight_of(target, k, valid)
+        acc[pl.ds(target * 8, 8), :] += (got[:8] + got[8:]) * weights[pl.ds(target_weight, 1), :]
         if both_ways:
             mine = halves[sixteen(target), :]
             got = dot_t(jnp.concatenate([mine, mine], axis=1), pair)
-            acc[pl.ds(source * 8, 8), :] += (got[:8] + got[8:]) * weight_of(source, 8 - k, both)
-
-    def stage(at, here, there):
+            acc[pl.ds(source * 8, 8), :] += (got[:8] + got[8:]) * weights[pl.ds(source_weight, 1), :]
+
+    def items_at(at):
+        return [fields(pieces, at + n) for n in range(batch)]
+
+    def stage(at, earlier, now, here, there):
+        later = items_at(at + batch)
         for n in range(batch):
-            apply(jnp.maximum(at - batch, 0), n, there[2])
+            apply(earlier[n], n, there[2])
         for n in range(batch):
-            subtract(at + batch, n, *there[:2])
+            subtract(later[n], n, *there[:2])
         for n in range(batch):
-            evaluate(at, n, *here)
+            evaluate(now[n], n, *here)
+        return now, later
 
     def body(trip, carry):
-        stage(trip * 2 * batch, buffers_a, buffers_b)
-        stage(trip * 2 * batch + batch, buffers_b, buffers_a)
-        return carry
-
+        carry = stage(trip * 2 * batch, *carry, buffers_a, buffers_b)
+        return stage(trip * 2 * batch + batch, *carry, buffers_b, buffers_a)
+
+    first = items_at(jnp.int32(0))
     for n in range(batch):
-        subtract(0, n, *buffers_a[:2])
-    lax.fori_loop(0, trips, body, 0)
+        subtract(first[n], n, *buffers_a[:2])
+    nothing = [[jnp.int32(0), jnp.int32(0), jnp.int32(zero_row), jnp.int32(zero_row)]] * batch
+    last, _ = lax.fori_loop(0, trips, body, (nothing, first))
     for n in range(batch):
-        apply(trips * 2 * batch - batch, n, buffers_b[2])
-
-
-def near_piece(items, both_ways, mask, source_tables, target_tables, seed):
-    table, trips = item_table(items)
+        apply(last[n], n, buffers_b[2])
+
+
+def near_piece(pieces, both_ways, weights, source_tables, target_tables, seed):
+    count = sum(high - low for _, low, high in pieces)
+    trips = -(-count // (2 * batch))
     left, _, source_heights, source_halves = source_tables
     _, right, heights, halves = target_tables
     return pl.pallas_call(
-        functools.partial(near_kernel, trips, both_ways),
+        functools.partial(near_kernel, pieces, trips, both_ways),
         out_shape=jax.ShapeDtypeStruct(seed.shape, f32),
-        in_specs=[smem, smem] + [vmem] * 7,
+        in_specs=[vmem] * 8,
         out_specs=vmem,
         scratch_shapes=[
             shape
@@ -344,9 +374,9 @@
             for _ in range(2)
         ],
         compiler_params=params(16),
-        cost_estimate=cost(len(items) * 110),
+        cost_estimate=cost(count * 110),
         name="near",
-    )(jnp.asarray(table), mask, left, source_heights, source_halves, right, heights, halves, seed)
+    )(weights, left, source_heights, source_halves, right, heights, halves, seed)
 
 
 def finish_kernel(coeffs, expand, acc, out):
@@ -382,12 +412,12 @@
     return jax.ShapeDtypeStruct(shape, f32)
 
 
-def small_call(body, name, out_shape, scalars, *operands):
+def small_call(body, name, out_shape, *operands):
     single = not isinstance(out_shape, tuple)
     return pl.pallas_call(
         body,
         out_shape=out_shape,
-        in_specs=[smem] * scalars + [vmem] * (len(operands) - scalars),
+        in_specs=[vmem] * len(operands),
         out_specs=vmem if single else (vmem,) * len(out_shape),
         compiler_params=params(16),
         cost_estimate=cost(600),
@@ -396,26 +426,34 @@
 
 
 def shards(coords, sources, neighbour_mask, compress, expand, row_transfer, col_transfer):
-    place = jnp.stack([lax.axis_index("row"), lax.axis_index("col")]).astype(jnp.int32)
     coords = coords.reshape(-1, points)
     sources = sources.reshape(-1, points)
     block_shape = jax.ShapeDtypeStruct((4, points, points), bf16)
-    *own, payload, row_blocks, col_blocks = pl.pallas_call(
+    *own, payload, row_blocks, col_blocks, weights = pl.pallas_call(
         prep_kernel,
-        out_shape=table_shapes(leaves) + (array(points + 2 * edge_rows, points), block_shape, block_shape),
-        in_specs=[smem] + [vmem] * 4 + [pl.BlockSpec(memory_space=pl.ANY)],
-        out_specs=(vmem,) * 7,
-        scratch_shapes=[pltpu.VMEM((leaves * 16, points), f32), pltpu.VMEM((leaves * rank, points), f32), pltpu.SemaphoreType.DMA],
+        out_shape=table_shapes(leaves) + (array(points + 2 * edge_rows, points), block_shape, block_shape, array(zero_row + 8, points)),
+        in_specs=[pl.BlockSpec(memory_space=pl.ANY)] * 6,
+        out_specs=(vmem,) * 8,
+        scratch_shapes=[
+            pltpu.VMEM((leaves * 16, points), f32),
+            pltpu.VMEM((3 * leaves, points), f32),
+            pltpu.VMEM((rhs * leaves, points), f32),
+            pltpu.VMEM((9, leaf_rows, leaf_cols), jnp.int32),
+            pltpu.VMEM((2, rank, rank), f32),
+            pltpu.VMEM((2, rank, rank), f32),
+            pltpu.VMEM((leaves * rank, points), f32),
+            pltpu.SemaphoreType.DMA((6,)),
+        ],
         compiler_params=params(24),
         cost_estimate=cost(3000),
         name="prep",
-    )(place, coords, sources, row_transfer[:, 0, 0], col_transfer[:, 0, 0], compress.reshape(-1, points))
-    items = interior_items()
-    row_items, col_items = halo_items(False), halo_items(True)
+    )(coords, sources, neighbour_mask, row_transfer[:, 0, 0], col_transfer[:, 0, 0], compress.reshape(-1, points))
     row_bits, col_bits = (lax.axis_size(axis).bit_length() - 1 for axis in ("row", "col"))
     inner_pieces = row_bits + col_bits - 2
-    cuts = [len(items) * n // inner_pieces // 8 * 8 for n in range(inner_pieces)] + [len(items)]
-    half = len(row_items) // 2 // 8 * 8
+    inner, edge, side = interior_runs(), edge_runs(), side_runs()
+    counts = [sum(run.count for run in runs) for runs in (inner, edge, side)]
+    cuts = [counts[0] * n // inner_pieces // 8 * 8 for n in range(inner_pieces)] + [counts[0]]
+    half = counts[1] // 2 // 8 * 8
     acc = jnp.zeros((leaves * rhs, points), f32)
     above_below = None
     received = []
@@ -425,10 +463,10 @@
         theirs = partner_of(payload, "row" if over_row else "col", n if over_row else n - row_bits)
         payload, acc = lax.optimization_barrier((payload, acc))
         if n < inner_pieces:
-            acc = near_piece(items[cuts[n] : cuts[n + 1]], True, neighbour_mask, own, own, acc)
+            acc = near_piece(cut_runs(inner, cuts[n], cuts[n + 1]), True, weights, own, own, acc)
         else:
-            some = row_items[:half] if n == inner_pieces else row_items[half:]
-            acc = near_piece(some, False, neighbour_mask, above_below, own, acc)
+            some = cut_runs(edge, 0, half) if n == inner_pieces else cut_runs(edge, half, counts[1])
+            acc = near_piece(some, False, weights, above_below, own, acc)
         theirs, acc = lax.optimization_barrier((theirs, acc))
         received.append(theirs)
         if n == row_bits - 1:
@@ -436,24 +474,22 @@
                 turn_kernel,
                 "turn",
                 (array(points + 2 * side_rows, points), array((3 + rhs) * edge_leaves, points)),
-                1,
-                place, payload, theirs, blocks, coords, sources, received[0], received[1],
+                payload, theirs, blocks, coords, sources, received[0], received[1],
             )
         elif n == row_bits + col_bits - 1:
             coeffs, sides = small_call(
                 sides_kernel,
                 "sides",
                 (array(points, points), array((3 + rhs) * side_leaves, points)),
-                1,
-                place, payload, theirs, blocks, received[row_bits], received[row_bits + 1], received[row_bits + 2],
+                payload, theirs, blocks, received[row_bits], received[row_bits + 1], received[row_bits + 2],
             )
         else:
             rows = edge_rows if over_row else side_rows
             skip = points + rows if n in (0, row_bits) else points
-            payload = small_call(functools.partial(level_kernel, skip), "level", array(points + rows, points), 0, payload, theirs, blocks)
+            payload = small_call(functools.partial(level_kernel, skip), "level", array(points + rows, points), payload, theirs, blocks)
         if n == row_bits:
             above_below = halo_prep(edge_leaves, coords, edges)
-    acc = near_piece(col_items, False, neighbour_mask, halo_prep(side_leaves, coords, sides), own, acc)
+    acc = near_piece(cut_runs(side, 0, counts[2]), False, weights, halo_prep(side_leaves, coords, sides), own, acc)
     out = pl.pallas_call(
         finish_kernel,
         out_shape=array(rhs * leaves, points),

time: 67.2 us -> 60.3 us (0.90)
  Pallas kernels: 47 us -> 38.8 us
    pallas_call x15, Pallas kernels: 42.1 us -> 34 us  [the longest x8 32.3 us: near_piece(): pl.pallas_call(functools.partial(near_kernel, pieces, trips, both_ways),...]
    unnamed x30 -> x14, local copies, waits for them, and re-layouts: 4.63 us -> 5.31 us
  transfers between devices with their start and end apart: 7 -> 7, of which waited for: 0 -> 2; matrix products, arithmetic and copies ran while one was open for 0% -> 0% of each run, Pallas kernels for 56% -> 52%
where the time goes in v4:
time: 60.3 us; the launch traced here: 59.9 us
  Pallas kernels  38.8 us (64%)
  starting transfers between devices  15.2 us (25%)
  local copies, waits for them, and re-layouts  5.32 us (9%)
    pallas_call x8, Pallas kernels, near_piece(): pl.pallas_call(functools.partial(near_kernel, pieces, trips, both_ways),...  32.3 us
    ppermute x7, starting transfers between devices, partner_of(): return lax.ppermute(block, axis, route)  15.2 us
    unnamed x14, local copies, waits for them, and re-layouts  5.31 us
    pallas_call x1, Pallas kernels, shards(): pl.pallas_call(prep_kernel, out_shape=table_shapes(leaves) + (array(point...  2.11 us
    pallas_call x7, Pallas kernels, small_call(): pl.pallas_call(body, out_shape=out_shape, in_specs=[vmem] * len(operands)...  1.69 us
    pallas_call x2, Pallas kernels, halo_prep(): pl.pallas_call(functools.partial(halo_prep_kernel, count), out_shape=tabl...  1.65 us
  transfers between devices with their start and end apart: 7, of which 2 were waited for; matrix products, arithmetic and copies ran while one was open for 0% of the time, Pallas kernels for 52%

profile of v4, /device:TPU:0, one launch (start us, length us, event | category | flops | bytes accessed | tf_op | source)
XLA Modules:
  0.0 59.9 jit_solution(6300513258099906207)
XLA Ops:
  0.0 0.0 copy-start
  0.0 0.9 %copy-done = f32[8,4,16,128]{3,2,1,0:T(8,128)S(1)} copy-done((f32[8,4,16,128]{3,2,1,0:T(8,128)S(1)}, f32[8,4,16,128]{3,2,1,0:T(8,128)}, u32[]{:S(2)}) %copy-start) | copy-done | bytes 262168
  1.0 0.0 copy-start.1
  1.0 0.9 %copy-done.1 = f32[3,4,16,128]{3,2,1,0:T(8,128)S(1)} copy-done((f32[3,4,16,128]{3,2,1,0:T(8,128)S(1)}, f32[3,4,16,128]{3,2,1,0:T(8,128)}, u32[]{:S(2)}) %copy-start.1) | copy-done | bytes 98328
  1.8 0.0 copy-start.2
  1.8 1.2 %copy-done.2 = f32[4,16,32,128]{3,2,1,0:T(8,128)S(1)} copy-done((f32[4,16,32,128]{3,2,1,0:T(8,128)S(1)}, f32[4,16,32,128]{3,2,1,0:T(8,128)}, u32[]{:S(2)}) %copy-start.2) | copy-done | bytes 1048600
  3.1 0.0 copy-start.4
  3.1 0.8 %copy-done.4 = f32[2,1,1,32,32]{4,3,2,1,0:T(8,128)S(1)} copy-done((f32[2,1,1,32,32]{4,3,2,1,0:T(8,128)S(1)}, f32[2,1,1,32,32]{4,3,2,1,0:T(8,128)}, u32[]{:S(2)}) %copy-start.4) | copy-done | bytes 8216
  3.8 0.0 copy-start.5
  3.8 0.8 %copy-done.5 = f32[2,1,1,32,32]{4,3,2,1,0:T(8,128)S(1)} copy-done((f32[2,1,1,32,32]{4,3,2,1,0:T(8,128)S(1)}, f32[2,1,1,32,32]{4,3,2,1,0:T(8,128)}, u32[]{:S(2)}) %copy-start.5) | copy-done | bytes 8216
  4.6 0.0 copy-start.6
  4.6 0.7 %copy-done.6 = s32[9,4,16]{2,1,0:T(4,128)S(1)} copy-done((s32[9,4,16]{2,1,0:T(4,128)S(1)}, s32[9,4,16]{2,1,0:T(4,128)}, u32[]{:S(2)}) %copy-start.6) | copy-done | bytes 2328
  5.3 2.1 %prep.1 = (bf16[8192,16]{1,0:T(8,128)(2,1)S(1)}, bf16[1024,256]{1,0:T(8,128)(2,1)S(1)}, f32[64,128]{1,0:T(8,128)S(1)}, bf16[1024,128]{1,0:T(8,128)(2,1)S(1)}, f3...) custom-call(f32[192,128]{1,0:T(8,128)S(1)} %bitcast.9, ...), custom_call_target="tpu_custom_call" | custom-call | flops 1200000000 | bytes 262144 | tf_op jit(solution)/shard_map/prep/pallas_call | solution.py:432
  7.4 0.1 collective-permute-start
  7.5 4.1 %near.8.seed = f32[512,128]{1,0:T(8,128)S(1)} custom-call(f32[584,128]{1,0:T(8,128)S(1)} %get-tuple-element.53.weights, bf16[8192,16]{1,0:T(8,128)(2,1)S(1)} %get-tuple-element.54.left, f32[64,128]{1,0:T(8,128)S(1)} %get-tuple-element.55.source_heights.heights, bf16[1024,128]{1,0:T(8,128)(2,1)S(1)} %get-tuple-element.56.source_halves.halves, ...), custom_call_target="tpu_custom_call" | custom-call | flops 2112000000 | bytes 262144 | tf_op jit(solution)/shard_map/near/pallas_call | solution.py:362
  11.6 0.0 collective-permute-done.theirs.first
  11.6 0.2 level.5.mine
  11.9 1.7 %collective-permute-start.1 = (f32[304,128]{1,0:T(8,128)S(1)}, f32[304,128]{1,0:T(8,128)S(1)}, u32[]{:S(2)}, u32[]{:S(2)}) collective-permute-start(f32[304,128]{1,0:T(8,128)S(1)} %level.5.mine), channel_id=1, source_target_pairs={{0,32},{16,48},{32,0},{48,16},{64,96},{80,112},{96,64},{112,80},{1... | collective-permute-start | bytes 466952 | tf_op jit(solution)/shard_map/ppermute | solution.py:408
  13.6 4.7 %near.9.seed = f32[512,128]{1,0:T(8,128)S(1)} custom-call(f32[584,128]{1,0:T(8,128)S(1)} %get-tuple-element.53.weights, bf16[8192,16]{1,0:T(8,128)(2,1)S(1)} %get-tuple-element.54.left, f32[64,128]{1,0:T(8,128)S(1)} %get-tuple-element.55.source_heights.heights, bf16[1024,128]{1,0:T(8,128)(2,1)S(1)} %get-tuple-element.56.source_halves.halves, ...), custom_call_target="tpu_custom_call" | custom-call | flops 2464000000 | bytes 262144 | tf_op jit(solution)/shard_map/near/pallas_call | solution.py:362
  18.3 0.1 collective-permute-done.1.theirs.second
  18.4 0.2 level.6.mine
  18.6 3.4 %collective-permute-start.2 = (f32[304,128]{1,0:T(8,128)S(1)}, f32[304,128]{1,0:T(8,128)S(1)}, u32[]{:S(2)}, u32[]{:S(2)}) collective-permute-start(f32[304,128]{1,0:T(8,128)S(1)} %level.6.mine), channel_id=1, source_target_pairs={{0,64},{16,80},{32,96},{48,112},{64,0},{80,16},{96,32},{112,48},{1... | collective-permute-start | bytes 466952 | tf_op jit(solution)/shard_map/ppermute | solution.py:408
  22.0 4.1 %near.10.seed = f32[512,128]{1,0:T(8,128)S(1)} custom-call(f32[584,128]{1,0:T(8,128)S(1)} %get-tuple-element.53.weights, bf16[8192,16]{1,0:T(8,128)(2,1)S(1)} %get-tuple-element.54.left, f32[64,128]{1,0:T(8,128)S(1)} %get-tuple-element.55.source_heights.heights, bf16[1024,128]{1,0:T(8,128)(2,1)S(1)} %get-tuple-element.56.source_halves.halves, ...), custom_call_target="tpu_custom_call" | custom-call | flops 2112000000 | bytes 262144 | tf_op jit(solution)/shard_map/near/pallas_call | solution.py:362
  26.0 0.2 collective-permute-done.2.theirs
  26.3 0.3 turn.1
  26.5 2.0 %collective-permute-start.3 = (f32[272,128]{1,0:T(8,128)S(1)}, f32[272,128]{1,0:T(8,128)S(1)}, u32[]{:S(2)}, u32[]{:S(2)}) collective-permute-start(f32[272,128]{1,0:T(8,128)S(1)} %get-tuple-element.71.mine), channel_id=1, source_target_pairs={{0,1},{1,0},{2,3},{3,2},{4,5},{5,4},{6,7},{7,6},{8,9},{9,8},{10,11... | collective-permute-start | bytes 417800 | tf_op jit(solution)/shard_map/ppermute | solution.py:408
  28.5 0.9 %halo_prep.2 = (bf16[4096,16]{1,0:T(8,128)(2,1)S(1)}, bf16[512,256]{1,0:T(8,128)(2,1)}, f32[32,128]{1,0:T(8,128)S(1)}, bf16[512,128]{1,0:T(8,128)(2,1)S(1)}) custom-call(f32[192,128]{1,0:T(8,128)S(1)} %bitcast.11, f32[352,128]{1,0:T(8,128)S(1)} %get-tuple-element.81.values), custom_call_target="tpu_custom_call" | custom-call | flops 400000000 | bytes 262144 | tf_op jit(solution)/shard_map/halo_prep/pallas_call | solution.py:225
  29.4 4.6 %near.11.seed = f32[512,128]{1,0:T(8,128)S(1)} custom-call(f32[584,128]{1,0:T(8,128)S(1)} %get-tuple-element.53.weights, bf16[8192,16]{1,0:T(8,128)(2,1)S(1)} %get-tuple-element.54.left, f32[64,128]{1,0:T(8,128)S(1)} %get-tuple-element.55.source_heights.heights, bf16[1024,128]{1,0:T(8,128)(2,1)S(1)} %get-tuple-element.56.source_halves.halves, ...), custom_call_target="tpu_custom_call" | custom-call | flops 2464000000 | bytes 262144 | tf_op jit(solution)/shard_map/near/pallas_call | solution.py:362
  34.1 0.0 collective-permute-done.3.theirs.first
  34.1 0.2 level.7.mine
  34.3 3.7 %collective-permute-start.4 = (f32[200,128]{1,0:T(8,128)S(1)}, f32[200,128]{1,0:T(8,128)S(1)}, u32[]{:S(2)}, u32[]{:S(2)}) collective-permute-start(f32[200,128]{1,0:T(8,128)S(1)} %level.7.mine), channel_id=1, source_target_pairs={{0,2},{1,3},{2,0},{3,1},{4,6},{5,7},{6,4},{7,5},{8,10},{9,11},{10,... | collective-permute-start | bytes 307208 | tf_op jit(solution)/shard_map/ppermute | solution.py:408
  38.0 4.7 %near.12.seed = f32[512,128]{1,0:T(8,128)S(1)} custom-call(f32[584,128]{1,0:T(8,128)S(1)} %get-tuple-element.53.weights, bf16[8192,16]{1,0:T(8,128)(2,1)S(1)} %get-tuple-element.54.left, f32[64,128]{1,0:T(8,128)S(1)} %get-tuple-element.55.source_heights.heights, bf16[1024,128]{1,0:T(8,128)(2,1)S(1)} %get-tuple-element.56.source_halves.halves, ...), custom_call_target="tpu_custom_call" | custom-call | flops 2376000000 | bytes 262144 | tf_op jit(solution)/shard_map/near/pallas_call | solution.py:362
  42.7 0.0 collective-permute-done.4.theirs.second
  42.7 0.2 level.8.mine
  42.9 1.6 %collective-permute-start.5 = (f32[200,128]{1,0:T(8,128)S(1)}, f32[200,128]{1,0:T(8,128)S(1)}, u32[]{:S(2)}, u32[]{:S(2)}) collective-permute-start(f32[200,128]{1,0:T(8,128)S(1)} %level.8.mine), channel_id=1, source_target_pairs={{0,4},{1,5},{2,6},{3,7},{4,0},{5,1},{6,2},{7,3},{8,12},{9,13},{10,... | collective-permute-start | bytes 307208 | tf_op jit(solution)/shard_map/ppermute | solution.py:408
  44.5 3.4 %near.13.seed = f32[512,128]{1,0:T(8,128)S(1)} custom-call(f32[584,128]{1,0:T(8,128)S(1)} %get-tuple-element.53.weights, bf16[4096,16]{1,0:T(8,128)(2,1)S(1)} %get-tuple-element.82.left, f32[32,128]{1,0:T(8,128)S(1)} %get-tuple-element.83.source_heights, bf16[512,128]{1,0:T(8,128)(2,1)S(1)} %get-tuple-element.84.source_halves, ...), custom_call_target="tpu_custom_call" | custom-call | flops 1760000000 | bytes 262144 | tf_op jit(solution)/shard_map/near/pallas_call | solution.py:362
  47.9 0.0 collective-permute-done.5.theirs.third
  47.9 0.2 level.9.mine
  48.2 2.8 %collective-permute-start.6 = (f32[200,128]{1,0:T(8,128)S(1)}, f32[200,128]{1,0:T(8,128)S(1)}, u32[]{:S(2)}, u32[]{:S(2)}) collective-permute-start(f32[200,128]{1,0:T(8,128)S(1)} %level.9.mine), channel_id=1, source_target_pairs={{0,8},{1,9},{2,10},{3,11},{4,12},{5,13},{6,14},{7,15},{8,0},{9,1},... | collective-permute-start | bytes 307208 | tf_op jit(solution)/shard_map/ppermute | solution.py:408
  51.0 4.7 %near.14.seed = f32[512,128]{1,0:T(8,128)S(1)} custom-call(f32[584,128]{1,0:T(8,128)S(1)} %get-tuple-element.53.weights, bf16[4096,16]{1,0:T(8,128)(2,1)S(1)} %get-tuple-element.82.left, f32[32,128]{1,0:T(8,128)S(1)} %get-tuple-element.83.source_heights, bf16[512,128]{1,0:T(8,128)(2,1)S(1)} %get-tuple-element.84.source_halves, ...), custom_call_target="tpu_custom_call" | custom-call | flops 2288000000 | bytes 262144 | tf_op jit(solution)/shard_map/near/pallas_call | solution.py:362
  55.7 0.0 collective-permute-done.6.theirs
  55.7 0.2 sides.1
  55.9 0.8 %halo_prep.3 = (bf16[2048,16]{1,0:T(8,128)(2,1)S(1)}, bf16[256,256]{1,0:T(8,128)(2,1)}, f32[16,128]{1,0:T(8,128)S(1)}, bf16[256,128]{1,0:T(8,128)(2,1)S(1)}) custom-call(f32[192,128]{1,0:T(8,128)S(1)} %bitcast.12, f32[176,128]{1,0:T(8,128)S(1)} %get-tuple-element.92.values), custom_call_target="tpu_custom_call" | custom-call | flops 400000000 | bytes 262144 | tf_op jit(solution)/shard_map/halo_prep/pallas_call | solution.py:225
  56.7 0.0 copy-start.3
  56.7 2.1 %near.15.acc = f32[512,128]{1,0:T(8,128)S(1)} custom-call(f32[584,128]{1,0:T(8,128)S(1)} %get-tuple-element.53.weights, bf16[2048,16]{1,0:T(8,128)(2,1)S(1)} %get-tuple-element.93.left, f32[16,128]{1,0:T(8,128)S(1)} %get-tuple-element.94.source_heights, bf16[256,128]{1,0:T(8,128)(2,1)S(1)} %get-tuple-element.95.source_halves, ...), custom_call_target="tpu_custom_call" | custom-call | flops 1056000000 | bytes 262144 | tf_op jit(solution)/shard_map/near/pallas_call | solution.py:362
  58.8 0.0 copy-done.3
  58.8 1.1 %finish.1 = f32[512,128]{1,0:T(8,128)} custom-call(f32[128,128]{1,0:T(8,128)S(1)} %get-tuple-element.91.coeffs, f32[2048,128]{1,0:T(8,128)S(1)} %bitcast.14, f32[512,128]{1,0:T(8,128)S(1)} %near.15.acc), custom_call_target="tpu_custom_call" | custom-call | flops 800000000 | bytes 262144 | tf_op jit(solution)/shard_map/finish/pallas_call | solution.py:493
  (1 shorter events, 0.0 us)
Async XLA Ops:
  0.0 0.9 %copy-start = (f32[8,4,16,128]{3,2,1,0:T(8,128)S(1)}, f32[8,4,16,128]{3,2,1,0:T(8,128)}, u32[]{:S(2)}) copy-start(f32[8,4,16,128]{3,2,1,0:T(8,128)} %param.8) | copy-start | bytes 786436
  1.0 0.9 %copy-start.1 = (f32[3,4,16,128]{3,2,1,0:T(8,128)S(1)}, f32[3,4,16,128]{3,2,1,0:T(8,128)}, u32[]{:S(2)}) copy-start(f32[3,4,16,128]{3,2,1,0:T(8,128)} %param.7) | copy-start | bytes 294916
  1.8 1.2 %copy-start.2 = (f32[4,16,32,128]{3,2,1,0:T(8,128)S(1)}, f32[4,16,32,128]{3,2,1,0:T(8,128)}, u32[]{:S(2)}) copy-start(f32[4,16,32,128]{3,2,1,0:T(8,128)} %param.10) | copy-start | bytes 3145732
  3.1 0.8 %copy-start.4 = (f32[2,1,1,32,32]{4,3,2,1,0:T(8,128)S(1)}, f32[2,1,1,32,32]{4,3,2,1,0:T(8,128)}, u32[]{:S(2)}) copy-start(f32[2,1,1,32,32]{4,3,2,1,0:T(8,128)} %param.12) | copy-start | bytes 24580
  3.8 0.8 %copy-start.5 = (f32[2,1,1,32,32]{4,3,2,1,0:T(8,128)S(1)}, f32[2,1,1,32,32]{4,3,2,1,0:T(8,128)}, u32[]{:S(2)}) copy-start(f32[2,1,1,32,32]{4,3,2,1,0:T(8,128)} %param.13) | copy-start | bytes 24580
  4.6 0.7 %copy-start.6 = (s32[9,4,16]{2,1,0:T(4,128)S(1)}, s32[9,4,16]{2,1,0:T(4,128)}, u32[]{:S(2)}) copy-start(s32[9,4,16]{2,1,0:T(4,128)} %mask_far.1) | copy-start | bytes 6916
  7.4 4.2 %collective-permute-start = (f32[480,128]{1,0:T(8,128)S(1)}, f32[480,128]{1,0:T(8,128)S(1)}, u32[]{:S(2)}, u32[]{:S(2)}) collective-permute-start(f32[480,128]{1,0:T(8,128)S(1)} %get-tuple-element.52.mine), channel_id=1, source_target_pairs={{0,16},{16,0},{32,48},{48,32},{64,80},{80,64},{96,112},{112,96},{1... | collective-permute-start | bytes 737288 | tf_op jit(solution)/shard_map/ppermute | solution.py:408
  11.9 6.5 %collective-permute-start.1 = (f32[304,128]{1,0:T(8,128)S(1)}, f32[304,128]{1,0:T(8,128)S(1)}, u32[]{:S(2)}, u32[]{:S(2)}) collective-permute-start(f32[304,128]{1,0:T(8,128)S(1)} %level.5.mine), channel_id=1, source_target_pairs={{0,32},{16,48},{32,0},{48,16},{64,96},{80,112},{96,64},{112,80},{1... | collective-permute-start | bytes 466952 | tf_op jit(solution)/shard_map/ppermute | solution.py:408
  18.6 7.7 %collective-permute-start.2 = (f32[304,128]{1,0:T(8,128)S(1)}, f32[304,128]{1,0:T(8,128)S(1)}, u32[]{:S(2)}, u32[]{:S(2)}) collective-permute-start(f32[304,128]{1,0:T(8,128)S(1)} %level.6.mine), channel_id=1, source_target_pairs={{0,64},{16,80},{32,96},{48,112},{64,0},{80,16},{96,32},{112,48},{1... | collective-permute-start | bytes 466952 | tf_op jit(solution)/shard_map/ppermute | solution.py:408
  26.5 7.5 %collective-permute-start.3 = (f32[272,128]{1,0:T(8,128)S(1)}, f32[272,128]{1,0:T(8,128)S(1)}, u32[]{:S(2)}, u32[]{:S(2)}) collective-permute-start(f32[272,128]{1,0:T(8,128)S(1)} %get-tuple-element.71.mine), channel_id=1, source_target_pairs={{0,1},{1,0},{2,3},{3,2},{4,5},{5,4},{6,7},{7,6},{8,9},{9,8},{10,11... | collective-permute-start | bytes 417800 | tf_op jit(solution)/shard_map/ppermute | solution.py:408
  34.3 8.3 %collective-permute-start.4 = (f32[200,128]{1,0:T(8,128)S(1)}, f32[200,128]{1,0:T(8,128)S(1)}, u32[]{:S(2)}, u32[]{:S(2)}) collective-permute-start(f32[200,128]{1,0:T(8,128)S(1)} %level.7.mine), channel_id=1, source_target_pairs={{0,2},{1,3},{2,0},{3,1},{4,6},{5,7},{6,4},{7,5},{8,10},{9,11},{10,... | collective-permute-start | bytes 307208 | tf_op jit(solution)/shard_map/ppermute | solution.py:408
  42.9 5.0 %collective-permute-start.5 = (f32[200,128]{1,0:T(8,128)S(1)}, f32[200,128]{1,0:T(8,128)S(1)}, u32[]{:S(2)}, u32[]{:S(2)}) collective-permute-start(f32[200,128]{1,0:T(8,128)S(1)} %level.8.mine), channel_id=1, source_target_pairs={{0,4},{1,5},{2,6},{3,7},{4,0},{5,1},{6,2},{7,3},{8,12},{9,13},{10,... | collective-permute-start | bytes 307208 | tf_op jit(solution)/shard_map/ppermute | solution.py:408
  48.2 7.5 %collective-permute-start.6 = (f32[200,128]{1,0:T(8,128)S(1)}, f32[200,128]{1,0:T(8,128)S(1)}, u32[]{:S(2)}, u32[]{:S(2)}) collective-permute-start(f32[200,128]{1,0:T(8,128)S(1)} %level.9.mine), channel_id=1, source_target_pairs={{0,8},{1,9},{2,10},{3,11},{4,12},{5,13},{6,14},{7,15},{8,0},{9,1},... | collective-permute-start | bytes 307208 | tf_op jit(solution)/shard_map/ppermute | solution.py:408
  56.7 2.1 %copy-start.3 = (f32[4,16,32,128]{3,2,1,0:T(8,128)S(1)}, f32[4,16,32,128]{3,2,1,0:T(8,128)}, u32[]{:S(2)}) copy-start(f32[4,16,32,128]{3,2,1,0:T(8,128)} %param.11) | copy-start | bytes 3145732

commit v5 on v4

--- a/solution.py
+++ b/solution.py
@@ -24,7 +24,7 @@
 leaf_rows, leaf_cols, points, rank, rhs = 4, 16, 128, 32, 8
 leaves = leaf_rows * leaf_cols
 edge_leaves = 2 * leaf_cols
-side_leaves = 16
+halo_leaves = edge_leaves + 16
 edge_rows = (3 + rhs) * leaf_cols
 side_rows = 72
 group = points // rank
@@ -70,7 +70,7 @@
 
 def side_runs():
     runs = []
-    for first, column, dj in ((0, 0, -1), (8, leaf_cols - 1, 1)):
+    for first, column, dj in ((edge_leaves, 0, -1), (edge_leaves + 8, leaf_cols - 1, 1)):
         for di in (-1, 0, 1):
             runs.append(Run(leaf_rows, 0, first + 1 + di, leaf_cols, column, 3 * (di + 1) + dj + 1, False))
     return runs
@@ -127,7 +127,7 @@
     return pl.ds(leaf * 16 if isinstance(leaf, int) else pl.multiple_of(leaf * 16, 16), 16)
 
 
-def fill_tables(count, start, coords, sources, left, right, heights, halves, wide):
+def fill_tables(count, start, coords, left, right, heights, wides):
     parts = []
     for c in range(3):
         moved = (coords[pl.ds(c * count, count), :] - start[c]) * turns
@@ -140,6 +140,7 @@
     ones_y = jnp.where((k >= 3) & (k < 6), 1.0, 0.0)
     ones_t = jnp.where((k >= 6) & (k < 9), 1.0, 0.0)
     for role in range(3):
+        wide = wides.at[role]
         for leaf in range(count):
             wide[pl.ds(leaf * 16, 16), :] = (ones_t, ones_x, ones_y)[role]
         for first in range(0, count, 8):
@@ -155,9 +156,6 @@
                 left[leaf * points : (leaf + 1) * points, :] = wide[leaf * 16 : leaf * 16 + 16, :].T.astype(bf16)
         else:
             right[:, points * (role - 1) : points * role] = wide[...].astype(bf16)
-    for leaf in range(count):
-        high, low = split(sources[pl.ds(leaf, rhs, stride=count), :])
-        halves[sixteen(leaf), :] = jnp.concatenate([high, low], axis=0)
 
 
 def lane_block(n):
@@ -172,27 +170,27 @@
         blocks[2 * n], blocks[2 * n + 1] = split(wide)
 
 
-def prep_kernel(
-    coords_far, sources_far, mask_far, row_far, col_far, compress_far,
-    left, right, heights, halves, payload, row_blocks, col_blocks, weights,
-    wide, coords, sources, mask, row_transfer, col_transfer, compress, arrived,
-):
-    fars = (coords_far, sources_far, compress_far, row_far, col_far, mask_far)
-    heres = (coords, sources, compress, row_transfer, col_transfer, mask)
+def start_copies(fars, heres, arrived):
     copies = [pltpu.make_async_copy(far, here, arrived.at[n]) for n, (far, here) in enumerate(zip(fars, heres))]
     for copy in copies:
         copy.start()
+    return copies
+
+
+def compress_kernel(coords_far, sources_far, compress_far, halves, payload, outer, coords, sources, compress, arrived):
+    copies = start_copies((sources_far, coords_far, compress_far), (sources, coords, compress), arrived)
     copies[0].wait()
+    for leaf in range(leaves):
+        high, low = split(sources[pl.ds(leaf, rhs, stride=leaves), :])
+        halves[sixteen(leaf), :] = jnp.concatenate([high, low], axis=0)
     copies[1].wait()
-    start = [coords[c * leaves : c * leaves + 1, 0:1] for c in range(3)]
-    fill_tables(leaves, start, coords, sources, left, right, heights, halves, wide)
     odd = lax.axis_index("row") % 2
     for k in range(2):
         row = (leaf_rows - 1) * (1 - odd if k == 0 else odd)
         for c in range(3 + rhs):
             ref, at = (coords, c) if c < 3 else (sources, c - 3)
-            to = points + k * edge_rows + c * leaf_cols
-            payload[to : to + leaf_cols, :] = ref[pl.ds(pl.multiple_of(at * leaves + row * leaf_cols, 8), leaf_cols), :]
+            to = (payload, points + c * leaf_cols) if k == 0 else (outer, c * leaf_cols)
+            to[0][to[1] : to[1] + leaf_cols, :] = ref[pl.ds(pl.multiple_of(at * leaves + row * leaf_cols, 8), leaf_cols), :]
     copies[2].wait()
     for g in range(groups):
         high, low = split(compress[g * points : (g + 1) * points, :])
@@ -202,8 +200,13 @@
         for n in range(group):
             total = jnp.where(lane_block(n), got[n * 16 : n * 16 + 8] + got[n * 16 + 8 : n * 16 + 16], total)
         payload[g * rhs : (g + 1) * rhs, :] = total
-    for copy in copies[3:]:
+
+
+def prep_kernel(coords_far, mask_far, row_far, col_far, left, right, heights, row_blocks, col_blocks, weights, wides, coords, mask, row_transfer, col_transfer, arrived):
+    for copy in start_copies((coords_far, mask_far, row_far, col_far), (coords, mask, row_transfer, col_transfer), arrived):
         copy.wait()
+    start = [coords[c * leaves : c * leaves + 1, 0:1] for c in range(3)]
+    fill_tables(leaves, start, coords, left, right, heights, wides)
     spread_blocks(row_transfer, row_blocks)
     spread_blocks(col_transfer, col_blocks)
     diagonal = lax.broadcasted_iota(jnp.int32, (leaf_cols, leaf_cols), 0) == lax.broadcasted_iota(jnp.int32, (leaf_cols, leaf_cols), 1)
@@ -216,22 +219,20 @@
     weights[zero_row : zero_row + 8, :] = jnp.zeros((8, points), f32)
 
 
-def halo_prep_kernel(count, start_at, values, left, right, heights, halves, wide):
+def halo_kernel(start_at, edges, first, second, left, right, heights, halves, wides, values):
     start = [start_at[c * leaves : c * leaves + 1, 0:1] for c in range(3)]
-    fill_tables(count, start, values.at[: 3 * count], values.at[3 * count :], left, right, heights, halves, wide)
-
-
-def halo_prep(count, coords, values):
-    return pl.pallas_call(
-        functools.partial(halo_prep_kernel, count),
-        out_shape=table_shapes(count),
-        in_specs=[vmem] * 2,
-        out_specs=(vmem,) * 4,
-        scratch_shapes=[pltpu.VMEM((count * 16, points), f32)],
-        compiler_params=params(16),
-        cost_estimate=cost(1000),
-        name="halo_prep",
-    )(coords, values)
+    odd = lax.axis_index("col") % 2 == 1
+    near, far = first[points : points + side_rows, :], second[...]
+    to_left, to_right = jnp.where(odd, near, far), jnp.where(odd, far, near)
+    gap = jnp.zeros((2, points), f32)
+    for c in range(3 + rhs):
+        values[c * halo_leaves : c * halo_leaves + edge_leaves, :] = edges[c * edge_leaves : (c + 1) * edge_leaves, :]
+        at = slice(6 * c, 6 * c + 6)
+        values[c * halo_leaves + edge_leaves : (c + 1) * halo_leaves, :] = jnp.concatenate([to_left[at], gap, to_right[at], gap], axis=0)
+    fill_tables(halo_leaves, start, values, left, right, heights, wides)
+    for leaf in range(halo_leaves):
+        high, low = split(values[pl.ds(3 * halo_leaves + leaf, rhs, stride=halo_leaves), :])
+        halves[sixteen(leaf), :] = jnp.concatenate([high, low], axis=0)
 
 
 def level(mine, theirs, blocks):
@@ -245,50 +246,29 @@
     return total
 
 
-def level_kernel(forward, mine, theirs, blocks, payload):
+def level_kernel(mine, theirs, blocks, payload):
+    payload[...] = level(mine[:points, :], theirs[:points, :], blocks)
+
+
+def turn_kernel(mine, theirs, blocks, coords, sources, first, second, payload, outer, edges):
     payload[:points, :] = level(mine[:points, :], theirs[:points, :], blocks)
-    payload[points:, :] = theirs[forward:, :]
-
-
-def turn_kernel(mine, theirs, blocks, coords, sources, first, second, payload, edges):
-    payload[:points, :] = level(mine[:points, :], theirs[:points, :], blocks)
-    row, col = lax.axis_index("row"), lax.axis_index("col")
-    odd = row % 2 == 1
-    around = (row % 4 == 1) | (row % 4 == 2)
-    inner = (row > 0) & (row < lax.axis_size("row") - 1)
+    odd = lax.axis_index("row") % 2 == 1
+    col = lax.axis_index("col")
     for c in range(3 + rhs):
-        at = slice(points + c * leaf_cols, points + (c + 1) * leaf_cols)
-        near = first[at, :]
-        far = jnp.where(inner, jnp.where(around, second[at, :], theirs[at, :]), 0.0)
+        near = first[points + c * leaf_cols : points + (c + 1) * leaf_cols, :]
+        far = second[c * leaf_cols : (c + 1) * leaf_cols, :]
         edges[c * edge_leaves : c * edge_leaves + leaf_cols, :] = jnp.where(odd, near, far)
         edges[c * edge_leaves + leaf_cols : (c + 1) * edge_leaves, :] = jnp.where(odd, far, near)
     for k in range(2):
         j = (leaf_cols - 1) * (1 - col % 2 if k == 0 else col % 2)
-        base = points + k * side_rows
+        to, base = (payload, points) if k == 0 else (outer, 0)
         for c in range(3 + rhs):
             ref, at = (coords, c) if c < 3 else (sources, c - 3)
-            payload[base + 6 * c : base + 6 * c + 1, :] = edges[pl.ds(c * edge_leaves + j, 1), :]
+            to[base + 6 * c : base + 6 * c + 1, :] = edges[pl.ds(c * edge_leaves + j, 1), :]
             for i in range(leaf_rows):
-                payload[base + 6 * c + 1 + i : base + 6 * c + 2 + i, :] = ref[pl.ds(at * leaves + i * leaf_cols + j, 1), :]
-            payload[base + 6 * c + 5 : base + 6 * c + 6, :] = edges[pl.ds(c * edge_leaves + leaf_cols + j, 1), :]
-        payload[base + 66 : base + side_rows, :] = jnp.zeros((side_rows - 66, points), f32)
-
-
-def sides_kernel(mine, theirs, blocks, first, second, third, coeffs, sides):
-    coeffs[...] = level(mine[:points, :], theirs[:points, :], blocks)
-    col = lax.axis_index("col")
-    odd = col % 2 == 1
-    inner = (col > 0) & (col < lax.axis_size("col") - 1)
-    at = slice(points, points + side_rows)
-    near = first[at, :]
-    far = jnp.where((col % 8 == 3) | (col % 8 == 4), third[at, :], theirs[at, :])
-    far = jnp.where((col % 4 == 1) | (col % 4 == 2), second[at, :], far)
-    far = jnp.where(inner, far, 0.0)
-    to_left, to_right = jnp.where(odd, near, far), jnp.where(odd, far, near)
-    gap = jnp.zeros((2, points), f32)
-    for c in range(3 + rhs):
-        at = slice(6 * c, 6 * c + 6)
-        sides[c * side_leaves : (c + 1) * side_leaves, :] = jnp.concatenate([to_left[at], gap, to_right[at], gap], axis=0)
+                to[base + 6 * c + 1 + i : base + 6 * c + 2 + i, :] = ref[pl.ds(at * leaves + i * leaf_cols + j, 1), :]
+            to[base + 6 * c + 5 : base + 6 * c + 6, :] = edges[pl.ds(c * edge_leaves + leaf_cols + j, 1), :]
+        to[base + 66 : base + side_rows, :] = jnp.zeros((side_rows - 66, points), f32)
 
 
 def near_kernel(pieces, trips, both_ways, weights, left, source_heights, source_halves, right, heights, halves, seed, acc, gap_a, gap_b, splat_a, splat_b, kern_a, kern_b):
@@ -379,10 +359,11 @@
     )(weights, left, source_heights, source_halves, right, heights, halves, seed)
 
 
-def finish_kernel(coeffs, expand, acc, out):
+def finish_kernel(mine, theirs, blocks, expand, acc, out):
+    coeffs = level(mine[...], theirs[...], blocks)
     for g in range(groups):
-        mine = coeffs[g * rhs : (g + 1) * rhs, :]
-        rows = jnp.concatenate([jnp.where(lane_block(n), mine, 0.0) for n in range(group)], axis=0)
+        here = coeffs[g * rhs : (g + 1) * rhs]
+        rows = jnp.concatenate([jnp.where(lane_block(n), here, 0.0) for n in range(group)], axis=0)
         high, low = split(rows)
         e_high, e_low = split(expand[g * points : (g + 1) * points, :])
         got = dot(jnp.concatenate([high, low], axis=0), jnp.concatenate([e_high, e_low], axis=1))
@@ -425,80 +406,110 @@
     )(*operands)
 
 
+def far_call(body, name, out_shape, scratch, *operands):
+    return pl.pallas_call(
+        body,
+        out_shape=out_shape,
+        in_specs=[pl.BlockSpec(memory_space=pltpu.HBM)] * len(operands),
+        out_specs=(vmem,) * len(out_shape),
+        scratch_shapes=scratch + [pltpu.SemaphoreType.DMA((len(operands),))],
+        compiler_params=params(24),
+        cost_estimate=cost(2000),
+        name=name,
+    )(*[pltpu.with_memory_space_constraint(operand, pltpu.HBM) for operand in operands])
+
+
+def outward(block, axis):
+    size = lax.axis_size(axis)
+    return lax.ppermute(block, axis, [(i, i + 1 if i % 2 else i - 1) for i in range(1, size - 1)])
+
+
 def shards(coords, sources, neighbour_mask, compress, expand, row_transfer, col_transfer):
     coords = coords.reshape(-1, points)
     sources = sources.reshape(-1, points)
+    halves, payload, outer = far_call(
+        compress_kernel,
+        "compress",
+        (table_shapes(leaves)[3], array(points + edge_rows, points), array(edge_rows, points)),
+        [pltpu.VMEM(shape, f32) for shape in ((3 * leaves, points), (rhs * leaves, points), (leaves * rank, points))],
+        coords, sources, compress.reshape(-1, points),
+    )
+    row_bits, col_bits = (lax.axis_size(axis).bit_length() - 1 for axis in ("row", "col"))
+    axes = ["row"] * row_bits + ["col"] * col_bits
+    bits = [*range(row_bits), *range(col_bits)]
+    theirs = partner_of(payload, "row", 0)
+    beyond = outward(outer, "row")
     block_shape = jax.ShapeDtypeStruct((4, points, points), bf16)
-    *own, payload, row_blocks, col_blocks, weights = pl.pallas_call(
+    coords_later, payload = lax.optimization_barrier((coords, payload))
+    left, right, heights, row_blocks, col_blocks, weights = far_call(
         prep_kernel,
-        out_shape=table_shapes(leaves) + (array(points + 2 * edge_rows, points), block_shape, block_shape, array(zero_row + 8, points)),
-        in_specs=[pl.BlockSpec(memory_space=pl.ANY)] * 6,
-        out_specs=(vmem,) * 8,
-        scratch_shapes=[
-            pltpu.VMEM((leaves * 16, points), f32),
+        "prep",
+        table_shapes(leaves)[:3] + (block_shape, block_shape, array(zero_row + 8, points)),
+        [
+            pltpu.VMEM((3, leaves * 16, points), f32),
             pltpu.VMEM((3 * leaves, points), f32),
-            pltpu.VMEM((rhs * leaves, points), f32),
             pltpu.VMEM((9, leaf_rows, leaf_cols), jnp.int32),
             pltpu.VMEM((2, rank, rank), f32),
             pltpu.VMEM((2, rank, rank), f32),
-            pltpu.VMEM((leaves * rank, points), f32),
-            pltpu.SemaphoreType.DMA((6,)),
         ],
-        compiler_params=params(24),
-        cost_estimate=cost(3000),
-        name="prep",
-    )(coords, sources, neighbour_mask, row_transfer[:, 0, 0], col_transfer[:, 0, 0], compress.reshape(-1, points))
-    row_bits, col_bits = (lax.axis_size(axis).bit_length() - 1 for axis in ("row", "col"))
-    inner_pieces = row_bits + col_bits - 2
-    inner, edge, side = interior_runs(), edge_runs(), side_runs()
-    counts = [sum(run.count for run in runs) for runs in (inner, edge, side)]
-    cuts = [counts[0] * n // inner_pieces // 8 * 8 for n in range(inner_pieces)] + [counts[0]]
-    half = counts[1] // 2 // 8 * 8
+        coords_later, neighbour_mask, row_transfer[:, 0, 0], col_transfer[:, 0, 0],
+    )
+    own = left, right, heights, halves
+    inner, around = interior_runs(), edge_runs() + side_runs()
+    counts = [sum(run.count for run in runs) for runs in (inner, around)]
+    windows = row_bits + col_bits - 1
+    inner_windows = windows - 2
+    step = 2 * batch
+    cuts = [counts[0] * n // inner_windows // step * step for n in range(inner_windows)] + [counts[0]]
+    half = counts[1] // 2 // step * step
     acc = jnp.zeros((leaves * rhs, points), f32)
-    above_below = None
-    received = []
-    for n in range(row_bits + col_bits):
-        over_row = n < row_bits
-        blocks = row_blocks if over_row else col_blocks
-        theirs = partner_of(payload, "row" if over_row else "col", n if over_row else n - row_bits)
-        payload, acc = lax.optimization_barrier((payload, acc))
-        if n < inner_pieces:
-            acc = near_piece(cut_runs(inner, cuts[n], cuts[n + 1]), True, weights, own, own, acc)
+    for n, (axis, bit) in enumerate(zip(axes, bits)):
+        blocks = row_blocks if axis == "row" else col_blocks
+        if n > 0:
+            theirs = partner_of(payload, axis, bit)
+            if n == row_bits:
+                beyond = outward(outer, "col")
+                first = theirs
+            payload, acc = lax.optimization_barrier((payload, acc))
+            if n <= inner_windows:
+                acc = near_piece(cut_runs(inner, cuts[n - 1], cuts[n]), True, weights, own, own, acc)
+            else:
+                some = cut_runs(around, 0, half) if n == windows - 1 else cut_runs(around, half, counts[1])
+                acc = near_piece(some, False, weights, halo, own, acc)
+            theirs, acc = lax.optimization_barrier((theirs, acc))
+            if n == row_bits:
+                first = theirs
         else:
-            some = cut_runs(edge, 0, half) if n == inner_pieces else cut_runs(edge, half, counts[1])
-            acc = near_piece(some, False, weights, above_below, own, acc)
-        theirs, acc = lax.optimization_barrier((theirs, acc))
-        received.append(theirs)
+            first = theirs
         if n == row_bits - 1:
-            payload, edges = small_call(
+            payload, outer, edges = small_call(
                 turn_kernel,
                 "turn",
-                (array(points + 2 * side_rows, points), array((3 + rhs) * edge_leaves, points)),
-                payload, theirs, blocks, coords, sources, received[0], received[1],
+                (array(points + side_rows, points), array(side_rows, points), array((3 + rhs) * edge_leaves, points)),
+                payload, theirs, blocks, coords, sources, first, beyond,
             )
-        elif n == row_bits + col_bits - 1:
-            coeffs, sides = small_call(
-                sides_kernel,
-                "sides",
-                (array(points, points), array((3 + rhs) * side_leaves, points)),
-                payload, theirs, blocks, received[row_bits], received[row_bits + 1], received[row_bits + 2],
-            )
-        else:
-            rows = edge_rows if over_row else side_rows
-            skip = points + rows if n in (0, row_bits) else points
-            payload = small_call(functools.partial(level_kernel, skip), "level", array(points + rows, points), payload, theirs, blocks)
+        elif n < windows:
+            payload = small_call(level_kernel, "level", array(points, points), payload, theirs, blocks)
         if n == row_bits:
-            above_below = halo_prep(edge_leaves, coords, edges)
-    acc = near_piece(cut_runs(side, 0, counts[2]), False, weights, halo_prep(side_leaves, coords, sides), own, acc)
+            halo = pl.pallas_call(
+                halo_kernel,
+                out_shape=table_shapes(halo_leaves),
+                in_specs=[vmem] * 4,
+                out_specs=(vmem,) * 4,
+                scratch_shapes=[pltpu.VMEM((3, halo_leaves * 16, points), f32), pltpu.VMEM(((3 + rhs) * halo_leaves, points), f32)],
+                compiler_params=params(16),
+                cost_estimate=cost(1000),
+                name="halo",
+            )(coords, edges, first, beyond)
     out = pl.pallas_call(
         finish_kernel,
         out_shape=array(rhs * leaves, points),
-        in_specs=[vmem] * 3,
+        in_specs=[vmem] * 5,
         out_specs=vmem,
         compiler_params=params(16),
         cost_estimate=cost(2000),
         name="finish",
-    )(coeffs, expand.reshape(-1, points), acc)
+    )(payload, theirs, blocks, expand.reshape(-1, points), acc)
     return out.reshape(rhs, leaf_rows, leaf_cols, points)
 
 

time: 60.3 us -> 58.8 us (0.975)
  local copies, waits for them, and re-layouts: 5.32 us -> 0.04 us
  starting transfers between devices: 15.2 us -> 19.5 us
    unnamed x14 -> x6, local copies, waits for them, and re-layouts: 5.31 us -> 0.02 us
    ppermute x7, starting transfers between devices: 15.2 us -> 18.2 us  [partner_of(): return lax.ppermute(block, axis, route)]
    ppermute x0 -> x2, starting transfers between devices: none -> 1.32 us  [outward(): lax.ppermute(block, axis, [(i, i + 1 if i % 2 else i - 1) for i in range(...]
    pallas_call x3, Pallas kernels: 3.76 us -> 4.85 us  [the longest x2 3.82 us: far_call(): pl.pallas_call(body, out_shape=out_shape, in_specs=[pl.BlockSpec(memory_s...]
    pallas_call x8 -> x6, Pallas kernels: 32.3 us -> 31.4 us  [near_piece(): pl.pallas_call(functools.partial(near_kernel, pieces, trips, both_ways),...]
    pallas_call x7 -> x6, Pallas kernels: 1.69 us -> 1.42 us  [small_call(): pl.pallas_call(body, out_shape=out_shape, in_specs=[vmem] * len(operands)...]
  transfers between devices with their start and end apart: 7 -> 9, of which waited for: 2 -> 0; matrix products, arithmetic and copies ran while one was open for 0% -> 0% of each run, Pallas kernels for 52% -> 60%
where the time goes in v5:
time: 58.8 us; the launch traced here: 58.7 us
  Pallas kernels  38.9 us (66%)
  starting transfers between devices  19.5 us (33%)
    pallas_call x6, Pallas kernels, near_piece(): pl.pallas_call(functools.partial(near_kernel, pieces, trips, both_ways),...  31.4 us
    ppermute x7, starting transfers between devices, partner_of(): return lax.ppermute(block, axis, route)  18.2 us
    pallas_call x2, Pallas kernels, far_call(): pl.pallas_call(body, out_shape=out_shape, in_specs=[pl.BlockSpec(memory_s...  3.82 us
    pallas_call x6, Pallas kernels, small_call(): pl.pallas_call(body, out_shape=out_shape, in_specs=[vmem] * len(operands)...  1.42 us
    ppermute x2, starting transfers between devices, outward(): lax.ppermute(block, axis, [(i, i + 1 if i % 2 else i - 1) for i in range(...  1.32 us
    pallas_call x1, Pallas kernels, shards(): pl.pallas_call(finish_kernel, out_shape=array(rhs * leaves, points), in_s...  1.25 us
  transfers between devices with their start and end apart: 9, of which 0 were waited for; matrix products, arithmetic and copies ran while one was open for 0% of the time, Pallas kernels for 60%

profile of v5, /device:TPU:0, one launch (start us, length us, event | category | flops | bytes accessed | tf_op | source)
XLA Modules:
  0.0 58.7 jit_solution(15306165748724808743)
XLA Ops:
  0.0 1.9 %compress.1 = (bf16[1024,128]{1,0:T(8,128)(2,1)S(1)}, f32[304,128]{1,0:T(8,128)S(1)}, f32[176,128]{1,0:T(8,128)S(1)}) custom-call(f32[192,128]{1,0:T(8,128)} %bitcast.10, f32[512,128]{1,0:T(8,128)} %bitcast.8, f32[2048,128]{1,0:T(8,128)} %bitcast.14), custom_call_target="tpu_custom_call" | custom-call | flops 800000000 | bytes 262144 | tf_op jit(solution)/shard_map/compress/pallas_call | solution.py:410
  1.9 0.1 collective-permute-start
  2.0 0.7 %collective-permute-start.3 = (f32[176,128]{1,0:T(8,128)S(1)}, f32[176,128]{1,0:T(8,128)S(1)}, u32[]{:S(2)}, u32[]{:S(2)}) collective-permute-start(f32[176,128]{1,0:T(8,128)S(1)} %get-tuple-element.62), channel_id=1, source_target_pairs={{16,32},{32,16},{48,64},{64,48},{80,96},{96,80},{17,33},{33,17},{4... | collective-permute-start | bytes 270344 | tf_op jit(solution)/shard_map/ppermute | solution.py:424
  2.6 2.0 %prep.1 = (bf16[8192,16]{1,0:T(8,128)(2,1)S(1)}, bf16[1024,256]{1,0:T(8,128)(2,1)S(1)}, f32[64,128]{1,0:T(8,128)S(1)}, bf16[4,128,128]{2,1,0:T(8,128)(2,1)S(1)},...) custom-call(f32[192,128]{1,0:T(8,128)} %bitcast.11, s32[9,4,16]{2,1,0:T(4,128)} %mask_far.1, ...), custom_call_target="tpu_custom_call" | custom-call | flops 800000000 | bytes 262144 | tf_op jit(solution)/shard_map/prep/pallas_call | solution.py:410
  4.6 0.0 collective-permute-done.theirs.first
  4.6 0.2 level.5.mine
  4.9 3.4 %collective-permute-start.1 = (f32[128,128]{1,0:T(8,128)S(1)}, f32[128,128]{1,0:T(8,128)S(1)}, u32[]{:S(2)}, u32[]{:S(2)}) collective-permute-start(f32[128,128]{1,0:T(8,128)S(1)} %level.5.mine), channel_id=1, source_target_pairs={{0,32},{16,48},{32,0},{48,16},{64,96},{80,112},{96,64},{112,80},{1... | collective-permute-start | bytes 196616 | tf_op jit(solution)/shard_map/ppermute | solution.py:389
  8.3 5.2 %near.6.seed = f32[512,128]{1,0:T(8,128)S(1)} custom-call(f32[584,128]{1,0:T(8,128)S(1)} %get-tuple-element.51.weights, bf16[8192,16]{1,0:T(8,128)(2,1)S(1)} %get-tuple-element.52.left, f32[64,128]{1,0:T(8,128)S(1)} %get-tuple-element.53.source_heights.heights, bf16[1024,128]{1,0:T(8,128)(2,1)S(1)} %get-tuple-element.54.source_halves.halves, ...), custom_call_target="tpu_custom_call" | custom-call | flops 2816000000 | bytes 262144 | tf_op jit(solution)/shard_map/near/pallas_call | solution.py:342
  13.6 0.0 collective-permute-done.1.theirs
  13.6 0.2 level.6.mine
  13.8 0.0 copy-start.1
  13.8 0.0 copy-start.2
  13.8 3.4 %collective-permute-start.2 = (f32[128,128]{1,0:T(8,128)S(1)}, f32[128,128]{1,0:T(8,128)S(1)}, u32[]{:S(2)}, u32[]{:S(2)}) collective-permute-start(f32[128,128]{1,0:T(8,128)S(1)} %level.6.mine), channel_id=1, source_target_pairs={{0,64},{16,80},{32,96},{48,112},{64,0},{80,16},{96,32},{112,48},{1... | collective-permute-start | bytes 196616 | tf_op jit(solution)/shard_map/ppermute | solution.py:389
  17.2 5.2 %near.7.seed = f32[512,128]{1,0:T(8,128)S(1)} custom-call(f32[584,128]{1,0:T(8,128)S(1)} %get-tuple-element.51.weights, bf16[8192,16]{1,0:T(8,128)(2,1)S(1)} %get-tuple-element.52.left, f32[64,128]{1,0:T(8,128)S(1)} %get-tuple-element.53.source_heights.heights, bf16[1024,128]{1,0:T(8,128)(2,1)S(1)} %get-tuple-element.54.source_halves.halves, ...), custom_call_target="tpu_custom_call" | custom-call | flops 2816000000 | bytes 262144 | tf_op jit(solution)/shard_map/near/pallas_call | solution.py:342
  22.4 0.0 collective-permute-done.2.theirs
  22.5 0.0 collective-permute-done.3.second
  22.5 0.0 copy-done.1
  22.5 0.0 copy-done.2
  22.5 0.2 turn.1
  22.7 2.0 %collective-permute-start.4 = (f32[200,128]{1,0:T(8,128)S(1)}, f32[200,128]{1,0:T(8,128)S(1)}, u32[]{:S(2)}, u32[]{:S(2)}) collective-permute-start(f32[200,128]{1,0:T(8,128)S(1)} %get-tuple-element.65.mine), channel_id=1, source_target_pairs={{0,1},{1,0},{2,3},{3,2},{4,5},{5,4},{6,7},{7,6},{8,9},{9,8},{10,11... | collective-permute-start | bytes 307208 | tf_op jit(solution)/shard_map/ppermute | solution.py:389
  24.7 0.7 %collective-permute-start.7 = (f32[72,128]{1,0:T(8,128)S(1)}, f32[72,128]{1,0:T(8,128)S(1)}, u32[]{:S(2)}, u32[]{:S(2)}) collective-permute-start(f32[72,128]{1,0:T(8,128)S(1)} %get-tuple-element.76), channel_id=1, source_target_pairs={{1,2},{2,1},{3,4},{4,3},{5,6},{6,5},{7,8},{8,7},{9,10},{10,9},{11,... | collective-permute-start | bytes 110600 | tf_op jit(solution)/shard_map/ppermute | solution.py:424
  25.4 5.2 %near.8.seed = f32[512,128]{1,0:T(8,128)S(1)} custom-call(f32[584,128]{1,0:T(8,128)S(1)} %get-tuple-element.51.weights, bf16[8192,16]{1,0:T(8,128)(2,1)S(1)} %get-tuple-element.52.left, f32[64,128]{1,0:T(8,128)S(1)} %get-tuple-element.53.source_heights.heights, bf16[1024,128]{1,0:T(8,128)(2,1)S(1)} %get-tuple-element.54.source_halves.halves, ...), custom_call_target="tpu_custom_call" | custom-call | flops 2816000000 | bytes 262144 | tf_op jit(solution)/shard_map/near/pallas_call | solution.py:342
  30.6 0.0 collective-permute-done.4.theirs.first
  30.6 0.2 level.7.mine
  30.9 4.9 %collective-permute-start.5 = (f32[128,128]{1,0:T(8,128)S(1)}, f32[128,128]{1,0:T(8,128)S(1)}, u32[]{:S(2)}, u32[]{:S(2)}) collective-permute-start(f32[128,128]{1,0:T(8,128)S(1)} %level.7.mine), channel_id=1, source_target_pairs={{0,2},{1,3},{2,0},{3,1},{4,6},{5,7},{6,4},{7,5},{8,10},{9,11},{10,... | collective-permute-start | bytes 196616 | tf_op jit(solution)/shard_map/ppermute | solution.py:389
  35.8 5.8 %near.9.seed = f32[512,128]{1,0:T(8,128)S(1)} custom-call(f32[584,128]{1,0:T(8,128)S(1)} %get-tuple-element.51.weights, bf16[8192,16]{1,0:T(8,128)(2,1)S(1)} %get-tuple-element.52.left, f32[64,128]{1,0:T(8,128)S(1)} %get-tuple-element.53.source_heights.heights, bf16[1024,128]{1,0:T(8,128)(2,1)S(1)} %get-tuple-element.54.source_halves.halves, ...), custom_call_target="tpu_custom_call" | custom-call | flops 3080000000 | bytes 262144 | tf_op jit(solution)/shard_map/near/pallas_call | solution.py:342
  41.6 0.0 collective-permute-done.7.second
  41.6 1.0 %halo.1 = (bf16[6144,16]{1,0:T(8,128)(2,1)S(1)}, bf16[768,256]{1,0:T(8,128)(2,1)}, f32[48,128]{1,0:T(8,128)S(1)}, bf16[768,128]{1,0:T(8,128)(2,1)S(1)}) custom-call(f32[192,128]{1,0:T(8,128)S(1)} %bitcast.13, f32[352,128]{1,0:T(8,128)S(1)} %get-tuple-element.75.edges, f32[200,128]{1,0:T(8,128)S(1)} %collective-permute-done.4.theirs.first, ...), custom_call_target="tpu_custom_call" | custom-call | flops 400000000 | bytes 262144 | tf_op jit(solution)/shard_map/halo/pallas_call | solution.py:494
  42.7 0.0 collective-permute-done.5.theirs
  42.7 0.2 level.8.mine
  42.9 1.6 %collective-permute-start.6 = (f32[128,128]{1,0:T(8,128)S(1)}, f32[128,128]{1,0:T(8,128)S(1)}, u32[]{:S(2)}, u32[]{:S(2)}) collective-permute-start(f32[128,128]{1,0:T(8,128)S(1)} %level.8.mine), channel_id=1, source_target_pairs={{0,4},{1,5},{2,6},{3,7},{4,0},{5,1},{6,2},{7,3},{8,12},{9,13},{10,... | collective-permute-start | bytes 196616 | tf_op jit(solution)/shard_map/ppermute | solution.py:389
  44.5 4.6 %near.10.seed = f32[512,128]{1,0:T(8,128)S(1)} custom-call(f32[584,128]{1,0:T(8,128)S(1)} %get-tuple-element.51.weights, bf16[6144,16]{1,0:T(8,128)(2,1)S(1)} %get-tuple-element.77.left, f32[48,128]{1,0:T(8,128)S(1)} %get-tuple-element.78.source_heights, bf16[768,128]{1,0:T(8,128)(2,1)S(1)} %get-tuple-element.79.source_halves, ...), custom_call_target="tpu_custom_call" | custom-call | flops 2464000000 | bytes 262144 | tf_op jit(solution)/shard_map/near/pallas_call | solution.py:342
  49.1 0.0 collective-permute-done.6.theirs
  49.1 0.2 level.9.mine
  49.4 0.0 copy-start
  49.4 2.8 %collective-permute-start.8 = (f32[128,128]{1,0:T(8,128)S(1)}, f32[128,128]{1,0:T(8,128)S(1)}, u32[]{:S(2)}, u32[]{:S(2)}) collective-permute-start(f32[128,128]{1,0:T(8,128)S(1)} %level.9.mine), channel_id=1, source_target_pairs={{0,8},{1,9},{2,10},{3,11},{4,12},{5,13},{6,14},{7,15},{8,0},{9,1},... | collective-permute-start | bytes 196616 | tf_op jit(solution)/shard_map/ppermute | solution.py:389
  52.2 5.2 %near.11.acc = f32[512,128]{1,0:T(8,128)S(1)} custom-call(f32[584,128]{1,0:T(8,128)S(1)} %get-tuple-element.51.weights, bf16[6144,16]{1,0:T(8,128)(2,1)S(1)} %get-tuple-element.77.left, f32[48,128]{1,0:T(8,128)S(1)} %get-tuple-element.78.source_heights, bf16[768,128]{1,0:T(8,128)(2,1)S(1)} %get-tuple-element.79.source_halves, ...), custom_call_target="tpu_custom_call" | custom-call | flops 2640000000 | bytes 262144 | tf_op jit(solution)/shard_map/near/pallas_call | solution.py:342
  57.4 0.0 collective-permute-done.8.theirs
  57.4 0.0 copy-done
  57.4 1.3 %finish.1 = f32[512,128]{1,0:T(8,128)} custom-call(f32[128,128]{1,0:T(8,128)S(1)} %level.9.mine, f32[128,128]{1,0:T(8,128)S(1)} %collective-permute-done.8.theirs, bf16[4,128,128]{2,1,0:T(8,128)(2,1)S(1)} %get-tuple-element.68.blocks, f32[2048,128]{1,0:T(8,128)S(1)} %bitcast.7, f32[512,128]{1,0:T(8,128)S(1)} %near.11.acc), custom_call_target="tpu_custom_call" | custom-call | flops 800000000 | bytes 262144 | tf_op jit(solution)/shard_map/finish/pallas_call | solution.py:504
  (1 shorter events, 0.0 us)
Async XLA Ops:
  1.9 2.7 %collective-permute-start = (f32[304,128]{1,0:T(8,128)S(1)}, f32[304,128]{1,0:T(8,128)S(1)}, u32[]{:S(2)}, u32[]{:S(2)}) collective-permute-start(f32[304,128]{1,0:T(8,128)S(1)} %get-tuple-element.47.mine), channel_id=1, source_target_pairs={{0,16},{16,0},{32,48},{48,32},{64,80},{80,64},{96,112},{112,96},{1... | collective-permute-start | bytes 466952 | tf_op jit(solution)/shard_map/ppermute | solution.py:389
  2.0 20.5 %collective-permute-start.3 = (f32[176,128]{1,0:T(8,128)S(1)}, f32[176,128]{1,0:T(8,128)S(1)}, u32[]{:S(2)}, u32[]{:S(2)}) collective-permute-start(f32[176,128]{1,0:T(8,128)S(1)} %get-tuple-element.62), channel_id=1, source_target_pairs={{16,32},{32,16},{48,64},{64,48},{80,96},{96,80},{17,33},{33,17},{4... | collective-permute-start | bytes 270344 | tf_op jit(solution)/shard_map/ppermute | solution.py:424
  4.9 8.7 %collective-permute-start.1 = (f32[128,128]{1,0:T(8,128)S(1)}, f32[128,128]{1,0:T(8,128)S(1)}, u32[]{:S(2)}, u32[]{:S(2)}) collective-permute-start(f32[128,128]{1,0:T(8,128)S(1)} %level.5.mine), channel_id=1, source_target_pairs={{0,32},{16,48},{32,0},{48,16},{64,96},{80,112},{96,64},{112,80},{1... | collective-permute-start | bytes 196616 | tf_op jit(solution)/shard_map/ppermute | solution.py:389
  13.8 8.7 %copy-start.1 = (f32[8,4,16,128]{3,2,1,0:T(8,128)S(1)}, f32[8,4,16,128]{3,2,1,0:T(8,128)}, u32[]{:S(2)}) copy-start(f32[8,4,16,128]{3,2,1,0:T(8,128)} %param.8) | copy-start | bytes 786436
  13.8 8.6 %copy-start.2 = (f32[3,4,16,128]{3,2,1,0:T(8,128)S(1)}, f32[3,4,16,128]{3,2,1,0:T(8,128)}, u32[]{:S(2)}) copy-start(f32[3,4,16,128]{3,2,1,0:T(8,128)} %param.7) | copy-start | bytes 294916
  13.8 8.6 %collective-permute-start.2 = (f32[128,128]{1,0:T(8,128)S(1)}, f32[128,128]{1,0:T(8,128)S(1)}, u32[]{:S(2)}, u32[]{:S(2)}) collective-permute-start(f32[128,128]{1,0:T(8,128)S(1)} %level.6.mine), channel_id=1, source_target_pairs={{0,64},{16,80},{32,96},{48,112},{64,0},{80,16},{96,32},{112,48},{1... | collective-permute-start | bytes 196616 | tf_op jit(solution)/shard_map/ppermute | solution.py:389
  22.7 7.9 %collective-permute-start.4 = (f32[200,128]{1,0:T(8,128)S(1)}, f32[200,128]{1,0:T(8,128)S(1)}, u32[]{:S(2)}, u32[]{:S(2)}) collective-permute-start(f32[200,128]{1,0:T(8,128)S(1)} %get-tuple-element.65.mine), channel_id=1, source_target_pairs={{0,1},{1,0},{2,3},{3,2},{4,5},{5,4},{6,7},{7,6},{8,9},{9,8},{10,11... | collective-permute-start | bytes 307208 | tf_op jit(solution)/shard_map/ppermute | solution.py:389
  24.7 16.9 %collective-permute-start.7 = (f32[72,128]{1,0:T(8,128)S(1)}, f32[72,128]{1,0:T(8,128)S(1)}, u32[]{:S(2)}, u32[]{:S(2)}) collective-permute-start(f32[72,128]{1,0:T(8,128)S(1)} %get-tuple-element.76), channel_id=1, source_target_pairs={{1,2},{2,1},{3,4},{4,3},{5,6},{6,5},{7,8},{8,7},{9,10},{10,9},{11,... | collective-permute-start | bytes 110600 | tf_op jit(solution)/shard_map/ppermute | solution.py:424
  30.9 11.8 %collective-permute-start.5 = (f32[128,128]{1,0:T(8,128)S(1)}, f32[128,128]{1,0:T(8,128)S(1)}, u32[]{:S(2)}, u32[]{:S(2)}) collective-permute-start(f32[128,128]{1,0:T(8,128)S(1)} %level.7.mine), channel_id=1, source_target_pairs={{0,2},{1,3},{2,0},{3,1},{4,6},{5,7},{6,4},{7,5},{8,10},{9,11},{10,... | collective-permute-start | bytes 196616 | tf_op jit(solution)/shard_map/ppermute | solution.py:389
  42.9 6.2 %collective-permute-start.6 = (f32[128,128]{1,0:T(8,128)S(1)}, f32[128,128]{1,0:T(8,128)S(1)}, u32[]{:S(2)}, u32[]{:S(2)}) collective-permute-start(f32[128,128]{1,0:T(8,128)S(1)} %level.8.mine), channel_id=1, source_target_pairs={{0,4},{1,5},{2,6},{3,7},{4,0},{5,1},{6,2},{7,3},{8,12},{9,13},{10,... | collective-permute-start | bytes 196616 | tf_op jit(solution)/shard_map/ppermute | solution.py:389
  49.4 8.0 %copy-start = (f32[4,16,32,128]{3,2,1,0:T(8,128)S(1)}, f32[4,16,32,128]{3,2,1,0:T(8,128)}, u32[]{:S(2)}) copy-start(f32[4,16,32,128]{3,2,1,0:T(8,128)} %param.11) | copy-start | bytes 3145732
  49.4 8.0 %collective-permute-start.8 = (f32[128,128]{1,0:T(8,128)S(1)}, f32[128,128]{1,0:T(8,128)S(1)}, u32[]{:S(2)}, u32[]{:S(2)}) collective-permute-start(f32[128,128]{1,0:T(8,128)S(1)} %level.9.mine), channel_id=1, source_target_pairs={{0,8},{1,9},{2,10},{3,11},{4,12},{5,13},{6,14},{7,15},{8,0},{9,1},... | collective-permute-start | bytes 196616 | tf_op jit(solution)/shard_map/ppermute | solution.py:389

commit v6 on v5

--- a/solution.py
+++ b/solution.py
@@ -24,7 +24,7 @@
 leaf_rows, leaf_cols, points, rank, rhs = 4, 16, 128, 32, 8
 leaves = leaf_rows * leaf_cols
 edge_leaves = 2 * leaf_cols
-halo_leaves = edge_leaves + 16
+side_leaves = 16
 edge_rows = (3 + rhs) * leaf_cols
 side_rows = 72
 group = points // rank
@@ -70,7 +70,7 @@
 
 def side_runs():
     runs = []
-    for first, column, dj in ((edge_leaves, 0, -1), (edge_leaves + 8, leaf_cols - 1, 1)):
+    for first, column, dj in ((0, 0, -1), (8, leaf_cols - 1, 1)):
         for di in (-1, 0, 1):
             runs.append(Run(leaf_rows, 0, first + 1 + di, leaf_cols, column, 3 * (di + 1) + dj + 1, False))
     return runs
@@ -177,7 +177,7 @@
     return copies
 
 
-def compress_kernel(coords_far, sources_far, compress_far, halves, payload, outer, coords, sources, compress, arrived):
+def compress_kernel(coords_far, sources_far, compress_far, halves, payload, coords, sources, compress, arrived):
     copies = start_copies((sources_far, coords_far, compress_far), (sources, coords, compress), arrived)
     copies[0].wait()
     for leaf in range(leaves):
@@ -189,8 +189,8 @@
         row = (leaf_rows - 1) * (1 - odd if k == 0 else odd)
         for c in range(3 + rhs):
             ref, at = (coords, c) if c < 3 else (sources, c - 3)
-            to = (payload, points + c * leaf_cols) if k == 0 else (outer, c * leaf_cols)
-            to[0][to[1] : to[1] + leaf_cols, :] = ref[pl.ds(pl.multiple_of(at * leaves + row * leaf_cols, 8), leaf_cols), :]
+            to = points + k * edge_rows + c * leaf_cols
+            payload[to : to + leaf_cols, :] = ref[pl.ds(pl.multiple_of(at * leaves + row * leaf_cols, 8), leaf_cols), :]
     copies[2].wait()
     for g in range(groups):
         high, low = split(compress[g * points : (g + 1) * points, :])
@@ -219,20 +219,33 @@
     weights[zero_row : zero_row + 8, :] = jnp.zeros((8, points), f32)
 
 
-def halo_kernel(start_at, edges, first, second, left, right, heights, halves, wides, values):
-    start = [start_at[c * leaves : c * leaves + 1, 0:1] for c in range(3)]
-    odd = lax.axis_index("col") % 2 == 1
-    near, far = first[points : points + side_rows, :], second[...]
+def halo_tables(count, coords, values, left, right, heights, halves, wides):
+    start = [coords[c * leaves : c * leaves + 1, 0:1] for c in range(3)]
+    fill_tables(count, start, values, left, right, heights, wides)
+    for leaf in range(count):
+        high, low = split(values[pl.ds(3 * count + leaf, rhs, stride=count), :])
+        halves[sixteen(leaf), :] = jnp.concatenate([high, low], axis=0)
+
+
+def edges_kernel(coords, edges, left, right, heights, halves, wides):
+    halo_tables(edge_leaves, coords, edges, left, right, heights, halves, wides)
+
+
+def sides_kernel(coords, first, second, third, fourth, left, right, heights, halves, wides, sides):
+    col = lax.axis_index("col")
+    odd = col % 2 == 1
+    inner = (col > 0) & (col < lax.axis_size("col") - 1)
+    at = slice(points, points + side_rows)
+    near = first[at, :]
+    far = jnp.where((col % 8 == 3) | (col % 8 == 4), third[at, :], fourth[at, :])
+    far = jnp.where((col % 4 == 1) | (col % 4 == 2), second[at, :], far)
+    far = jnp.where(inner, far, 0.0)
     to_left, to_right = jnp.where(odd, near, far), jnp.where(odd, far, near)
     gap = jnp.zeros((2, points), f32)
     for c in range(3 + rhs):
-        values[c * halo_leaves : c * halo_leaves + edge_leaves, :] = edges[c * edge_leaves : (c + 1) * edge_leaves, :]
         at = slice(6 * c, 6 * c + 6)
-        values[c * halo_leaves + edge_leaves : (c + 1) * halo_leaves, :] = jnp.concatenate([to_left[at], gap, to_right[at], gap], axis=0)
-    fill_tables(halo_leaves, start, values, left, right, heights, wides)
-    for leaf in range(halo_leaves):
-        high, low = split(values[pl.ds(3 * halo_leaves + leaf, rhs, stride=halo_leaves), :])
-        halves[sixteen(leaf), :] = jnp.concatenate([high, low], axis=0)
+        sides[c * side_leaves : (c + 1) * side_leaves, :] = jnp.concatenate([to_left[at], gap, to_right[at], gap], axis=0)
+    halo_tables(side_leaves, coords, sides, left, right, heights, halves, wides)
 
 
 def level(mine, theirs, blocks):
@@ -246,29 +259,33 @@
     return total
 
 
-def level_kernel(mine, theirs, blocks, payload):
-    payload[...] = level(mine[:points, :], theirs[:points, :], blocks)
-
-
-def turn_kernel(mine, theirs, blocks, coords, sources, first, second, payload, outer, edges):
+def level_kernel(forward, mine, theirs, blocks, payload):
     payload[:points, :] = level(mine[:points, :], theirs[:points, :], blocks)
-    odd = lax.axis_index("row") % 2 == 1
-    col = lax.axis_index("col")
+    payload[points:, :] = theirs[forward:, :]
+
+
+def turn_kernel(mine, theirs, blocks, coords, sources, first, second, payload, edges):
+    payload[:points, :] = level(mine[:points, :], theirs[:points, :], blocks)
+    row, col = lax.axis_index("row"), lax.axis_index("col")
+    odd = row % 2 == 1
+    around = (row % 4 == 1) | (row % 4 == 2)
+    inner = (row > 0) & (row < lax.axis_size("row") - 1)
     for c in range(3 + rhs):
-        near = first[points + c * leaf_cols : points + (c + 1) * leaf_cols, :]
-        far = second[c * leaf_cols : (c + 1) * leaf_cols, :]
+        at = slice(points + c * leaf_cols, points + (c + 1) * leaf_cols)
+        near = first[at, :]
+        far = jnp.where(inner, jnp.where(around, second[at, :], theirs[at, :]), 0.0)
         edges[c * edge_leaves : c * edge_leaves + leaf_cols, :] = jnp.where(odd, near, far)
         edges[c * edge_leaves + leaf_cols : (c + 1) * edge_leaves, :] = jnp.where(odd, far, near)
     for k in range(2):
         j = (leaf_cols - 1) * (1 - col % 2 if k == 0 else col % 2)
-        to, base = (payload, points) if k == 0 else (outer, 0)
+        base = points + k * side_rows
         for c in range(3 + rhs):
             ref, at = (coords, c) if c < 3 else (sources, c - 3)
-            to[base + 6 * c : base + 6 * c + 1, :] = edges[pl.ds(c * edge_leaves + j, 1), :]
+            payload[base + 6 * c : base + 6 * c + 1, :] = edges[pl.ds(c * edge_leaves + j, 1), :]
             for i in range(leaf_rows):
-                to[base + 6 * c + 1 + i : base + 6 * c + 2 + i, :] = ref[pl.ds(at * leaves + i * leaf_cols + j, 1), :]
-            to[base + 6 * c + 5 : base + 6 * c + 6, :] = edges[pl.ds(c * edge_leaves + leaf_cols + j, 1), :]
-        to[base + 66 : base + side_rows, :] = jnp.zeros((side_rows - 66, points), f32)
+                payload[base + 6 * c + 1 + i : base + 6 * c + 2 + i, :] = ref[pl.ds(at * leaves + i * leaf_cols + j, 1), :]
+            payload[base + 6 * c + 5 : base + 6 * c + 6, :] = edges[pl.ds(c * edge_leaves + leaf_cols + j, 1), :]
+        payload[base + 66 : base + side_rows, :] = jnp.zeros((side_rows - 66, points), f32)
 
 
 def near_kernel(pieces, trips, both_ways, weights, left, source_heights, source_halves, right, heights, halves, seed, acc, gap_a, gap_b, splat_a, splat_b, kern_a, kern_b):
@@ -360,7 +377,7 @@
 
 
 def finish_kernel(mine, theirs, blocks, expand, acc, out):
-    coeffs = level(mine[...], theirs[...], blocks)
+    coeffs = level(mine[:points, :], theirs[:points, :], blocks)
     for g in range(groups):
         here = coeffs[g * rhs : (g + 1) * rhs]
         rows = jnp.concatenate([jnp.where(lane_block(n), here, 0.0) for n in range(group)], axis=0)
@@ -419,18 +436,26 @@
     )(*[pltpu.with_memory_space_constraint(operand, pltpu.HBM) for operand in operands])
 
 
-def outward(block, axis):
-    size = lax.axis_size(axis)
-    return lax.ppermute(block, axis, [(i, i + 1 if i % 2 else i - 1) for i in range(1, size - 1)])
+def tables_call(body, name, count, scratch, *operands):
+    return pl.pallas_call(
+        body,
+        out_shape=table_shapes(count),
+        in_specs=[vmem] * len(operands),
+        out_specs=(vmem,) * 4,
+        scratch_shapes=[pltpu.VMEM((3, count * 16, points), f32)] + scratch,
+        compiler_params=params(16),
+        cost_estimate=cost(1000),
+        name=name,
+    )(*operands)
 
 
 def shards(coords, sources, neighbour_mask, compress, expand, row_transfer, col_transfer):
     coords = coords.reshape(-1, points)
     sources = sources.reshape(-1, points)
-    halves, payload, outer = far_call(
+    halves, payload = far_call(
         compress_kernel,
         "compress",
-        (table_shapes(leaves)[3], array(points + edge_rows, points), array(edge_rows, points)),
+        (table_shapes(leaves)[3], array(points + 2 * edge_rows, points)),
         [pltpu.VMEM(shape, f32) for shape in ((3 * leaves, points), (rhs * leaves, points), (leaves * rank, points))],
         coords, sources, compress.reshape(-1, points),
     )
@@ -438,7 +463,6 @@
     axes = ["row"] * row_bits + ["col"] * col_bits
     bits = [*range(row_bits), *range(col_bits)]
     theirs = partner_of(payload, "row", 0)
-    beyond = outward(outer, "row")
     block_shape = jax.ShapeDtypeStruct((4, points, points), bf16)
     coords_later, payload = lax.optimization_barrier((coords, payload))
     left, right, heights, row_blocks, col_blocks, weights = far_call(
@@ -455,52 +479,45 @@
         coords_later, neighbour_mask, row_transfer[:, 0, 0], col_transfer[:, 0, 0],
     )
     own = left, right, heights, halves
-    inner, around = interior_runs(), edge_runs() + side_runs()
-    counts = [sum(run.count for run in runs) for runs in (inner, around)]
+    inner, edge, side = interior_runs(), edge_runs(), side_runs()
+    counts = [sum(run.count for run in runs) for runs in (inner, edge, side)]
+    step = 2 * batch
     windows = row_bits + col_bits - 1
-    inner_windows = windows - 2
-    step = 2 * batch
-    cuts = [counts[0] * n // inner_windows // step * step for n in range(inner_windows)] + [counts[0]]
-    half = counts[1] // 2 // step * step
+    edge_windows = (row_bits, row_bits + 2)
+    inner_windows = [n for n in range(1, windows + 1) if n not in edge_windows]
+    cuts = [counts[0] * k // len(inner_windows) // step * step for k in range(len(inner_windows))] + [counts[0]]
+    half = -(-counts[1] // 2 // step) * step
     acc = jnp.zeros((leaves * rhs, points), f32)
+    received = [theirs]
     for n, (axis, bit) in enumerate(zip(axes, bits)):
         blocks = row_blocks if axis == "row" else col_blocks
         if n > 0:
             theirs = partner_of(payload, axis, bit)
+            payload, acc = lax.optimization_barrier((payload, acc))
             if n == row_bits:
-                beyond = outward(outer, "col")
-                first = theirs
-            payload, acc = lax.optimization_barrier((payload, acc))
-            if n <= inner_windows:
-                acc = near_piece(cut_runs(inner, cuts[n - 1], cuts[n]), True, weights, own, own, acc)
+                edges, acc = lax.optimization_barrier((edges, acc))
+                edge_tables = tables_call(edges_kernel, "edges", edge_leaves, [], coords, edges)
+            if n in edge_windows:
+                some = cut_runs(edge, 0, half) if n == row_bits else cut_runs(edge, half, counts[1])
+                acc = near_piece(some, False, weights, edge_tables, own, acc)
             else:
-                some = cut_runs(around, 0, half) if n == windows - 1 else cut_runs(around, half, counts[1])
-                acc = near_piece(some, False, weights, halo, own, acc)
+                k = inner_windows.index(n)
+                acc = near_piece(cut_runs(inner, cuts[k], cuts[k + 1]), True, weights, own, own, acc)
             theirs, acc = lax.optimization_barrier((theirs, acc))
-            if n == row_bits:
-                first = theirs
-        else:
-            first = theirs
+            received.append(theirs)
         if n == row_bits - 1:
-            payload, outer, edges = small_call(
+            payload, edges = small_call(
                 turn_kernel,
                 "turn",
-                (array(points + side_rows, points), array(side_rows, points), array((3 + rhs) * edge_leaves, points)),
-                payload, theirs, blocks, coords, sources, first, beyond,
+                (array(points + 2 * side_rows, points), array((3 + rhs) * edge_leaves, points)),
+                payload, theirs, blocks, coords, sources, received[0], received[1],
             )
         elif n < windows:
-            payload = small_call(level_kernel, "level", array(points, points), payload, theirs, blocks)
-        if n == row_bits:
-            halo = pl.pallas_call(
-                halo_kernel,
-                out_shape=table_shapes(halo_leaves),
-                in_specs=[vmem] * 4,
-                out_specs=(vmem,) * 4,
-                scratch_shapes=[pltpu.VMEM((3, halo_leaves * 16, points), f32), pltpu.VMEM(((3 + rhs) * halo_leaves, points), f32)],
-                compiler_params=params(16),
-                cost_estimate=cost(1000),
-                name="halo",
-            )(coords, edges, first, beyond)
+            rows = edge_rows if axis == "row" else side_rows
+            skip = points + rows if bit == 0 else points
+            payload = small_call(functools.partial(level_kernel, skip), "level", array(points + rows, points), payload, theirs, blocks)
+    side_tables = tables_call(sides_kernel, "sides", side_leaves, [pltpu.VMEM(((3 + rhs) * side_leaves, points), f32)], coords, *received[row_bits:])
+    acc = near_piece(cut_runs(side, 0, counts[2]), False, weights, side_tables, own, acc)
     out = pl.pallas_call(
         finish_kernel,
         out_shape=array(rhs * leaves, points),

time: 58.8 us -> 55.5 us (0.944)
  starting transfers between devices: 19.5 us -> 14.8 us
  Pallas kernels: 38.9 us -> 40.2 us
    ppermute x7, starting transfers between devices: 18.2 us -> 14.8 us  [partner_of(): return lax.ppermute(block, axis, route)]
    ppermute x2 -> x0, starting transfers between devices: 1.32 us -> none  [outward(): lax.ppermute(block, axis, [(i, i + 1 if i % 2 else i - 1) for i in range(...]
    pallas_call x1 -> x2, Pallas kernels: 1.03 us -> 1.98 us  [tables_call(): pl.pallas_call(body, out_shape=table_shapes(count), in_specs=[vmem] * len...]
    pallas_call x6 -> x7, Pallas kernels: 31.4 us -> 31.7 us  [near_piece(): pl.pallas_call(functools.partial(near_kernel, pieces, trips, both_ways),...]
  transfers between devices with their start and end apart: 9 -> 7, of which waited for: 0 -> 0; matrix products, arithmetic and copies ran while one was open for 0% -> 0% of each run, Pallas kernels for 60% -> 59%
where the time goes in v6:
time: 55.5 us; the launch traced here: 55.3 us
  Pallas kernels  40.2 us (72%)
  starting transfers between devices  14.8 us (27%)
    pallas_call x7, Pallas kernels, near_piece(): pl.pallas_call(functools.partial(near_kernel, pieces, trips, both_ways),...  31.7 us
    ppermute x7, starting transfers between devices, partner_of(): return lax.ppermute(block, axis, route)  14.8 us
    pallas_call x2, Pallas kernels, far_call(): pl.pallas_call(body, out_shape=out_shape, in_specs=[pl.BlockSpec(memory_s...  3.83 us
    pallas_call x2, Pallas kernels, tables_call(): pl.pallas_call(body, out_shape=table_shapes(count), in_specs=[vmem] * len...  1.98 us
    pallas_call x6, Pallas kernels, small_call(): pl.pallas_call(body, out_shape=out_shape, in_specs=[vmem] * len(operands)...  1.44 us
    pallas_call x1, Pallas kernels, shards(): pl.pallas_call(finish_kernel, out_shape=array(rhs * leaves, points), in_s...  1.26 us
  transfers between devices with their start and end apart: 7, of which 0 were waited for; matrix products, arithmetic and copies ran while one was open for 0% of the time, Pallas kernels for 59%

profile of v6, /device:TPU:0, one launch (start us, length us, event | category | flops | bytes accessed | tf_op | source)
XLA Modules:
  0.0 55.3 jit_solution(15904449507626942435)
XLA Ops:
  0.0 1.9 %compress.1 = (bf16[1024,128]{1,0:T(8,128)(2,1)S(1)}, f32[480,128]{1,0:T(8,128)S(1)}) custom-call(f32[192,128]{1,0:T(8,128)} %bitcast.9, f32[512,128]{1,0:T(8,128)} %bitcast.7, f32[2048,128]{1,0:T(8,128)} %bitcast.15), custom_call_target="tpu_custom_call" | custom-call | flops 800000000 | bytes 262144 | tf_op jit(solution)/shard_map/compress/pallas_call | solution.py:427
  1.9 0.1 collective-permute-start
  2.0 2.0 %prep.1 = (bf16[8192,16]{1,0:T(8,128)(2,1)S(1)}, bf16[1024,256]{1,0:T(8,128)(2,1)S(1)}, f32[64,128]{1,0:T(8,128)S(1)}, bf16[4,128,128]{2,1,0:T(8,128)(2,1)S(1)},...) custom-call(f32[192,128]{1,0:T(8,128)} %bitcast.10, s32[9,4,16]{2,1,0:T(4,128)} %mask_far.1, ...), custom_call_target="tpu_custom_call" | custom-call | flops 800000000 | bytes 262144 | tf_op jit(solution)/shard_map/prep/pallas_call | solution.py:427
  3.9 0.0 collective-permute-done.theirs.first
  3.9 0.2 level.5.mine
  4.2 1.7 %collective-permute-start.1 = (f32[304,128]{1,0:T(8,128)S(1)}, f32[304,128]{1,0:T(8,128)S(1)}, u32[]{:S(2)}, u32[]{:S(2)}) collective-permute-start(f32[304,128]{1,0:T(8,128)S(1)} %level.5.mine), channel_id=1, source_target_pairs={{0,32},{16,48},{32,0},{48,16},{64,96},{80,112},{96,64},{112,80},{1... | collective-permute-start | bytes 466952 | tf_op jit(solution)/shard_map/ppermute | solution.py:406
  6.0 5.3 %near.7.seed = f32[512,128]{1,0:T(8,128)S(1)} custom-call(f32[584,128]{1,0:T(8,128)S(1)} %get-tuple-element.54.weights, bf16[8192,16]{1,0:T(8,128)(2,1)S(1)} %get-tuple-element.55.left, f32[64,128]{1,0:T(8,128)S(1)} %get-tuple-element.56.source_heights.heights, bf16[1024,128]{1,0:T(8,128)(2,1)S(1)} %get-tuple-element.57.source_halves.halves, ...), custom_call_target="tpu_custom_call" | custom-call | flops 2816000000 | bytes 262144 | tf_op jit(solution)/shard_map/near/pallas_call | solution.py:359
  11.2 0.0 collective-permute-done.1.theirs.second
  11.2 0.2 level.6.mine
  11.5 0.0 copy-start
  11.5 0.0 copy-start.1
  11.5 3.0 %collective-permute-start.2 = (f32[304,128]{1,0:T(8,128)S(1)}, f32[304,128]{1,0:T(8,128)S(1)}, u32[]{:S(2)}, u32[]{:S(2)}) collective-permute-start(f32[304,128]{1,0:T(8,128)S(1)} %level.6.mine), channel_id=1, source_target_pairs={{0,64},{16,80},{32,96},{48,112},{64,0},{80,16},{96,32},{112,48},{1... | collective-permute-start | bytes 466952 | tf_op jit(solution)/shard_map/ppermute | solution.py:406
  14.5 5.2 %near.8.seed = f32[512,128]{1,0:T(8,128)S(1)} custom-call(f32[584,128]{1,0:T(8,128)S(1)} %get-tuple-element.54.weights, bf16[8192,16]{1,0:T(8,128)(2,1)S(1)} %get-tuple-element.55.left, f32[64,128]{1,0:T(8,128)S(1)} %get-tuple-element.56.source_heights.heights, bf16[1024,128]{1,0:T(8,128)(2,1)S(1)} %get-tuple-element.57.source_halves.halves, ...), custom_call_target="tpu_custom_call" | custom-call | flops 2816000000 | bytes 262144 | tf_op jit(solution)/shard_map/near/pallas_call | solution.py:359
  19.7 0.0 collective-permute-done.2.theirs
  19.7 0.0 copy-done
  19.7 0.0 copy-done.1
  19.7 0.3 turn.1
  20.0 2.0 %collective-permute-start.3 = (f32[272,128]{1,0:T(8,128)S(1)}, f32[272,128]{1,0:T(8,128)S(1)}, u32[]{:S(2)}, u32[]{:S(2)}) collective-permute-start(f32[272,128]{1,0:T(8,128)S(1)} %get-tuple-element.67.mine), channel_id=1, source_target_pairs={{0,1},{1,0},{2,3},{3,2},{4,5},{5,4},{6,7},{7,6},{8,9},{9,8},{10,11... | collective-permute-start | bytes 417800 | tf_op jit(solution)/shard_map/ppermute | solution.py:406
  22.0 1.1 %edges.1 = (bf16[4096,16]{1,0:T(8,128)(2,1)S(1)}, bf16[512,256]{1,0:T(8,128)(2,1)}, f32[32,128]{1,0:T(8,128)S(1)}, bf16[512,128]{1,0:T(8,128)(2,1)S(1)}) custom-call(f32[192,128]{1,0:T(8,128)S(1)} %bitcast.12, f32[352,128]{1,0:T(8,128)S(1)} %get-tuple-element.70.edges), custom_call_target="tpu_custom_call" | custom-call | flops 400000000 | bytes 262144 | tf_op jit(solution)/shard_map/edges/pallas_call | solution.py:440
  23.1 4.0 %near.9.seed = f32[512,128]{1,0:T(8,128)S(1)} custom-call(f32[584,128]{1,0:T(8,128)S(1)} %get-tuple-element.54.weights, bf16[4096,16]{1,0:T(8,128)(2,1)S(1)} %get-tuple-element.71.left, f32[32,128]{1,0:T(8,128)S(1)} %get-tuple-element.72.source_heights, bf16[512,128]{1,0:T(8,128)(2,1)S(1)} %get-tuple-element.73.source_halves, ...), custom_call_target="tpu_custom_call" | custom-call | flops 2112000000 | bytes 262144 | tf_op jit(solution)/shard_map/near/pallas_call | solution.py:359
  27.1 0.0 collective-permute-done.3.theirs.first
  27.1 0.2 level.7.mine
  27.4 3.7 %collective-permute-start.4 = (f32[200,128]{1,0:T(8,128)S(1)}, f32[200,128]{1,0:T(8,128)S(1)}, u32[]{:S(2)}, u32[]{:S(2)}) collective-permute-start(f32[200,128]{1,0:T(8,128)S(1)} %level.7.mine), channel_id=1, source_target_pairs={{0,2},{1,3},{2,0},{3,1},{4,6},{5,7},{6,4},{7,5},{8,10},{9,11},{10,... | collective-permute-start | bytes 307208 | tf_op jit(solution)/shard_map/ppermute | solution.py:406
  31.1 5.2 %near.10.seed = f32[512,128]{1,0:T(8,128)S(1)} custom-call(f32[584,128]{1,0:T(8,128)S(1)} %get-tuple-element.54.weights, bf16[8192,16]{1,0:T(8,128)(2,1)S(1)} %get-tuple-element.55.left, f32[64,128]{1,0:T(8,128)S(1)} %get-tuple-element.56.source_heights.heights, bf16[1024,128]{1,0:T(8,128)(2,1)S(1)} %get-tuple-element.57.source_halves.halves, ...), custom_call_target="tpu_custom_call" | custom-call | flops 2816000000 | bytes 262144 | tf_op jit(solution)/shard_map/near/pallas_call | solution.py:359
  36.3 0.0 collective-permute-done.4.theirs.second
  36.3 0.2 level.8.mine
  36.5 1.6 %collective-permute-start.5 = (f32[200,128]{1,0:T(8,128)S(1)}, f32[200,128]{1,0:T(8,128)S(1)}, u32[]{:S(2)}, u32[]{:S(2)}) collective-permute-start(f32[200,128]{1,0:T(8,128)S(1)} %level.8.mine), channel_id=1, source_target_pairs={{0,4},{1,5},{2,6},{3,7},{4,0},{5,1},{6,2},{7,3},{8,12},{9,13},{10,... | collective-permute-start | bytes 307208 | tf_op jit(solution)/shard_map/ppermute | solution.py:406
  38.1 4.1 %near.11.seed = f32[512,128]{1,0:T(8,128)S(1)} custom-call(f32[584,128]{1,0:T(8,128)S(1)} %get-tuple-element.54.weights, bf16[4096,16]{1,0:T(8,128)(2,1)S(1)} %get-tuple-element.71.left, f32[32,128]{1,0:T(8,128)S(1)} %get-tuple-element.72.source_heights, bf16[512,128]{1,0:T(8,128)(2,1)S(1)} %get-tuple-element.73.source_halves, ...), custom_call_target="tpu_custom_call" | custom-call | flops 1936000000 | bytes 262144 | tf_op jit(solution)/shard_map/near/pallas_call | solution.py:359
  42.2 0.0 collective-permute-done.5.theirs.third
  42.2 0.2 level.9.mine
  42.4 2.8 %collective-permute-start.6 = (f32[200,128]{1,0:T(8,128)S(1)}, f32[200,128]{1,0:T(8,128)S(1)}, u32[]{:S(2)}, u32[]{:S(2)}) collective-permute-start(f32[200,128]{1,0:T(8,128)S(1)} %level.9.mine), channel_id=1, source_target_pairs={{0,8},{1,9},{2,10},{3,11},{4,12},{5,13},{6,14},{7,15},{8,0},{9,1},... | collective-permute-start | bytes 307208 | tf_op jit(solution)/shard_map/ppermute | solution.py:406
  45.2 5.8 %near.12.seed = f32[512,128]{1,0:T(8,128)S(1)} custom-call(f32[584,128]{1,0:T(8,128)S(1)} %get-tuple-element.54.weights, bf16[8192,16]{1,0:T(8,128)(2,1)S(1)} %get-tuple-element.55.left, f32[64,128]{1,0:T(8,128)S(1)} %get-tuple-element.56.source_heights.heights, bf16[1024,128]{1,0:T(8,128)(2,1)S(1)} %get-tuple-element.57.source_halves.halves, ...), custom_call_target="tpu_custom_call" | custom-call | flops 3080000000 | bytes 262144 | tf_op jit(solution)/shard_map/near/pallas_call | solution.py:359
  51.1 0.0 collective-permute-done.6.fourth.theirs
  51.1 0.9 %sides.1 = (bf16[2048,16]{1,0:T(8,128)(2,1)S(1)}, bf16[256,256]{1,0:T(8,128)(2,1)}, f32[16,128]{1,0:T(8,128)S(1)}, bf16[256,128]{1,0:T(8,128)(2,1)S(1)}) custom-call(f32[192,128]{1,0:T(8,128)S(1)} %bitcast.13, f32[272,128]{1,0:T(8,128)S(1)} %collective-permute-done.3.theirs.first, f32[200,128]{1,0:T(8,128)S(1)} %collective-permute-done.4.theirs.second, ...), custom_call_target="tpu_custom_call" | custom-call | flops 400000000 | bytes 262144 | tf_op jit(solution)/shard_map/sides/pallas_call | solution.py:440
  51.9 0.0 copy-start.2
  52.0 2.1 %near.13.acc = f32[512,128]{1,0:T(8,128)S(1)} custom-call(f32[584,128]{1,0:T(8,128)S(1)} %get-tuple-element.54.weights, bf16[2048,16]{1,0:T(8,128)(2,1)S(1)} %get-tuple-element.89.left, f32[16,128]{1,0:T(8,128)S(1)} %get-tuple-element.90.source_heights, bf16[256,128]{1,0:T(8,128)(2,1)S(1)} %get-tuple-element.91.source_halves, ...), custom_call_target="tpu_custom_call" | custom-call | flops 1056000000 | bytes 262144 | tf_op jit(solution)/shard_map/near/pallas_call | solution.py:359
  54.1 0.0 copy-done.2
  54.1 1.3 %finish.1 = f32[512,128]{1,0:T(8,128)} custom-call(f32[200,128]{1,0:T(8,128)S(1)} %level.9.mine, f32[200,128]{1,0:T(8,128)S(1)} %collective-permute-done.6.fourth.theirs, bf16[4,128,128]{2,1,0:T(8,128)(2,1)S(1)} %get-tuple-element.76.blocks, f32[2048,128]{1,0:T(8,128)S(1)} %bitcast.14, f32[512,128]{1,0:T(8,128)S(1)} %near.13.acc), custom_call_target="tpu_custom_call" | custom-call | flops 800000000 | bytes 262144 | tf_op jit(solution)/shard_map/finish/pallas_call | solution.py:521
  (1 shorter events, 0.0 us)
Async XLA Ops:
  1.9 2.1 %collective-permute-start = (f32[480,128]{1,0:T(8,128)S(1)}, f32[480,128]{1,0:T(8,128)S(1)}, u32[]{:S(2)}, u32[]{:S(2)}) collective-permute-start(f32[480,128]{1,0:T(8,128)S(1)} %get-tuple-element.50.mine), channel_id=1, source_target_pairs={{0,16},{16,0},{32,48},{48,32},{64,80},{80,64},{96,112},{112,96},{1... | collective-permute-start | bytes 737288 | tf_op jit(solution)/shard_map/ppermute | solution.py:406
  4.2 7.0 %collective-permute-start.1 = (f32[304,128]{1,0:T(8,128)S(1)}, f32[304,128]{1,0:T(8,128)S(1)}, u32[]{:S(2)}, u32[]{:S(2)}) collective-permute-start(f32[304,128]{1,0:T(8,128)S(1)} %level.5.mine), channel_id=1, source_target_pairs={{0,32},{16,48},{32,0},{48,16},{64,96},{80,112},{96,64},{112,80},{1... | collective-permute-start | bytes 466952 | tf_op jit(solution)/shard_map/ppermute | solution.py:406
  11.5 8.3 %copy-start = (f32[8,4,16,128]{3,2,1,0:T(8,128)S(1)}, f32[8,4,16,128]{3,2,1,0:T(8,128)}, u32[]{:S(2)}) copy-start(f32[8,4,16,128]{3,2,1,0:T(8,128)} %param.8) | copy-start | bytes 786436
  11.5 8.2 %copy-start.1 = (f32[3,4,16,128]{3,2,1,0:T(8,128)S(1)}, f32[3,4,16,128]{3,2,1,0:T(8,128)}, u32[]{:S(2)}) copy-start(f32[3,4,16,128]{3,2,1,0:T(8,128)} %param.7) | copy-start | bytes 294916
  11.5 8.2 %collective-permute-start.2 = (f32[304,128]{1,0:T(8,128)S(1)}, f32[304,128]{1,0:T(8,128)S(1)}, u32[]{:S(2)}, u32[]{:S(2)}) collective-permute-start(f32[304,128]{1,0:T(8,128)S(1)} %level.6.mine), channel_id=1, source_target_pairs={{0,64},{16,80},{32,96},{48,112},{64,0},{80,16},{96,32},{112,48},{1... | collective-permute-start | bytes 466952 | tf_op jit(solution)/shard_map/ppermute | solution.py:406
  20.0 7.1 %collective-permute-start.3 = (f32[272,128]{1,0:T(8,128)S(1)}, f32[272,128]{1,0:T(8,128)S(1)}, u32[]{:S(2)}, u32[]{:S(2)}) collective-permute-start(f32[272,128]{1,0:T(8,128)S(1)} %get-tuple-element.67.mine), channel_id=1, source_target_pairs={{0,1},{1,0},{2,3},{3,2},{4,5},{5,4},{6,7},{7,6},{8,9},{9,8},{10,11... | collective-permute-start | bytes 417800 | tf_op jit(solution)/shard_map/ppermute | solution.py:406
  27.4 8.9 %collective-permute-start.4 = (f32[200,128]{1,0:T(8,128)S(1)}, f32[200,128]{1,0:T(8,128)S(1)}, u32[]{:S(2)}, u32[]{:S(2)}) collective-permute-start(f32[200,128]{1,0:T(8,128)S(1)} %level.7.mine), channel_id=1, source_target_pairs={{0,2},{1,3},{2,0},{3,1},{4,6},{5,7},{6,4},{7,5},{8,10},{9,11},{10,... | collective-permute-start | bytes 307208 | tf_op jit(solution)/shard_map/ppermute | solution.py:406
  36.5 5.6 %collective-permute-start.5 = (f32[200,128]{1,0:T(8,128)S(1)}, f32[200,128]{1,0:T(8,128)S(1)}, u32[]{:S(2)}, u32[]{:S(2)}) collective-permute-start(f32[200,128]{1,0:T(8,128)S(1)} %level.8.mine), channel_id=1, source_target_pairs={{0,4},{1,5},{2,6},{3,7},{4,0},{5,1},{6,2},{7,3},{8,12},{9,13},{10,... | collective-permute-start | bytes 307208 | tf_op jit(solution)/shard_map/ppermute | solution.py:406
  42.4 8.7 %collective-permute-start.6 = (f32[200,128]{1,0:T(8,128)S(1)}, f32[200,128]{1,0:T(8,128)S(1)}, u32[]{:S(2)}, u32[]{:S(2)}) collective-permute-start(f32[200,128]{1,0:T(8,128)S(1)} %level.9.mine), channel_id=1, source_target_pairs={{0,8},{1,9},{2,10},{3,11},{4,12},{5,13},{6,14},{7,15},{8,0},{9,1},... | collective-permute-start | bytes 307208 | tf_op jit(solution)/shard_map/ppermute | solution.py:406
  51.9 2.1 %copy-start.2 = (f32[4,16,32,128]{3,2,1,0:T(8,128)S(1)}, f32[4,16,32,128]{3,2,1,0:T(8,128)}, u32[]{:S(2)}) copy-start(f32[4,16,32,128]{3,2,1,0:T(8,128)} %param.11) | copy-start | bytes 3145732

commit v7 on v6

--- a/solution.py
+++ b/solution.py
@@ -30,6 +30,8 @@
 group = points // rank
 groups = leaves // group
 batch = 4
+step = 2 * batch
+unroll = 2
 vmem = pl.BlockSpec(memory_space=pltpu.VMEM)
 
 
@@ -202,9 +204,7 @@
         payload[g * rhs : (g + 1) * rhs, :] = total
 
 
-def prep_kernel(coords_far, mask_far, row_far, col_far, left, right, heights, row_blocks, col_blocks, weights, wides, coords, mask, row_transfer, col_transfer, arrived):
-    for copy in start_copies((coords_far, mask_far, row_far, col_far), (coords, mask, row_transfer, col_transfer), arrived):
-        copy.wait()
+def prep_kernel(coords, mask, row_transfer, col_transfer, left, right, heights, row_blocks, col_blocks, weights, wides):
     start = [coords[c * leaves : c * leaves + 1, 0:1] for c in range(3)]
     fill_tables(leaves, start, coords, left, right, heights, wides)
     spread_blocks(row_transfer, row_blocks)
@@ -288,7 +288,7 @@
         payload[base + 66 : base + side_rows, :] = jnp.zeros((side_rows - 66, points), f32)
 
 
-def near_kernel(pieces, trips, both_ways, weights, left, source_heights, source_halves, right, heights, halves, seed, acc, gap_a, gap_b, splat_a, splat_b, kern_a, kern_b):
+def near_kernel(pieces, pairs, both_ways, weights, left, source_heights, source_halves, right, heights, halves, seed, acc, gap_a, gap_b, splat_a, splat_b, kern_a, kern_b):
     acc[...] = seed[...]
     kern_b[...] = jnp.zeros_like(kern_b)
     buffers_a, buffers_b = (gap_a, splat_a, kern_a), (gap_b, splat_b, kern_b)
@@ -338,26 +338,34 @@
             evaluate(now[n], n, *here)
         return now, later
 
+    def pair(at, carry):
+        carry = stage(at, *carry, buffers_a, buffers_b)
+        return stage(at + batch, *carry, buffers_b, buffers_a)
+
     def body(trip, carry):
-        carry = stage(trip * 2 * batch, *carry, buffers_a, buffers_b)
-        return stage(trip * 2 * batch + batch, *carry, buffers_b, buffers_a)
+        for k in range(unroll):
+            carry = pair(trip * step * unroll + k * step, carry)
+        return carry
 
     first = items_at(jnp.int32(0))
     for n in range(batch):
         subtract(first[n], n, *buffers_a[:2])
     nothing = [[jnp.int32(0), jnp.int32(0), jnp.int32(zero_row), jnp.int32(zero_row)]] * batch
-    last, _ = lax.fori_loop(0, trips, body, (nothing, first))
+    carry = lax.fori_loop(0, pairs // unroll, body, (nothing, first))
+    for k in range(pairs // unroll * unroll, pairs):
+        carry = pair(jnp.int32(k * step), carry)
+    last = carry[0]
     for n in range(batch):
         apply(last[n], n, buffers_b[2])
 
 
 def near_piece(pieces, both_ways, weights, source_tables, target_tables, seed):
     count = sum(high - low for _, low, high in pieces)
-    trips = -(-count // (2 * batch))
+    pairs = -(-count // step)
     left, _, source_heights, source_halves = source_tables
     _, right, heights, halves = target_tables
     return pl.pallas_call(
-        functools.partial(near_kernel, pieces, trips, both_ways),
+        functools.partial(near_kernel, pieces, pairs, both_ways),
         out_shape=jax.ShapeDtypeStruct(seed.shape, f32),
         in_specs=[vmem] * 8,
         out_specs=vmem,
@@ -465,23 +473,19 @@
     theirs = partner_of(payload, "row", 0)
     block_shape = jax.ShapeDtypeStruct((4, points, points), bf16)
     coords_later, payload = lax.optimization_barrier((coords, payload))
-    left, right, heights, row_blocks, col_blocks, weights = far_call(
+    left, right, heights, row_blocks, col_blocks, weights = pl.pallas_call(
         prep_kernel,
-        "prep",
-        table_shapes(leaves)[:3] + (block_shape, block_shape, array(zero_row + 8, points)),
-        [
-            pltpu.VMEM((3, leaves * 16, points), f32),
-            pltpu.VMEM((3 * leaves, points), f32),
-            pltpu.VMEM((9, leaf_rows, leaf_cols), jnp.int32),
-            pltpu.VMEM((2, rank, rank), f32),
-            pltpu.VMEM((2, rank, rank), f32),
-        ],
-        coords_later, neighbour_mask, row_transfer[:, 0, 0], col_transfer[:, 0, 0],
-    )
+        out_shape=table_shapes(leaves)[:3] + (block_shape, block_shape, array(zero_row + 8, points)),
+        in_specs=[vmem] * 4,
+        out_specs=(vmem,) * 6,
+        scratch_shapes=[pltpu.VMEM((3, leaves * 16, points), f32)],
+        compiler_params=params(16),
+        cost_estimate=cost(2000),
+        name="prep",
+    )(coords_later, neighbour_mask, row_transfer[:, 0, 0], col_transfer[:, 0, 0])
     own = left, right, heights, halves
     inner, edge, side = interior_runs(), edge_runs(), side_runs()
     counts = [sum(run.count for run in runs) for runs in (inner, edge, side)]
-    step = 2 * batch
     windows = row_bits + col_bits - 1
     edge_windows = (row_bits, row_bits + 2)
     inner_windows = [n for n in range(1, windows + 1) if n not in edge_windows]

time: 55.5 us -> 53.8 us (0.969)
  Pallas kernels: 40.2 us -> 38 us
    pallas_call x2 -> x1, Pallas kernels: 3.83 us -> 1.9 us  [far_call(): pl.pallas_call(body, out_shape=out_shape, in_specs=[pl.BlockSpec(memory_s...]
    pallas_call x7 -> x8, Pallas kernels: 31.7 us -> 31.4 us  [the longest x7 30.4 us: near_piece(): pl.pallas_call(functools.partial(near_kernel, pieces, pairs, both_ways),...]
  transfers between devices with their start and end apart: 7 -> 7, of which waited for: 0 -> 1; matrix products, arithmetic and copies ran while one was open for 0% -> 0% of each run, Pallas kernels for 59% -> 57%
where the time goes in v7:
time: 53.8 us; the launch traced here: 53.7 us
  Pallas kernels  38 us (71%)
  starting transfers between devices  15 us (28%)
    pallas_call x7, Pallas kernels, near_piece(): pl.pallas_call(functools.partial(near_kernel, pieces, pairs, both_ways),...  30.4 us
    ppermute x7, starting transfers between devices, partner_of(): return lax.ppermute(block, axis, route)  15 us
    pallas_call x2, Pallas kernels, tables_call(): pl.pallas_call(body, out_shape=table_shapes(count), in_specs=[vmem] * len...  1.98 us
    pallas_call x1, Pallas kernels, far_call(): pl.pallas_call(body, out_shape=out_shape, in_specs=[pl.BlockSpec(memory_s...  1.9 us
    pallas_call x6, Pallas kernels, small_call(): pl.pallas_call(body, out_shape=out_shape, in_specs=[vmem] * len(operands)...  1.44 us
    pallas_call x1, Pallas kernels, shards(): pl.pallas_call(finish_kernel, out_shape=array(rhs * leaves, points), in_s...  1.26 us
  transfers between devices with their start and end apart: 7, of which 1 were waited for; matrix products, arithmetic and copies ran while one was open for 0% of the time, Pallas kernels for 57%

profile of v7, /device:TPU:0, one launch (start us, length us, event | category | flops | bytes accessed | tf_op | source)
XLA Modules:
  0.0 53.7 jit_solution(7388012225725224906)
XLA Ops:
  0.0 0.0 copy-start.1
  0.0 0.0 copy-start.3
  0.0 0.0 copy-start.4
  0.0 0.0 copy-start.5
  0.0 1.9 %compress.1 = (bf16[1024,128]{1,0:T(8,128)(2,1)S(1)}, f32[480,128]{1,0:T(8,128)S(1)}) custom-call(f32[192,128]{1,0:T(8,128)} %bitcast.9, f32[512,128]{1,0:T(8,128)} %bitcast.7, f32[2048,128]{1,0:T(8,128)} %bitcast.17), custom_call_target="tpu_custom_call" | custom-call | flops 800000000 | bytes 262144 | tf_op jit(solution)/shard_map/compress/pallas_call | solution.py:435
  1.9 0.1 collective-permute-start
  2.0 0.0 copy-done.1
  2.0 0.0 copy-done.3
  2.0 0.0 copy-done.4
  2.0 0.0 copy-done.5
  2.0 1.0 %prep.1 = (bf16[8192,16]{1,0:T(8,128)(2,1)S(1)}, bf16[1024,256]{1,0:T(8,128)(2,1)S(1)}, f32[64,128]{1,0:T(8,128)S(1)}, bf16[4,128,128]{2,1,0:T(8,128)(2,1)S(1)},...) custom-call(f32[192,128]{1,0:T(8,128)S(1)} %bitcast.10, s32[9,4,16]{2,1,0:T(4,128)S(1)} %copy-done.5, ...), custom_call_target="tpu_custom_call" | custom-call | flops 800000000 | bytes 262144 | tf_op jit(solution)/shard_map/prep/pallas_call | solution.py:476
  3.1 0.5 collective-permute-done.theirs.first
  3.5 0.2 level.5.mine
  3.7 1.8 %collective-permute-start.1 = (f32[304,128]{1,0:T(8,128)S(1)}, f32[304,128]{1,0:T(8,128)S(1)}, u32[]{:S(2)}, u32[]{:S(2)}) collective-permute-start(f32[304,128]{1,0:T(8,128)S(1)} %level.5.mine), channel_id=1, source_target_pairs={{0,32},{16,48},{32,0},{48,16},{64,96},{80,112},{96,64},{112,80},{1... | collective-permute-start | bytes 466952 | tf_op jit(solution)/shard_map/ppermute | solution.py:414
  5.5 5.0 %near.7.seed = f32[512,128]{1,0:T(8,128)S(1)} custom-call(f32[584,128]{1,0:T(8,128)S(1)} %get-tuple-element.54.weights, bf16[8192,16]{1,0:T(8,128)(2,1)S(1)} %get-tuple-element.55.left, f32[64,128]{1,0:T(8,128)S(1)} %get-tuple-element.56.source_heights.heights, bf16[1024,128]{1,0:T(8,128)(2,1)S(1)} %get-tuple-element.57.source_halves.halves, ...), custom_call_target="tpu_custom_call" | custom-call | flops 2816000000 | bytes 262144 | tf_op jit(solution)/shard_map/near/pallas_call | solution.py:367
  10.5 0.0 collective-permute-done.1.theirs.second
  10.5 0.2 level.6.mine
  10.8 0.0 copy-start
  10.8 3.0 %collective-permute-start.2 = (f32[304,128]{1,0:T(8,128)S(1)}, f32[304,128]{1,0:T(8,128)S(1)}, u32[]{:S(2)}, u32[]{:S(2)}) collective-permute-start(f32[304,128]{1,0:T(8,128)S(1)} %level.6.mine), channel_id=1, source_target_pairs={{0,64},{16,80},{32,96},{48,112},{64,0},{80,16},{96,32},{112,48},{1... | collective-permute-start | bytes 466952 | tf_op jit(solution)/shard_map/ppermute | solution.py:414
  13.7 5.0 %near.8.seed = f32[512,128]{1,0:T(8,128)S(1)} custom-call(f32[584,128]{1,0:T(8,128)S(1)} %get-tuple-element.54.weights, bf16[8192,16]{1,0:T(8,128)(2,1)S(1)} %get-tuple-element.55.left, f32[64,128]{1,0:T(8,128)S(1)} %get-tuple-element.56.source_heights.heights, bf16[1024,128]{1,0:T(8,128)(2,1)S(1)} %get-tuple-element.57.source_halves.halves, ...), custom_call_target="tpu_custom_call" | custom-call | flops 2816000000 | bytes 262144 | tf_op jit(solution)/shard_map/near/pallas_call | solution.py:367
  18.7 0.0 collective-permute-done.2.theirs
  18.8 0.0 copy-done
  18.8 0.3 turn.1
  19.0 2.0 %collective-permute-start.3 = (f32[272,128]{1,0:T(8,128)S(1)}, f32[272,128]{1,0:T(8,128)S(1)}, u32[]{:S(2)}, u32[]{:S(2)}) collective-permute-start(f32[272,128]{1,0:T(8,128)S(1)} %get-tuple-element.67.mine), channel_id=1, source_target_pairs={{0,1},{1,0},{2,3},{3,2},{4,5},{5,4},{6,7},{7,6},{8,9},{9,8},{10,11... | collective-permute-start | bytes 417800 | tf_op jit(solution)/shard_map/ppermute | solution.py:414
  21.0 1.1 %edges.1 = (bf16[4096,16]{1,0:T(8,128)(2,1)S(1)}, bf16[512,256]{1,0:T(8,128)(2,1)}, f32[32,128]{1,0:T(8,128)S(1)}, bf16[512,128]{1,0:T(8,128)(2,1)S(1)}) custom-call(f32[192,128]{1,0:T(8,128)S(1)} %bitcast.12, f32[352,128]{1,0:T(8,128)S(1)} %get-tuple-element.70.edges), custom_call_target="tpu_custom_call" | custom-call | flops 400000000 | bytes 262144 | tf_op jit(solution)/shard_map/edges/pallas_call | solution.py:448
  22.2 3.9 %near.9.seed = f32[512,128]{1,0:T(8,128)S(1)} custom-call(f32[584,128]{1,0:T(8,128)S(1)} %get-tuple-element.54.weights, bf16[4096,16]{1,0:T(8,128)(2,1)S(1)} %get-tuple-element.71.left, f32[32,128]{1,0:T(8,128)S(1)} %get-tuple-element.72.source_heights, bf16[512,128]{1,0:T(8,128)(2,1)S(1)} %get-tuple-element.73.source_halves, ...), custom_call_target="tpu_custom_call" | custom-call | flops 2112000000 | bytes 262144 | tf_op jit(solution)/shard_map/near/pallas_call | solution.py:367
  26.1 0.0 collective-permute-done.3.theirs.first
  26.1 0.2 level.7.mine
  26.3 3.7 %collective-permute-start.4 = (f32[200,128]{1,0:T(8,128)S(1)}, f32[200,128]{1,0:T(8,128)S(1)}, u32[]{:S(2)}, u32[]{:S(2)}) collective-permute-start(f32[200,128]{1,0:T(8,128)S(1)} %level.7.mine), channel_id=1, source_target_pairs={{0,2},{1,3},{2,0},{3,1},{4,6},{5,7},{6,4},{7,5},{8,10},{9,11},{10,... | collective-permute-start | bytes 307208 | tf_op jit(solution)/shard_map/ppermute | solution.py:414
  30.0 5.0 %near.10.seed = f32[512,128]{1,0:T(8,128)S(1)} custom-call(f32[584,128]{1,0:T(8,128)S(1)} %get-tuple-element.54.weights, bf16[8192,16]{1,0:T(8,128)(2,1)S(1)} %get-tuple-element.55.left, f32[64,128]{1,0:T(8,128)S(1)} %get-tuple-element.56.source_heights.heights, bf16[1024,128]{1,0:T(8,128)(2,1)S(1)} %get-tuple-element.57.source_halves.halves, ...), custom_call_target="tpu_custom_call" | custom-call | flops 2816000000 | bytes 262144 | tf_op jit(solution)/shard_map/near/pallas_call | solution.py:367
  34.9 0.0 collective-permute-done.4.theirs.second
  35.0 0.2 level.8.mine
  35.2 1.6 %collective-permute-start.5 = (f32[200,128]{1,0:T(8,128)S(1)}, f32[200,128]{1,0:T(8,128)S(1)}, u32[]{:S(2)}, u32[]{:S(2)}) collective-permute-start(f32[200,128]{1,0:T(8,128)S(1)} %level.8.mine), channel_id=1, source_target_pairs={{0,4},{1,5},{2,6},{3,7},{4,0},{5,1},{6,2},{7,3},{8,12},{9,13},{10,... | collective-permute-start | bytes 307208 | tf_op jit(solution)/shard_map/ppermute | solution.py:414
  36.8 3.9 %near.11.seed = f32[512,128]{1,0:T(8,128)S(1)} custom-call(f32[584,128]{1,0:T(8,128)S(1)} %get-tuple-element.54.weights, bf16[4096,16]{1,0:T(8,128)(2,1)S(1)} %get-tuple-element.71.left, f32[32,128]{1,0:T(8,128)S(1)} %get-tuple-element.72.source_heights, bf16[512,128]{1,0:T(8,128)(2,1)S(1)} %get-tuple-element.73.source_halves, ...), custom_call_target="tpu_custom_call" | custom-call | flops 1936000000 | bytes 262144 | tf_op jit(solution)/shard_map/near/pallas_call | solution.py:367
  40.7 0.0 collective-permute-done.5.theirs.third
  40.7 0.2 level.9.mine
  41.0 3.0 %collective-permute-start.6 = (f32[200,128]{1,0:T(8,128)S(1)}, f32[200,128]{1,0:T(8,128)S(1)}, u32[]{:S(2)}, u32[]{:S(2)}) collective-permute-start(f32[200,128]{1,0:T(8,128)S(1)} %level.9.mine), channel_id=1, source_target_pairs={{0,8},{1,9},{2,10},{3,11},{4,12},{5,13},{6,14},{7,15},{8,0},{9,1},... | collective-permute-start | bytes 307208 | tf_op jit(solution)/shard_map/ppermute | solution.py:414
  44.0 5.7 %near.12.seed = f32[512,128]{1,0:T(8,128)S(1)} custom-call(f32[584,128]{1,0:T(8,128)S(1)} %get-tuple-element.54.weights, bf16[8192,16]{1,0:T(8,128)(2,1)S(1)} %get-tuple-element.55.left, f32[64,128]{1,0:T(8,128)S(1)} %get-tuple-element.56.source_heights.heights, bf16[1024,128]{1,0:T(8,128)(2,1)S(1)} %get-tuple-element.57.source_halves.halves, ...), custom_call_target="tpu_custom_call" | custom-call | flops 3080000000 | bytes 262144 | tf_op jit(solution)/shard_map/near/pallas_call | solution.py:367
  49.7 0.0 collective-permute-done.6.fourth.theirs
  49.7 0.9 %sides.1 = (bf16[2048,16]{1,0:T(8,128)(2,1)S(1)}, bf16[256,256]{1,0:T(8,128)(2,1)}, f32[16,128]{1,0:T(8,128)S(1)}, bf16[256,128]{1,0:T(8,128)(2,1)S(1)}) custom-call(f32[192,128]{1,0:T(8,128)S(1)} %bitcast.13, f32[272,128]{1,0:T(8,128)S(1)} %collective-permute-done.3.theirs.first, f32[200,128]{1,0:T(8,128)S(1)} %collective-permute-done.4.theirs.second, ...), custom_call_target="tpu_custom_call" | custom-call | flops 400000000 | bytes 262144 | tf_op jit(solution)/shard_map/sides/pallas_call | solution.py:448
  50.5 0.0 copy-start.2
  50.6 1.9 %near.13.acc = f32[512,128]{1,0:T(8,128)S(1)} custom-call(f32[584,128]{1,0:T(8,128)S(1)} %get-tuple-element.54.weights, bf16[2048,16]{1,0:T(8,128)(2,1)S(1)} %get-tuple-element.89.left, f32[16,128]{1,0:T(8,128)S(1)} %get-tuple-element.90.source_heights, bf16[256,128]{1,0:T(8,128)(2,1)S(1)} %get-tuple-element.91.source_halves, ...), custom_call_target="tpu_custom_call" | custom-call | flops 1056000000 | bytes 262144 | tf_op jit(solution)/shard_map/near/pallas_call | solution.py:367
  52.4 0.0 copy-done.2
  52.4 1.3 %finish.1 = f32[512,128]{1,0:T(8,128)} custom-call(f32[200,128]{1,0:T(8,128)S(1)} %level.9.mine, f32[200,128]{1,0:T(8,128)S(1)} %collective-permute-done.6.fourth.theirs, bf16[4,128,128]{2,1,0:T(8,128)(2,1)S(1)} %get-tuple-element.76.blocks, f32[2048,128]{1,0:T(8,128)S(1)} %bitcast.14, f32[512,128]{1,0:T(8,128)S(1)} %near.13.acc), custom_call_target="tpu_custom_call" | custom-call | flops 800000000 | bytes 262144 | tf_op jit(solution)/shard_map/finish/pallas_call | solution.py:525
  (1 shorter events, 0.0 us)
Async XLA Ops:
  0.0 2.0 %copy-start.1 = (f32[3,4,16,128]{3,2,1,0:T(8,128)S(1)}, f32[3,4,16,128]{3,2,1,0:T(8,128)}, u32[]{:S(2)}) copy-start(f32[3,4,16,128]{3,2,1,0:T(8,128)} %param.7) | copy-start | bytes 294916
  0.0 2.0 %copy-start.3 = (f32[2,1,1,32,32]{4,3,2,1,0:T(8,128)S(1)}, f32[2,1,1,32,32]{4,3,2,1,0:T(8,128)}, u32[]{:S(2)}) copy-start(f32[2,1,1,32,32]{4,3,2,1,0:T(8,128)} %param.12) | copy-start | bytes 24580
  0.0 2.0 %copy-start.4 = (f32[2,1,1,32,32]{4,3,2,1,0:T(8,128)S(1)}, f32[2,1,1,32,32]{4,3,2,1,0:T(8,128)}, u32[]{:S(2)}) copy-start(f32[2,1,1,32,32]{4,3,2,1,0:T(8,128)} %param.13) | copy-start | bytes 24580
  0.0 2.0 %copy-start.5 = (s32[9,4,16]{2,1,0:T(4,128)S(1)}, s32[9,4,16]{2,1,0:T(4,128)}, u32[]{:S(2)}) copy-start(s32[9,4,16]{2,1,0:T(4,128)} %mask.1) | copy-start | bytes 6916
  1.9 1.6 %collective-permute-start = (f32[480,128]{1,0:T(8,128)S(1)}, f32[480,128]{1,0:T(8,128)S(1)}, u32[]{:S(2)}, u32[]{:S(2)}) collective-permute-start(f32[480,128]{1,0:T(8,128)S(1)} %get-tuple-element.50.mine), channel_id=1, source_target_pairs={{0,16},{16,0},{32,48},{48,32},{64,80},{80,64},{96,112},{112,96},{1... | collective-permute-start | bytes 737288 | tf_op jit(solution)/shard_map/ppermute | solution.py:414
  3.7 6.8 %collective-permute-start.1 = (f32[304,128]{1,0:T(8,128)S(1)}, f32[304,128]{1,0:T(8,128)S(1)}, u32[]{:S(2)}, u32[]{:S(2)}) collective-permute-start(f32[304,128]{1,0:T(8,128)S(1)} %level.5.mine), channel_id=1, source_target_pairs={{0,32},{16,48},{32,0},{48,16},{64,96},{80,112},{96,64},{112,80},{1... | collective-permute-start | bytes 466952 | tf_op jit(solution)/shard_map/ppermute | solution.py:414
  10.8 8.0 %copy-start = (f32[8,4,16,128]{3,2,1,0:T(8,128)S(1)}, f32[8,4,16,128]{3,2,1,0:T(8,128)}, u32[]{:S(2)}) copy-start(f32[8,4,16,128]{3,2,1,0:T(8,128)} %param.8) | copy-start | bytes 786436
  10.8 8.0 %collective-permute-start.2 = (f32[304,128]{1,0:T(8,128)S(1)}, f32[304,128]{1,0:T(8,128)S(1)}, u32[]{:S(2)}, u32[]{:S(2)}) collective-permute-start(f32[304,128]{1,0:T(8,128)S(1)} %level.6.mine), channel_id=1, source_target_pairs={{0,64},{16,80},{32,96},{48,112},{64,0},{80,16},{96,32},{112,48},{1... | collective-permute-start | bytes 466952 | tf_op jit(solution)/shard_map/ppermute | solution.py:414
  19.0 7.0 %collective-permute-start.3 = (f32[272,128]{1,0:T(8,128)S(1)}, f32[272,128]{1,0:T(8,128)S(1)}, u32[]{:S(2)}, u32[]{:S(2)}) collective-permute-start(f32[272,128]{1,0:T(8,128)S(1)} %get-tuple-element.67.mine), channel_id=1, source_target_pairs={{0,1},{1,0},{2,3},{3,2},{4,5},{5,4},{6,7},{7,6},{8,9},{9,8},{10,11... | collective-permute-start | bytes 417800 | tf_op jit(solution)/shard_map/ppermute | solution.py:414
  26.3 8.6 %collective-permute-start.4 = (f32[200,128]{1,0:T(8,128)S(1)}, f32[200,128]{1,0:T(8,128)S(1)}, u32[]{:S(2)}, u32[]{:S(2)}) collective-permute-start(f32[200,128]{1,0:T(8,128)S(1)} %level.7.mine), channel_id=1, source_target_pairs={{0,2},{1,3},{2,0},{3,1},{4,6},{5,7},{6,4},{7,5},{8,10},{9,11},{10,... | collective-permute-start | bytes 307208 | tf_op jit(solution)/shard_map/ppermute | solution.py:414
  35.2 5.5 %collective-permute-start.5 = (f32[200,128]{1,0:T(8,128)S(1)}, f32[200,128]{1,0:T(8,128)S(1)}, u32[]{:S(2)}, u32[]{:S(2)}) collective-permute-start(f32[200,128]{1,0:T(8,128)S(1)} %level.8.mine), channel_id=1, source_target_pairs={{0,4},{1,5},{2,6},{3,7},{4,0},{5,1},{6,2},{7,3},{8,12},{9,13},{10,... | collective-permute-start | bytes 307208 | tf_op jit(solution)/shard_map/ppermute | solution.py:414
  41.0 8.7 %collective-permute-start.6 = (f32[200,128]{1,0:T(8,128)S(1)}, f32[200,128]{1,0:T(8,128)S(1)}, u32[]{:S(2)}, u32[]{:S(2)}) collective-permute-start(f32[200,128]{1,0:T(8,128)S(1)} %level.9.mine), channel_id=1, source_target_pairs={{0,8},{1,9},{2,10},{3,11},{4,12},{5,13},{6,14},{7,15},{8,0},{9,1},... | collective-permute-start | bytes 307208 | tf_op jit(solution)/shard_map/ppermute | solution.py:414
  50.5 1.9 %copy-start.2 = (f32[4,16,32,128]{3,2,1,0:T(8,128)S(1)}, f32[4,16,32,128]{3,2,1,0:T(8,128)}, u32[]{:S(2)}) copy-start(f32[4,16,32,128]{3,2,1,0:T(8,128)} %param.11) | copy-start | bytes 3145732

commit v8 on v7

--- a/solution.py
+++ b/solution.py
@@ -29,9 +29,7 @@
 side_rows = 72
 group = points // rank
 groups = leaves // group
-batch = 4
-step = 2 * batch
-unroll = 2
+ring = 2
 vmem = pl.BlockSpec(memory_space=pltpu.VMEM)
 
 
@@ -91,18 +89,15 @@
 zero_row = 9 * leaves
 
 
-def fields(pieces, at):
-    found, begin = None, 0
+def listed(pieces):
+    items = []
     for run, low, high in pieces:
-        q = at - begin + low
-        begin += high - low
-        moved = q + (q * 274 >> 12) if run.skip else q
-        source, target = moved + run.source, run.step * moved + run.target
-        here = [source, target, run.offset * leaves + target, (8 - run.offset) * leaves + source if run.both else zero_row]
-        found = here if found is None else [jnp.where(inside_run, old, new) for old, new in zip(found, here)]
-        inside_run = at < begin
-    idle = [0, 0, zero_row, zero_row]
-    return [jnp.where(inside_run, old, new) for old, new in zip(found, idle)]
+        for q in range(low, high):
+            moved = q + run.skip * (q // (leaf_cols - 1))
+            source, target = moved + run.source, run.step * moved + run.target
+            back = (8 - run.offset) * leaves + source if run.both else None
+            items.append((source, target, run.offset * leaves + target, back))
+    return items
 
 
 def split(value):
@@ -288,18 +283,16 @@
         payload[base + 66 : base + side_rows, :] = jnp.zeros((side_rows - 66, points), f32)
 
 
-def near_kernel(pieces, pairs, both_ways, weights, left, source_heights, source_halves, right, heights, halves, seed, acc, gap_a, gap_b, splat_a, splat_b, kern_a, kern_b):
+def near_kernel(items, batch, weights, left, source_heights, source_halves, right, heights, halves, seed, acc, gaps, splats, kerns):
     acc[...] = seed[...]
-    kern_b[...] = jnp.zeros_like(kern_b)
-    buffers_a, buffers_b = (gap_a, splat_a, kern_a), (gap_b, splat_b, kern_b)
 
     def subtract(item, n, gap, splat):
         source, target = item[:2]
-        gap[n] = dot(left[pl.ds(pl.multiple_of(source * points, points), points), :], right[sixteen(target), :])
-        splat[n] = jnp.broadcast_to(source_heights[pl.ds(source, 1), :], (points, points)).T
+        gap[n] = dot(left[source * points : (source + 1) * points, :], right[sixteen(target), :])
+        splat[n] = jnp.broadcast_to(source_heights[source : source + 1, :], (points, points)).T
 
     def evaluate(item, n, gap, splat, kern):
-        height = heights[pl.ds(item[1], 1), :]
+        height = heights[item[1] : item[1] + 1, :]
         for g in range(points // 32):
             at_rows = slice(32 * g, 32 * g + 32)
             dx, dy, dz = gap[n, at_rows, :points], gap[n, at_rows, points:], splat[n, at_rows] - height
@@ -314,72 +307,49 @@
             kern[n, 0, at_rows] = high
             kern[n, 1, at_rows] = low
 
+    def receive(leaf, weight, got):
+        at = slice(leaf * rhs, (leaf + 1) * rhs)
+        acc[at, :] += (got[:rhs] + got[rhs:]) * weights[weight : weight + 1, :]
+
     def apply(item, n, kern):
-        source, target, target_weight, source_weight = item
+        source, target, weight, back = item
         pair = jnp.concatenate([kern[n, 0], kern[n, 1]], axis=1)
         got = dot(source_halves[sixteen(source), :], pair)
-        got = got[:, :points] + got[:, points:]
-        acc[pl.ds(target * 8, 8), :] += (got[:8] + got[8:]) * weights[pl.ds(target_weight, 1), :]
-        if both_ways:
+        receive(target, weight, got[:, :points] + got[:, points:])
+        if back is not None:
             mine = halves[sixteen(target), :]
-            got = dot_t(jnp.concatenate([mine, mine], axis=1), pair)
-            acc[pl.ds(source * 8, 8), :] += (got[:8] + got[8:]) * weights[pl.ds(source_weight, 1), :]
-
-    def items_at(at):
-        return [fields(pieces, at + n) for n in range(batch)]
-
-    def stage(at, earlier, now, here, there):
-        later = items_at(at + batch)
-        for n in range(batch):
-            apply(earlier[n], n, there[2])
-        for n in range(batch):
-            subtract(later[n], n, *there[:2])
-        for n in range(batch):
-            evaluate(now[n], n, *here)
-        return now, later
-
-    def pair(at, carry):
-        carry = stage(at, *carry, buffers_a, buffers_b)
-        return stage(at + batch, *carry, buffers_b, buffers_a)
-
-    def body(trip, carry):
-        for k in range(unroll):
-            carry = pair(trip * step * unroll + k * step, carry)
-        return carry
-
-    first = items_at(jnp.int32(0))
-    for n in range(batch):
-        subtract(first[n], n, *buffers_a[:2])
-    nothing = [[jnp.int32(0), jnp.int32(0), jnp.int32(zero_row), jnp.int32(zero_row)]] * batch
-    carry = lax.fori_loop(0, pairs // unroll, body, (nothing, first))
-    for k in range(pairs // unroll * unroll, pairs):
-        carry = pair(jnp.int32(k * step), carry)
-    last = carry[0]
-    for n in range(batch):
-        apply(last[n], n, buffers_b[2])
-
-
-def near_piece(pieces, both_ways, weights, source_tables, target_tables, seed):
-    count = sum(high - low for _, low, high in pieces)
-    pairs = -(-count // step)
+            receive(source, back, dot_t(jnp.concatenate([mine, mine], axis=1), pair))
+
+    stages = [items[at : at + batch] for at in range(0, len(items), batch)]
+    for k in range(-1, len(stages) + 1):
+        if k >= 1:
+            for n, item in enumerate(stages[k - 1]):
+                apply(item, n, kerns.at[(k - 1) % ring])
+        if k + 1 < len(stages):
+            for n, item in enumerate(stages[k + 1]):
+                subtract(item, n, gaps.at[(k + 1) % ring], splats.at[(k + 1) % ring])
+        if 0 <= k < len(stages):
+            for n, item in enumerate(stages[k]):
+                evaluate(item, n, gaps.at[k % ring], splats.at[k % ring], kerns.at[k % ring])
+
+
+def near_piece(pieces, weights, source_tables, target_tables, seed):
+    items = listed(pieces)
+    batch = 4 if any(item[3] is not None for item in items) else 8
     left, _, source_heights, source_halves = source_tables
     _, right, heights, halves = target_tables
     return pl.pallas_call(
-        functools.partial(near_kernel, pieces, pairs, both_ways),
+        functools.partial(near_kernel, items, batch),
         out_shape=jax.ShapeDtypeStruct(seed.shape, f32),
         in_specs=[vmem] * 8,
         out_specs=vmem,
         scratch_shapes=[
-            shape
-            for shape in (
-                pltpu.VMEM((batch, points, 2 * points), f32),
-                pltpu.VMEM((batch, points, points), f32),
-                pltpu.VMEM((batch, 2, points, points), bf16),
-            )
-            for _ in range(2)
+            pltpu.VMEM((ring, batch, points, 2 * points), f32),
+            pltpu.VMEM((ring, batch, points, points), f32),
+            pltpu.VMEM((ring, batch, 2, points, points), bf16),
         ],
-        compiler_params=params(16),
-        cost_estimate=cost(count * 110),
+        compiler_params=params(24),
+        cost_estimate=cost(len(items) * 110),
         name="near",
     )(weights, left, source_heights, source_halves, right, heights, halves, seed)
 
@@ -489,8 +459,8 @@
     windows = row_bits + col_bits - 1
     edge_windows = (row_bits, row_bits + 2)
     inner_windows = [n for n in range(1, windows + 1) if n not in edge_windows]
-    cuts = [counts[0] * k // len(inner_windows) // step * step for k in range(len(inner_windows))] + [counts[0]]
-    half = -(-counts[1] // 2 // step) * step
+    cuts = [counts[0] * k // len(inner_windows) // 4 * 4 for k in range(len(inner_windows))] + [counts[0]]
+    half = -(-counts[1] // 2 // 8) * 8
     acc = jnp.zeros((leaves * rhs, points), f32)
     received = [theirs]
     for n, (axis, bit) in enumerate(zip(axes, bits)):
@@ -503,10 +473,10 @@
                 edge_tables = tables_call(edges_kernel, "edges", edge_leaves, [], coords, edges)
             if n in edge_windows:
                 some = cut_runs(edge, 0, half) if n == row_bits else cut_runs(edge, half, counts[1])
-                acc = near_piece(some, False, weights, edge_tables, own, acc)
+                acc = near_piece(some, weights, edge_tables, own, acc)
             else:
                 k = inner_windows.index(n)
-                acc = near_piece(cut_runs(inner, cuts[k], cuts[k + 1]), True, weights, own, own, acc)
+                acc = near_piece(cut_runs(inner, cuts[k], cuts[k + 1]), weights, own, own, acc)
             theirs, acc = lax.optimization_barrier((theirs, acc))
             received.append(theirs)
         if n == row_bits - 1:
@@ -521,7 +491,7 @@
             skip = points + rows if bit == 0 else points
             payload = small_call(functools.partial(level_kernel, skip), "level", array(points + rows, points), payload, theirs, blocks)
     side_tables = tables_call(sides_kernel, "sides", side_leaves, [pltpu.VMEM(((3 + rhs) * side_leaves, points), f32)], coords, *received[row_bits:])
-    acc = near_piece(cut_runs(side, 0, counts[2]), False, weights, side_tables, own, acc)
+    acc = near_piece(cut_runs(side, 0, counts[2]), weights, side_tables, own, acc)
     out = pl.pallas_call(
         finish_kernel,
         out_shape=array(rhs * leaves, points),

time: 53.8 us -> 50 us (0.929)
  Pallas kernels: 38 us -> 32.7 us
  starting transfers between devices: 15 us -> 15.9 us
    pallas_call x7, Pallas kernels: 30.4 us -> 25.1 us  [near_piece(): pl.pallas_call(functools.partial(near_kernel, items, batch), out_shape=ja...]
    ppermute x7, starting transfers between devices: 15 us -> 15.9 us  [partner_of(): return lax.ppermute(block, axis, route)]
  transfers between devices with their start and end apart: 7 -> 7, of which waited for: 1 -> 3; matrix products, arithmetic and copies ran while one was open for 0% -> 0% of each run, Pallas kernels for 57% -> 51%
where the time goes in v8:
time: 50 us; the launch traced here: 49.9 us
  Pallas kernels  32.7 us (65%)
  starting transfers between devices  15.9 us (32%)
  waiting for transfers between devices  1.01 us (2%)
    pallas_call x7, Pallas kernels, near_piece(): pl.pallas_call(functools.partial(near_kernel, items, batch), out_shape=ja...  25.1 us
    ppermute x7, starting transfers between devices, partner_of(): return lax.ppermute(block, axis, route)  15.9 us
    pallas_call x2, Pallas kernels, tables_call(): pl.pallas_call(body, out_shape=table_shapes(count), in_specs=[vmem] * len...  2 us
    pallas_call x1, Pallas kernels, far_call(): pl.pallas_call(body, out_shape=out_shape, in_specs=[pl.BlockSpec(memory_s...  1.9 us
    pallas_call x6, Pallas kernels, small_call(): pl.pallas_call(body, out_shape=out_shape, in_specs=[vmem] * len(operands)...  1.48 us
    pallas_call x1, Pallas kernels, shards(): pl.pallas_call(finish_kernel, out_shape=array(rhs * leaves, points), in_s...  1.26 us
    ppermute x7, waiting for transfers between devices, partner_of(): return lax.ppermute(block, axis, route)  1.01 us
  transfers between devices with their start and end apart: 7, of which 3 were waited for; matrix products, arithmetic and copies ran while one was open for 0% of the time, Pallas kernels for 51%

profile of v8, /device:TPU:0, one launch (start us, length us, event | category | flops | bytes accessed | tf_op | source)
XLA Modules:
  0.0 49.9 jit_solution(1261193566660201217)
XLA Ops:
  0.0 0.0 copy-start.1
  0.0 0.0 copy-start.3
  0.0 0.0 copy-start.4
  0.0 0.0 copy-start.5
  0.0 1.9 %compress.1 = (bf16[1024,128]{1,0:T(8,128)(2,1)S(1)}, f32[480,128]{1,0:T(8,128)S(1)}) custom-call(f32[192,128]{1,0:T(8,128)} %bitcast.9, f32[512,128]{1,0:T(8,128)} %bitcast.7, f32[2048,128]{1,0:T(8,128)} %bitcast.17), custom_call_target="tpu_custom_call" | custom-call | flops 800000000 | bytes 262144 | tf_op jit(solution)/shard_map/compress/pallas_call | solution.py:405
  1.9 0.1 collective-permute-start
  2.0 0.0 copy-done.1
  2.0 0.0 copy-done.3
  2.0 0.0 copy-done.4
  2.0 0.0 copy-done.5
  2.0 1.0 %prep.1 = (bf16[8192,16]{1,0:T(8,128)(2,1)S(1)}, bf16[1024,256]{1,0:T(8,128)(2,1)S(1)}, f32[64,128]{1,0:T(8,128)S(1)}, bf16[4,128,128]{2,1,0:T(8,128)(2,1)S(1)},...) custom-call(f32[192,128]{1,0:T(8,128)S(1)} %bitcast.10, s32[9,4,16]{2,1,0:T(4,128)S(1)} %copy-done.5, ...), custom_call_target="tpu_custom_call" | custom-call | flops 800000000 | bytes 262144 | tf_op jit(solution)/shard_map/prep/pallas_call | solution.py:446
  3.0 0.5 collective-permute-done.theirs.first
  3.5 0.2 level.5.mine
  3.7 1.8 %collective-permute-start.1 = (f32[304,128]{1,0:T(8,128)S(1)}, f32[304,128]{1,0:T(8,128)S(1)}, u32[]{:S(2)}, u32[]{:S(2)}) collective-permute-start(f32[304,128]{1,0:T(8,128)S(1)} %level.5.mine), channel_id=1, source_target_pairs={{0,32},{16,48},{32,0},{48,16},{64,96},{80,112},{96,64},{112,80},{1... | collective-permute-start | bytes 466952 | tf_op jit(solution)/shard_map/ppermute | solution.py:384
  5.5 4.1 %near.7.seed = f32[512,128]{1,0:T(8,128)S(1)} custom-call(f32[584,128]{1,0:T(8,128)S(1)} %get-tuple-element.54.weights, bf16[8192,16]{1,0:T(8,128)(2,1)S(1)} %get-tuple-element.55.left, f32[64,128]{1,0:T(8,128)S(1)} %get-tuple-element.56.source_heights.heights, bf16[1024,128]{1,0:T(8,128)(2,1)S(1)} %get-tuple-element.57.source_halves.halves, ...), custom_call_target="tpu_custom_call" | custom-call | flops 2816000000 | bytes 262144 | tf_op jit(solution)/shard_map/near/pallas_call | solution.py:341
  9.6 0.3 collective-permute-done.1.theirs.second
  9.9 0.2 level.6.mine
  10.1 0.0 copy-start
  10.1 3.4 %collective-permute-start.2 = (f32[304,128]{1,0:T(8,128)S(1)}, f32[304,128]{1,0:T(8,128)S(1)}, u32[]{:S(2)}, u32[]{:S(2)}) collective-permute-start(f32[304,128]{1,0:T(8,128)S(1)} %level.6.mine), channel_id=1, source_target_pairs={{0,64},{16,80},{32,96},{48,112},{64,0},{80,16},{96,32},{112,48},{1... | collective-permute-start | bytes 466952 | tf_op jit(solution)/shard_map/ppermute | solution.py:384
  13.5 4.4 %near.8.seed = f32[512,128]{1,0:T(8,128)S(1)} custom-call(f32[584,128]{1,0:T(8,128)S(1)} %get-tuple-element.54.weights, bf16[8192,16]{1,0:T(8,128)(2,1)S(1)} %get-tuple-element.55.left, f32[64,128]{1,0:T(8,128)S(1)} %get-tuple-element.56.source_heights.heights, bf16[1024,128]{1,0:T(8,128)(2,1)S(1)} %get-tuple-element.57.source_halves.halves, ...), custom_call_target="tpu_custom_call" | custom-call | flops 2816000000 | bytes 262144 | tf_op jit(solution)/shard_map/near/pallas_call | solution.py:341
  17.9 0.0 collective-permute-done.2.theirs
  17.9 0.0 copy-done
  17.9 0.3 turn.1
  18.2 2.2 %collective-permute-start.3 = (f32[272,128]{1,0:T(8,128)S(1)}, f32[272,128]{1,0:T(8,128)S(1)}, u32[]{:S(2)}, u32[]{:S(2)}) collective-permute-start(f32[272,128]{1,0:T(8,128)S(1)} %get-tuple-element.67.mine), channel_id=1, source_target_pairs={{0,1},{1,0},{2,3},{3,2},{4,5},{5,4},{6,7},{7,6},{8,9},{9,8},{10,11... | collective-permute-start | bytes 417800 | tf_op jit(solution)/shard_map/ppermute | solution.py:384
  20.4 1.1 %edges.1 = (bf16[4096,16]{1,0:T(8,128)(2,1)S(1)}, bf16[512,256]{1,0:T(8,128)(2,1)}, f32[32,128]{1,0:T(8,128)S(1)}, bf16[512,128]{1,0:T(8,128)(2,1)S(1)}) custom-call(f32[192,128]{1,0:T(8,128)S(1)} %bitcast.12, f32[352,128]{1,0:T(8,128)S(1)} %get-tuple-element.70.edges), custom_call_target="tpu_custom_call" | custom-call | flops 400000000 | bytes 262144 | tf_op jit(solution)/shard_map/edges/pallas_call | solution.py:418
  21.5 3.1 %near.9.seed = f32[512,128]{1,0:T(8,128)S(1)} custom-call(f32[584,128]{1,0:T(8,128)S(1)} %get-tuple-element.54.weights, bf16[4096,16]{1,0:T(8,128)(2,1)S(1)} %get-tuple-element.71.left, f32[32,128]{1,0:T(8,128)S(1)} %get-tuple-element.72.source_heights, bf16[512,128]{1,0:T(8,128)(2,1)S(1)} %get-tuple-element.73.source_halves, ...), custom_call_target="tpu_custom_call" | custom-call | flops 2112000000 | bytes 262144 | tf_op jit(solution)/shard_map/near/pallas_call | solution.py:341
  24.6 0.0 collective-permute-done.3.theirs.first
  24.6 0.2 level.7.mine
  24.9 3.6 %collective-permute-start.4 = (f32[200,128]{1,0:T(8,128)S(1)}, f32[200,128]{1,0:T(8,128)S(1)}, u32[]{:S(2)}, u32[]{:S(2)}) collective-permute-start(f32[200,128]{1,0:T(8,128)S(1)} %level.7.mine), channel_id=1, source_target_pairs={{0,2},{1,3},{2,0},{3,1},{4,6},{5,7},{6,4},{7,5},{8,10},{9,11},{10,... | collective-permute-start | bytes 307208 | tf_op jit(solution)/shard_map/ppermute | solution.py:384
  28.5 4.5 %near.10.seed = f32[512,128]{1,0:T(8,128)S(1)} custom-call(f32[584,128]{1,0:T(8,128)S(1)} %get-tuple-element.54.weights, bf16[8192,16]{1,0:T(8,128)(2,1)S(1)} %get-tuple-element.55.left, f32[64,128]{1,0:T(8,128)S(1)} %get-tuple-element.56.source_heights.heights, bf16[1024,128]{1,0:T(8,128)(2,1)S(1)} %get-tuple-element.57.source_halves.halves, ...), custom_call_target="tpu_custom_call" | custom-call | flops 2992000000 | bytes 262144 | tf_op jit(solution)/shard_map/near/pallas_call | solution.py:341
  33.0 0.0 collective-permute-done.4.theirs.second
  33.0 0.3 level.8.mine
  33.3 1.6 %collective-permute-start.5 = (f32[200,128]{1,0:T(8,128)S(1)}, f32[200,128]{1,0:T(8,128)S(1)}, u32[]{:S(2)}, u32[]{:S(2)}) collective-permute-start(f32[200,128]{1,0:T(8,128)S(1)} %level.8.mine), channel_id=1, source_target_pairs={{0,4},{1,5},{2,6},{3,7},{4,0},{5,1},{6,2},{7,3},{8,12},{9,13},{10,... | collective-permute-start | bytes 307208 | tf_op jit(solution)/shard_map/ppermute | solution.py:384
  34.8 2.9 %near.11.seed = f32[512,128]{1,0:T(8,128)S(1)} custom-call(f32[584,128]{1,0:T(8,128)S(1)} %get-tuple-element.54.weights, bf16[4096,16]{1,0:T(8,128)(2,1)S(1)} %get-tuple-element.71.left, f32[32,128]{1,0:T(8,128)S(1)} %get-tuple-element.72.source_heights, bf16[512,128]{1,0:T(8,128)(2,1)S(1)} %get-tuple-element.73.source_halves, ...), custom_call_target="tpu_custom_call" | custom-call | flops 1936000000 | bytes 262144 | tf_op jit(solution)/shard_map/near/pallas_call | solution.py:341
  37.7 0.3 collective-permute-done.5.theirs.third
  38.0 0.2 level.9.mine
  38.3 3.3 %collective-permute-start.6 = (f32[200,128]{1,0:T(8,128)S(1)}, f32[200,128]{1,0:T(8,128)S(1)}, u32[]{:S(2)}, u32[]{:S(2)}) collective-permute-start(f32[200,128]{1,0:T(8,128)S(1)} %level.9.mine), channel_id=1, source_target_pairs={{0,8},{1,9},{2,10},{3,11},{4,12},{5,13},{6,14},{7,15},{8,0},{9,1},... | collective-permute-start | bytes 307208 | tf_op jit(solution)/shard_map/ppermute | solution.py:384
  41.6 4.4 %near.12.seed = f32[512,128]{1,0:T(8,128)S(1)} custom-call(f32[584,128]{1,0:T(8,128)S(1)} %get-tuple-element.54.weights, bf16[8192,16]{1,0:T(8,128)(2,1)S(1)} %get-tuple-element.55.left, f32[64,128]{1,0:T(8,128)S(1)} %get-tuple-element.56.source_heights.heights, bf16[1024,128]{1,0:T(8,128)(2,1)S(1)} %get-tuple-element.57.source_halves.halves, ...), custom_call_target="tpu_custom_call" | custom-call | flops 2904000000 | bytes 262144 | tf_op jit(solution)/shard_map/near/pallas_call | solution.py:341
  46.0 0.0 collective-permute-done.6.fourth.theirs
  46.0 0.9 %sides.1 = (bf16[2048,16]{1,0:T(8,128)(2,1)S(1)}, bf16[256,256]{1,0:T(8,128)(2,1)}, f32[16,128]{1,0:T(8,128)S(1)}, bf16[256,128]{1,0:T(8,128)(2,1)S(1)}) custom-call(f32[192,128]{1,0:T(8,128)S(1)} %bitcast.13, f32[272,128]{1,0:T(8,128)S(1)} %collective-permute-done.3.theirs.first, f32[200,128]{1,0:T(8,128)S(1)} %collective-permute-done.4.theirs.second, ...), custom_call_target="tpu_custom_call" | custom-call | flops 400000000 | bytes 262144 | tf_op jit(solution)/shard_map/sides/pallas_call | solution.py:418
  46.9 0.0 copy-start.2
  46.9 1.7 %near.13.acc = f32[512,128]{1,0:T(8,128)S(1)} custom-call(f32[584,128]{1,0:T(8,128)S(1)} %get-tuple-element.54.weights, bf16[2048,16]{1,0:T(8,128)(2,1)S(1)} %get-tuple-element.89.left, f32[16,128]{1,0:T(8,128)S(1)} %get-tuple-element.90.source_heights, bf16[256,128]{1,0:T(8,128)(2,1)S(1)} %get-tuple-element.91.source_halves, ...), custom_call_target="tpu_custom_call" | custom-call | flops 1056000000 | bytes 262144 | tf_op jit(solution)/shard_map/near/pallas_call | solution.py:341
  48.6 0.0 copy-done.2
  48.6 1.3 %finish.1 = f32[512,128]{1,0:T(8,128)} custom-call(f32[200,128]{1,0:T(8,128)S(1)} %level.9.mine, f32[200,128]{1,0:T(8,128)S(1)} %collective-permute-done.6.fourth.theirs, bf16[4,128,128]{2,1,0:T(8,128)(2,1)S(1)} %get-tuple-element.76.blocks, f32[2048,128]{1,0:T(8,128)S(1)} %bitcast.14, f32[512,128]{1,0:T(8,128)S(1)} %near.13.acc), custom_call_target="tpu_custom_call" | custom-call | flops 800000000 | bytes 262144 | tf_op jit(solution)/shard_map/finish/pallas_call | solution.py:495
  (1 shorter events, 0.0 us)
Async XLA Ops:
  0.0 2.0 %copy-start.1 = (f32[3,4,16,128]{3,2,1,0:T(8,128)S(1)}, f32[3,4,16,128]{3,2,1,0:T(8,128)}, u32[]{:S(2)}) copy-start(f32[3,4,16,128]{3,2,1,0:T(8,128)} %param.7) | copy-start | bytes 294916
  0.0 2.0 %copy-start.3 = (f32[2,1,1,32,32]{4,3,2,1,0:T(8,128)S(1)}, f32[2,1,1,32,32]{4,3,2,1,0:T(8,128)}, u32[]{:S(2)}) copy-start(f32[2,1,1,32,32]{4,3,2,1,0:T(8,128)} %param.12) | copy-start | bytes 24580
  0.0 2.0 %copy-start.4 = (f32[2,1,1,32,32]{4,3,2,1,0:T(8,128)S(1)}, f32[2,1,1,32,32]{4,3,2,1,0:T(8,128)}, u32[]{:S(2)}) copy-start(f32[2,1,1,32,32]{4,3,2,1,0:T(8,128)} %param.13) | copy-start | bytes 24580
  0.0 2.0 %copy-start.5 = (s32[9,4,16]{2,1,0:T(4,128)S(1)}, s32[9,4,16]{2,1,0:T(4,128)}, u32[]{:S(2)}) copy-start(s32[9,4,16]{2,1,0:T(4,128)} %mask.1) | copy-start | bytes 6916
  1.9 1.6 %collective-permute-start = (f32[480,128]{1,0:T(8,128)S(1)}, f32[480,128]{1,0:T(8,128)S(1)}, u32[]{:S(2)}, u32[]{:S(2)}) collective-permute-start(f32[480,128]{1,0:T(8,128)S(1)} %get-tuple-element.50.mine), channel_id=1, source_target_pairs={{0,16},{16,0},{32,48},{48,32},{64,80},{80,64},{96,112},{112,96},{1... | collective-permute-start | bytes 737288 | tf_op jit(solution)/shard_map/ppermute | solution.py:384
  3.7 6.1 %collective-permute-start.1 = (f32[304,128]{1,0:T(8,128)S(1)}, f32[304,128]{1,0:T(8,128)S(1)}, u32[]{:S(2)}, u32[]{:S(2)}) collective-permute-start(f32[304,128]{1,0:T(8,128)S(1)} %level.5.mine), channel_id=1, source_target_pairs={{0,32},{16,48},{32,0},{48,16},{64,96},{80,112},{96,64},{112,80},{1... | collective-permute-start | bytes 466952 | tf_op jit(solution)/shard_map/ppermute | solution.py:384
  10.1 7.7 %copy-start = (f32[8,4,16,128]{3,2,1,0:T(8,128)S(1)}, f32[8,4,16,128]{3,2,1,0:T(8,128)}, u32[]{:S(2)}) copy-start(f32[8,4,16,128]{3,2,1,0:T(8,128)} %param.8) | copy-start | bytes 786436
  10.1 7.7 %collective-permute-start.2 = (f32[304,128]{1,0:T(8,128)S(1)}, f32[304,128]{1,0:T(8,128)S(1)}, u32[]{:S(2)}, u32[]{:S(2)}) collective-permute-start(f32[304,128]{1,0:T(8,128)S(1)} %level.6.mine), channel_id=1, source_target_pairs={{0,64},{16,80},{32,96},{48,112},{64,0},{80,16},{96,32},{112,48},{1... | collective-permute-start | bytes 466952 | tf_op jit(solution)/shard_map/ppermute | solution.py:384
  18.2 6.4 %collective-permute-start.3 = (f32[272,128]{1,0:T(8,128)S(1)}, f32[272,128]{1,0:T(8,128)S(1)}, u32[]{:S(2)}, u32[]{:S(2)}) collective-permute-start(f32[272,128]{1,0:T(8,128)S(1)} %get-tuple-element.67.mine), channel_id=1, source_target_pairs={{0,1},{1,0},{2,3},{3,2},{4,5},{5,4},{6,7},{7,6},{8,9},{9,8},{10,11... | collective-permute-start | bytes 417800 | tf_op jit(solution)/shard_map/ppermute | solution.py:384
  24.9 8.1 %collective-permute-start.4 = (f32[200,128]{1,0:T(8,128)S(1)}, f32[200,128]{1,0:T(8,128)S(1)}, u32[]{:S(2)}, u32[]{:S(2)}) collective-permute-start(f32[200,128]{1,0:T(8,128)S(1)} %level.7.mine), channel_id=1, source_target_pairs={{0,2},{1,3},{2,0},{3,1},{4,6},{5,7},{6,4},{7,5},{8,10},{9,11},{10,... | collective-permute-start | bytes 307208 | tf_op jit(solution)/shard_map/ppermute | solution.py:384
  33.3 4.7 %collective-permute-start.5 = (f32[200,128]{1,0:T(8,128)S(1)}, f32[200,128]{1,0:T(8,128)S(1)}, u32[]{:S(2)}, u32[]{:S(2)}) collective-permute-start(f32[200,128]{1,0:T(8,128)S(1)} %level.8.mine), channel_id=1, source_target_pairs={{0,4},{1,5},{2,6},{3,7},{4,0},{5,1},{6,2},{7,3},{8,12},{9,13},{10,... | collective-permute-start | bytes 307208 | tf_op jit(solution)/shard_map/ppermute | solution.py:384
  38.3 7.8 %collective-permute-start.6 = (f32[200,128]{1,0:T(8,128)S(1)}, f32[200,128]{1,0:T(8,128)S(1)}, u32[]{:S(2)}, u32[]{:S(2)}) collective-permute-start(f32[200,128]{1,0:T(8,128)S(1)} %level.9.mine), channel_id=1, source_target_pairs={{0,8},{1,9},{2,10},{3,11},{4,12},{5,13},{6,14},{7,15},{8,0},{9,1},... | collective-permute-start | bytes 307208 | tf_op jit(solution)/shard_map/ppermute | solution.py:384
  46.9 1.7 %copy-start.2 = (f32[4,16,32,128]{3,2,1,0:T(8,128)S(1)}, f32[4,16,32,128]{3,2,1,0:T(8,128)}, u32[]{:S(2)}) copy-start(f32[4,16,32,128]{3,2,1,0:T(8,128)} %param.11) | copy-start | bytes 3145732

commit v9 on v8

--- a/solution.py
+++ b/solution.py
@@ -136,7 +136,7 @@
     ones_x = jnp.where(k < 3, 1.0, 0.0)
     ones_y = jnp.where((k >= 3) & (k < 6), 1.0, 0.0)
     ones_t = jnp.where((k >= 6) & (k < 9), 1.0, 0.0)
-    for role in range(3):
+    for role in range(1 if right is None else 3):
         wide = wides.at[role]
         for leaf in range(count):
             wide[pl.ds(leaf * 16, 16), :] = (ones_t, ones_x, ones_y)[role]
@@ -175,7 +175,11 @@
 
 
 def compress_kernel(coords_far, sources_far, compress_far, halves, payload, coords, sources, compress, arrived):
-    copies = start_copies((sources_far, coords_far, compress_far), (sources, coords, compress), arrived)
+    chunk = groups // 4 * points
+    chunks = [slice(n * chunk, (n + 1) * chunk) for n in range(4)]
+    copies = start_copies(
+        [sources_far, coords_far] + [compress_far.at[rows] for rows in chunks], [sources, coords] + [compress.at[rows] for rows in chunks], arrived
+    )
     copies[0].wait()
     for leaf in range(leaves):
         high, low = split(sources[pl.ds(leaf, rhs, stride=leaves), :])
@@ -188,8 +192,9 @@
             ref, at = (coords, c) if c < 3 else (sources, c - 3)
             to = points + k * edge_rows + c * leaf_cols
             payload[to : to + leaf_cols, :] = ref[pl.ds(pl.multiple_of(at * leaves + row * leaf_cols, 8), leaf_cols), :]
-    copies[2].wait()
     for g in range(groups):
+        if g % (groups // 4) == 0:
+            copies[2 + g // (groups // 4)].wait()
         high, low = split(compress[g * points : (g + 1) * points, :])
         got = dot_t(halves[g * 16 * group : (g + 1) * 16 * group, :], jnp.concatenate([high, low], axis=0))
         got = got[:, :points] + got[:, points:]
@@ -214,19 +219,19 @@
     weights[zero_row : zero_row + 8, :] = jnp.zeros((8, points), f32)
 
 
-def halo_tables(count, coords, values, left, right, heights, halves, wides):
+def halo_tables(count, coords, values, left, heights, halves, wides):
     start = [coords[c * leaves : c * leaves + 1, 0:1] for c in range(3)]
-    fill_tables(count, start, values, left, right, heights, wides)
+    fill_tables(count, start, values, left, None, heights, wides)
     for leaf in range(count):
         high, low = split(values[pl.ds(3 * count + leaf, rhs, stride=count), :])
         halves[sixteen(leaf), :] = jnp.concatenate([high, low], axis=0)
 
 
-def edges_kernel(coords, edges, left, right, heights, halves, wides):
-    halo_tables(edge_leaves, coords, edges, left, right, heights, halves, wides)
-
-
-def sides_kernel(coords, first, second, third, fourth, left, right, heights, halves, wides, sides):
+def edges_kernel(coords, edges, left, heights, halves, wides):
+    halo_tables(edge_leaves, coords, edges, left, heights, halves, wides)
+
+
+def side_tables(coords, first, second, third, fourth, left, heights, halves, wides, sides):
     col = lax.axis_index("col")
     odd = col % 2 == 1
     inner = (col > 0) & (col < lax.axis_size("col") - 1)
@@ -240,7 +245,7 @@
     for c in range(3 + rhs):
         at = slice(6 * c, 6 * c + 6)
         sides[c * side_leaves : (c + 1) * side_leaves, :] = jnp.concatenate([to_left[at], gap, to_right[at], gap], axis=0)
-    halo_tables(side_leaves, coords, sides, left, right, heights, halves, wides)
+    halo_tables(side_leaves, coords, sides, left, heights, halves, wides)
 
 
 def level(mine, theirs, blocks):
@@ -333,28 +338,36 @@
                 evaluate(item, n, gaps.at[k % ring], splats.at[k % ring], kerns.at[k % ring])
 
 
+def near_scratch(batch):
+    return [
+        pltpu.VMEM((ring, batch, points, 2 * points), f32),
+        pltpu.VMEM((ring, batch, points, points), f32),
+        pltpu.VMEM((ring, batch, 2, points, points), bf16),
+    ]
+
+
 def near_piece(pieces, weights, source_tables, target_tables, seed):
     items = listed(pieces)
     batch = 4 if any(item[3] is not None for item in items) else 8
-    left, _, source_heights, source_halves = source_tables
-    _, right, heights, halves = target_tables
+    left, source_heights, source_halves = source_tables
+    right, heights, halves = target_tables
     return pl.pallas_call(
         functools.partial(near_kernel, items, batch),
         out_shape=jax.ShapeDtypeStruct(seed.shape, f32),
         in_specs=[vmem] * 8,
         out_specs=vmem,
-        scratch_shapes=[
-            pltpu.VMEM((ring, batch, points, 2 * points), f32),
-            pltpu.VMEM((ring, batch, points, points), f32),
-            pltpu.VMEM((ring, batch, 2, points, points), bf16),
-        ],
+        scratch_shapes=near_scratch(batch),
         compiler_params=params(24),
         cost_estimate=cost(len(items) * 110),
         name="near",
     )(weights, left, source_heights, source_halves, right, heights, halves, seed)
 
 
-def finish_kernel(mine, theirs, blocks, expand, acc, out):
+def finish_kernel(
+    items, weights, coords, first, second, third, theirs, mine, blocks, expand, right, heights, halves, seed, out,
+    left, source_heights, source_halves, wides, sides, acc, gaps, splats, kerns, *far,
+):
+    side_tables(coords, first, second, third, theirs, left, source_heights, source_halves, wides, sides)
     coeffs = level(mine[:points, :], theirs[:points, :], blocks)
     for g in range(groups):
         here = coeffs[g * rhs : (g + 1) * rhs]
@@ -363,11 +376,12 @@
         e_high, e_low = split(expand[g * points : (g + 1) * points, :])
         got = dot(jnp.concatenate([high, low], axis=0), jnp.concatenate([e_high, e_low], axis=1))
         got = got[:, :points] + got[:, points:]
-        got = got[: group * rhs] + got[group * rhs :]
-        for n in range(group):
-            leaf = g * group + n
-            near = acc[leaf * rhs : (leaf + 1) * rhs, :] * near_gain
-            out[pl.ds(leaf, rhs, stride=leaves), :] = near + got[n * rhs : (n + 1) * rhs]
+        far[0][g * group * rhs : (g + 1) * group * rhs, :] = got[: group * rhs] + got[group * rhs :]
+    near_kernel(items, 8, weights, left, source_heights, source_halves, right, heights, halves, seed, acc, gaps, splats, kerns)
+    order = sorted(range(leaves), key=lambda leaf: leaf % leaf_cols in (0, leaf_cols - 1))
+    for leaf in order:
+        at = slice(leaf * rhs, (leaf + 1) * rhs)
+        out[pl.ds(leaf, rhs, stride=leaves), :] = acc[at, :] * near_gain + far[0][at, :]
 
 
 def table_shapes(count):
@@ -407,24 +421,11 @@
         out_shape=out_shape,
         in_specs=[pl.BlockSpec(memory_space=pltpu.HBM)] * len(operands),
         out_specs=(vmem,) * len(out_shape),
-        scratch_shapes=scratch + [pltpu.SemaphoreType.DMA((len(operands),))],
+        scratch_shapes=scratch + [pltpu.SemaphoreType.DMA((8,))],
         compiler_params=params(24),
         cost_estimate=cost(2000),
         name=name,
     )(*[pltpu.with_memory_space_constraint(operand, pltpu.HBM) for operand in operands])
-
-
-def tables_call(body, name, count, scratch, *operands):
-    return pl.pallas_call(
-        body,
-        out_shape=table_shapes(count),
-        in_specs=[vmem] * len(operands),
-        out_specs=(vmem,) * 4,
-        scratch_shapes=[pltpu.VMEM((3, count * 16, points), f32)] + scratch,
-        compiler_params=params(16),
-        cost_estimate=cost(1000),
-        name=name,
-    )(*operands)
 
 
 def shards(coords, sources, neighbour_mask, compress, expand, row_transfer, col_transfer):
@@ -453,7 +454,7 @@
         cost_estimate=cost(2000),
         name="prep",
     )(coords_later, neighbour_mask, row_transfer[:, 0, 0], col_transfer[:, 0, 0])
-    own = left, right, heights, halves
+    own, targets = (left, heights, halves), (right, heights, halves)
     inner, edge, side = interior_runs(), edge_runs(), side_runs()
     counts = [sum(run.count for run in runs) for runs in (inner, edge, side)]
     windows = row_bits + col_bits - 1
@@ -470,13 +471,23 @@
             payload, acc = lax.optimization_barrier((payload, acc))
             if n == row_bits:
                 edges, acc = lax.optimization_barrier((edges, acc))
-                edge_tables = tables_call(edges_kernel, "edges", edge_leaves, [], coords, edges)
+                shapes = table_shapes(edge_leaves)
+                edge_tables = pl.pallas_call(
+                    edges_kernel,
+                    out_shape=(shapes[0], shapes[2], shapes[3]),
+                    in_specs=[vmem] * 2,
+                    out_specs=(vmem,) * 3,
+                    scratch_shapes=[pltpu.VMEM((1, edge_leaves * 16, points), f32)],
+                    compiler_params=params(16),
+                    cost_estimate=cost(1000),
+                    name="edges",
+                )(coords, edges)
             if n in edge_windows:
                 some = cut_runs(edge, 0, half) if n == row_bits else cut_runs(edge, half, counts[1])
-                acc = near_piece(some, weights, edge_tables, own, acc)
+                acc = near_piece(some, weights, edge_tables, targets, acc)
             else:
                 k = inner_windows.index(n)
-                acc = near_piece(cut_runs(inner, cuts[k], cuts[k + 1]), weights, own, own, acc)
+                acc = near_piece(cut_runs(inner, cuts[k], cuts[k + 1]), weights, own, targets, acc)
             theirs, acc = lax.optimization_barrier((theirs, acc))
             received.append(theirs)
         if n == row_bits - 1:
@@ -490,17 +501,25 @@
             rows = edge_rows if axis == "row" else side_rows
             skip = points + rows if bit == 0 else points
             payload = small_call(functools.partial(level_kernel, skip), "level", array(points + rows, points), payload, theirs, blocks)
-    side_tables = tables_call(sides_kernel, "sides", side_leaves, [pltpu.VMEM(((3 + rhs) * side_leaves, points), f32)], coords, *received[row_bits:])
-    acc = near_piece(cut_runs(side, 0, counts[2]), weights, side_tables, own, acc)
+    shapes = table_shapes(side_leaves)
+    operands = (weights, coords, *received[row_bits:], payload, blocks, expand.reshape(-1, points), *targets, acc)
     out = pl.pallas_call(
-        finish_kernel,
+        functools.partial(finish_kernel, listed(cut_runs(side, 0, counts[2]))),
         out_shape=array(rhs * leaves, points),
-        in_specs=[vmem] * 5,
+        in_specs=[vmem] * len(operands),
         out_specs=vmem,
-        compiler_params=params(16),
-        cost_estimate=cost(2000),
+        scratch_shapes=[pltpu.VMEM(shape.shape, shape.dtype) for shape in (shapes[0], shapes[2], shapes[3])]
+        + [
+            pltpu.VMEM((1, side_leaves * 16, points), f32),
+            pltpu.VMEM(((3 + rhs) * side_leaves, points), f32),
+            pltpu.VMEM((rhs * leaves, points), f32),
+        ]
+        + near_scratch(8)
+        + [pltpu.VMEM((rhs * leaves, points), f32)],
+        compiler_params=params(24),
+        cost_estimate=cost(5000),
         name="finish",
-    )(payload, theirs, blocks, expand.reshape(-1, points), acc)
+    )(*operands)
     return out.reshape(rhs, leaf_rows, leaf_cols, points)
 
 

time: 50 us -> 48.8 us (0.976)
  Pallas kernels: 32.7 us -> 31.5 us
    pallas_call x7 -> x6, Pallas kernels: 25.1 us -> 23.4 us  [near_piece(): pl.pallas_call(functools.partial(near_kernel, items, batch), out_shape=ja...]
    pallas_call x3 -> x2, Pallas kernels: 3.25 us -> 3.5 us  [the longest x1 3.02 us: shards(): pl.pallas_call(functools.partial(finish_kernel, listed(cut_runs(side, 0,...]
where the time goes in v9:
time: 48.8 us; the launch traced here: 48.7 us
  Pallas kernels  31.5 us (65%)
  starting transfers between devices  15.9 us (33%)
  waiting for transfers between devices  1.02 us (2%)
    pallas_call x6, Pallas kernels, near_piece(): pl.pallas_call(functools.partial(near_kernel, items, batch), out_shape=ja...  23.4 us
    ppermute x7, starting transfers between devices, partner_of(): return lax.ppermute(block, axis, route)  15.9 us
    pallas_call x1, Pallas kernels, shards(): pl.pallas_call(functools.partial(finish_kernel, listed(cut_runs(side, 0,...  3.02 us
    pallas_call x1, Pallas kernels, far_call(): pl.pallas_call(body, out_shape=out_shape, in_specs=[pl.BlockSpec(memory_s...  2.12 us
    pallas_call x6, Pallas kernels, small_call(): pl.pallas_call(body, out_shape=out_shape, in_specs=[vmem] * len(operands)...  1.47 us
    ppermute x7, waiting for transfers between devices, partner_of(): return lax.ppermute(block, axis, route)  1.02 us
    pallas_call x1, Pallas kernels, shards(): pl.pallas_call(prep_kernel, out_shape=table_shapes(leaves)[:3] + (block_s...  1 us
  transfers between devices with their start and end apart: 7, of which 3 were waited for; matrix products, arithmetic and copies ran while one was open for 0% of the time, Pallas kernels for 51%

profile of v9, /device:TPU:0, one launch (start us, length us, event | category | flops | bytes accessed | tf_op | source)
XLA Modules:
  0.0 48.7 jit_solution(12038745728029430538)
XLA Ops:
  0.0 0.0 copy-start.1
  0.0 0.0 copy-start.4
  0.0 0.0 copy-start.3
  0.0 0.0 copy-start.5
  0.0 2.1 %compress.1 = (bf16[1024,128]{1,0:T(8,128)(2,1)S(1)}, f32[480,128]{1,0:T(8,128)S(1)}) custom-call(f32[192,128]{1,0:T(8,128)} %bitcast.9, f32[512,128]{1,0:T(8,128)} %bitcast.7, f32[2048,128]{1,0:T(8,128)} %bitcast.17), custom_call_target="tpu_custom_call" | custom-call | flops 800000000 | bytes 262144 | tf_op jit(solution)/shard_map/compress/pallas_call | solution.py:419
  2.1 0.1 collective-permute-start
  2.2 0.0 copy-done.1
  2.2 0.0 copy-done.4
  2.3 0.0 copy-done.3
  2.3 0.0 copy-done.5
  2.3 1.0 %prep.1 = (bf16[8192,16]{1,0:T(8,128)(2,1)S(1)}, bf16[1024,256]{1,0:T(8,128)(2,1)S(1)}, f32[64,128]{1,0:T(8,128)S(1)}, bf16[4,128,128]{2,1,0:T(8,128)(2,1)S(1)},...) custom-call(f32[192,128]{1,0:T(8,128)S(1)} %bitcast.10, s32[9,4,16]{2,1,0:T(4,128)S(1)} %copy-done.5, ...), custom_call_target="tpu_custom_call" | custom-call | flops 800000000 | bytes 262144 | tf_op jit(solution)/shard_map/prep/pallas_call | solution.py:447
  3.3 0.5 collective-permute-done.theirs.first
  3.7 0.2 level.5.mine
  4.0 1.8 %collective-permute-start.1 = (f32[304,128]{1,0:T(8,128)S(1)}, f32[304,128]{1,0:T(8,128)S(1)}, u32[]{:S(2)}, u32[]{:S(2)}) collective-permute-start(f32[304,128]{1,0:T(8,128)S(1)} %level.5.mine), channel_id=1, source_target_pairs={{0,32},{16,48},{32,0},{48,16},{64,96},{80,112},{96,64},{112,80},{1... | collective-permute-start | bytes 466952 | tf_op jit(solution)/shard_map/ppermute | solution.py:398
  5.7 4.1 %near.6.seed = f32[512,128]{1,0:T(8,128)S(1)} custom-call(f32[584,128]{1,0:T(8,128)S(1)} %get-tuple-element.48.weights, bf16[8192,16]{1,0:T(8,128)(2,1)S(1)} %get-tuple-element.52.left, f32[64,128]{1,0:T(8,128)S(1)} %get-tuple-element.53.source_heights.heights, bf16[1024,128]{1,0:T(8,128)(2,1)S(1)} %get-tuple-element.54.source_halves.halves, ...), custom_call_target="tpu_custom_call" | custom-call | flops 2816000000 | bytes 262144 | tf_op jit(solution)/shard_map/near/pallas_call | solution.py:354
  9.8 0.3 collective-permute-done.1.theirs.second
  10.1 0.2 level.6.mine
  10.4 0.0 copy-start
  10.4 3.4 %collective-permute-start.2 = (f32[304,128]{1,0:T(8,128)S(1)}, f32[304,128]{1,0:T(8,128)S(1)}, u32[]{:S(2)}, u32[]{:S(2)}) collective-permute-start(f32[304,128]{1,0:T(8,128)S(1)} %level.6.mine), channel_id=1, source_target_pairs={{0,64},{16,80},{32,96},{48,112},{64,0},{80,16},{96,32},{112,48},{1... | collective-permute-start | bytes 466952 | tf_op jit(solution)/shard_map/ppermute | solution.py:398
  13.7 4.4 %near.7.seed = f32[512,128]{1,0:T(8,128)S(1)} custom-call(f32[584,128]{1,0:T(8,128)S(1)} %get-tuple-element.48.weights, bf16[8192,16]{1,0:T(8,128)(2,1)S(1)} %get-tuple-element.52.left, f32[64,128]{1,0:T(8,128)S(1)} %get-tuple-element.53.source_heights.heights, bf16[1024,128]{1,0:T(8,128)(2,1)S(1)} %get-tuple-element.54.source_halves.halves, ...), custom_call_target="tpu_custom_call" | custom-call | flops 2816000000 | bytes 262144 | tf_op jit(solution)/shard_map/near/pallas_call | solution.py:354
  18.1 0.0 collective-permute-done.2.theirs
  18.1 0.0 copy-done
  18.1 0.3 turn.1
  18.4 2.2 %collective-permute-start.3 = (f32[272,128]{1,0:T(8,128)S(1)}, f32[272,128]{1,0:T(8,128)S(1)}, u32[]{:S(2)}, u32[]{:S(2)}) collective-permute-start(f32[272,128]{1,0:T(8,128)S(1)} %get-tuple-element.72.mine), channel_id=1, source_target_pairs={{0,1},{1,0},{2,3},{3,2},{4,5},{5,4},{6,7},{7,6},{8,9},{9,8},{10,11... | collective-permute-start | bytes 417800 | tf_op jit(solution)/shard_map/ppermute | solution.py:398
  20.6 0.5 edges.1
  21.1 3.1 %near.8.seed = f32[512,128]{1,0:T(8,128)S(1)} custom-call(f32[584,128]{1,0:T(8,128)S(1)} %get-tuple-element.48.weights, bf16[4096,16]{1,0:T(8,128)(2,1)S(1)} %get-tuple-element.67.left, f32[32,128]{1,0:T(8,128)S(1)} %get-tuple-element.68.source_heights, bf16[512,128]{1,0:T(8,128)(2,1)S(1)} %get-tuple-element.69.source_halves, ...), custom_call_target="tpu_custom_call" | custom-call | flops 2112000000 | bytes 262144 | tf_op jit(solution)/shard_map/near/pallas_call | solution.py:354
  24.2 0.0 collective-permute-done.3.theirs.first
  24.2 0.2 level.7.mine
  24.4 3.7 %collective-permute-start.4 = (f32[200,128]{1,0:T(8,128)S(1)}, f32[200,128]{1,0:T(8,128)S(1)}, u32[]{:S(2)}, u32[]{:S(2)}) collective-permute-start(f32[200,128]{1,0:T(8,128)S(1)} %level.7.mine), channel_id=1, source_target_pairs={{0,2},{1,3},{2,0},{3,1},{4,6},{5,7},{6,4},{7,5},{8,10},{9,11},{10,... | collective-permute-start | bytes 307208 | tf_op jit(solution)/shard_map/ppermute | solution.py:398
  28.1 4.5 %near.9.seed = f32[512,128]{1,0:T(8,128)S(1)} custom-call(f32[584,128]{1,0:T(8,128)S(1)} %get-tuple-element.48.weights, bf16[8192,16]{1,0:T(8,128)(2,1)S(1)} %get-tuple-element.52.left, f32[64,128]{1,0:T(8,128)S(1)} %get-tuple-element.53.source_heights.heights, bf16[1024,128]{1,0:T(8,128)(2,1)S(1)} %get-tuple-element.54.source_halves.halves, ...), custom_call_target="tpu_custom_call" | custom-call | flops 2992000000 | bytes 262144 | tf_op jit(solution)/shard_map/near/pallas_call | solution.py:354
  32.6 0.0 collective-permute-done.4.theirs.second
  32.6 0.3 level.8.mine
  32.9 1.6 %collective-permute-start.5 = (f32[200,128]{1,0:T(8,128)S(1)}, f32[200,128]{1,0:T(8,128)S(1)}, u32[]{:S(2)}, u32[]{:S(2)}) collective-permute-start(f32[200,128]{1,0:T(8,128)S(1)} %level.8.mine), channel_id=1, source_target_pairs={{0,4},{1,5},{2,6},{3,7},{4,0},{5,1},{6,2},{7,3},{8,12},{9,13},{10,... | collective-permute-start | bytes 307208 | tf_op jit(solution)/shard_map/ppermute | solution.py:398
  34.5 2.9 %near.10.seed = f32[512,128]{1,0:T(8,128)S(1)} custom-call(f32[584,128]{1,0:T(8,128)S(1)} %get-tuple-element.48.weights, bf16[4096,16]{1,0:T(8,128)(2,1)S(1)} %get-tuple-element.67.left, f32[32,128]{1,0:T(8,128)S(1)} %get-tuple-element.68.source_heights, bf16[512,128]{1,0:T(8,128)(2,1)S(1)} %get-tuple-element.69.source_halves, ...), custom_call_target="tpu_custom_call" | custom-call | flops 1936000000 | bytes 262144 | tf_op jit(solution)/shard_map/near/pallas_call | solution.py:354
  37.4 0.3 collective-permute-done.5.theirs.third
  37.6 0.2 level.9.mine
  37.9 0.0 copy-start.2
  37.9 3.3 %collective-permute-start.6 = (f32[200,128]{1,0:T(8,128)S(1)}, f32[200,128]{1,0:T(8,128)S(1)}, u32[]{:S(2)}, u32[]{:S(2)}) collective-permute-start(f32[200,128]{1,0:T(8,128)S(1)} %level.9.mine), channel_id=1, source_target_pairs={{0,8},{1,9},{2,10},{3,11},{4,12},{5,13},{6,14},{7,15},{8,0},{9,1},... | collective-permute-start | bytes 307208 | tf_op jit(solution)/shard_map/ppermute | solution.py:398
  41.2 4.4 %near.11.seed = f32[512,128]{1,0:T(8,128)S(1)} custom-call(f32[584,128]{1,0:T(8,128)S(1)} %get-tuple-element.48.weights, bf16[8192,16]{1,0:T(8,128)(2,1)S(1)} %get-tuple-element.52.left, f32[64,128]{1,0:T(8,128)S(1)} %get-tuple-element.53.source_heights.heights, bf16[1024,128]{1,0:T(8,128)(2,1)S(1)} %get-tuple-element.54.source_halves.halves, ...), custom_call_target="tpu_custom_call" | custom-call | flops 2904000000 | bytes 262144 | tf_op jit(solution)/shard_map/near/pallas_call | solution.py:354
  45.6 0.0 collective-permute-done.6.theirs
  45.6 0.0 copy-done.2
  45.6 3.0 %finish.1 = f32[512,128]{1,0:T(8,128)} custom-call(f32[584,128]{1,0:T(8,128)S(1)} %get-tuple-element.48.weights, f32[192,128]{1,0:T(8,128)S(1)} %bitcast.13, f32[272,128]{1,0:T(8,128)S(1)} %collective-permute-done.3.theirs.first, f32[200,128]{1,0:T(8,128)S(1)} %collective-permute-done.4.theirs.second, f32[200,128]{1,0:T(8,128)S(1)} %collective-permute-done.5.theirs.third, ...), custom_call_target="tpu_custom_call" | custom-call | flops 2000000000 | bytes 262144 | tf_op jit(solution)/shard_map/finish/pallas_call | solution.py:506
  (1 shorter events, 0.0 us)
Async XLA Ops:
  0.0 2.2 %copy-start.1 = (f32[3,4,16,128]{3,2,1,0:T(8,128)S(1)}, f32[3,4,16,128]{3,2,1,0:T(8,128)}, u32[]{:S(2)}) copy-start(f32[3,4,16,128]{3,2,1,0:T(8,128)} %param.7) | copy-start | bytes 294916
  0.0 2.2 %copy-start.4 = (f32[2,1,1,32,32]{4,3,2,1,0:T(8,128)S(1)}, f32[2,1,1,32,32]{4,3,2,1,0:T(8,128)}, u32[]{:S(2)}) copy-start(f32[2,1,1,32,32]{4,3,2,1,0:T(8,128)} %param.13) | copy-start | bytes 24580
  0.0 2.3 %copy-start.3 = (f32[2,1,1,32,32]{4,3,2,1,0:T(8,128)S(1)}, f32[2,1,1,32,32]{4,3,2,1,0:T(8,128)}, u32[]{:S(2)}) copy-start(f32[2,1,1,32,32]{4,3,2,1,0:T(8,128)} %param.12) | copy-start | bytes 24580
  0.0 2.3 %copy-start.5 = (s32[9,4,16]{2,1,0:T(4,128)S(1)}, s32[9,4,16]{2,1,0:T(4,128)}, u32[]{:S(2)}) copy-start(s32[9,4,16]{2,1,0:T(4,128)} %mask.1) | copy-start | bytes 6916
  2.1 1.6 %collective-permute-start = (f32[480,128]{1,0:T(8,128)S(1)}, f32[480,128]{1,0:T(8,128)S(1)}, u32[]{:S(2)}, u32[]{:S(2)}) collective-permute-start(f32[480,128]{1,0:T(8,128)S(1)} %get-tuple-element.49.mine), channel_id=1, source_target_pairs={{0,16},{16,0},{32,48},{48,32},{64,80},{80,64},{96,112},{112,96},{1... | collective-permute-start | bytes 737288 | tf_op jit(solution)/shard_map/ppermute | solution.py:398
  4.0 6.1 %collective-permute-start.1 = (f32[304,128]{1,0:T(8,128)S(1)}, f32[304,128]{1,0:T(8,128)S(1)}, u32[]{:S(2)}, u32[]{:S(2)}) collective-permute-start(f32[304,128]{1,0:T(8,128)S(1)} %level.5.mine), channel_id=1, source_target_pairs={{0,32},{16,48},{32,0},{48,16},{64,96},{80,112},{96,64},{112,80},{1... | collective-permute-start | bytes 466952 | tf_op jit(solution)/shard_map/ppermute | solution.py:398
  10.4 7.7 %copy-start = (f32[8,4,16,128]{3,2,1,0:T(8,128)S(1)}, f32[8,4,16,128]{3,2,1,0:T(8,128)}, u32[]{:S(2)}) copy-start(f32[8,4,16,128]{3,2,1,0:T(8,128)} %param.8) | copy-start | bytes 786436
  10.4 7.7 %collective-permute-start.2 = (f32[304,128]{1,0:T(8,128)S(1)}, f32[304,128]{1,0:T(8,128)S(1)}, u32[]{:S(2)}, u32[]{:S(2)}) collective-permute-start(f32[304,128]{1,0:T(8,128)S(1)} %level.6.mine), channel_id=1, source_target_pairs={{0,64},{16,80},{32,96},{48,112},{64,0},{80,16},{96,32},{112,48},{1... | collective-permute-start | bytes 466952 | tf_op jit(solution)/shard_map/ppermute | solution.py:398
  18.4 5.8 %collective-permute-start.3 = (f32[272,128]{1,0:T(8,128)S(1)}, f32[272,128]{1,0:T(8,128)S(1)}, u32[]{:S(2)}, u32[]{:S(2)}) collective-permute-start(f32[272,128]{1,0:T(8,128)S(1)} %get-tuple-element.72.mine), channel_id=1, source_target_pairs={{0,1},{1,0},{2,3},{3,2},{4,5},{5,4},{6,7},{7,6},{8,9},{9,8},{10,11... | collective-permute-start | bytes 417800 | tf_op jit(solution)/shard_map/ppermute | solution.py:398
  24.4 8.2 %collective-permute-start.4 = (f32[200,128]{1,0:T(8,128)S(1)}, f32[200,128]{1,0:T(8,128)S(1)}, u32[]{:S(2)}, u32[]{:S(2)}) collective-permute-start(f32[200,128]{1,0:T(8,128)S(1)} %level.7.mine), channel_id=1, source_target_pairs={{0,2},{1,3},{2,0},{3,1},{4,6},{5,7},{6,4},{7,5},{8,10},{9,11},{10,... | collective-permute-start | bytes 307208 | tf_op jit(solution)/shard_map/ppermute | solution.py:398
  32.9 4.7 %collective-permute-start.5 = (f32[200,128]{1,0:T(8,128)S(1)}, f32[200,128]{1,0:T(8,128)S(1)}, u32[]{:S(2)}, u32[]{:S(2)}) collective-permute-start(f32[200,128]{1,0:T(8,128)S(1)} %level.8.mine), channel_id=1, source_target_pairs={{0,4},{1,5},{2,6},{3,7},{4,0},{5,1},{6,2},{7,3},{8,12},{9,13},{10,... | collective-permute-start | bytes 307208 | tf_op jit(solution)/shard_map/ppermute | solution.py:398
  37.9 7.8 %copy-start.2 = (f32[4,16,32,128]{3,2,1,0:T(8,128)S(1)}, f32[4,16,32,128]{3,2,1,0:T(8,128)}, u32[]{:S(2)}) copy-start(f32[4,16,32,128]{3,2,1,0:T(8,128)} %param.11) | copy-start | bytes 3145732
  37.9 7.8 %collective-permute-start.6 = (f32[200,128]{1,0:T(8,128)S(1)}, f32[200,128]{1,0:T(8,128)S(1)}, u32[]{:S(2)}, u32[]{:S(2)}) collective-permute-start(f32[200,128]{1,0:T(8,128)S(1)} %level.9.mine), channel_id=1, source_target_pairs={{0,8},{1,9},{2,10},{3,11},{4,12},{5,13},{6,14},{7,15},{8,0},{9,1},... | collective-permute-start | bytes 307208 | tf_op jit(solution)/shard_map/ppermute | solution.py:398

commit v10 on v9

--- a/solution.py
+++ b/solution.py
@@ -24,7 +24,7 @@
 leaf_rows, leaf_cols, points, rank, rhs = 4, 16, 128, 32, 8
 leaves = leaf_rows * leaf_cols
 edge_leaves = 2 * leaf_cols
-side_leaves = 16
+side_leaves = 8
 edge_rows = (3 + rhs) * leaf_cols
 side_rows = 72
 group = points // rank
@@ -68,12 +68,15 @@
     return runs
 
 
-def side_runs():
-    runs = []
-    for first, column, dj in ((0, 0, -1), (8, leaf_cols - 1, 1)):
-        for di in (-1, 0, 1):
-            runs.append(Run(leaf_rows, 0, first + 1 + di, leaf_cols, column, 3 * (di + 1) + dj + 1, False))
-    return runs
+def column_items(facing):
+    right = lax.axis_index("col") % 2
+    right = 1 - right if facing else right
+    items = []
+    for di in (-1, 0, 1):
+        for i in range(leaf_rows):
+            target = i * leaf_cols + (leaf_cols - 1) * right
+            items.append((i + 1 + di, target, (3 * (di + 1) + 2 * right) * leaves + target, None))
+    return items
 
 
 def cut_runs(runs, first, last):
@@ -175,11 +178,7 @@
 
 
 def compress_kernel(coords_far, sources_far, compress_far, halves, payload, coords, sources, compress, arrived):
-    chunk = groups // 4 * points
-    chunks = [slice(n * chunk, (n + 1) * chunk) for n in range(4)]
-    copies = start_copies(
-        [sources_far, coords_far] + [compress_far.at[rows] for rows in chunks], [sources, coords] + [compress.at[rows] for rows in chunks], arrived
-    )
+    copies = start_copies((sources_far, coords_far, compress_far), (sources, coords, compress), arrived)
     copies[0].wait()
     for leaf in range(leaves):
         high, low = split(sources[pl.ds(leaf, rhs, stride=leaves), :])
@@ -192,9 +191,8 @@
             ref, at = (coords, c) if c < 3 else (sources, c - 3)
             to = points + k * edge_rows + c * leaf_cols
             payload[to : to + leaf_cols, :] = ref[pl.ds(pl.multiple_of(at * leaves + row * leaf_cols, 8), leaf_cols), :]
+    copies[2].wait()
     for g in range(groups):
-        if g % (groups // 4) == 0:
-            copies[2 + g // (groups // 4)].wait()
         high, low = split(compress[g * points : (g + 1) * points, :])
         got = dot_t(halves[g * 16 * group : (g + 1) * 16 * group, :], jnp.concatenate([high, low], axis=0))
         got = got[:, :points] + got[:, points:]
@@ -231,21 +229,24 @@
     halo_tables(edge_leaves, coords, edges, left, heights, halves, wides)
 
 
-def side_tables(coords, first, second, third, fourth, left, heights, halves, wides, sides):
+def column_tables(coords, column, left, heights, halves, wides, values):
+    for c in range(3 + rhs):
+        values[c * side_leaves : c * side_leaves + 6, :] = column[6 * c : 6 * c + 6]
+        values[c * side_leaves + 6 : (c + 1) * side_leaves, :] = jnp.zeros((2, points), f32)
+    halo_tables(side_leaves, coords, values, left, heights, halves, wides)
+
+
+def facing_kernel(coords, first, left, heights, halves, wides, values):
+    column_tables(coords, first[points : points + side_rows, :], left, heights, halves, wides, values)
+
+
+def far_column(second, third, fourth):
     col = lax.axis_index("col")
-    odd = col % 2 == 1
     inner = (col > 0) & (col < lax.axis_size("col") - 1)
     at = slice(points, points + side_rows)
-    near = first[at, :]
     far = jnp.where((col % 8 == 3) | (col % 8 == 4), third[at, :], fourth[at, :])
     far = jnp.where((col % 4 == 1) | (col % 4 == 2), second[at, :], far)
-    far = jnp.where(inner, far, 0.0)
-    to_left, to_right = jnp.where(odd, near, far), jnp.where(odd, far, near)
-    gap = jnp.zeros((2, points), f32)
-    for c in range(3 + rhs):
-        at = slice(6 * c, 6 * c + 6)
-        sides[c * side_leaves : (c + 1) * side_leaves, :] = jnp.concatenate([to_left[at], gap, to_right[at], gap], axis=0)
-    halo_tables(side_leaves, coords, sides, left, heights, halves, wides)
+    return jnp.where(inner, far, 0.0)
 
 
 def level(mine, theirs, blocks):
@@ -290,6 +291,7 @@
 
 def near_kernel(items, batch, weights, left, source_heights, source_halves, right, heights, halves, seed, acc, gaps, splats, kerns):
     acc[...] = seed[...]
+    items = items() if callable(items) else items
 
     def subtract(item, n, gap, splat):
         source, target = item[:2]
@@ -297,7 +299,7 @@
         splat[n] = jnp.broadcast_to(source_heights[source : source + 1, :], (points, points)).T
 
     def evaluate(item, n, gap, splat, kern):
-        height = heights[item[1] : item[1] + 1, :]
+        height = heights[pl.ds(item[1], 1), :]
         for g in range(points // 32):
             at_rows = slice(32 * g, 32 * g + 32)
             dx, dy, dz = gap[n, at_rows, :points], gap[n, at_rows, points:], splat[n, at_rows] - height
@@ -313,8 +315,8 @@
             kern[n, 1, at_rows] = low
 
     def receive(leaf, weight, got):
-        at = slice(leaf * rhs, (leaf + 1) * rhs)
-        acc[at, :] += (got[:rhs] + got[rhs:]) * weights[weight : weight + 1, :]
+        at = pl.ds(leaf * rhs if isinstance(leaf, int) else pl.multiple_of(leaf * rhs, rhs), rhs)
+        acc[at, :] += (got[:rhs] + got[rhs:]) * weights[pl.ds(weight, 1), :]
 
     def apply(item, n, kern):
         source, target, weight, back = item
@@ -346,9 +348,11 @@
     ]
 
 
-def near_piece(pieces, weights, source_tables, target_tables, seed):
-    items = listed(pieces)
-    batch = 4 if any(item[3] is not None for item in items) else 8
+def near_piece(items, weights, source_tables, target_tables, seed):
+    if callable(items):
+        count, batch = 3 * leaf_rows, 4
+    else:
+        count, batch = len(items), 4 if any(item[3] is not None for item in items) else 8
     left, source_heights, source_halves = source_tables
     right, heights, halves = target_tables
     return pl.pallas_call(
@@ -358,16 +362,16 @@
         out_specs=vmem,
         scratch_shapes=near_scratch(batch),
         compiler_params=params(24),
-        cost_estimate=cost(len(items) * 110),
+        cost_estimate=cost(count * 110),
         name="near",
     )(weights, left, source_heights, source_halves, right, heights, halves, seed)
 
 
 def finish_kernel(
-    items, weights, coords, first, second, third, theirs, mine, blocks, expand, right, heights, halves, seed, out,
+    weights, coords, second, third, theirs, mine, blocks, expand, right, heights, halves, seed, out,
     left, source_heights, source_halves, wides, sides, acc, gaps, splats, kerns, *far,
 ):
-    side_tables(coords, first, second, third, theirs, left, source_heights, source_halves, wides, sides)
+    column_tables(coords, far_column(second, third, theirs), left, source_heights, source_halves, wides, sides)
     coeffs = level(mine[:points, :], theirs[:points, :], blocks)
     for g in range(groups):
         here = coeffs[g * rhs : (g + 1) * rhs]
@@ -377,7 +381,7 @@
         got = dot(jnp.concatenate([high, low], axis=0), jnp.concatenate([e_high, e_low], axis=1))
         got = got[:, :points] + got[:, points:]
         far[0][g * group * rhs : (g + 1) * group * rhs, :] = got[: group * rhs] + got[group * rhs :]
-    near_kernel(items, 8, weights, left, source_heights, source_halves, right, heights, halves, seed, acc, gaps, splats, kerns)
+    near_kernel(functools.partial(column_items, False), 4, weights, left, source_heights, source_halves, right, heights, halves, seed, acc, gaps, splats, kerns)
     order = sorted(range(leaves), key=lambda leaf: leaf % leaf_cols in (0, leaf_cols - 1))
     for leaf in order:
         at = slice(leaf * rhs, (leaf + 1) * rhs)
@@ -426,6 +430,20 @@
         cost_estimate=cost(2000),
         name=name,
     )(*[pltpu.with_memory_space_constraint(operand, pltpu.HBM) for operand in operands])
+
+
+def tables_call(body, name, count, scratch, *operands):
+    shapes = table_shapes(count)
+    return pl.pallas_call(
+        body,
+        out_shape=(shapes[0], shapes[2], shapes[3]),
+        in_specs=[vmem] * len(operands),
+        out_specs=(vmem,) * 3,
+        scratch_shapes=[pltpu.VMEM(shape, f32) for shape in [(1, count * 16, points)] + scratch],
+        compiler_params=params(16),
+        cost_estimate=cost(1000),
+        name=name,
+    )(*operands)
 
 
 def shards(coords, sources, neighbour_mask, compress, expand, row_transfer, col_transfer):
@@ -455,12 +473,13 @@
         name="prep",
     )(coords_later, neighbour_mask, row_transfer[:, 0, 0], col_transfer[:, 0, 0])
     own, targets = (left, heights, halves), (right, heights, halves)
-    inner, edge, side = interior_runs(), edge_runs(), side_runs()
-    counts = [sum(run.count for run in runs) for runs in (inner, edge, side)]
+    inner, edge = interior_runs(), edge_runs()
+    counts = [sum(run.count for run in runs) for runs in (inner, edge)]
     windows = row_bits + col_bits - 1
     edge_windows = (row_bits, row_bits + 2)
     inner_windows = [n for n in range(1, windows + 1) if n not in edge_windows]
-    cuts = [counts[0] * k // len(inner_windows) // 4 * 4 for k in range(len(inner_windows))] + [counts[0]]
+    parts = (72, 72, 64, 54)
+    cuts = [counts[0] * sum(parts[:k]) // sum(parts) // 4 * 4 for k in range(len(parts))] + [counts[0]]
     half = -(-counts[1] // 2 // 8) * 8
     acc = jnp.zeros((leaves * rhs, points), f32)
     received = [theirs]
@@ -471,23 +490,18 @@
             payload, acc = lax.optimization_barrier((payload, acc))
             if n == row_bits:
                 edges, acc = lax.optimization_barrier((edges, acc))
-                shapes = table_shapes(edge_leaves)
-                edge_tables = pl.pallas_call(
-                    edges_kernel,
-                    out_shape=(shapes[0], shapes[2], shapes[3]),
-                    in_specs=[vmem] * 2,
-                    out_specs=(vmem,) * 3,
-                    scratch_shapes=[pltpu.VMEM((1, edge_leaves * 16, points), f32)],
-                    compiler_params=params(16),
-                    cost_estimate=cost(1000),
-                    name="edges",
-                )(coords, edges)
+                edge_tables = tables_call(edges_kernel, "edges", edge_leaves, [], coords, edges)
+            if n == row_bits + 1:
+                first, acc = lax.optimization_barrier((received[row_bits], acc))
+                facing_tables = tables_call(facing_kernel, "facing", side_leaves, [((3 + rhs) * side_leaves, points)], coords, first)
             if n in edge_windows:
                 some = cut_runs(edge, 0, half) if n == row_bits else cut_runs(edge, half, counts[1])
-                acc = near_piece(some, weights, edge_tables, targets, acc)
+                acc = near_piece(listed(some), weights, edge_tables, targets, acc)
             else:
                 k = inner_windows.index(n)
-                acc = near_piece(cut_runs(inner, cuts[k], cuts[k + 1]), weights, own, targets, acc)
+                acc = near_piece(listed(cut_runs(inner, cuts[k], cuts[k + 1])), weights, own, targets, acc)
+            if n == windows:
+                acc = near_piece(functools.partial(column_items, True), weights, facing_tables, targets, acc)
             theirs, acc = lax.optimization_barrier((theirs, acc))
             received.append(theirs)
         if n == row_bits - 1:
@@ -502,9 +516,9 @@
             skip = points + rows if bit == 0 else points
             payload = small_call(functools.partial(level_kernel, skip), "level", array(points + rows, points), payload, theirs, blocks)
     shapes = table_shapes(side_leaves)
-    operands = (weights, coords, *received[row_bits:], payload, blocks, expand.reshape(-1, points), *targets, acc)
+    operands = (weights, coords, *received[row_bits + 1 :], payload, blocks, expand.reshape(-1, points), *targets, acc)
     out = pl.pallas_call(
-        functools.partial(finish_kernel, listed(cut_runs(side, 0, counts[2]))),
+        finish_kernel,
         out_shape=array(rhs * leaves, points),
         in_specs=[vmem] * len(operands),
         out_specs=vmem,
@@ -514,7 +528,7 @@
             pltpu.VMEM(((3 + rhs) * side_leaves, points), f32),
             pltpu.VMEM((rhs * leaves, points), f32),
         ]
-        + near_scratch(8)
+        + near_scratch(4)
         + [pltpu.VMEM((rhs * leaves, points), f32)],
         compiler_params=params(24),
         cost_estimate=cost(5000),

time: 48.8 us -> 49.4 us (1.012)
  Pallas kernels: 31.5 us -> 32.5 us
    pallas_call x6 -> x7, Pallas kernels: 23.4 us -> 25.2 us  [near_piece(): pl.pallas_call(functools.partial(near_kernel, items, batch), out_shape=ja...]
    pallas_call x2 -> x3, Pallas kernels: 3.5 us -> 2.88 us  [the longest x1 2.2 us: shards(): pl.pallas_call(finish_kernel, out_shape=array(rhs * leaves, points), in_s...]
  transfers between devices with their start and end apart: 7 -> 7, of which waited for: 3 -> 2; matrix products, arithmetic and copies ran while one was open for 0% -> 0% of each run, Pallas kernels for 51% -> 55%
where the time goes in v10:
time: 49.4 us; the launch traced here: 49.3 us
  Pallas kernels  32.5 us (66%)
  starting transfers between devices  15.8 us (32%)
  waiting for transfers between devices  0.74 us (1%)
    pallas_call x7, Pallas kernels, near_piece(): pl.pallas_call(functools.partial(near_kernel, items, batch), out_shape=ja...  25.2 us
    ppermute x7, starting transfers between devices, partner_of(): return lax.ppermute(block, axis, route)  15.8 us
    pallas_call x1, Pallas kernels, shards(): pl.pallas_call(finish_kernel, out_shape=array(rhs * leaves, points), in_s...  2.2 us
    pallas_call x1, Pallas kernels, far_call(): pl.pallas_call(body, out_shape=out_shape, in_specs=[pl.BlockSpec(memory_s...  1.94 us
    pallas_call x6, Pallas kernels, small_call(): pl.pallas_call(body, out_shape=out_shape, in_specs=[vmem] * len(operands)...  1.46 us
    pallas_call x1, Pallas kernels, shards(): pl.pallas_call(prep_kernel, out_shape=table_shapes(leaves)[:3] + (block_s...  1 us
  transfers between devices with their start and end apart: 7, of which 2 were waited for; matrix products, arithmetic and copies ran while one was open for 0% of the time, Pallas kernels for 55%

profile of v10, /device:TPU:0, one launch (start us, length us, event | category | flops | bytes accessed | tf_op | source)
XLA Modules:
  0.0 49.3 jit_solution(15248356807260264513)
XLA Ops:
  0.0 0.0 copy-start.1
  0.0 0.0 copy-start.4
  0.0 0.0 copy-start.3
  0.0 0.0 copy-start.5
  0.0 1.9 %compress.1 = (bf16[1024,128]{1,0:T(8,128)(2,1)S(1)}, f32[480,128]{1,0:T(8,128)S(1)}) custom-call(f32[192,128]{1,0:T(8,128)} %bitcast.9, f32[512,128]{1,0:T(8,128)} %bitcast.7, f32[2048,128]{1,0:T(8,128)} %bitcast.18), custom_call_target="tpu_custom_call" | custom-call | flops 800000000 | bytes 262144 | tf_op jit(solution)/shard_map/compress/pallas_call | solution.py:423
  2.0 0.1 collective-permute-start
  2.1 0.0 copy-done.1
  2.1 0.0 copy-done.4
  2.1 0.0 copy-done.3
  2.1 0.0 copy-done.5
  2.1 1.0 %prep.1 = (bf16[8192,16]{1,0:T(8,128)(2,1)S(1)}, bf16[1024,256]{1,0:T(8,128)(2,1)S(1)}, f32[64,128]{1,0:T(8,128)S(1)}, bf16[4,128,128]{2,1,0:T(8,128)(2,1)S(1)},...) custom-call(f32[192,128]{1,0:T(8,128)S(1)} %bitcast.10, s32[9,4,16]{2,1,0:T(4,128)S(1)} %copy-done.5, ...), custom_call_target="tpu_custom_call" | custom-call | flops 800000000 | bytes 262144 | tf_op jit(solution)/shard_map/prep/pallas_call | solution.py:465
  3.1 0.5 collective-permute-done.theirs.first
  3.5 0.2 level.5.mine
  3.8 1.8 %collective-permute-start.1 = (f32[304,128]{1,0:T(8,128)S(1)}, f32[304,128]{1,0:T(8,128)S(1)}, u32[]{:S(2)}, u32[]{:S(2)}) collective-permute-start(f32[304,128]{1,0:T(8,128)S(1)} %level.5.mine), channel_id=1, source_target_pairs={{0,32},{16,48},{32,0},{48,16},{64,96},{80,112},{96,64},{112,80},{1... | collective-permute-start | bytes 466952 | tf_op jit(solution)/shard_map/ppermute | solution.py:402
  5.6 5.2 %near.7.seed = f32[512,128]{1,0:T(8,128)S(1)} custom-call(f32[584,128]{1,0:T(8,128)S(1)} %get-tuple-element.53.weights, bf16[8192,16]{1,0:T(8,128)(2,1)S(1)} %get-tuple-element.57.left, f32[64,128]{1,0:T(8,128)S(1)} %get-tuple-element.58.source_heights.heights, bf16[1024,128]{1,0:T(8,128)(2,1)S(1)} %get-tuple-element.59.source_halves.halves, ...), custom_call_target="tpu_custom_call" | custom-call | flops 3168000000 | bytes 262144 | tf_op jit(solution)/shard_map/near/pallas_call | solution.py:358
  10.7 0.0 collective-permute-done.1.theirs.second
  10.7 0.3 level.6.mine
  11.0 0.0 copy-start
  11.0 3.2 %collective-permute-start.2 = (f32[304,128]{1,0:T(8,128)S(1)}, f32[304,128]{1,0:T(8,128)S(1)}, u32[]{:S(2)}, u32[]{:S(2)}) collective-permute-start(f32[304,128]{1,0:T(8,128)S(1)} %level.6.mine), channel_id=1, source_target_pairs={{0,64},{16,80},{32,96},{48,112},{64,0},{80,16},{96,32},{112,48},{1... | collective-permute-start | bytes 466952 | tf_op jit(solution)/shard_map/ppermute | solution.py:402
  14.2 4.8 %near.8.seed = f32[512,128]{1,0:T(8,128)S(1)} custom-call(f32[584,128]{1,0:T(8,128)S(1)} %get-tuple-element.53.weights, bf16[8192,16]{1,0:T(8,128)(2,1)S(1)} %get-tuple-element.57.left, f32[64,128]{1,0:T(8,128)S(1)} %get-tuple-element.58.source_heights.heights, bf16[1024,128]{1,0:T(8,128)(2,1)S(1)} %get-tuple-element.59.source_halves.halves, ...), custom_call_target="tpu_custom_call" | custom-call | flops 3168000000 | bytes 262144 | tf_op jit(solution)/shard_map/near/pallas_call | solution.py:358
  19.0 0.0 collective-permute-done.2.theirs
  19.0 0.0 copy-done
  19.0 0.3 turn.1
  19.3 2.0 %collective-permute-start.3 = (f32[272,128]{1,0:T(8,128)S(1)}, f32[272,128]{1,0:T(8,128)S(1)}, u32[]{:S(2)}, u32[]{:S(2)}) collective-permute-start(f32[272,128]{1,0:T(8,128)S(1)} %get-tuple-element.69.mine), channel_id=1, source_target_pairs={{0,1},{1,0},{2,3},{3,2},{4,5},{5,4},{6,7},{7,6},{8,9},{9,8},{10,11... | collective-permute-start | bytes 417800 | tf_op jit(solution)/shard_map/ppermute | solution.py:402
  21.3 0.5 edges.1
  21.8 3.1 %near.9.seed = f32[512,128]{1,0:T(8,128)S(1)} custom-call(f32[584,128]{1,0:T(8,128)S(1)} %get-tuple-element.53.weights, bf16[4096,16]{1,0:T(8,128)(2,1)S(1)} %get-tuple-element.73.left, f32[32,128]{1,0:T(8,128)S(1)} %get-tuple-element.74.source_heights, bf16[512,128]{1,0:T(8,128)(2,1)S(1)} %get-tuple-element.75.source_halves, ...), custom_call_target="tpu_custom_call" | custom-call | flops 2112000000 | bytes 262144 | tf_op jit(solution)/shard_map/near/pallas_call | solution.py:358
  24.9 0.0 collective-permute-done.3.theirs.first
  25.0 0.2 level.7.mine
  25.2 3.9 %collective-permute-start.4 = (f32[200,128]{1,0:T(8,128)S(1)}, f32[200,128]{1,0:T(8,128)S(1)}, u32[]{:S(2)}, u32[]{:S(2)}) collective-permute-start(f32[200,128]{1,0:T(8,128)S(1)} %level.7.mine), channel_id=1, source_target_pairs={{0,2},{1,3},{2,0},{3,1},{4,6},{5,7},{6,4},{7,5},{8,10},{9,11},{10,... | collective-permute-start | bytes 307208 | tf_op jit(solution)/shard_map/ppermute | solution.py:402
  29.1 4.3 %near.10.seed = f32[512,128]{1,0:T(8,128)S(1)} custom-call(f32[584,128]{1,0:T(8,128)S(1)} %get-tuple-element.53.weights, bf16[8192,16]{1,0:T(8,128)(2,1)S(1)} %get-tuple-element.57.left, f32[64,128]{1,0:T(8,128)S(1)} %get-tuple-element.58.source_heights.heights, bf16[1024,128]{1,0:T(8,128)(2,1)S(1)} %get-tuple-element.59.source_halves.halves, ...), custom_call_target="tpu_custom_call" | custom-call | flops 2816000000 | bytes 262144 | tf_op jit(solution)/shard_map/near/pallas_call | solution.py:358
  33.4 0.2 facing.1
  33.6 0.0 collective-permute-done.4.theirs.second
  33.6 0.2 level.8.mine
  33.9 1.6 %collective-permute-start.5 = (f32[200,128]{1,0:T(8,128)S(1)}, f32[200,128]{1,0:T(8,128)S(1)}, u32[]{:S(2)}, u32[]{:S(2)}) collective-permute-start(f32[200,128]{1,0:T(8,128)S(1)} %level.8.mine), channel_id=1, source_target_pairs={{0,4},{1,5},{2,6},{3,7},{4,0},{5,1},{6,2},{7,3},{8,12},{9,13},{10,... | collective-permute-start | bytes 307208 | tf_op jit(solution)/shard_map/ppermute | solution.py:402
  35.4 2.9 %near.11.seed = f32[512,128]{1,0:T(8,128)S(1)} custom-call(f32[584,128]{1,0:T(8,128)S(1)} %get-tuple-element.53.weights, bf16[4096,16]{1,0:T(8,128)(2,1)S(1)} %get-tuple-element.73.left, f32[32,128]{1,0:T(8,128)S(1)} %get-tuple-element.74.source_heights, bf16[512,128]{1,0:T(8,128)(2,1)S(1)} %get-tuple-element.75.source_halves, ...), custom_call_target="tpu_custom_call" | custom-call | flops 1936000000 | bytes 262144 | tf_op jit(solution)/shard_map/near/pallas_call | solution.py:358
  38.3 0.3 collective-permute-done.5.theirs.third
  38.6 0.2 level.9.mine
  38.8 0.0 copy-start.2
  38.9 3.4 %collective-permute-start.6 = (f32[200,128]{1,0:T(8,128)S(1)}, f32[200,128]{1,0:T(8,128)S(1)}, u32[]{:S(2)}, u32[]{:S(2)}) collective-permute-start(f32[200,128]{1,0:T(8,128)S(1)} %level.9.mine), channel_id=1, source_target_pairs={{0,8},{1,9},{2,10},{3,11},{4,12},{5,13},{6,14},{7,15},{8,0},{9,1},... | collective-permute-start | bytes 307208 | tf_op jit(solution)/shard_map/ppermute | solution.py:402
  42.2 3.8 %near.12.seed = f32[512,128]{1,0:T(8,128)S(1)} custom-call(f32[584,128]{1,0:T(8,128)S(1)} %get-tuple-element.53.weights, bf16[8192,16]{1,0:T(8,128)(2,1)S(1)} %get-tuple-element.57.left, f32[64,128]{1,0:T(8,128)S(1)} %get-tuple-element.58.source_heights.heights, bf16[1024,128]{1,0:T(8,128)(2,1)S(1)} %get-tuple-element.59.source_halves.halves, ...), custom_call_target="tpu_custom_call" | custom-call | flops 2376000000 | bytes 262144 | tf_op jit(solution)/shard_map/near/pallas_call | solution.py:358
  46.0 1.1 %near.13.seed = f32[512,128]{1,0:T(8,128)S(1)} custom-call(f32[584,128]{1,0:T(8,128)S(1)} %get-tuple-element.53.weights, bf16[1024,16]{1,0:T(8,128)(2,1)S(1)} %get-tuple-element.89.left, f32[8,128]{1,0:T(8,128)S(1)} %get-tuple-element.90.source_heights, bf16[128,128]{1,0:T(8,128)(2,1)S(1)} %get-tuple-element.91.source_halves, ...), custom_call_target="tpu_custom_call" | custom-call | flops 528000000 | bytes 262144 | tf_op jit(solution)/shard_map/near/pallas_call | solution.py:358
  47.1 0.0 collective-permute-done.6.theirs
  47.1 0.0 copy-done.2
  47.1 2.2 %finish.1 = f32[512,128]{1,0:T(8,128)} custom-call(f32[584,128]{1,0:T(8,128)S(1)} %get-tuple-element.53.weights, f32[192,128]{1,0:T(8,128)S(1)} %bitcast.14, f32[200,128]{1,0:T(8,128)S(1)} %collective-permute-done.4.theirs.second, f32[200,128]{1,0:T(8,128)S(1)} %collective-permute-done.5.theirs.third, f32[200,128]{1,0:T(8,128)S(1)} %collective-permute-done.6.theirs, ...), custom_call_target="tpu_custom_call" | custom-call | flops 2000000000 | bytes 262144 | tf_op jit(solution)/shard_map/finish/pallas_call | solution.py:520
  (1 shorter events, 0.0 us)
Async XLA Ops:
  0.0 2.1 %copy-start.1 = (f32[3,4,16,128]{3,2,1,0:T(8,128)S(1)}, f32[3,4,16,128]{3,2,1,0:T(8,128)}, u32[]{:S(2)}) copy-start(f32[3,4,16,128]{3,2,1,0:T(8,128)} %param.7) | copy-start | bytes 294916
  0.0 2.1 %copy-start.4 = (f32[2,1,1,32,32]{4,3,2,1,0:T(8,128)S(1)}, f32[2,1,1,32,32]{4,3,2,1,0:T(8,128)}, u32[]{:S(2)}) copy-start(f32[2,1,1,32,32]{4,3,2,1,0:T(8,128)} %param.13) | copy-start | bytes 24580
  0.0 2.1 %copy-start.3 = (f32[2,1,1,32,32]{4,3,2,1,0:T(8,128)S(1)}, f32[2,1,1,32,32]{4,3,2,1,0:T(8,128)}, u32[]{:S(2)}) copy-start(f32[2,1,1,32,32]{4,3,2,1,0:T(8,128)} %param.12) | copy-start | bytes 24580
  0.0 2.1 %copy-start.5 = (s32[9,4,16]{2,1,0:T(4,128)S(1)}, s32[9,4,16]{2,1,0:T(4,128)}, u32[]{:S(2)}) copy-start(s32[9,4,16]{2,1,0:T(4,128)} %mask.1) | copy-start | bytes 6916
  2.0 1.6 %collective-permute-start = (f32[480,128]{1,0:T(8,128)S(1)}, f32[480,128]{1,0:T(8,128)S(1)}, u32[]{:S(2)}, u32[]{:S(2)}) collective-permute-start(f32[480,128]{1,0:T(8,128)S(1)} %get-tuple-element.54.mine), channel_id=1, source_target_pairs={{0,16},{16,0},{32,48},{48,32},{64,80},{80,64},{96,112},{112,96},{1... | collective-permute-start | bytes 737288 | tf_op jit(solution)/shard_map/ppermute | solution.py:402
  3.8 7.0 %collective-permute-start.1 = (f32[304,128]{1,0:T(8,128)S(1)}, f32[304,128]{1,0:T(8,128)S(1)}, u32[]{:S(2)}, u32[]{:S(2)}) collective-permute-start(f32[304,128]{1,0:T(8,128)S(1)} %level.5.mine), channel_id=1, source_target_pairs={{0,32},{16,48},{32,0},{48,16},{64,96},{80,112},{96,64},{112,80},{1... | collective-permute-start | bytes 466952 | tf_op jit(solution)/shard_map/ppermute | solution.py:402
  11.0 8.0 %copy-start = (f32[8,4,16,128]{3,2,1,0:T(8,128)S(1)}, f32[8,4,16,128]{3,2,1,0:T(8,128)}, u32[]{:S(2)}) copy-start(f32[8,4,16,128]{3,2,1,0:T(8,128)} %param.8) | copy-start | bytes 786436
  11.0 8.0 %collective-permute-start.2 = (f32[304,128]{1,0:T(8,128)S(1)}, f32[304,128]{1,0:T(8,128)S(1)}, u32[]{:S(2)}, u32[]{:S(2)}) collective-permute-start(f32[304,128]{1,0:T(8,128)S(1)} %level.6.mine), channel_id=1, source_target_pairs={{0,64},{16,80},{32,96},{48,112},{64,0},{80,16},{96,32},{112,48},{1... | collective-permute-start | bytes 466952 | tf_op jit(solution)/shard_map/ppermute | solution.py:402
  19.3 5.6 %collective-permute-start.3 = (f32[272,128]{1,0:T(8,128)S(1)}, f32[272,128]{1,0:T(8,128)S(1)}, u32[]{:S(2)}, u32[]{:S(2)}) collective-permute-start(f32[272,128]{1,0:T(8,128)S(1)} %get-tuple-element.69.mine), channel_id=1, source_target_pairs={{0,1},{1,0},{2,3},{3,2},{4,5},{5,4},{6,7},{7,6},{8,9},{9,8},{10,11... | collective-permute-start | bytes 417800 | tf_op jit(solution)/shard_map/ppermute | solution.py:402
  25.2 8.4 %collective-permute-start.4 = (f32[200,128]{1,0:T(8,128)S(1)}, f32[200,128]{1,0:T(8,128)S(1)}, u32[]{:S(2)}, u32[]{:S(2)}) collective-permute-start(f32[200,128]{1,0:T(8,128)S(1)} %level.7.mine), channel_id=1, source_target_pairs={{0,2},{1,3},{2,0},{3,1},{4,6},{5,7},{6,4},{7,5},{8,10},{9,11},{10,... | collective-permute-start | bytes 307208 | tf_op jit(solution)/shard_map/ppermute | solution.py:402
  33.9 4.7 %collective-permute-start.5 = (f32[200,128]{1,0:T(8,128)S(1)}, f32[200,128]{1,0:T(8,128)S(1)}, u32[]{:S(2)}, u32[]{:S(2)}) collective-permute-start(f32[200,128]{1,0:T(8,128)S(1)} %level.8.mine), channel_id=1, source_target_pairs={{0,4},{1,5},{2,6},{3,7},{4,0},{5,1},{6,2},{7,3},{8,12},{9,13},{10,... | collective-permute-start | bytes 307208 | tf_op jit(solution)/shard_map/ppermute | solution.py:402
  38.8 8.2 %copy-start.2 = (f32[4,16,32,128]{3,2,1,0:T(8,128)S(1)}, f32[4,16,32,128]{3,2,1,0:T(8,128)}, u32[]{:S(2)}) copy-start(f32[4,16,32,128]{3,2,1,0:T(8,128)} %param.11) | copy-start | bytes 3145732
  38.9 8.2 %collective-permute-start.6 = (f32[200,128]{1,0:T(8,128)S(1)}, f32[200,128]{1,0:T(8,128)S(1)}, u32[]{:S(2)}, u32[]{:S(2)}) collective-permute-start(f32[200,128]{1,0:T(8,128)S(1)} %level.9.mine), channel_id=1, source_target_pairs={{0,8},{1,9},{2,10},{3,11},{4,12},{5,13},{6,14},{7,15},{8,0},{9,1},... | collective-permute-start | bytes 307208 | tf_op jit(solution)/shard_map/ppermute | solution.py:402

commit v11 on v8

--- a/solution.py
+++ b/solution.py
@@ -136,7 +136,7 @@
     ones_x = jnp.where(k < 3, 1.0, 0.0)
     ones_y = jnp.where((k >= 3) & (k < 6), 1.0, 0.0)
     ones_t = jnp.where((k >= 6) & (k < 9), 1.0, 0.0)
-    for role in range(3):
+    for role in range(1 if right is None else 3):
         wide = wides.at[role]
         for leaf in range(count):
             wide[pl.ds(leaf * 16, 16), :] = (ones_t, ones_x, ones_y)[role]
@@ -174,7 +174,7 @@
     return copies
 
 
-def compress_kernel(coords_far, sources_far, compress_far, halves, payload, coords, sources, compress, arrived):
+def compress_kernel(coords_far, sources_far, compress_far, halves, payload, outer, coords, sources, compress, arrived):
     copies = start_copies((sources_far, coords_far, compress_far), (sources, coords, compress), arrived)
     copies[0].wait()
     for leaf in range(leaves):
@@ -186,8 +186,8 @@
         row = (leaf_rows - 1) * (1 - odd if k == 0 else odd)
         for c in range(3 + rhs):
             ref, at = (coords, c) if c < 3 else (sources, c - 3)
-            to = points + k * edge_rows + c * leaf_cols
-            payload[to : to + leaf_cols, :] = ref[pl.ds(pl.multiple_of(at * leaves + row * leaf_cols, 8), leaf_cols), :]
+            to, base = (payload, points) if k == 0 else (outer, 0)
+            to[base + c * leaf_cols : base + (c + 1) * leaf_cols, :] = ref[pl.ds(pl.multiple_of(at * leaves + row * leaf_cols, 8), leaf_cols), :]
     copies[2].wait()
     for g in range(groups):
         high, low = split(compress[g * points : (g + 1) * points, :])
@@ -214,33 +214,27 @@
     weights[zero_row : zero_row + 8, :] = jnp.zeros((8, points), f32)
 
 
-def halo_tables(count, coords, values, left, right, heights, halves, wides):
+def halo_tables(count, coords, values, left, heights, halves, wides):
     start = [coords[c * leaves : c * leaves + 1, 0:1] for c in range(3)]
-    fill_tables(count, start, values, left, right, heights, wides)
+    fill_tables(count, start, values, left, None, heights, wides)
     for leaf in range(count):
         high, low = split(values[pl.ds(3 * count + leaf, rhs, stride=count), :])
         halves[sixteen(leaf), :] = jnp.concatenate([high, low], axis=0)
 
 
-def edges_kernel(coords, edges, left, right, heights, halves, wides):
-    halo_tables(edge_leaves, coords, edges, left, right, heights, halves, wides)
-
-
-def sides_kernel(coords, first, second, third, fourth, left, right, heights, halves, wides, sides):
-    col = lax.axis_index("col")
-    odd = col % 2 == 1
-    inner = (col > 0) & (col < lax.axis_size("col") - 1)
-    at = slice(points, points + side_rows)
-    near = first[at, :]
-    far = jnp.where((col % 8 == 3) | (col % 8 == 4), third[at, :], fourth[at, :])
-    far = jnp.where((col % 4 == 1) | (col % 4 == 2), second[at, :], far)
-    far = jnp.where(inner, far, 0.0)
+def edges_kernel(coords, edges, left, heights, halves, wides):
+    halo_tables(edge_leaves, coords, edges, left, heights, halves, wides)
+
+
+def sides_kernel(coords, facing, beyond, left, heights, halves, wides, sides):
+    odd = lax.axis_index("col") % 2 == 1
+    near, far = facing[points : points + side_rows, :], beyond[...]
     to_left, to_right = jnp.where(odd, near, far), jnp.where(odd, far, near)
     gap = jnp.zeros((2, points), f32)
     for c in range(3 + rhs):
         at = slice(6 * c, 6 * c + 6)
         sides[c * side_leaves : (c + 1) * side_leaves, :] = jnp.concatenate([to_left[at], gap, to_right[at], gap], axis=0)
-    halo_tables(side_leaves, coords, sides, left, right, heights, halves, wides)
+    halo_tables(side_leaves, coords, sides, left, heights, halves, wides)
 
 
 def level(mine, theirs, blocks):
@@ -254,33 +248,29 @@
     return total
 
 
-def level_kernel(forward, mine, theirs, blocks, payload):
+def level_kernel(mine, theirs, blocks, payload):
+    payload[...] = level(mine[:points, :], theirs[:points, :], blocks)
+
+
+def turn_kernel(mine, theirs, blocks, coords, sources, facing, beyond, payload, outer, edges):
     payload[:points, :] = level(mine[:points, :], theirs[:points, :], blocks)
-    payload[points:, :] = theirs[forward:, :]
-
-
-def turn_kernel(mine, theirs, blocks, coords, sources, first, second, payload, edges):
-    payload[:points, :] = level(mine[:points, :], theirs[:points, :], blocks)
-    row, col = lax.axis_index("row"), lax.axis_index("col")
-    odd = row % 2 == 1
-    around = (row % 4 == 1) | (row % 4 == 2)
-    inner = (row > 0) & (row < lax.axis_size("row") - 1)
+    odd = lax.axis_index("row") % 2 == 1
+    col = lax.axis_index("col")
     for c in range(3 + rhs):
-        at = slice(points + c * leaf_cols, points + (c + 1) * leaf_cols)
-        near = first[at, :]
-        far = jnp.where(inner, jnp.where(around, second[at, :], theirs[at, :]), 0.0)
+        near = facing[points + c * leaf_cols : points + (c + 1) * leaf_cols, :]
+        far = beyond[c * leaf_cols : (c + 1) * leaf_cols, :]
         edges[c * edge_leaves : c * edge_leaves + leaf_cols, :] = jnp.where(odd, near, far)
         edges[c * edge_leaves + leaf_cols : (c + 1) * edge_leaves, :] = jnp.where(odd, far, near)
     for k in range(2):
         j = (leaf_cols - 1) * (1 - col % 2 if k == 0 else col % 2)
-        base = points + k * side_rows
+        to, base = (payload, points) if k == 0 else (outer, 0)
         for c in range(3 + rhs):
             ref, at = (coords, c) if c < 3 else (sources, c - 3)
-            payload[base + 6 * c : base + 6 * c + 1, :] = edges[pl.ds(c * edge_leaves + j, 1), :]
+            to[base + 6 * c : base + 6 * c + 1, :] = edges[pl.ds(c * edge_leaves + j, 1), :]
             for i in range(leaf_rows):
-                payload[base + 6 * c + 1 + i : base + 6 * c + 2 + i, :] = ref[pl.ds(at * leaves + i * leaf_cols + j, 1), :]
-            payload[base + 6 * c + 5 : base + 6 * c + 6, :] = edges[pl.ds(c * edge_leaves + leaf_cols + j, 1), :]
-        payload[base + 66 : base + side_rows, :] = jnp.zeros((side_rows - 66, points), f32)
+                to[base + 6 * c + 1 + i : base + 6 * c + 2 + i, :] = ref[pl.ds(at * leaves + i * leaf_cols + j, 1), :]
+            to[base + 6 * c + 5 : base + 6 * c + 6, :] = edges[pl.ds(c * edge_leaves + leaf_cols + j, 1), :]
+        to[base + 66 : base + side_rows, :] = jnp.zeros((side_rows - 66, points), f32)
 
 
 def near_kernel(items, batch, weights, left, source_heights, source_halves, right, heights, halves, seed, acc, gaps, splats, kerns):
@@ -292,7 +282,7 @@
         splat[n] = jnp.broadcast_to(source_heights[source : source + 1, :], (points, points)).T
 
     def evaluate(item, n, gap, splat, kern):
-        height = heights[item[1] : item[1] + 1, :]
+        height = heights[pl.ds(item[1], 1), :]
         for g in range(points // 32):
             at_rows = slice(32 * g, 32 * g + 32)
             dx, dy, dz = gap[n, at_rows, :points], gap[n, at_rows, points:], splat[n, at_rows] - height
@@ -308,8 +298,8 @@
             kern[n, 1, at_rows] = low
 
     def receive(leaf, weight, got):
-        at = slice(leaf * rhs, (leaf + 1) * rhs)
-        acc[at, :] += (got[:rhs] + got[rhs:]) * weights[weight : weight + 1, :]
+        at = pl.ds(leaf * rhs if isinstance(leaf, int) else pl.multiple_of(leaf * rhs, rhs), rhs)
+        acc[at, :] += (got[:rhs] + got[rhs:]) * weights[pl.ds(weight, 1), :]
 
     def apply(item, n, kern):
         source, target, weight, back = item
@@ -333,21 +323,24 @@
                 evaluate(item, n, gaps.at[k % ring], splats.at[k % ring], kerns.at[k % ring])
 
 
-def near_piece(pieces, weights, source_tables, target_tables, seed):
-    items = listed(pieces)
+def near_scratch(batch):
+    return [
+        pltpu.VMEM((ring, batch, points, 2 * points), f32),
+        pltpu.VMEM((ring, batch, points, points), f32),
+        pltpu.VMEM((ring, batch, 2, points, points), bf16),
+    ]
+
+
+def near_piece(items, weights, source_tables, target_tables, seed):
     batch = 4 if any(item[3] is not None for item in items) else 8
-    left, _, source_heights, source_halves = source_tables
-    _, right, heights, halves = target_tables
+    left, source_heights, source_halves = source_tables
+    right, heights, halves = target_tables
     return pl.pallas_call(
         functools.partial(near_kernel, items, batch),
         out_shape=jax.ShapeDtypeStruct(seed.shape, f32),
         in_specs=[vmem] * 8,
         out_specs=vmem,
-        scratch_shapes=[
-            pltpu.VMEM((ring, batch, points, 2 * points), f32),
-            pltpu.VMEM((ring, batch, points, points), f32),
-            pltpu.VMEM((ring, batch, 2, points, points), bf16),
-        ],
+        scratch_shapes=near_scratch(batch),
         compiler_params=params(24),
         cost_estimate=cost(len(items) * 110),
         name="near",
@@ -407,7 +400,7 @@
         out_shape=out_shape,
         in_specs=[pl.BlockSpec(memory_space=pltpu.HBM)] * len(operands),
         out_specs=(vmem,) * len(out_shape),
-        scratch_shapes=scratch + [pltpu.SemaphoreType.DMA((len(operands),))],
+        scratch_shapes=scratch + [pltpu.SemaphoreType.DMA((8,))],
         compiler_params=params(24),
         cost_estimate=cost(2000),
         name=name,
@@ -415,32 +408,35 @@
 
 
 def tables_call(body, name, count, scratch, *operands):
+    shapes = table_shapes(count)
     return pl.pallas_call(
         body,
-        out_shape=table_shapes(count),
+        out_shape=(shapes[0], shapes[2], shapes[3]),
         in_specs=[vmem] * len(operands),
-        out_specs=(vmem,) * 4,
-        scratch_shapes=[pltpu.VMEM((3, count * 16, points), f32)] + scratch,
+        out_specs=(vmem,) * 3,
+        scratch_shapes=[pltpu.VMEM(shape, f32) for shape in [(1, count * 16, points)] + scratch],
         compiler_params=params(16),
         cost_estimate=cost(1000),
         name=name,
     )(*operands)
 
 
+def outward(block, axis):
+    size = lax.axis_size(axis)
+    return lax.ppermute(block, axis, [(i, i + 1 if i % 2 else i - 1) for i in range(1, size - 1)])
+
+
 def shards(coords, sources, neighbour_mask, compress, expand, row_transfer, col_transfer):
     coords = coords.reshape(-1, points)
     sources = sources.reshape(-1, points)
-    halves, payload = far_call(
+    halves, payload, outer = far_call(
         compress_kernel,
         "compress",
-        (table_shapes(leaves)[3], array(points + 2 * edge_rows, points)),
+        (table_shapes(leaves)[3], array(points + edge_rows, points), array(edge_rows, points)),
         [pltpu.VMEM(shape, f32) for shape in ((3 * leaves, points), (rhs * leaves, points), (leaves * rank, points))],
         coords, sources, compress.reshape(-1, points),
     )
-    row_bits, col_bits = (lax.axis_size(axis).bit_length() - 1 for axis in ("row", "col"))
-    axes = ["row"] * row_bits + ["col"] * col_bits
-    bits = [*range(row_bits), *range(col_bits)]
-    theirs = partner_of(payload, "row", 0)
+    facing_row = partner_of(payload, "row", 0)
     block_shape = jax.ShapeDtypeStruct((4, points, points), bf16)
     coords_later, payload = lax.optimization_barrier((coords, payload))
     left, right, heights, row_blocks, col_blocks, weights = pl.pallas_call(
@@ -453,45 +449,67 @@
         cost_estimate=cost(2000),
         name="prep",
     )(coords_later, neighbour_mask, row_transfer[:, 0, 0], col_transfer[:, 0, 0])
-    own = left, right, heights, halves
+    own, targets = (left, heights, halves), (right, heights, halves)
+    acc = jnp.zeros((leaves * rhs, points), f32)
+    facing_row, acc, outer, weights = lax.optimization_barrier((facing_row, acc, outer, weights))
+
     inner, edge, side = interior_runs(), edge_runs(), side_runs()
-    counts = [sum(run.count for run in runs) for runs in (inner, edge, side)]
-    windows = row_bits + col_bits - 1
-    edge_windows = (row_bits, row_bits + 2)
-    inner_windows = [n for n in range(1, windows + 1) if n not in edge_windows]
-    cuts = [counts[0] * k // len(inner_windows) // 4 * 4 for k in range(len(inner_windows))] + [counts[0]]
-    half = -(-counts[1] // 2 // 8) * 8
-    acc = jnp.zeros((leaves * rhs, points), f32)
-    received = [theirs]
-    for n, (axis, bit) in enumerate(zip(axes, bits)):
-        blocks = row_blocks if axis == "row" else col_blocks
-        if n > 0:
-            theirs = partner_of(payload, axis, bit)
-            payload, acc = lax.optimization_barrier((payload, acc))
-            if n == row_bits:
-                edges, acc = lax.optimization_barrier((edges, acc))
-                edge_tables = tables_call(edges_kernel, "edges", edge_leaves, [], coords, edges)
-            if n in edge_windows:
-                some = cut_runs(edge, 0, half) if n == row_bits else cut_runs(edge, half, counts[1])
-                acc = near_piece(some, weights, edge_tables, own, acc)
-            else:
-                k = inner_windows.index(n)
-                acc = near_piece(cut_runs(inner, cuts[k], cuts[k + 1]), weights, own, own, acc)
-            theirs, acc = lax.optimization_barrier((theirs, acc))
-            received.append(theirs)
-        if n == row_bits - 1:
-            payload, edges = small_call(
-                turn_kernel,
-                "turn",
-                (array(points + 2 * side_rows, points), array((3 + rhs) * edge_leaves, points)),
-                payload, theirs, blocks, coords, sources, received[0], received[1],
-            )
-        elif n < windows:
-            rows = edge_rows if axis == "row" else side_rows
-            skip = points + rows if bit == 0 else points
-            payload = small_call(functools.partial(level_kernel, skip), "level", array(points + rows, points), payload, theirs, blocks)
-    side_tables = tables_call(sides_kernel, "sides", side_leaves, [pltpu.VMEM(((3 + rhs) * side_leaves, points), f32)], coords, *received[row_bits:])
-    acc = near_piece(cut_runs(side, 0, counts[2]), weights, side_tables, own, acc)
+    taken = {"inner": 0, "edge": 0, "side": 0}
+
+    def some(kind, count):
+        runs = {"inner": inner, "edge": edge, "side": side}[kind]
+        first = taken[kind]
+        taken[kind] = min(first + count, sum(run.count for run in runs))
+        return listed(cut_runs(runs, first, taken[kind]))
+
+    def window(sent, arriving, acc, *work):
+        sent, acc = lax.optimization_barrier((sent, acc))
+        for make, kind, count in work:
+            acc = near_piece(some(kind, count), weights, make(acc), targets, acc)
+        arriving, acc = lax.optimization_barrier((arriving, acc))
+        return sent, arriving, acc
+
+    def mine(acc):
+        return own
+
+    def next_level(payload, theirs, blocks):
+        return small_call(level_kernel, "level", array(points, points), payload, theirs, blocks)
+
+    outer, beyond_row, acc = window(outer, outward(outer, "row"), acc, (mine, "inner", 36))
+    facing_row, beyond_row = lax.optimization_barrier((facing_row, beyond_row))
+    payload = next_level(payload, facing_row, row_blocks)
+    for bit, count in ((1, 52), (2, 60)):
+        payload, theirs, acc = window(payload, partner_of(payload, "row", bit), acc, (mine, "inner", count))
+        if bit == 1:
+            payload = next_level(payload, theirs, row_blocks)
+    payload, outer, edges = small_call(
+        turn_kernel,
+        "turn",
+        (array(points + side_rows, points), array(side_rows, points), array((3 + rhs) * edge_leaves, points)),
+        payload, theirs, row_blocks, coords, sources, facing_row, beyond_row,
+    )
+    tables = {}
+
+    def around(acc):
+        if "edge" not in tables:
+            values, _ = lax.optimization_barrier((edges, acc))
+            tables["edge"] = tables_call(edges_kernel, "edges", edge_leaves, [], coords, values)
+        return tables["edge"]
+
+    def beside(acc):
+        values, _ = lax.optimization_barrier((beyond_col, acc))
+        return tables_call(sides_kernel, "sides", side_leaves, [((3 + rhs) * side_leaves, points)], coords, facing_col, values)
+
+    payload, facing_col, acc = window(payload, partner_of(payload, "col", 0), acc, (around, "edge", 48))
+    outer, acc = lax.optimization_barrier((outer, acc))
+    outer, beyond_col, acc = window(outer, outward(outer, "col"), acc, (mine, "inner", 36))
+    facing_col, beyond_col = lax.optimization_barrier((facing_col, beyond_col))
+    payload = next_level(payload, facing_col, col_blocks)
+    works = {1: ((around, "edge", 48),), 2: ((beside, "side", 24), (mine, "inner", 16)), 3: ((mine, "inner", leaves * 9),)}
+    for bit in range(1, lax.axis_size("col").bit_length() - 1):
+        payload, theirs, acc = window(payload, partner_of(payload, "col", bit), acc, *works[bit])
+        if bit < max(works):
+            payload = next_level(payload, theirs, col_blocks)
     out = pl.pallas_call(
         finish_kernel,
         out_shape=array(rhs * leaves, points),
@@ -500,7 +518,7 @@
         compiler_params=params(16),
         cost_estimate=cost(2000),
         name="finish",
-    )(payload, theirs, blocks, expand.reshape(-1, points), acc)
+    )(payload, theirs, col_blocks, expand.reshape(-1, points), acc)
     return out.reshape(rhs, leaf_rows, leaf_cols, points)
 
 

time: 50 us -> 56.4 us (1.13)
  starting transfers between devices: 15.9 us -> 23.3 us
  waiting for transfers between devices: 1.01 us -> 0.35 us
    ppermute x7, starting transfers between devices: 15.9 us -> 22 us  [partner_of(): return lax.ppermute(block, axis, route)]
    ppermute x0 -> x2, starting transfers between devices: none -> 1.32 us  [outward(): lax.ppermute(block, axis, [(i, i + 1 if i % 2 else i - 1) for i in range(...]
    pallas_call x2, Pallas kernels: 2 us -> 0.75 us  [tables_call(): pl.pallas_call(body, out_shape=(shapes[0], shapes[2], shapes[3]), in_spec...]
    pallas_call x7 -> x9, Pallas kernels: 25.1 us -> 25.9 us  [near_piece(): pl.pallas_call(functools.partial(near_kernel, items, batch), out_shape=ja...]
    ppermute x7, waiting for transfers between devices: 1.01 us -> 0.34 us  [partner_of(): return lax.ppermute(block, axis, route)]
  transfers between devices with their start and end apart: 7 -> 9, of which waited for: 3 -> 1; matrix products, arithmetic and copies ran while one was open for 0% -> 0% of each run, Pallas kernels for 51% -> 49%
where the time goes in v11:
time: 56.4 us; the launch traced here: 56.3 us
  Pallas kernels  32.3 us (57%)
  starting transfers between devices  23.3 us (41%)
    pallas_call x9, Pallas kernels, near_piece(): pl.pallas_call(functools.partial(near_kernel, items, batch), out_shape=ja...  25.9 us
    ppermute x7, starting transfers between devices, partner_of(): return lax.ppermute(block, axis, route)  22 us
    pallas_call x1, Pallas kernels, far_call(): pl.pallas_call(body, out_shape=out_shape, in_specs=[pl.BlockSpec(memory_s...  1.94 us
    pallas_call x6, Pallas kernels, small_call(): pl.pallas_call(body, out_shape=out_shape, in_specs=[vmem] * len(operands)...  1.48 us
    ppermute x2, starting transfers between devices, outward(): lax.ppermute(block, axis, [(i, i + 1 if i % 2 else i - 1) for i in range(...  1.32 us
    pallas_call x1, Pallas kernels, shards(): pl.pallas_call(finish_kernel, out_shape=array(rhs * leaves, points), in_s...  1.26 us
  transfers between devices with their start and end apart: 9, of which 1 were waited for; matrix products, arithmetic and copies ran while one was open for 0% of the time, Pallas kernels for 49%

profile of v11, /device:TPU:0, one launch (start us, length us, event | category | flops | bytes accessed | tf_op | source)
XLA Modules:
  0.0 56.3 jit_solution(8416954903165414120)
XLA Ops:
  0.0 0.0 copy-start.2
  0.0 0.0 copy-start.4
  0.0 0.0 copy-start.3
  0.0 0.0 copy-start.5
  0.0 1.9 %compress.1 = (bf16[1024,128]{1,0:T(8,128)(2,1)S(1)}, f32[304,128]{1,0:T(8,128)S(1)}, f32[176,128]{1,0:T(8,128)S(1)}) custom-call(f32[192,128]{1,0:T(8,128)} %bitcast.10, f32[512,128]{1,0:T(8,128)} %bitcast.8, f32[2048,128]{1,0:T(8,128)} %bitcast.17), custom_call_target="tpu_custom_call" | custom-call | flops 800000000 | bytes 262144 | tf_op jit(solution)/shard_map/compress/pallas_call | solution.py:398
  2.0 0.1 collective-permute-start
  2.1 0.0 copy-done.2
  2.1 0.0 copy-done.4
  2.1 0.0 copy-done.3
  2.1 0.0 copy-done.5
  2.1 1.0 %prep.1 = (bf16[8192,16]{1,0:T(8,128)(2,1)S(1)}, bf16[1024,256]{1,0:T(8,128)(2,1)S(1)}, f32[64,128]{1,0:T(8,128)S(1)}, bf16[4,128,128]{2,1,0:T(8,128)(2,1)S(1)},...) custom-call(f32[192,128]{1,0:T(8,128)S(1)} %bitcast.11, s32[9,4,16]{2,1,0:T(4,128)S(1)} %copy-done.5, ...), custom_call_target="tpu_custom_call" | custom-call | flops 800000000 | bytes 262144 | tf_op jit(solution)/shard_map/prep/pallas_call | solution.py:442
  3.1 0.3 collective-permute-done.theirs.facing
  3.4 0.7 %collective-permute-start.1 = (f32[176,128]{1,0:T(8,128)S(1)}, f32[176,128]{1,0:T(8,128)S(1)}, u32[]{:S(2)}, u32[]{:S(2)}) collective-permute-start(f32[176,128]{1,0:T(8,128)S(1)} %get-tuple-element.73), channel_id=1, source_target_pairs={{16,32},{32,16},{48,64},{64,48},{80,96},{96,80},{17,33},{33,17},{4... | collective-permute-start | bytes 270344 | tf_op jit(solution)/shard_map/ppermute | solution.py:426
  4.1 2.4 %near.9.seed = f32[512,128]{1,0:T(8,128)S(1)} custom-call(f32[584,128]{1,0:T(8,128)S(1)} %get-tuple-element.74.weights, bf16[8192,16]{1,0:T(8,128)(2,1)S(1)} %get-tuple-element.75.left, f32[64,128]{1,0:T(8,128)S(1)} %get-tuple-element.76.source_heights.heights, bf16[1024,128]{1,0:T(8,128)(2,1)S(1)} %get-tuple-element.77.source_halves.halves, ...), custom_call_target="tpu_custom_call" | custom-call | flops 1584000000 | bytes 262144 | tf_op jit(solution)/shard_map/near/pallas_call | solution.py:338
  6.5 0.0 collective-permute-done.1.beyond
  6.5 0.2 level.5.mine
  6.8 4.5 %collective-permute-start.2 = (f32[128,128]{1,0:T(8,128)S(1)}, f32[128,128]{1,0:T(8,128)S(1)}, u32[]{:S(2)}, u32[]{:S(2)}) collective-permute-start(f32[128,128]{1,0:T(8,128)S(1)} %level.5.mine), channel_id=1, source_target_pairs={{0,32},{16,48},{32,0},{48,16},{64,96},{80,112},{96,64},{112,80},{1... | collective-permute-start | bytes 196616 | tf_op jit(solution)/shard_map/ppermute | solution.py:377
  11.3 3.7 %near.10.seed = f32[512,128]{1,0:T(8,128)S(1)} custom-call(f32[584,128]{1,0:T(8,128)S(1)} %get-tuple-element.74.weights, bf16[8192,16]{1,0:T(8,128)(2,1)S(1)} %get-tuple-element.75.left, f32[64,128]{1,0:T(8,128)S(1)} %get-tuple-element.76.source_heights.heights, bf16[1024,128]{1,0:T(8,128)(2,1)S(1)} %get-tuple-element.77.source_halves.halves, ...), custom_call_target="tpu_custom_call" | custom-call | flops 2288000000 | bytes 262144 | tf_op jit(solution)/shard_map/near/pallas_call | solution.py:338
  14.9 0.0 collective-permute-done.2.theirs
  15.0 0.3 level.6.mine
  15.2 0.0 copy-start.1
  15.2 3.2 %collective-permute-start.3 = (f32[128,128]{1,0:T(8,128)S(1)}, f32[128,128]{1,0:T(8,128)S(1)}, u32[]{:S(2)}, u32[]{:S(2)}) collective-permute-start(f32[128,128]{1,0:T(8,128)S(1)} %level.6.mine), channel_id=1, source_target_pairs={{0,64},{16,80},{32,96},{48,112},{64,0},{80,16},{96,32},{112,48},{1... | collective-permute-start | bytes 196616 | tf_op jit(solution)/shard_map/ppermute | solution.py:377
  18.4 4.0 %near.11.seed = f32[512,128]{1,0:T(8,128)S(1)} custom-call(f32[584,128]{1,0:T(8,128)S(1)} %get-tuple-element.74.weights, bf16[8192,16]{1,0:T(8,128)(2,1)S(1)} %get-tuple-element.75.left, f32[64,128]{1,0:T(8,128)S(1)} %get-tuple-element.76.source_heights.heights, bf16[1024,128]{1,0:T(8,128)(2,1)S(1)} %get-tuple-element.77.source_halves.halves, ...), custom_call_target="tpu_custom_call" | custom-call | flops 2640000000 | bytes 262144 | tf_op jit(solution)/shard_map/near/pallas_call | solution.py:338
  22.4 0.0 collective-permute-done.3.theirs
  22.4 0.0 copy-done.1
  22.4 0.2 turn.1
  22.7 2.0 %collective-permute-start.4 = (f32[200,128]{1,0:T(8,128)S(1)}, f32[200,128]{1,0:T(8,128)S(1)}, u32[]{:S(2)}, u32[]{:S(2)}) collective-permute-start(f32[200,128]{1,0:T(8,128)S(1)} %get-tuple-element.95.mine), channel_id=1, source_target_pairs={{0,1},{1,0},{2,3},{3,2},{4,5},{5,4},{6,7},{7,6},{8,9},{9,8},{10,11... | collective-permute-start | bytes 307208 | tf_op jit(solution)/shard_map/ppermute | solution.py:377
  24.7 0.5 edges.1
  25.2 3.1 %near.12.seed = f32[512,128]{1,0:T(8,128)S(1)} custom-call(f32[584,128]{1,0:T(8,128)S(1)} %get-tuple-element.74.weights, bf16[4096,16]{1,0:T(8,128)(2,1)S(1)} %get-tuple-element.99.left, f32[32,128]{1,0:T(8,128)S(1)} %get-tuple-element.100.source_heights, bf16[512,128]{1,0:T(8,128)(2,1)S(1)} %get-tuple-element.101.source_halves, ...), custom_call_target="tpu_custom_call" | custom-call | flops 2112000000 | bytes 262144 | tf_op jit(solution)/shard_map/near/pallas_call | solution.py:338
  28.3 0.0 collective-permute-done.4.theirs.facing
  28.3 0.7 %collective-permute-start.5 = (f32[72,128]{1,0:T(8,128)S(1)}, f32[72,128]{1,0:T(8,128)S(1)}, u32[]{:S(2)}, u32[]{:S(2)}) collective-permute-start(f32[72,128]{1,0:T(8,128)S(1)} %get-tuple-element.105), channel_id=1, source_target_pairs={{1,2},{2,1},{3,4},{4,3},{5,6},{6,5},{7,8},{8,7},{9,10},{10,9},{11,... | collective-permute-start | bytes 110600 | tf_op jit(solution)/shard_map/ppermute | solution.py:426
  29.0 2.5 %near.13.seed = f32[512,128]{1,0:T(8,128)S(1)} custom-call(f32[584,128]{1,0:T(8,128)S(1)} %get-tuple-element.74.weights, bf16[8192,16]{1,0:T(8,128)(2,1)S(1)} %get-tuple-element.75.left, f32[64,128]{1,0:T(8,128)S(1)} %get-tuple-element.76.source_heights.heights, bf16[1024,128]{1,0:T(8,128)(2,1)S(1)} %get-tuple-element.77.source_halves.halves, ...), custom_call_target="tpu_custom_call" | custom-call | flops 1584000000 | bytes 262144 | tf_op jit(solution)/shard_map/near/pallas_call | solution.py:338
  31.5 0.0 collective-permute-done.5.beyond
  31.5 0.2 level.7.mine
  31.8 6.5 %collective-permute-start.6 = (f32[128,128]{1,0:T(8,128)S(1)}, f32[128,128]{1,0:T(8,128)S(1)}, u32[]{:S(2)}, u32[]{:S(2)}) collective-permute-start(f32[128,128]{1,0:T(8,128)S(1)} %level.7.mine), channel_id=1, source_target_pairs={{0,2},{1,3},{2,0},{3,1},{4,6},{5,7},{6,4},{7,5},{8,10},{9,11},{10,... | collective-permute-start | bytes 196616 | tf_op jit(solution)/shard_map/ppermute | solution.py:377
  38.3 2.9 %near.14.seed = f32[512,128]{1,0:T(8,128)S(1)} custom-call(f32[584,128]{1,0:T(8,128)S(1)} %get-tuple-element.74.weights, bf16[4096,16]{1,0:T(8,128)(2,1)S(1)} %get-tuple-element.99.left, f32[32,128]{1,0:T(8,128)S(1)} %get-tuple-element.100.source_heights, bf16[512,128]{1,0:T(8,128)(2,1)S(1)} %get-tuple-element.101.source_halves, ...), custom_call_target="tpu_custom_call" | custom-call | flops 1936000000 | bytes 262144 | tf_op jit(solution)/shard_map/near/pallas_call | solution.py:338
  41.2 0.0 collective-permute-done.6.theirs
  41.2 0.2 level.8.mine
  41.4 3.0 %collective-permute-start.7 = (f32[128,128]{1,0:T(8,128)S(1)}, f32[128,128]{1,0:T(8,128)S(1)}, u32[]{:S(2)}, u32[]{:S(2)}) collective-permute-start(f32[128,128]{1,0:T(8,128)S(1)} %level.8.mine), channel_id=1, source_target_pairs={{0,4},{1,5},{2,6},{3,7},{4,0},{5,1},{6,2},{7,3},{8,12},{9,13},{10,... | collective-permute-start | bytes 196616 | tf_op jit(solution)/shard_map/ppermute | solution.py:377
  44.4 0.3 sides.1
  44.7 1.7 %near.15.seed = f32[512,128]{1,0:T(8,128)S(1)} custom-call(f32[584,128]{1,0:T(8,128)S(1)} %get-tuple-element.74.weights, bf16[2048,16]{1,0:T(8,128)(2,1)S(1)} %get-tuple-element.119.left, f32[16,128]{1,0:T(8,128)S(1)} %get-tuple-element.120.source_heights, bf16[256,128]{1,0:T(8,128)(2,1)S(1)} %get-tuple-element.121.source_halves, ...), custom_call_target="tpu_custom_call" | custom-call | flops 1056000000 | bytes 262144 | tf_op jit(solution)/shard_map/near/pallas_call | solution.py:338
  46.4 1.3 %near.16.seed = f32[512,128]{1,0:T(8,128)S(1)} custom-call(f32[584,128]{1,0:T(8,128)S(1)} %get-tuple-element.74.weights, bf16[8192,16]{1,0:T(8,128)(2,1)S(1)} %get-tuple-element.75.left, f32[64,128]{1,0:T(8,128)S(1)} %get-tuple-element.76.source_heights.heights, bf16[1024,128]{1,0:T(8,128)(2,1)S(1)} %get-tuple-element.77.source_halves.halves, ...), custom_call_target="tpu_custom_call" | custom-call | flops 704000000 | bytes 262144 | tf_op jit(solution)/shard_map/near/pallas_call | solution.py:338
  47.7 0.0 collective-permute-done.7.theirs
  47.7 0.3 level.9.mine
  47.9 0.0 copy-start
  47.9 2.8 %collective-permute-start.8 = (f32[128,128]{1,0:T(8,128)S(1)}, f32[128,128]{1,0:T(8,128)S(1)}, u32[]{:S(2)}, u32[]{:S(2)}) collective-permute-start(f32[128,128]{1,0:T(8,128)S(1)} %level.9.mine), channel_id=1, source_target_pairs={{0,8},{1,9},{2,10},{3,11},{4,12},{5,13},{6,14},{7,15},{8,0},{9,1},... | collective-permute-start | bytes 196616 | tf_op jit(solution)/shard_map/ppermute | solution.py:377
  50.8 4.2 %near.17.acc = f32[512,128]{1,0:T(8,128)S(1)} custom-call(f32[584,128]{1,0:T(8,128)S(1)} %get-tuple-element.74.weights, bf16[8192,16]{1,0:T(8,128)(2,1)S(1)} %get-tuple-element.75.left, f32[64,128]{1,0:T(8,128)S(1)} %get-tuple-element.76.source_heights.heights, bf16[1024,128]{1,0:T(8,128)(2,1)S(1)} %get-tuple-element.77.source_halves.halves, ...), custom_call_target="tpu_custom_call" | custom-call | flops 2728000000 | bytes 262144 | tf_op jit(solution)/shard_map/near/pallas_call | solution.py:338
  55.0 0.0 collective-permute-done.8.theirs
  55.0 0.0 copy-done
  55.0 1.3 %finish.1 = f32[512,128]{1,0:T(8,128)} custom-call(f32[128,128]{1,0:T(8,128)S(1)} %level.9.mine, f32[128,128]{1,0:T(8,128)S(1)} %collective-permute-done.8.theirs, bf16[4,128,128]{2,1,0:T(8,128)(2,1)S(1)} %get-tuple-element.109.blocks, f32[2048,128]{1,0:T(8,128)S(1)} %bitcast.7, f32[512,128]{1,0:T(8,128)S(1)} %near.17.acc), custom_call_target="tpu_custom_call" | custom-call | flops 800000000 | bytes 262144 | tf_op jit(solution)/shard_map/finish/pallas_call | solution.py:513
  (1 shorter events, 0.0 us)
Async XLA Ops:
  0.0 2.1 %copy-start.2 = (f32[3,4,16,128]{3,2,1,0:T(8,128)S(1)}, f32[3,4,16,128]{3,2,1,0:T(8,128)}, u32[]{:S(2)}) copy-start(f32[3,4,16,128]{3,2,1,0:T(8,128)} %param.7) | copy-start | bytes 294916
  0.0 2.1 %copy-start.4 = (f32[2,1,1,32,32]{4,3,2,1,0:T(8,128)S(1)}, f32[2,1,1,32,32]{4,3,2,1,0:T(8,128)}, u32[]{:S(2)}) copy-start(f32[2,1,1,32,32]{4,3,2,1,0:T(8,128)} %param.13) | copy-start | bytes 24580
  0.0 2.1 %copy-start.3 = (f32[2,1,1,32,32]{4,3,2,1,0:T(8,128)S(1)}, f32[2,1,1,32,32]{4,3,2,1,0:T(8,128)}, u32[]{:S(2)}) copy-start(f32[2,1,1,32,32]{4,3,2,1,0:T(8,128)} %param.12) | copy-start | bytes 24580
  0.0 2.1 %copy-start.5 = (s32[9,4,16]{2,1,0:T(4,128)S(1)}, s32[9,4,16]{2,1,0:T(4,128)}, u32[]{:S(2)}) copy-start(s32[9,4,16]{2,1,0:T(4,128)} %mask.1) | copy-start | bytes 6916
  2.0 1.5 %collective-permute-start = (f32[304,128]{1,0:T(8,128)S(1)}, f32[304,128]{1,0:T(8,128)S(1)}, u32[]{:S(2)}, u32[]{:S(2)}) collective-permute-start(f32[304,128]{1,0:T(8,128)S(1)} %get-tuple-element.68.mine), channel_id=1, source_target_pairs={{0,16},{16,0},{32,48},{48,32},{64,80},{80,64},{96,112},{112,96},{1... | collective-permute-start | bytes 466952 | tf_op jit(solution)/shard_map/ppermute | solution.py:377
  3.4 3.1 %collective-permute-start.1 = (f32[176,128]{1,0:T(8,128)S(1)}, f32[176,128]{1,0:T(8,128)S(1)}, u32[]{:S(2)}, u32[]{:S(2)}) collective-permute-start(f32[176,128]{1,0:T(8,128)S(1)} %get-tuple-element.73), channel_id=1, source_target_pairs={{16,32},{32,16},{48,64},{64,48},{80,96},{96,80},{17,33},{33,17},{4... | collective-permute-start | bytes 270344 | tf_op jit(solution)/shard_map/ppermute | solution.py:426
  6.8 8.2 %collective-permute-start.2 = (f32[128,128]{1,0:T(8,128)S(1)}, f32[128,128]{1,0:T(8,128)S(1)}, u32[]{:S(2)}, u32[]{:S(2)}) collective-permute-start(f32[128,128]{1,0:T(8,128)S(1)} %level.5.mine), channel_id=1, source_target_pairs={{0,32},{16,48},{32,0},{48,16},{64,96},{80,112},{96,64},{112,80},{1... | collective-permute-start | bytes 196616 | tf_op jit(solution)/shard_map/ppermute | solution.py:377
  15.2 7.2 %copy-start.1 = (f32[8,4,16,128]{3,2,1,0:T(8,128)S(1)}, f32[8,4,16,128]{3,2,1,0:T(8,128)}, u32[]{:S(2)}) copy-start(f32[8,4,16,128]{3,2,1,0:T(8,128)} %param.8) | copy-start | bytes 786436
  15.2 7.2 %collective-permute-start.3 = (f32[128,128]{1,0:T(8,128)S(1)}, f32[128,128]{1,0:T(8,128)S(1)}, u32[]{:S(2)}, u32[]{:S(2)}) collective-permute-start(f32[128,128]{1,0:T(8,128)S(1)} %level.6.mine), channel_id=1, source_target_pairs={{0,64},{16,80},{32,96},{48,112},{64,0},{80,16},{96,32},{112,48},{1... | collective-permute-start | bytes 196616 | tf_op jit(solution)/shard_map/ppermute | solution.py:377
  22.7 5.6 %collective-permute-start.4 = (f32[200,128]{1,0:T(8,128)S(1)}, f32[200,128]{1,0:T(8,128)S(1)}, u32[]{:S(2)}, u32[]{:S(2)}) collective-permute-start(f32[200,128]{1,0:T(8,128)S(1)} %get-tuple-element.95.mine), channel_id=1, source_target_pairs={{0,1},{1,0},{2,3},{3,2},{4,5},{5,4},{6,7},{7,6},{8,9},{9,8},{10,11... | collective-permute-start | bytes 307208 | tf_op jit(solution)/shard_map/ppermute | solution.py:377
  28.3 3.2 %collective-permute-start.5 = (f32[72,128]{1,0:T(8,128)S(1)}, f32[72,128]{1,0:T(8,128)S(1)}, u32[]{:S(2)}, u32[]{:S(2)}) collective-permute-start(f32[72,128]{1,0:T(8,128)S(1)} %get-tuple-element.105), channel_id=1, source_target_pairs={{1,2},{2,1},{3,4},{4,3},{5,6},{6,5},{7,8},{8,7},{9,10},{10,9},{11,... | collective-permute-start | bytes 110600 | tf_op jit(solution)/shard_map/ppermute | solution.py:426
  31.8 9.4 %collective-permute-start.6 = (f32[128,128]{1,0:T(8,128)S(1)}, f32[128,128]{1,0:T(8,128)S(1)}, u32[]{:S(2)}, u32[]{:S(2)}) collective-permute-start(f32[128,128]{1,0:T(8,128)S(1)} %level.7.mine), channel_id=1, source_target_pairs={{0,2},{1,3},{2,0},{3,1},{4,6},{5,7},{6,4},{7,5},{8,10},{9,11},{10,... | collective-permute-start | bytes 196616 | tf_op jit(solution)/shard_map/ppermute | solution.py:377
  41.4 6.2 %collective-permute-start.7 = (f32[128,128]{1,0:T(8,128)S(1)}, f32[128,128]{1,0:T(8,128)S(1)}, u32[]{:S(2)}, u32[]{:S(2)}) collective-permute-start(f32[128,128]{1,0:T(8,128)S(1)} %level.8.mine), channel_id=1, source_target_pairs={{0,4},{1,5},{2,6},{3,7},{4,0},{5,1},{6,2},{7,3},{8,12},{9,13},{10,... | collective-permute-start | bytes 196616 | tf_op jit(solution)/shard_map/ppermute | solution.py:377
  47.9 7.1 %copy-start = (f32[4,16,32,128]{3,2,1,0:T(8,128)S(1)}, f32[4,16,32,128]{3,2,1,0:T(8,128)}, u32[]{:S(2)}) copy-start(f32[4,16,32,128]{3,2,1,0:T(8,128)} %param.11) | copy-start | bytes 3145732
  47.9 7.0 %collective-permute-start.8 = (f32[128,128]{1,0:T(8,128)S(1)}, f32[128,128]{1,0:T(8,128)S(1)}, u32[]{:S(2)}, u32[]{:S(2)}) collective-permute-start(f32[128,128]{1,0:T(8,128)S(1)} %level.9.mine), channel_id=1, source_target_pairs={{0,8},{1,9},{2,10},{3,11},{4,12},{5,13},{6,14},{7,15},{8,0},{9,1},... | collective-permute-start | bytes 196616 | tf_op jit(solution)/shard_map/ppermute | solution.py:377

commit v12 on v9

--- a/solution.py
+++ b/solution.py
@@ -130,22 +130,23 @@
         moved = (coords[pl.ds(c * count, count), :] - start[c]) * turns
         if c == 2:
             heights[...] = moved
-        else:
-            parts.append(thirds(moved))
+        parts.append(thirds(moved))
     k = lax.broadcasted_iota(jnp.int32, (16, points), 0)
     ones_x = jnp.where(k < 3, 1.0, 0.0)
     ones_y = jnp.where((k >= 3) & (k < 6), 1.0, 0.0)
     ones_t = jnp.where((k >= 6) & (k < 9), 1.0, 0.0)
-    for role in range(1 if right is None else 3):
+    ones_z = jnp.where((k >= 9) & (k < 12), 1.0, 0.0)
+    base = (0, 3, 9)
+    for role in range(1 if right is None else 4):
         wide = wides.at[role]
         for leaf in range(count):
-            wide[pl.ds(leaf * 16, 16), :] = (ones_t, ones_x, ones_y)[role]
+            wide[pl.ds(leaf * 16, 16), :] = (ones_t, ones_x, ones_y, ones_z)[role]
         for first in range(0, count, 8):
             for m in range(3):
-                for c in range(2):
+                for c in range(3):
                     part = parts[c][m][first : first + 8]
                     if role == 0:
-                        wide[pl.ds(first * 16 + 3 * c + m, 8, stride=16), :] = part
+                        wide[pl.ds(first * 16 + base[c] + m, 8, stride=16), :] = part
                     elif role == c + 1:
                         wide[pl.ds(first * 16 + 6 + m, 8, stride=16), :] = -part
         if role == 0:
@@ -175,11 +176,7 @@
 
 
 def compress_kernel(coords_far, sources_far, compress_far, halves, payload, coords, sources, compress, arrived):
-    chunk = groups // 4 * points
-    chunks = [slice(n * chunk, (n + 1) * chunk) for n in range(4)]
-    copies = start_copies(
-        [sources_far, coords_far] + [compress_far.at[rows] for rows in chunks], [sources, coords] + [compress.at[rows] for rows in chunks], arrived
-    )
+    copies = start_copies((sources_far, coords_far, compress_far), (sources, coords, compress), arrived)
     copies[0].wait()
     for leaf in range(leaves):
         high, low = split(sources[pl.ds(leaf, rhs, stride=leaves), :])
@@ -192,9 +189,8 @@
             ref, at = (coords, c) if c < 3 else (sources, c - 3)
             to = points + k * edge_rows + c * leaf_cols
             payload[to : to + leaf_cols, :] = ref[pl.ds(pl.multiple_of(at * leaves + row * leaf_cols, 8), leaf_cols), :]
+    copies[2].wait()
     for g in range(groups):
-        if g % (groups // 4) == 0:
-            copies[2 + g // (groups // 4)].wait()
         high, low = split(compress[g * points : (g + 1) * points, :])
         got = dot_t(halves[g * 16 * group : (g + 1) * 16 * group, :], jnp.concatenate([high, low], axis=0))
         got = got[:, :points] + got[:, points:]
@@ -290,17 +286,23 @@
 
 def near_kernel(items, batch, weights, left, source_heights, source_halves, right, heights, halves, seed, acc, gaps, splats, kerns):
     acc[...] = seed[...]
+    one_way = all(item[3] is None for item in items)
 
     def subtract(item, n, gap, splat):
         source, target = item[:2]
-        gap[n] = dot(left[source * points : (source + 1) * points, :], right[sixteen(target), :])
+        here = left[source * points : (source + 1) * points, :]
+        if one_way:
+            gap[n] = dot(here, right[sixteen(target), :])
+            return
+        gap[n, :, : 2 * points] = dot(here, right[sixteen(target), : 2 * points])
         splat[n] = jnp.broadcast_to(source_heights[source : source + 1, :], (points, points)).T
 
     def evaluate(item, n, gap, splat, kern):
         height = heights[item[1] : item[1] + 1, :]
         for g in range(points // 32):
             at_rows = slice(32 * g, 32 * g + 32)
-            dx, dy, dz = gap[n, at_rows, :points], gap[n, at_rows, points:], splat[n, at_rows] - height
+            dx, dy = gap[n, at_rows, :points], gap[n, at_rows, points : 2 * points]
+            dz = gap[n, at_rows, 2 * points :] if one_way else splat[n, at_rows] - height
             distance_sq = dx * dx + dy * dy + dz * dz
             safe = jnp.maximum(distance_sq, 1e-30)
             turn = safe * lax.rsqrt(safe)
@@ -340,7 +342,7 @@
 
 def near_scratch(batch):
     return [
-        pltpu.VMEM((ring, batch, points, 2 * points), f32),
+        pltpu.VMEM((ring, batch, points, 3 * points), f32),
         pltpu.VMEM((ring, batch, points, points), f32),
         pltpu.VMEM((ring, batch, 2, points, points), bf16),
     ]
@@ -387,7 +389,7 @@
 def table_shapes(count):
     return (
         jax.ShapeDtypeStruct((count * points, 16), bf16),
-        jax.ShapeDtypeStruct((count * 16, 2 * points), bf16),
+        jax.ShapeDtypeStruct((count * 16, 3 * points), bf16),
         jax.ShapeDtypeStruct((count, points), f32),
         jax.ShapeDtypeStruct((count * 16, points), bf16),
     )
@@ -449,7 +451,7 @@
         out_shape=table_shapes(leaves)[:3] + (block_shape, block_shape, array(zero_row + 8, points)),
         in_specs=[vmem] * 4,
         out_specs=(vmem,) * 6,
-        scratch_shapes=[pltpu.VMEM((3, leaves * 16, points), f32)],
+        scratch_shapes=[pltpu.VMEM((4, leaves * 16, points), f32)],
         compiler_params=params(16),
         cost_estimate=cost(2000),
         name="prep",

time: 48.8 us -> 48.6 us (level)
  transfers between devices with their start and end apart: 7 -> 7, of which waited for: 3 -> 3; matrix products, arithmetic and copies ran while one was open for 0% -> 0% of each run, Pallas kernels for 51% -> 52%
where the time goes in v12:
time: 48.6 us; the launch traced here: 48.5 us
  Pallas kernels  31.5 us (65%)
  starting transfers between devices  15.9 us (33%)
  waiting for transfers between devices  0.84 us (2%)
    pallas_call x6, Pallas kernels, near_piece(): pl.pallas_call(functools.partial(near_kernel, items, batch), out_shape=ja...  23.5 us
    ppermute x7, starting transfers between devices, partner_of(): return lax.ppermute(block, axis, route)  15.9 us
    pallas_call x1, Pallas kernels, shards(): pl.pallas_call(functools.partial(finish_kernel, listed(cut_runs(side, 0,...  2.92 us
    pallas_call x1, Pallas kernels, far_call(): pl.pallas_call(body, out_shape=out_shape, in_specs=[pl.BlockSpec(memory_s...  1.94 us
    pallas_call x6, Pallas kernels, small_call(): pl.pallas_call(body, out_shape=out_shape, in_specs=[vmem] * len(operands)...  1.47 us
    pallas_call x1, Pallas kernels, shards(): pl.pallas_call(prep_kernel, out_shape=table_shapes(leaves)[:3] + (block_s...  1.14 us
  transfers between devices with their start and end apart: 7, of which 3 were waited for; matrix products, arithmetic and copies ran while one was open for 0% of the time, Pallas kernels for 52%

profile of v12, /device:TPU:0, one launch (start us, length us, event | category | flops | bytes accessed | tf_op | source)
XLA Modules:
  0.0 48.5 jit_solution(16496390223463432968)
XLA Ops:
  0.0 0.0 copy-start.1
  0.0 0.0 copy-start.4
  0.0 0.0 copy-start.3
  0.0 0.0 copy-start.5
  0.0 1.9 %compress.1 = (bf16[1024,128]{1,0:T(8,128)(2,1)S(1)}, f32[480,128]{1,0:T(8,128)S(1)}) custom-call(f32[192,128]{1,0:T(8,128)} %bitcast.9, f32[512,128]{1,0:T(8,128)} %bitcast.7, f32[2048,128]{1,0:T(8,128)} %bitcast.17), custom_call_target="tpu_custom_call" | custom-call | flops 800000000 | bytes 262144 | tf_op jit(solution)/shard_map/compress/pallas_call | solution.py:421
  2.0 0.1 collective-permute-start
  2.1 0.0 copy-done.1
  2.1 0.0 copy-done.4
  2.1 0.0 copy-done.3
  2.1 0.0 copy-done.5
  2.1 1.1 %prep.1 = (bf16[8192,16]{1,0:T(8,128)(2,1)S(1)}, bf16[1024,384]{1,0:T(8,128)(2,1)S(1)}, f32[64,128]{1,0:T(8,128)S(1)}, bf16[4,128,128]{2,1,0:T(8,128)(2,1)S(1)},...) custom-call(f32[192,128]{1,0:T(8,128)S(1)} %bitcast.10, s32[9,4,16]{2,1,0:T(4,128)S(1)} %copy-done.5, ...), custom_call_target="tpu_custom_call" | custom-call | flops 800000000 | bytes 262144 | tf_op jit(solution)/shard_map/prep/pallas_call | solution.py:449
  3.2 0.3 collective-permute-done.theirs.first
  3.6 0.2 level.5.mine
  3.8 1.8 %collective-permute-start.1 = (f32[304,128]{1,0:T(8,128)S(1)}, f32[304,128]{1,0:T(8,128)S(1)}, u32[]{:S(2)}, u32[]{:S(2)}) collective-permute-start(f32[304,128]{1,0:T(8,128)S(1)} %level.5.mine), channel_id=1, source_target_pairs={{0,32},{16,48},{32,0},{48,16},{64,96},{80,112},{96,64},{112,80},{1... | collective-permute-start | bytes 466952 | tf_op jit(solution)/shard_map/ppermute | solution.py:400
  5.6 4.1 %near.6.seed = f32[512,128]{1,0:T(8,128)S(1)} custom-call(f32[584,128]{1,0:T(8,128)S(1)} %get-tuple-element.48.weights, bf16[8192,16]{1,0:T(8,128)(2,1)S(1)} %get-tuple-element.52.left, f32[64,128]{1,0:T(8,128)S(1)} %get-tuple-element.53.source_heights.heights, bf16[1024,128]{1,0:T(8,128)(2,1)S(1)} %get-tuple-element.54.source_halves.halves, ...), custom_call_target="tpu_custom_call" | custom-call | flops 2816000000 | bytes 262144 | tf_op jit(solution)/shard_map/near/pallas_call | solution.py:356
  9.7 0.3 collective-permute-done.1.theirs.second
  10.0 0.2 level.6.mine
  10.2 0.0 copy-start
  10.2 3.4 %collective-permute-start.2 = (f32[304,128]{1,0:T(8,128)S(1)}, f32[304,128]{1,0:T(8,128)S(1)}, u32[]{:S(2)}, u32[]{:S(2)}) collective-permute-start(f32[304,128]{1,0:T(8,128)S(1)} %level.6.mine), channel_id=1, source_target_pairs={{0,64},{16,80},{32,96},{48,112},{64,0},{80,16},{96,32},{112,48},{1... | collective-permute-start | bytes 466952 | tf_op jit(solution)/shard_map/ppermute | solution.py:400
  13.6 4.4 %near.7.seed = f32[512,128]{1,0:T(8,128)S(1)} custom-call(f32[584,128]{1,0:T(8,128)S(1)} %get-tuple-element.48.weights, bf16[8192,16]{1,0:T(8,128)(2,1)S(1)} %get-tuple-element.52.left, f32[64,128]{1,0:T(8,128)S(1)} %get-tuple-element.53.source_heights.heights, bf16[1024,128]{1,0:T(8,128)(2,1)S(1)} %get-tuple-element.54.source_halves.halves, ...), custom_call_target="tpu_custom_call" | custom-call | flops 2816000000 | bytes 262144 | tf_op jit(solution)/shard_map/near/pallas_call | solution.py:356
  18.0 0.0 collective-permute-done.2.theirs
  18.0 0.0 copy-done
  18.0 0.3 turn.1
  18.3 2.2 %collective-permute-start.3 = (f32[272,128]{1,0:T(8,128)S(1)}, f32[272,128]{1,0:T(8,128)S(1)}, u32[]{:S(2)}, u32[]{:S(2)}) collective-permute-start(f32[272,128]{1,0:T(8,128)S(1)} %get-tuple-element.72.mine), channel_id=1, source_target_pairs={{0,1},{1,0},{2,3},{3,2},{4,5},{5,4},{6,7},{7,6},{8,9},{9,8},{10,11... | collective-permute-start | bytes 417800 | tf_op jit(solution)/shard_map/ppermute | solution.py:400
  20.5 0.5 %edges.1 = (bf16[4096,16]{1,0:T(8,128)(2,1)S(1)}, f32[32,128]{1,0:T(8,128)S(1)}, bf16[512,128]{1,0:T(8,128)(2,1)S(1)}) custom-call(f32[192,128]{1,0:T(8,128)S(1)} %bitcast.12, f32[352,128]{1,0:T(8,128)S(1)} %get-tuple-element.66.edges), custom_call_target="tpu_custom_call" | custom-call | flops 400000000 | bytes 262144 | tf_op jit(solution)/shard_map/edges/pallas_call | solution.py:477
  21.0 3.1 %near.8.seed = f32[512,128]{1,0:T(8,128)S(1)} custom-call(f32[584,128]{1,0:T(8,128)S(1)} %get-tuple-element.48.weights, bf16[4096,16]{1,0:T(8,128)(2,1)S(1)} %get-tuple-element.67.left, f32[32,128]{1,0:T(8,128)S(1)} %get-tuple-element.68.source_heights, bf16[512,128]{1,0:T(8,128)(2,1)S(1)} %get-tuple-element.69.source_halves, ...), custom_call_target="tpu_custom_call" | custom-call | flops 2112000000 | bytes 262144 | tf_op jit(solution)/shard_map/near/pallas_call | solution.py:356
  24.1 0.0 collective-permute-done.3.theirs.first
  24.1 0.2 level.7.mine
  24.4 3.7 %collective-permute-start.4 = (f32[200,128]{1,0:T(8,128)S(1)}, f32[200,128]{1,0:T(8,128)S(1)}, u32[]{:S(2)}, u32[]{:S(2)}) collective-permute-start(f32[200,128]{1,0:T(8,128)S(1)} %level.7.mine), channel_id=1, source_target_pairs={{0,2},{1,3},{2,0},{3,1},{4,6},{5,7},{6,4},{7,5},{8,10},{9,11},{10,... | collective-permute-start | bytes 307208 | tf_op jit(solution)/shard_map/ppermute | solution.py:400
  28.0 4.5 %near.9.seed = f32[512,128]{1,0:T(8,128)S(1)} custom-call(f32[584,128]{1,0:T(8,128)S(1)} %get-tuple-element.48.weights, bf16[8192,16]{1,0:T(8,128)(2,1)S(1)} %get-tuple-element.52.left, f32[64,128]{1,0:T(8,128)S(1)} %get-tuple-element.53.source_heights.heights, bf16[1024,128]{1,0:T(8,128)(2,1)S(1)} %get-tuple-element.54.source_halves.halves, ...), custom_call_target="tpu_custom_call" | custom-call | flops 2992000000 | bytes 262144 | tf_op jit(solution)/shard_map/near/pallas_call | solution.py:356
  32.5 0.0 collective-permute-done.4.theirs.second
  32.5 0.2 level.8.mine
  32.8 1.6 %collective-permute-start.5 = (f32[200,128]{1,0:T(8,128)S(1)}, f32[200,128]{1,0:T(8,128)S(1)}, u32[]{:S(2)}, u32[]{:S(2)}) collective-permute-start(f32[200,128]{1,0:T(8,128)S(1)} %level.8.mine), channel_id=1, source_target_pairs={{0,4},{1,5},{2,6},{3,7},{4,0},{5,1},{6,2},{7,3},{8,12},{9,13},{10,... | collective-permute-start | bytes 307208 | tf_op jit(solution)/shard_map/ppermute | solution.py:400
  34.4 3.0 %near.10.seed = f32[512,128]{1,0:T(8,128)S(1)} custom-call(f32[584,128]{1,0:T(8,128)S(1)} %get-tuple-element.48.weights, bf16[4096,16]{1,0:T(8,128)(2,1)S(1)} %get-tuple-element.67.left, f32[32,128]{1,0:T(8,128)S(1)} %get-tuple-element.68.source_heights, bf16[512,128]{1,0:T(8,128)(2,1)S(1)} %get-tuple-element.69.source_halves, ...), custom_call_target="tpu_custom_call" | custom-call | flops 1936000000 | bytes 262144 | tf_op jit(solution)/shard_map/near/pallas_call | solution.py:356
  37.3 0.2 collective-permute-done.5.theirs.third
  37.5 0.2 level.9.mine
  37.8 0.0 copy-start.2
  37.8 3.3 %collective-permute-start.6 = (f32[200,128]{1,0:T(8,128)S(1)}, f32[200,128]{1,0:T(8,128)S(1)}, u32[]{:S(2)}, u32[]{:S(2)}) collective-permute-start(f32[200,128]{1,0:T(8,128)S(1)} %level.9.mine), channel_id=1, source_target_pairs={{0,8},{1,9},{2,10},{3,11},{4,12},{5,13},{6,14},{7,15},{8,0},{9,1},... | collective-permute-start | bytes 307208 | tf_op jit(solution)/shard_map/ppermute | solution.py:400
  41.1 4.4 %near.11.seed = f32[512,128]{1,0:T(8,128)S(1)} custom-call(f32[584,128]{1,0:T(8,128)S(1)} %get-tuple-element.48.weights, bf16[8192,16]{1,0:T(8,128)(2,1)S(1)} %get-tuple-element.52.left, f32[64,128]{1,0:T(8,128)S(1)} %get-tuple-element.53.source_heights.heights, bf16[1024,128]{1,0:T(8,128)(2,1)S(1)} %get-tuple-element.54.source_halves.halves, ...), custom_call_target="tpu_custom_call" | custom-call | flops 2904000000 | bytes 262144 | tf_op jit(solution)/shard_map/near/pallas_call | solution.py:356
  45.5 0.0 collective-permute-done.6.theirs
  45.5 0.0 copy-done.2
  45.6 2.9 %finish.1 = f32[512,128]{1,0:T(8,128)} custom-call(f32[584,128]{1,0:T(8,128)S(1)} %get-tuple-element.48.weights, f32[192,128]{1,0:T(8,128)S(1)} %bitcast.13, f32[272,128]{1,0:T(8,128)S(1)} %collective-permute-done.3.theirs.first, f32[200,128]{1,0:T(8,128)S(1)} %collective-permute-done.4.theirs.second, f32[200,128]{1,0:T(8,128)S(1)} %collective-permute-done.5.theirs.third, ...), custom_call_target="tpu_custom_call" | custom-call | flops 2000000000 | bytes 262144 | tf_op jit(solution)/shard_map/finish/pallas_call | solution.py:508
  (1 shorter events, 0.0 us)
Async XLA Ops:
  0.0 2.1 %copy-start.1 = (f32[3,4,16,128]{3,2,1,0:T(8,128)S(1)}, f32[3,4,16,128]{3,2,1,0:T(8,128)}, u32[]{:S(2)}) copy-start(f32[3,4,16,128]{3,2,1,0:T(8,128)} %param.7) | copy-start | bytes 294916
  0.0 2.1 %copy-start.4 = (f32[2,1,1,32,32]{4,3,2,1,0:T(8,128)S(1)}, f32[2,1,1,32,32]{4,3,2,1,0:T(8,128)}, u32[]{:S(2)}) copy-start(f32[2,1,1,32,32]{4,3,2,1,0:T(8,128)} %param.13) | copy-start | bytes 24580
  0.0 2.1 %copy-start.3 = (f32[2,1,1,32,32]{4,3,2,1,0:T(8,128)S(1)}, f32[2,1,1,32,32]{4,3,2,1,0:T(8,128)}, u32[]{:S(2)}) copy-start(f32[2,1,1,32,32]{4,3,2,1,0:T(8,128)} %param.12) | copy-start | bytes 24580
  0.0 2.1 %copy-start.5 = (s32[9,4,16]{2,1,0:T(4,128)S(1)}, s32[9,4,16]{2,1,0:T(4,128)}, u32[]{:S(2)}) copy-start(s32[9,4,16]{2,1,0:T(4,128)} %mask.1) | copy-start | bytes 6916
  2.0 1.6 %collective-permute-start = (f32[480,128]{1,0:T(8,128)S(1)}, f32[480,128]{1,0:T(8,128)S(1)}, u32[]{:S(2)}, u32[]{:S(2)}) collective-permute-start(f32[480,128]{1,0:T(8,128)S(1)} %get-tuple-element.49.mine), channel_id=1, source_target_pairs={{0,16},{16,0},{32,48},{48,32},{64,80},{80,64},{96,112},{112,96},{1... | collective-permute-start | bytes 737288 | tf_op jit(solution)/shard_map/ppermute | solution.py:400
  3.8 6.2 %collective-permute-start.1 = (f32[304,128]{1,0:T(8,128)S(1)}, f32[304,128]{1,0:T(8,128)S(1)}, u32[]{:S(2)}, u32[]{:S(2)}) collective-permute-start(f32[304,128]{1,0:T(8,128)S(1)} %level.5.mine), channel_id=1, source_target_pairs={{0,32},{16,48},{32,0},{48,16},{64,96},{80,112},{96,64},{112,80},{1... | collective-permute-start | bytes 466952 | tf_op jit(solution)/shard_map/ppermute | solution.py:400
  10.2 7.8 %copy-start = (f32[8,4,16,128]{3,2,1,0:T(8,128)S(1)}, f32[8,4,16,128]{3,2,1,0:T(8,128)}, u32[]{:S(2)}) copy-start(f32[8,4,16,128]{3,2,1,0:T(8,128)} %param.8) | copy-start | bytes 786436
  10.2 7.8 %collective-permute-start.2 = (f32[304,128]{1,0:T(8,128)S(1)}, f32[304,128]{1,0:T(8,128)S(1)}, u32[]{:S(2)}, u32[]{:S(2)}) collective-permute-start(f32[304,128]{1,0:T(8,128)S(1)} %level.6.mine), channel_id=1, source_target_pairs={{0,64},{16,80},{32,96},{48,112},{64,0},{80,16},{96,32},{112,48},{1... | collective-permute-start | bytes 466952 | tf_op jit(solution)/shard_map/ppermute | solution.py:400
  18.3 5.8 %collective-permute-start.3 = (f32[272,128]{1,0:T(8,128)S(1)}, f32[272,128]{1,0:T(8,128)S(1)}, u32[]{:S(2)}, u32[]{:S(2)}) collective-permute-start(f32[272,128]{1,0:T(8,128)S(1)} %get-tuple-element.72.mine), channel_id=1, source_target_pairs={{0,1},{1,0},{2,3},{3,2},{4,5},{5,4},{6,7},{7,6},{8,9},{9,8},{10,11... | collective-permute-start | bytes 417800 | tf_op jit(solution)/shard_map/ppermute | solution.py:400
  24.4 8.2 %collective-permute-start.4 = (f32[200,128]{1,0:T(8,128)S(1)}, f32[200,128]{1,0:T(8,128)S(1)}, u32[]{:S(2)}, u32[]{:S(2)}) collective-permute-start(f32[200,128]{1,0:T(8,128)S(1)} %level.7.mine), channel_id=1, source_target_pairs={{0,2},{1,3},{2,0},{3,1},{4,6},{5,7},{6,4},{7,5},{8,10},{9,11},{10,... | collective-permute-start | bytes 307208 | tf_op jit(solution)/shard_map/ppermute | solution.py:400
  32.8 4.7 %collective-permute-start.5 = (f32[200,128]{1,0:T(8,128)S(1)}, f32[200,128]{1,0:T(8,128)S(1)}, u32[]{:S(2)}, u32[]{:S(2)}) collective-permute-start(f32[200,128]{1,0:T(8,128)S(1)} %level.8.mine), channel_id=1, source_target_pairs={{0,4},{1,5},{2,6},{3,7},{4,0},{5,1},{6,2},{7,3},{8,12},{9,13},{10,... | collective-permute-start | bytes 307208 | tf_op jit(solution)/shard_map/ppermute | solution.py:400
  37.8 7.8 %copy-start.2 = (f32[4,16,32,128]{3,2,1,0:T(8,128)S(1)}, f32[4,16,32,128]{3,2,1,0:T(8,128)}, u32[]{:S(2)}) copy-start(f32[4,16,32,128]{3,2,1,0:T(8,128)} %param.11) | copy-start | bytes 3145732
  37.8 7.8 %collective-permute-start.6 = (f32[200,128]{1,0:T(8,128)S(1)}, f32[200,128]{1,0:T(8,128)S(1)}, u32[]{:S(2)}, u32[]{:S(2)}) collective-permute-start(f32[200,128]{1,0:T(8,128)S(1)} %level.9.mine), channel_id=1, source_target_pairs={{0,8},{1,9},{2,10},{3,11},{4,12},{5,13},{6,14},{7,15},{8,0},{9,1},... | collective-permute-start | bytes 307208 | tf_op jit(solution)/shard_map/ppermute | solution.py:400

commit v13 on v10

--- a/solution.py
+++ b/solution.py
@@ -478,9 +478,9 @@
     windows = row_bits + col_bits - 1
     edge_windows = (row_bits, row_bits + 2)
     inner_windows = [n for n in range(1, windows + 1) if n not in edge_windows]
-    parts = (72, 72, 64, 54)
+    parts = (64, 66, 64, 68)
     cuts = [counts[0] * sum(parts[:k]) // sum(parts) // 4 * 4 for k in range(len(parts))] + [counts[0]]
-    half = -(-counts[1] // 2 // 8) * 8
+    half = counts[1] // 2 // 8 * 8 + 12
     acc = jnp.zeros((leaves * rhs, points), f32)
     received = [theirs]
     for n, (axis, bit) in enumerate(zip(axes, bits)):
@@ -500,7 +500,7 @@
             else:
                 k = inner_windows.index(n)
                 acc = near_piece(listed(cut_runs(inner, cuts[k], cuts[k + 1])), weights, own, targets, acc)
-            if n == windows:
+            if n == edge_windows[1]:
                 acc = near_piece(functools.partial(column_items, True), weights, facing_tables, targets, acc)
             theirs, acc = lax.optimization_barrier((theirs, acc))
             received.append(theirs)

time: 49.4 us -> 48.7 us (0.986)
  Pallas kernels: 32.5 us -> 32 us
    pallas_call x7, Pallas kernels: 25.2 us -> 24.7 us  [near_piece(): pl.pallas_call(functools.partial(near_kernel, items, batch), out_shape=ja...]
  transfers between devices with their start and end apart: 7 -> 7, of which waited for: 2 -> 2; matrix products, arithmetic and copies ran while one was open for 0% -> 0% of each run, Pallas kernels for 55% -> 54%
where the time goes in v13:
time: 48.7 us; the launch traced here: 48.6 us
  Pallas kernels  32 us (66%)
  starting transfers between devices  15.7 us (32%)
  waiting for transfers between devices  0.74 us (2%)
    pallas_call x7, Pallas kernels, near_piece(): pl.pallas_call(functools.partial(near_kernel, items, batch), out_shape=ja...  24.7 us
    ppermute x7, starting transfers between devices, partner_of(): return lax.ppermute(block, axis, route)  15.7 us
    pallas_call x1, Pallas kernels, shards(): pl.pallas_call(finish_kernel, out_shape=array(rhs * leaves, points), in_s...  2.2 us
    pallas_call x1, Pallas kernels, far_call(): pl.pallas_call(body, out_shape=out_shape, in_specs=[pl.BlockSpec(memory_s...  1.94 us
    pallas_call x6, Pallas kernels, small_call(): pl.pallas_call(body, out_shape=out_shape, in_specs=[vmem] * len(operands)...  1.46 us
    pallas_call x1, Pallas kernels, shards(): pl.pallas_call(prep_kernel, out_shape=table_shapes(leaves)[:3] + (block_s...  1 us
  transfers between devices with their start and end apart: 7, of which 2 were waited for; matrix products, arithmetic and copies ran while one was open for 0% of the time, Pallas kernels for 54%

profile of v13, /device:TPU:0, one launch (start us, length us, event | category | flops | bytes accessed | tf_op | source)
XLA Modules:
  0.0 48.6 jit_solution(4099823613999481219)
XLA Ops:
  0.0 0.0 copy-start.1
  0.0 0.0 copy-start.4
  0.0 0.0 copy-start.3
  0.0 0.0 copy-start.5
  0.0 1.9 %compress.1 = (bf16[1024,128]{1,0:T(8,128)(2,1)S(1)}, f32[480,128]{1,0:T(8,128)S(1)}) custom-call(f32[192,128]{1,0:T(8,128)} %bitcast.9, f32[512,128]{1,0:T(8,128)} %bitcast.7, f32[2048,128]{1,0:T(8,128)} %bitcast.18), custom_call_target="tpu_custom_call" | custom-call | flops 800000000 | bytes 262144 | tf_op jit(solution)/shard_map/compress/pallas_call | solution.py:423
  2.0 0.1 collective-permute-start
  2.1 0.0 copy-done.1
  2.1 0.0 copy-done.4
  2.1 0.0 copy-done.3
  2.1 0.0 copy-done.5
  2.1 1.0 %prep.1 = (bf16[8192,16]{1,0:T(8,128)(2,1)S(1)}, bf16[1024,256]{1,0:T(8,128)(2,1)S(1)}, f32[64,128]{1,0:T(8,128)S(1)}, bf16[4,128,128]{2,1,0:T(8,128)(2,1)S(1)},...) custom-call(f32[192,128]{1,0:T(8,128)S(1)} %bitcast.10, s32[9,4,16]{2,1,0:T(4,128)S(1)} %copy-done.5, ...), custom_call_target="tpu_custom_call" | custom-call | flops 800000000 | bytes 262144 | tf_op jit(solution)/shard_map/prep/pallas_call | solution.py:465
  3.1 0.5 collective-permute-done.theirs.first
  3.5 0.2 level.5.mine
  3.8 1.8 %collective-permute-start.1 = (f32[304,128]{1,0:T(8,128)S(1)}, f32[304,128]{1,0:T(8,128)S(1)}, u32[]{:S(2)}, u32[]{:S(2)}) collective-permute-start(f32[304,128]{1,0:T(8,128)S(1)} %level.5.mine), channel_id=1, source_target_pairs={{0,32},{16,48},{32,0},{48,16},{64,96},{80,112},{96,64},{112,80},{1... | collective-permute-start | bytes 466952 | tf_op jit(solution)/shard_map/ppermute | solution.py:402
  5.6 4.1 %near.7.seed = f32[512,128]{1,0:T(8,128)S(1)} custom-call(f32[584,128]{1,0:T(8,128)S(1)} %get-tuple-element.53.weights, bf16[8192,16]{1,0:T(8,128)(2,1)S(1)} %get-tuple-element.57.left, f32[64,128]{1,0:T(8,128)S(1)} %get-tuple-element.58.source_heights.heights, bf16[1024,128]{1,0:T(8,128)(2,1)S(1)} %get-tuple-element.59.source_halves.halves, ...), custom_call_target="tpu_custom_call" | custom-call | flops 2816000000 | bytes 262144 | tf_op jit(solution)/shard_map/near/pallas_call | solution.py:358
  9.7 0.3 collective-permute-done.1.theirs.second
  9.9 0.2 level.6.mine
  10.2 0.0 copy-start
  10.2 3.4 %collective-permute-start.2 = (f32[304,128]{1,0:T(8,128)S(1)}, f32[304,128]{1,0:T(8,128)S(1)}, u32[]{:S(2)}, u32[]{:S(2)}) collective-permute-start(f32[304,128]{1,0:T(8,128)S(1)} %level.6.mine), channel_id=1, source_target_pairs={{0,64},{16,80},{32,96},{48,112},{64,0},{80,16},{96,32},{112,48},{1... | collective-permute-start | bytes 466952 | tf_op jit(solution)/shard_map/ppermute | solution.py:402
  13.6 4.4 %near.8.seed = f32[512,128]{1,0:T(8,128)S(1)} custom-call(f32[584,128]{1,0:T(8,128)S(1)} %get-tuple-element.53.weights, bf16[8192,16]{1,0:T(8,128)(2,1)S(1)} %get-tuple-element.57.left, f32[64,128]{1,0:T(8,128)S(1)} %get-tuple-element.58.source_heights.heights, bf16[1024,128]{1,0:T(8,128)(2,1)S(1)} %get-tuple-element.59.source_halves.halves, ...), custom_call_target="tpu_custom_call" | custom-call | flops 2816000000 | bytes 262144 | tf_op jit(solution)/shard_map/near/pallas_call | solution.py:358
  17.9 0.0 collective-permute-done.2.theirs
  17.9 0.0 copy-done
  17.9 0.3 turn.1
  18.2 2.2 %collective-permute-start.3 = (f32[272,128]{1,0:T(8,128)S(1)}, f32[272,128]{1,0:T(8,128)S(1)}, u32[]{:S(2)}, u32[]{:S(2)}) collective-permute-start(f32[272,128]{1,0:T(8,128)S(1)} %get-tuple-element.69.mine), channel_id=1, source_target_pairs={{0,1},{1,0},{2,3},{3,2},{4,5},{5,4},{6,7},{7,6},{8,9},{9,8},{10,11... | collective-permute-start | bytes 417800 | tf_op jit(solution)/shard_map/ppermute | solution.py:402
  20.4 0.5 edges.1
  20.9 3.4 %near.9.seed = f32[512,128]{1,0:T(8,128)S(1)} custom-call(f32[584,128]{1,0:T(8,128)S(1)} %get-tuple-element.53.weights, bf16[4096,16]{1,0:T(8,128)(2,1)S(1)} %get-tuple-element.73.left, f32[32,128]{1,0:T(8,128)S(1)} %get-tuple-element.74.source_heights, bf16[512,128]{1,0:T(8,128)(2,1)S(1)} %get-tuple-element.75.source_halves, ...), custom_call_target="tpu_custom_call" | custom-call | flops 2288000000 | bytes 262144 | tf_op jit(solution)/shard_map/near/pallas_call | solution.py:358
  24.3 0.0 collective-permute-done.3.theirs.first
  24.3 0.2 level.7.mine
  24.5 3.7 %collective-permute-start.4 = (f32[200,128]{1,0:T(8,128)S(1)}, f32[200,128]{1,0:T(8,128)S(1)}, u32[]{:S(2)}, u32[]{:S(2)}) collective-permute-start(f32[200,128]{1,0:T(8,128)S(1)} %level.7.mine), channel_id=1, source_target_pairs={{0,2},{1,3},{2,0},{3,1},{4,6},{5,7},{6,4},{7,5},{8,10},{9,11},{10,... | collective-permute-start | bytes 307208 | tf_op jit(solution)/shard_map/ppermute | solution.py:402
  28.2 4.3 %near.10.seed = f32[512,128]{1,0:T(8,128)S(1)} custom-call(f32[584,128]{1,0:T(8,128)S(1)} %get-tuple-element.53.weights, bf16[8192,16]{1,0:T(8,128)(2,1)S(1)} %get-tuple-element.57.left, f32[64,128]{1,0:T(8,128)S(1)} %get-tuple-element.58.source_heights.heights, bf16[1024,128]{1,0:T(8,128)(2,1)S(1)} %get-tuple-element.59.source_halves.halves, ...), custom_call_target="tpu_custom_call" | custom-call | flops 2816000000 | bytes 262144 | tf_op jit(solution)/shard_map/near/pallas_call | solution.py:358
  32.5 0.2 facing.1
  32.8 0.0 collective-permute-done.4.theirs.second
  32.8 0.2 level.8.mine
  33.0 1.8 %collective-permute-start.5 = (f32[200,128]{1,0:T(8,128)S(1)}, f32[200,128]{1,0:T(8,128)S(1)}, u32[]{:S(2)}, u32[]{:S(2)}) collective-permute-start(f32[200,128]{1,0:T(8,128)S(1)} %level.8.mine), channel_id=1, source_target_pairs={{0,4},{1,5},{2,6},{3,7},{4,0},{5,1},{6,2},{7,3},{8,12},{9,13},{10,... | collective-permute-start | bytes 307208 | tf_op jit(solution)/shard_map/ppermute | solution.py:402
  34.8 2.7 %near.11.seed = f32[512,128]{1,0:T(8,128)S(1)} custom-call(f32[584,128]{1,0:T(8,128)S(1)} %get-tuple-element.53.weights, bf16[4096,16]{1,0:T(8,128)(2,1)S(1)} %get-tuple-element.73.left, f32[32,128]{1,0:T(8,128)S(1)} %get-tuple-element.74.source_heights, bf16[512,128]{1,0:T(8,128)(2,1)S(1)} %get-tuple-element.75.source_halves, ...), custom_call_target="tpu_custom_call" | custom-call | flops 1760000000 | bytes 262144 | tf_op jit(solution)/shard_map/near/pallas_call | solution.py:358
  37.5 1.1 %near.12.seed = f32[512,128]{1,0:T(8,128)S(1)} custom-call(f32[584,128]{1,0:T(8,128)S(1)} %get-tuple-element.53.weights, bf16[1024,16]{1,0:T(8,128)(2,1)S(1)} %get-tuple-element.85.left, f32[8,128]{1,0:T(8,128)S(1)} %get-tuple-element.86.source_heights, bf16[128,128]{1,0:T(8,128)(2,1)S(1)} %get-tuple-element.87.source_halves, ...), custom_call_target="tpu_custom_call" | custom-call | flops 528000000 | bytes 262144 | tf_op jit(solution)/shard_map/near/pallas_call | solution.py:358
  38.5 0.0 collective-permute-done.5.theirs.third
  38.5 0.2 level.9.mine
  38.8 0.0 copy-start.2
  38.8 2.8 %collective-permute-start.6 = (f32[200,128]{1,0:T(8,128)S(1)}, f32[200,128]{1,0:T(8,128)S(1)}, u32[]{:S(2)}, u32[]{:S(2)}) collective-permute-start(f32[200,128]{1,0:T(8,128)S(1)} %level.9.mine), channel_id=1, source_target_pairs={{0,8},{1,9},{2,10},{3,11},{4,12},{5,13},{6,14},{7,15},{8,0},{9,1},... | collective-permute-start | bytes 307208 | tf_op jit(solution)/shard_map/ppermute | solution.py:402
  41.6 4.8 %near.13.seed = f32[512,128]{1,0:T(8,128)S(1)} custom-call(f32[584,128]{1,0:T(8,128)S(1)} %get-tuple-element.53.weights, bf16[8192,16]{1,0:T(8,128)(2,1)S(1)} %get-tuple-element.57.left, f32[64,128]{1,0:T(8,128)S(1)} %get-tuple-element.58.source_heights.heights, bf16[1024,128]{1,0:T(8,128)(2,1)S(1)} %get-tuple-element.59.source_halves.halves, ...), custom_call_target="tpu_custom_call" | custom-call | flops 3080000000 | bytes 262144 | tf_op jit(solution)/shard_map/near/pallas_call | solution.py:358
  46.4 0.0 collective-permute-done.6.theirs
  46.4 0.0 copy-done.2
  46.4 2.2 %finish.1 = f32[512,128]{1,0:T(8,128)} custom-call(f32[584,128]{1,0:T(8,128)S(1)} %get-tuple-element.53.weights, f32[192,128]{1,0:T(8,128)S(1)} %bitcast.14, f32[200,128]{1,0:T(8,128)S(1)} %collective-permute-done.4.theirs.second, f32[200,128]{1,0:T(8,128)S(1)} %collective-permute-done.5.theirs.third, f32[200,128]{1,0:T(8,128)S(1)} %collective-permute-done.6.theirs, ...), custom_call_target="tpu_custom_call" | custom-call | flops 2000000000 | bytes 262144 | tf_op jit(solution)/shard_map/finish/pallas_call | solution.py:520
  (1 shorter events, 0.0 us)
Async XLA Ops:
  0.0 2.1 %copy-start.1 = (f32[3,4,16,128]{3,2,1,0:T(8,128)S(1)}, f32[3,4,16,128]{3,2,1,0:T(8,128)}, u32[]{:S(2)}) copy-start(f32[3,4,16,128]{3,2,1,0:T(8,128)} %param.7) | copy-start | bytes 294916
  0.0 2.1 %copy-start.4 = (f32[2,1,1,32,32]{4,3,2,1,0:T(8,128)S(1)}, f32[2,1,1,32,32]{4,3,2,1,0:T(8,128)}, u32[]{:S(2)}) copy-start(f32[2,1,1,32,32]{4,3,2,1,0:T(8,128)} %param.13) | copy-start | bytes 24580
  0.0 2.1 %copy-start.3 = (f32[2,1,1,32,32]{4,3,2,1,0:T(8,128)S(1)}, f32[2,1,1,32,32]{4,3,2,1,0:T(8,128)}, u32[]{:S(2)}) copy-start(f32[2,1,1,32,32]{4,3,2,1,0:T(8,128)} %param.12) | copy-start | bytes 24580
  0.0 2.1 %copy-start.5 = (s32[9,4,16]{2,1,0:T(4,128)S(1)}, s32[9,4,16]{2,1,0:T(4,128)}, u32[]{:S(2)}) copy-start(s32[9,4,16]{2,1,0:T(4,128)} %mask.1) | copy-start | bytes 6916
  2.0 1.6 %collective-permute-start = (f32[480,128]{1,0:T(8,128)S(1)}, f32[480,128]{1,0:T(8,128)S(1)}, u32[]{:S(2)}, u32[]{:S(2)}) collective-permute-start(f32[480,128]{1,0:T(8,128)S(1)} %get-tuple-element.54.mine), channel_id=1, source_target_pairs={{0,16},{16,0},{32,48},{48,32},{64,80},{80,64},{96,112},{112,96},{1... | collective-permute-start | bytes 737288 | tf_op jit(solution)/shard_map/ppermute | solution.py:402
  3.8 6.1 %collective-permute-start.1 = (f32[304,128]{1,0:T(8,128)S(1)}, f32[304,128]{1,0:T(8,128)S(1)}, u32[]{:S(2)}, u32[]{:S(2)}) collective-permute-start(f32[304,128]{1,0:T(8,128)S(1)} %level.5.mine), channel_id=1, source_target_pairs={{0,32},{16,48},{32,0},{48,16},{64,96},{80,112},{96,64},{112,80},{1... | collective-permute-start | bytes 466952 | tf_op jit(solution)/shard_map/ppermute | solution.py:402
  10.2 7.8 %copy-start = (f32[8,4,16,128]{3,2,1,0:T(8,128)S(1)}, f32[8,4,16,128]{3,2,1,0:T(8,128)}, u32[]{:S(2)}) copy-start(f32[8,4,16,128]{3,2,1,0:T(8,128)} %param.8) | copy-start | bytes 786436
  10.2 7.7 %collective-permute-start.2 = (f32[304,128]{1,0:T(8,128)S(1)}, f32[304,128]{1,0:T(8,128)S(1)}, u32[]{:S(2)}, u32[]{:S(2)}) collective-permute-start(f32[304,128]{1,0:T(8,128)S(1)} %level.6.mine), channel_id=1, source_target_pairs={{0,64},{16,80},{32,96},{48,112},{64,0},{80,16},{96,32},{112,48},{1... | collective-permute-start | bytes 466952 | tf_op jit(solution)/shard_map/ppermute | solution.py:402
  18.2 6.1 %collective-permute-start.3 = (f32[272,128]{1,0:T(8,128)S(1)}, f32[272,128]{1,0:T(8,128)S(1)}, u32[]{:S(2)}, u32[]{:S(2)}) collective-permute-start(f32[272,128]{1,0:T(8,128)S(1)} %get-tuple-element.69.mine), channel_id=1, source_target_pairs={{0,1},{1,0},{2,3},{3,2},{4,5},{5,4},{6,7},{7,6},{8,9},{9,8},{10,11... | collective-permute-start | bytes 417800 | tf_op jit(solution)/shard_map/ppermute | solution.py:402
  24.5 8.2 %collective-permute-start.4 = (f32[200,128]{1,0:T(8,128)S(1)}, f32[200,128]{1,0:T(8,128)S(1)}, u32[]{:S(2)}, u32[]{:S(2)}) collective-permute-start(f32[200,128]{1,0:T(8,128)S(1)} %level.7.mine), channel_id=1, source_target_pairs={{0,2},{1,3},{2,0},{3,1},{4,6},{5,7},{6,4},{7,5},{8,10},{9,11},{10,... | collective-permute-start | bytes 307208 | tf_op jit(solution)/shard_map/ppermute | solution.py:402
  33.0 5.5 %collective-permute-start.5 = (f32[200,128]{1,0:T(8,128)S(1)}, f32[200,128]{1,0:T(8,128)S(1)}, u32[]{:S(2)}, u32[]{:S(2)}) collective-permute-start(f32[200,128]{1,0:T(8,128)S(1)} %level.8.mine), channel_id=1, source_target_pairs={{0,4},{1,5},{2,6},{3,7},{4,0},{5,1},{6,2},{7,3},{8,12},{9,13},{10,... | collective-permute-start | bytes 307208 | tf_op jit(solution)/shard_map/ppermute | solution.py:402
  38.8 7.6 %copy-start.2 = (f32[4,16,32,128]{3,2,1,0:T(8,128)S(1)}, f32[4,16,32,128]{3,2,1,0:T(8,128)}, u32[]{:S(2)}) copy-start(f32[4,16,32,128]{3,2,1,0:T(8,128)} %param.11) | copy-start | bytes 3145732
  38.8 7.6 %collective-permute-start.6 = (f32[200,128]{1,0:T(8,128)S(1)}, f32[200,128]{1,0:T(8,128)S(1)}, u32[]{:S(2)}, u32[]{:S(2)}) collective-permute-start(f32[200,128]{1,0:T(8,128)S(1)} %level.9.mine), channel_id=1, source_target_pairs={{0,8},{1,9},{2,10},{3,11},{4,12},{5,13},{6,14},{7,15},{8,0},{9,1},... | collective-permute-start | bytes 307208 | tf_op jit(solution)/shard_map/ppermute | solution.py:402
